TPU v7x, 32 devices: a whole 2x2x4 slice. The times are simulated.
32 devices in a mesh: groups: 2 (over y), st: 4 (over x, core), ch: 4 (over z).
Axes of the slice: x: 2, y: 2, z: 4, core: 2. Of those that a mesh axis runs over, the one named last changes fastest.
Arguments:
- latents: bfloat16 [1280, 1024], P('ch', ('groups', 'st')), parts along dimension 1, may hold values from -6 to 6
- spatial_weight: bfloat16 [9, 1280, 1280], P(None, 'ch'), may hold values from -0.0546875 to 0.0546875
- temporal_weight: bfloat16 [3, 1280, 1280], P(None, 'ch'), may hold values from -0.09375 to 0.09375
- cotangent: bfloat16 [1280, 1024], P('ch', ('groups', 'st')), parts along dimension 1, may hold values from -6 to 6
Outputs:
- temporal_out: bfloat16 [1280, 1024], P('ch', ('groups', 'st')), parts along dimension 1
- latent_grad: bfloat16 [1280, 1024], P('ch', ('groups', 'st')), parts along dimension 1
- spatial_grad: float32 [18, 1280, 1280], P('groups', 'ch', 'st'), parts along dimension 0
- temporal_grad: float32 [6, 1280, 1280], P('groups', 'ch', 'st'), parts along dimension 0
There are 2 independent parts, one for each index of `groups`. A program takes and returns all parts, laid end to end along the dimension named above; an argument that names none is the same for every part. Nothing has to cross between parts.
All inputs are finite; a program needn't handle non-finite values.
Results may differ from a plain program's by a relative error of at most 0.008.
Values may be sent and summed in bfloat16 or wider, within the bound.
No kernel may reach another device: no remote copies, remote signals or barrier semaphores. Data moves between devices by JAX's collectives and lax.ppermute only.
A program may use at most 192 MiB of HBM per device.

v0:
```python
import math

import jax
import jax.numpy as jnp
from jax import lax
from jax.sharding import PartitionSpec as P

FT = 2
RT = 2
W = 32
RBANDS = 2


spatial_offsets = tuple(
    ((row_step, col_step) for row_step in (-1, 0, 1) for col_step in (-1, 0, 1))
)
frame_offsets = (-1, 0, 1)


def passed_along(shard, axis, by):
    devices = lax.axis_size(axis)
    pairs = [(i, i + by) for i in range(devices) if 0 <= i + by < devices]
    return lax.ppermute(shard, axis, pairs)


def neighbour(slab, distance):
    return passed_along(slab, "st", distance)


def circulate(data, fold, initial):
    return fold(initial, lax.all_gather(data, "ch", axis=0, tiled=True), jnp.int32(0))


def regather(data, build):
    return build(lax.all_gather(data, "ch", axis=0, tiled=True), jnp.int32(0))


def pad_rows(field):
    channels = field.shape[0]
    layered = field.reshape(channels, FT, RT * W)
    band = lax.axis_index("st") % RBANDS
    upper = neighbour(layered[:, :, (RT - 1) * W :], 1)
    lower = neighbour(layered[:, :, :W], -1)
    upper = jnp.where(band > 0, upper, jnp.zeros_like(upper))
    lower = jnp.where(band < RBANDS - 1, lower, jnp.zeros_like(lower))
    margin = jnp.zeros((channels, FT, 1), field.dtype)
    return jnp.concatenate([margin, upper, layered, lower, margin], axis=2)


def spatial_piece(padded, row_step, col_step):
    first_cell = 1 + (1 + row_step) * W + col_step
    window = lax.slice_in_dim(padded, first_cell, first_cell + RT * W, axis=2)
    column = jnp.arange(RT * W, dtype=jnp.int32) % W + col_step
    inside = (column >= 0) & (column < W)
    window = jnp.where(inside, window, jnp.zeros_like(window))
    return window.reshape(padded.shape[0], FT * RT * W)


def pad_frames(field):
    frame_cells = RT * W
    earlier = neighbour(field[:, (FT - 1) * frame_cells :], RBANDS)
    following = neighbour(field[:, :frame_cells], -RBANDS)
    return jnp.concatenate([earlier, field, following], axis=1)


def frame_piece(padded, frame_step):
    frame_cells = RT * W
    first_cell = (1 + frame_step) * frame_cells
    return lax.slice_in_dim(padded, first_cell, first_cell + FT * frame_cells, axis=1)


def contract(weights, pieces):
    running = jnp.dot(weights[0], pieces[0], preferred_element_type=jnp.float32)
    for position in range(1, len(pieces)):
        running = running + jnp.dot(
            weights[position], pieces[position], preferred_element_type=jnp.float32
        )
    return running


def outer_sums(gradient, pieces):
    contraction = (((1,), (1,)), ((), ()))
    return jnp.stack(
        [
            lax.dot_general(gradient, tap_piece, contraction, preferred_element_type=jnp.float32)
            for tap_piece in pieces
        ]
    )


def on_device(latents, spatial_weight, temporal_weight, cotangent):
    channels, tile_cells = latents.shape
    grad_scale = 1.0 / math.sqrt(tile_cells * lax.axis_size("st"))
    spatial_back, temporal_back = (
        lax.all_to_all(
            jnp.transpose(spatial_weight, (0, 2, 1)), "ch", split_axis=1, concat_axis=2, tiled=True
        ),
        lax.all_to_all(
            jnp.transpose(temporal_weight, (0, 2, 1)), "ch", split_axis=1, concat_axis=2, tiled=True
        ),
    )
    empty_sum = jnp.zeros((channels, tile_cells), jnp.float32)
    latent_pad = pad_rows(latents)
    latent_store = jnp.zeros((1,), jnp.bfloat16)

    def spatial_forward(carry, portion, offset):
        running, stored = carry
        running = contract(
            spatial_weight,
            [spatial_piece(portion, row_step, col_step) for row_step, col_step in spatial_offsets],
        )
        return (running, stored)

    spatial_sum, latent_store = circulate(latent_pad, spatial_forward, (empty_sum, latent_store))
    hidden = (latents.astype(jnp.float32) + spatial_sum).astype(jnp.bfloat16)
    hidden_pad = pad_frames(hidden)
    hidden_store = jnp.zeros((1,), jnp.bfloat16)

    def temporal_forward(carry, portion, offset):
        running, stored = carry
        running = contract(
            temporal_weight, [frame_piece(portion, frame_step) for frame_step in frame_offsets]
        )
        return (running, stored)

    temporal_sum, hidden_store = circulate(hidden_pad, temporal_forward, (empty_sum, hidden_store))
    temporal_out = (hidden.astype(jnp.float32) + temporal_sum).astype(jnp.bfloat16)
    upstream_pad = pad_frames(cotangent)

    def temporal_backward(running, portion, offset):
        return contract(
            temporal_back, [frame_piece(portion, -frame_step) for frame_step in frame_offsets]
        )

    hidden_back = circulate(upstream_pad, temporal_backward, empty_sum)

    def temporal_terms(portion, offset):
        return outer_sums(
            cotangent, [frame_piece(portion, frame_step) for frame_step in frame_offsets]
        )

    temporal_grads = regather(hidden_pad, temporal_terms)
    hidden_grad = (cotangent.astype(jnp.float32) + hidden_back).astype(jnp.bfloat16)
    grad_pad = pad_rows(hidden_grad)

    def spatial_backward(running, portion, offset):
        return contract(
            spatial_back,
            [
                spatial_piece(portion, -row_step, -col_step)
                for row_step, col_step in spatial_offsets
            ],
        )

    latent_back = circulate(grad_pad, spatial_backward, empty_sum)

    def spatial_terms(portion, offset):
        return outer_sums(
            hidden_grad,
            [spatial_piece(portion, row_step, col_step) for row_step, col_step in spatial_offsets],
        )

    spatial_grads = regather(latent_pad, spatial_terms)
    latent_grad = (hidden_grad.astype(jnp.float32) + latent_back).astype(jnp.bfloat16)
    spatial_total, temporal_total = (
        lax.psum_scatter(
            spatial_grads.astype(jnp.bfloat16), "st", scatter_dimension=2, tiled=True
        ).astype(jnp.float32),
        lax.psum_scatter(
            temporal_grads.astype(jnp.bfloat16), "st", scatter_dimension=2, tiled=True
        ).astype(jnp.float32),
    )
    return (temporal_out, latent_grad, spatial_total * grad_scale, temporal_total * grad_scale)


def solution(mesh):
    return jax.shard_map(
        on_device,
        mesh=mesh,
        in_specs=(
            P("ch", ("groups", "st")),
            P(None, "ch", None),
            P(None, "ch", None),
            P("ch", ("groups", "st")),
        ),
        out_specs=(
            P("ch", ("groups", "st")),
            P("ch", ("groups", "st")),
            P("groups", "ch", "st"),
            P("groups", "ch", "st"),
        ),
        check_vma=False,
    )
```

profile of v0, /device:TPU:0, one launch (start us, length us, event | category | flops | bytes accessed | tf_op | source)
XLA Modules:
  0.0 649.0 jit_solution(954349262117856633)
XLA Ops:
  7.2 7.7 %copy.23 = bf16[3,320,1280]{1,0,2:T(4,128)(2,1)} copy(bf16[3,320,1280]{2,1,0:T(8,128)(2,1)} %param.6) | data formatting | bytes 4915200 | tf_op args[2]
  14.9 6.3 all-to-all-start
  22.6 4.6 collective-permute-start.4
  30.0 1.7 collective-permute-done.1
  33.0 87.4 %all_gather.16 = bf16[1280,256]{1,0:T(8,128)(2,1)S(1)} all-gather(bf16[320,256]{1,0:T(8,128)(2,1)S(1)} %pad_maximum_fusion.2), channel_id=1, replica_groups=mesh['groups'=2,'st'=4,'ch'=4] {'ch'}, dimensions={0}, use_global_device_ids=true | all-gather | bytes 819200 | tf_op jit(solution)/shard_map/all_gather | solution.py:31
  120.4 24.1 %all_gather.14 = bf16[1280,2,130]{2,1,0:T(2,128)(2,1)S(1)} all-gather(bf16[320,2,130]{2,1,0:T(2,128)(2,1)S(1)} %copy.13), channel_id=1, replica_groups=mesh['groups'=2,'st'=4,'ch'=4] {'ch'}, dimensions={0}, use_global_device_ids=true | all-gather | bytes 832000 | tf_op jit(solution)/shard_map/all_gather | solution.py:31
  144.4 4.9 copy.63
  149.3 2.3 fusion.70
  151.6 2.8 squeeze.85
  154.4 2.8 squeeze.84
  157.1 1.7 squeeze.86
  158.8 1.6 fusion.60
  161.9 1.5 fusion.29
  163.6 1.8 collective-permute-start.6
  165.4 6.9 %fusion.72 = (bf16[1280,2,64]{2,1,0:T(2,128)(2,1)S(1)}, bf16[1280,2,64]{2,1,0:T(2,128)(2,1)}, bf16[1280,2,64]{2,1,0:T(2,128)(2,1)}, bf16[1280,2,64]{2,1,0:T(2,12...) fusion(bf16[1280,2,130]{2,1,0:T(2,128)(2,1)S(1)} %all_gather.14), kind=kLoop, calls=%fused_computation.137 | loop fusion | bytes 5898240 | tf_op jit(solution)/shard_map/slice | solution.py:52
  172.3 2.0 copy.45
  174.4 2.0 copy.48
  176.4 2.0 copy.42
  178.4 2.0 copy.46
  180.4 2.0 copy.49
  182.4 2.0 copy.43
  184.5 2.0 copy.47
  190.0 3.7 collective-permute-done.7
  194.7 24.4 %all_gather.17 = bf16[1280,2,130]{2,1,0:T(2,128)(2,1)S(1)} all-gather(bf16[320,2,130]{2,1,0:T(2,128)(2,1)S(1)} %copy.26), channel_id=1, replica_groups=mesh['groups'=2,'st'=4,'ch'=4] {'ch'}, dimensions={0}, use_global_device_ids=true | all-gather | bytes 832000 | tf_op jit(solution)/shard_map/all_gather | solution.py:31
  219.1 6.9 %fusion.71 = (bf16[1280,2,64]{2,1,0:T(2,128)(2,1)S(1)}, bf16[1280,2,64]{2,1,0:T(2,128)(2,1)}, bf16[1280,2,64]{2,1,0:T(2,128)(2,1)}, bf16[1280,2,64]{2,1,0:T(2,12...) fusion(bf16[1280,2,130]{2,1,0:T(2,128)(2,1)S(1)} %all_gather.17), kind=kLoop, calls=%fused_computation.136 | loop fusion | bytes 5898240 | tf_op jit(solution)/shard_map/slice | solution.py:52
  229.3 2.2 copy.58
  231.5 2.0 copy.52
  233.5 2.0 copy.55
  235.5 2.0 copy.57
  237.5 2.0 copy.51
  239.5 2.0 copy.54
  241.6 2.7 broadcast_select_fusion.12
  246.5 2.5 broadcast_select_fusion.6
  254.7 4.6 collective-permute-start.2
  259.8 1.6 collective-permute-done.2
  261.5 17.6 %all_gather.15 = bf16[1280,256]{1,0:T(8,128)(2,1)S(1)} all-gather(bf16[320,256]{1,0:T(8,128)(2,1)S(1)} %pad_maximum_fusion.1), channel_id=1, replica_groups=mesh['groups'=2,'st'=4,'ch'=4] {'ch'}, dimensions={0}, use_global_device_ids=true | all-gather | bytes 819200 | tf_op jit(solution)/shard_map/all_gather | solution.py:31
  280.7 6.0 copy.40
  286.7 8.3 %reshape.123 = bf16[1280,960]{1,0:T(8,128)(2,1)} reshape(bf16[1280,3,320]{2,1,0:T(4,128)(2,1)} %bitcast.203) | data formatting | bytes 4915200
  295.1 20.9 %copy.28 = bf16[9,320,1280]{1,0,2:T(8,128)(2,1)} copy(bf16[9,320,1280]{2,1,0:T(8,128)(2,1)} %param.5) | data formatting | bytes 14745600 | tf_op args[1]
  327.6 20.2 %copy.38 = bf16[9,320,1280]{1,0,2:T(8,128)(2,1)} copy(bf16[9,320,1280]{2,1,0:T(8,128)(2,1)} %fusion.17) | data formatting | bytes 14745600
  347.8 18.7 %reshape.121 = bf16[1280,2880]{1,0:T(8,128)(2,1)} reshape(bf16[1280,9,320]{2,1,0:T(8,128)(2,1)} %bitcast.197) | data formatting | bytes 14745600
  366.5 14.2 %bitcast_bitcast_fusion = bf16[1280,9,320]{2,1,0:T(8,128)(2,1)} fusion(bf16[9,320,1280]{1,0,2:T(8,128)(2,1)} %copy.28), kind=kLoop, calls=%fused_computation.142 | loop fusion | bytes 14745600
  380.7 15.3 %reshape.125 = bf16[4,2,460800]{2,1,0:T(2,128)(2,1)} reshape(bf16[1280,9,320]{2,1,0:T(8,128)(2,1)} %bitcast_bitcast_fusion) | data formatting | bytes 14745600
  396.1 5.8 all-to-all-start.1
  403.8 2.5 reshape.124
  408.7 152.5 %all-to-all-done.1 = bf16[4,2,460800]{2,1,0:T(2,128)(2,1)} async-done(((bf16[4,2,460800]{2,1,0:T(2,128)(2,1)}), bf16[4,2,460800]{2,1,0:T(2,128)(2,1)}, u32[]{:S(2)}, u32[]{:S(2)}) %all-to-all-start.1) | async-done | bytes 7372832 | tf_op jit(solution)/shard_map/all_to_all | solution.py:95
  561.2 16.0 %reshape.126 = bf16[1280,9,320]{2,1,0:T(8,128)(2,1)} reshape(bf16[4,2,460800]{2,1,0:T(2,128)(2,1)} %all-to-all-done.1) | data formatting | bytes 14745600
  577.1 12.7 %copy.62 = bf16[9,4,320,320]{3,1,2,0:T(4,128)(2,1)S(1)} copy(bf16[9,4,320,320]{3,0,2,1:T(8,128)(2,1)} %bitcast.198) | data formatting | bytes 14745600 | tf_op jit(solution)/shard_map/all_to_all | solution.py:95
  589.9 4.4 fusion.69
  594.3 2.8 squeeze.87
  597.0 2.8 squeeze.88
  599.8 2.8 squeeze.89
  602.6 3.0 squeeze.90
  605.6 2.8 squeeze.91
  608.3 2.8 squeeze.92
  611.1 1.7 squeeze.93
  614.3 1.7 fusion.77
  616.1 1.6 convolution_add_fusion.11
  617.7 1.6 convolution_add_fusion.10
  619.3 1.6 convolution_add_fusion.9
  620.9 1.6 convolution_add_fusion.8
  627.7 5.6 reshape.122
  633.3 6.0 copy.39
  639.3 2.5 convert_multiply_fusion
  (142 shorter events, 47.3 us)
Async XLA Ops:
  7.2 14.0 %copy-start = (bf16[320,128]{1,0:T(8,128)(2,1)S(1)}, bf16[320,128]{1,0:T(8,128)(2,1)}, u32[]{:S(2)}) copy-start(bf16[320,128]{1,0:T(8,128)(2,1)} %param.7) | copy-start | bytes 245764
  7.2 20.0 %copy-start.29 = (bf16[320,128]{1,0:T(8,128)(2,1)S(1)}, bf16[320,128]{1,0:T(8,128)(2,1)}, u32[]{:S(2)}) copy-start(bf16[320,128]{1,0:T(8,128)(2,1)} %param.4) | copy-start | bytes 245764
  14.9 129.6 %all-to-all-start = ((bf16[3,1280,320]{2,0,1:T(4,128)(2,1)}), bf16[3,1280,320]{2,0,1:T(4,128)(2,1)}, u32[]{:S(2)}, u32[]{:S(2)}) async-start(bf16[3,1280,320]{2,0,1:T(4,128)(2,1)} %bitcast.202), calls=%async_computation | async-start | bytes 7864320 | tf_op jit(solution)/shard_map/all_to_all | solution.py:98
  21.2 382.6 %reduce-scatter.9.cloned.1.call-start = ((), (), s32[]{:S(2)}) async-start(), calls=%async_computation.5 | async-start | bytes 3276800
  21.3 11.5 %collective-permute-start.5 = (bf16[320,64]{1,0:T(8,128)(2,1)S(1)}, bf16[320,64]{1,0:T(8,128)(2,1)S(1)}, u32[]{:S(2)}, u32[]{:S(2)}) collective-permute-start(bf16[320,64]{1,0:T(8,128)(2,1)S(1)} %get-tuple-element.39), channel_id=1, source_target_pairs={{8,0},{12,4},{9,1},{13,5},{10,2},{14,6},{11,3},{15,7},{24,16},{28,... | collective-permute-start | bytes 122888 | tf_op jit(solution)/shard_map/ppermute | solution.py:23
  22.6 10.2 %collective-permute-start.4 = (bf16[320,64]{1,0:T(8,128)(2,1)S(1)}, bf16[320,64]{1,0:T(8,128)(2,1)S(1)}, u32[]{:S(2)}, u32[]{:S(2)}) collective-permute-start(bf16[320,64]{1,0:T(8,128)(2,1)S(1)} %get-tuple-element.38), channel_id=1, source_target_pairs={{0,8},{4,12},{1,9},{5,13},{2,10},{6,14},{3,11},{7,15},{16,24},{20,... | collective-permute-start | bytes 122888 | tf_op jit(solution)/shard_map/ppermute | solution.py:23
  27.3 2.7 collective-permute-start
  28.6 3.1 collective-permute-start.1
  163.6 26.4 %collective-permute-start.6 = (bf16[320,2,32]{0,2,1:T(8,128)(2,1)S(1)}, bf16[320,2,32]{0,2,1:T(8,128)(2,1)S(1)}, u32[]{:S(2)}, u32[]{:S(2)}) collective-permute-start(bf16[320,2,32]{0,2,1:T(8,128)(2,1)S(1)} %get-tuple-element.35), channel_id=1, source_target_pairs={{0,4},{4,8},{8,12},{1,5},{5,9},{9,13},{2,6},{6,10},{10,14},{3,7},{... | collective-permute-start | bytes 122888 | tf_op jit(solution)/shard_map/ppermute | solution.py:23
  188.7 5.0 collective-permute-start.7
  229.3 19.7 %slice-start = ((s8[7372800]{0:T(1024)(128)(4,1)}), s8[3178496]{0:T(1024)(128)(4,1)S(1)}, s32[]{:S(2)}) async-start(s8[7372800]{0:T(1024)(128)(4,1)} %bitcast.200), calls=%async_computation.6 | async-start | bytes 6356992
  241.5 7.5 %slice-start.1 = ((s8[7372800]{0:T(1024)(128)(4,1)}), s8[4194304]{0:T(1024)(128)(4,1)S(1)}, s32[]{:S(2)}) async-start(s8[7372800]{0:T(1024)(128)(4,1)} %bitcast.200), calls=%async_computation.7 | async-start | bytes 8388608
  241.5 7.9 %copy-start.21 = (bf16[1280,2,64]{0,2,1:T(8,128)(2,1)S(1)}, bf16[1280,2,64]{0,2,1:T(8,128)(2,1)}, u32[]{:S(2)}) copy-start(bf16[1280,2,64]{0,2,1:T(8,128)(2,1)} %copy.47) | copy-start | bytes 983044
  241.5 7.9 %copy-start.22 = (bf16[1280,2,64]{0,2,1:T(8,128)(2,1)S(1)}, bf16[1280,2,64]{0,2,1:T(8,128)(2,1)}, u32[]{:S(2)}) copy-start(bf16[1280,2,64]{0,2,1:T(8,128)(2,1)} %copy.50) | copy-start | bytes 983044
  241.5 7.9 %copy-start.23 = (bf16[1280,2,64]{0,2,1:T(8,128)(2,1)S(1)}, bf16[1280,2,64]{0,2,1:T(8,128)(2,1)}, u32[]{:S(2)}) copy-start(bf16[1280,2,64]{0,2,1:T(8,128)(2,1)} %copy.44) | copy-start | bytes 983044
  241.6 7.9 %copy-start.26 = (bf16[1280,2,64]{0,2,1:T(8,128)(2,1)S(1)}, bf16[1280,2,64]{0,2,1:T(8,128)(2,1)}, u32[]{:S(2)}) copy-start(bf16[1280,2,64]{0,2,1:T(8,128)(2,1)} %copy.57) | copy-start | bytes 983044
  241.6 7.9 %copy-start.27 = (bf16[1280,2,64]{0,2,1:T(8,128)(2,1)S(1)}, bf16[1280,2,64]{0,2,1:T(8,128)(2,1)}, u32[]{:S(2)}) copy-start(bf16[1280,2,64]{0,2,1:T(8,128)(2,1)} %copy.51) | copy-start | bytes 983044
  241.6 7.9 %copy-start.28 = (bf16[1280,2,64]{0,2,1:T(8,128)(2,1)S(1)}, bf16[1280,2,64]{0,2,1:T(8,128)(2,1)}, u32[]{:S(2)}) copy-start(bf16[1280,2,64]{0,2,1:T(8,128)(2,1)} %copy.54) | copy-start | bytes 983044
  244.3 0.7 copy-start.19
  244.3 7.5 %copy-start.5 = (bf16[1280,2,64]{0,2,1:T(8,128)(2,1)}, bf16[1280,2,64]{0,2,1:T(8,128)(2,1)S(1)}, u32[]{:S(2)}) copy-start(bf16[1280,2,64]{0,2,1:T(8,128)(2,1)S(1)} %get-tuple-element.43) | copy-start | bytes 983044
  244.3 7.9 %copy-start.3 = (bf16[1280,2,64]{0,2,1:T(8,128)(2,1)}, bf16[1280,2,64]{0,2,1:T(8,128)(2,1)S(1)}, u32[]{:S(2)}) copy-start(bf16[1280,2,64]{0,2,1:T(8,128)(2,1)S(1)} %get-tuple-element.44) | copy-start | bytes 983044
  249.0 4.3 copy-start.7
  249.0 4.3 copy-start.9
  249.0 4.3 copy-start.11
  250.6 29.4 %copy-start.13 = (bf16[1280,2,64]{0,2,1:T(8,128)(2,1)}, bf16[1280,2,64]{0,2,1:T(8,128)(2,1)S(1)}, u32[]{:S(2)}) copy-start(bf16[1280,2,64]{0,2,1:T(8,128)(2,1)S(1)} %get-tuple-element.55) | copy-start | bytes 983044
  250.6 29.4 %copy-start.15 = (bf16[1280,2,64]{0,2,1:T(8,128)(2,1)}, bf16[1280,2,64]{0,2,1:T(8,128)(2,1)S(1)}, u32[]{:S(2)}) copy-start(bf16[1280,2,64]{0,2,1:T(8,128)(2,1)S(1)} %get-tuple-element.59) | copy-start | bytes 983044
  250.6 29.4 %copy-start.24 = (bf16[1280,2,64]{0,2,1:T(8,128)(2,1)}, bf16[1280,2,64]{0,2,1:T(8,128)(2,1)S(1)}, u32[]{:S(2)}) copy-start(bf16[1280,2,64]{0,2,1:T(8,128)(2,1)S(1)} %get-tuple-element.56) | copy-start | bytes 983044
  253.4 6.3 collective-permute-start.3
  254.7 6.6 %collective-permute-start.2 = (bf16[320,64]{1,0:T(8,128)(2,1)S(1)}, bf16[320,64]{1,0:T(8,128)(2,1)S(1)}, u32[]{:S(2)}, u32[]{:S(2)}) collective-permute-start(bf16[320,64]{1,0:T(8,128)(2,1)S(1)} %get-tuple-element.40), channel_id=1, source_target_pairs={{0,8},{4,12},{1,9},{5,13},{2,10},{6,14},{3,11},{7,15},{16,24},{20,... | collective-permute-start | bytes 122888 | tf_op jit(solution)/shard_map/ppermute | solution.py:23
  295.0 21.0 %copy-start.20 = (bf16[1280,2,64]{0,2,1:T(8,128)(2,1)S(1)}, bf16[1280,2,64]{0,2,1:T(8,128)(2,1)}, u32[]{:S(2)}) copy-start(bf16[1280,2,64]{0,2,1:T(8,128)(2,1)} %copy-done.19) | copy-start | bytes 983044
  295.0 22.3 %copy-start.12 = (bf16[1280,2,64]{0,2,1:T(8,128)(2,1)S(1)}, bf16[1280,2,64]{0,2,1:T(8,128)(2,1)}, u32[]{:S(2)}) copy-start(bf16[1280,2,64]{0,2,1:T(8,128)(2,1)} %copy-done.11) | copy-start | bytes 983044
  295.0 23.6 %copy-start.16 = (bf16[1280,2,64]{0,2,1:T(8,128)(2,1)S(1)}, bf16[1280,2,64]{0,2,1:T(8,128)(2,1)}, u32[]{:S(2)}) copy-start(bf16[1280,2,64]{0,2,1:T(8,128)(2,1)} %copy-done.15) | copy-start | bytes 983044
  295.1 24.9 %copy-start.6 = (bf16[1280,2,64]{0,2,1:T(8,128)(2,1)S(1)}, bf16[1280,2,64]{0,2,1:T(8,128)(2,1)}, u32[]{:S(2)}) copy-start(bf16[1280,2,64]{0,2,1:T(8,128)(2,1)} %copy-done.5) | copy-start | bytes 983044
  295.1 26.1 %copy-start.10 = (bf16[1280,2,64]{0,2,1:T(8,128)(2,1)S(1)}, bf16[1280,2,64]{0,2,1:T(8,128)(2,1)}, u32[]{:S(2)}) copy-start(bf16[1280,2,64]{0,2,1:T(8,128)(2,1)} %copy-done.9) | copy-start | bytes 983044
  295.1 27.4 %copy-start.14 = (bf16[1280,2,64]{0,2,1:T(8,128)(2,1)S(1)}, bf16[1280,2,64]{0,2,1:T(8,128)(2,1)}, u32[]{:S(2)}) copy-start(bf16[1280,2,64]{0,2,1:T(8,128)(2,1)} %copy-done.13) | copy-start | bytes 983044
  295.1 332.6 %reduce-scatter.7.cloned.1.call-start = ((), (), s32[]{:S(2)}) async-start(), calls=%async_computation.4 | async-start | bytes 9420800
  316.0 7.7 %copy-start.4 = (bf16[1280,2,64]{0,2,1:T(8,128)(2,1)S(1)}, bf16[1280,2,64]{0,2,1:T(8,128)(2,1)}, u32[]{:S(2)}) copy-start(bf16[1280,2,64]{0,2,1:T(8,128)(2,1)} %copy-done.3) | copy-start | bytes 983044
  316.0 9.0 %copy-start.8 = (bf16[1280,2,64]{0,2,1:T(8,128)(2,1)S(1)}, bf16[1280,2,64]{0,2,1:T(8,128)(2,1)}, u32[]{:S(2)}) copy-start(bf16[1280,2,64]{0,2,1:T(8,128)(2,1)} %copy-done.7) | copy-start | bytes 983044
  316.0 10.3 %copy-start.25 = (bf16[1280,2,64]{0,2,1:T(8,128)(2,1)S(1)}, bf16[1280,2,64]{0,2,1:T(8,128)(2,1)}, u32[]{:S(2)}) copy-start(bf16[1280,2,64]{0,2,1:T(8,128)(2,1)} %copy-done.24) | copy-start | bytes 983044
  396.1 5.8 copy-start.17
  396.1 165.1 %all-to-all-start.1 = ((bf16[4,2,460800]{2,1,0:T(2,128)(2,1)}), bf16[4,2,460800]{2,1,0:T(2,128)(2,1)}, u32[]{:S(2)}, u32[]{:S(2)}) async-start(bf16[4,2,460800]{2,1,0:T(2,128)(2,1)} %reshape.125), calls=%async_computation.1 | async-start | bytes 14745600 | tf_op jit(solution)/shard_map/all_to_all | solution.py:95
  612.8 13.9 %copy-start.18 = (bf16[1280,2,64]{0,2,1:T(8,128)(2,1)S(1)}, bf16[1280,2,64]{0,2,1:T(8,128)(2,1)}, u32[]{:S(2)}) copy-start(bf16[1280,2,64]{0,2,1:T(8,128)(2,1)} %get-tuple-element.42) | copy-start | bytes 983044
  614.3 8.3 %copy-start.2 = (bf16[320,1280]{1,0:T(8,128)(2,1)S(1)}, bf16[320,1280]{1,0:T(8,128)(2,1)}, u32[]{:S(2)}) copy-start(bf16[320,1280]{1,0:T(8,128)(2,1)} %squeeze.92) | copy-start | bytes 2457604
  614.3 9.6 %copy-start.1 = (bf16[320,1280]{1,0:T(8,128)(2,1)S(1)}, bf16[320,1280]{1,0:T(8,128)(2,1)}, u32[]{:S(2)}) copy-start(bf16[320,1280]{1,0:T(8,128)(2,1)} %squeeze.93) | copy-start | bytes 2457604
Sparse Core Ops, SparseCore 0:
  295.1 35.7 reduce-scatter.8
  366.6 67.7 reduce-scatter.6
where the time goes:
time: 659 us; the launch traced here: 649 us
  local copies, waits for them, and re-layouts  243 us (37%)
  waiting for transfers between devices  160 us (24%)
  blocking collectives  154 us (23%)
  matrix products  37.1 us (6%)
  starting transfers between devices  29.4 us (4%)
  between operations  15.2 us (2%)
  other arithmetic  10.6 us (2%)
    unnamed x96, local copies, waits for them, and re-layouts  175 us
    all_gather x4, blocking collectives, circulate(): lax.all_gather(data, 'ch', axis=0, tiled=True)  154 us
    all_to_all x1, waiting for transfers between devices, on_device(): lax.all_to_all(jnp.transpose(spatial_weight, (0, 2, 1)), 'ch', split_axis...  152 us
    squeeze x10, local copies, waits for them, and re-layouts, contract(): weights[position]  21.6 us
    dot_general x20, matrix products, contract(): jnp.dot(weights[position], pieces[position], preferred_element_type=jnp.f...  19.2 us
    ppermute x8, starting transfers between devices, passed_along(): return lax.ppermute(shard, axis, pairs)  17.3 us
    slice x2, local copies, waits for them, and re-layouts, spatial_piece(): window = lax.slice_in_dim(padded, first_cell, first_cell + RT * W, axis=2)  13.8 us
  transfers between devices with their start and end apart: 12, of which 5 were waited for; matrix products, arithmetic and copies ran while one was open for 31% of the time, Pallas kernels for 0%

commit v1 on v0

v1 whole, which is shorter than its diff:
```python
import math

import jax
import jax.numpy as jnp
from jax import lax
from jax.experimental import pallas as pl
from jax.experimental.pallas import tpu as pltpu
from jax.sharding import PartitionSpec as P

FT = 2
RT = 2
W = 32
RBANDS = 2
TILE = FT * RT * W
HALF = RT * W
ROWS = RBANDS * RT
FRAME = ROWS * W
MIB = 1 << 20
BF = jnp.bfloat16
F32 = jnp.float32


def sizes():
    return lax.axis_size("ch"), lax.axis_size("st") // RBANDS


def place():
    st = lax.axis_index("st")
    return lax.axis_index("ch"), st // RBANDS, st % RBANDS


def send(data, axis, by):
    n = lax.axis_size(axis)
    return lax.ppermute(data, axis, [(i, (i + by) % n) for i in range(n)])


def swap_band(data):
    n = lax.axis_size("st")
    return lax.ppermute(data, "st", [(i, i ^ 1) for i in range(n)])


def gather_ch(shard):
    n_ch, _ = sizes()
    return jnp.stack([shard] + [send(shard, "ch", k) for k in range(1, n_ch)])


def ring_blocks(data):
    _, n_x = sizes()
    return [send(data, "st", RBANDS * j) for j in range(1, n_x)]


def neighbours(data):
    _, n_x = sizes()
    if n_x == 2:
        other = send(data, "st", RBANDS)
        return other, other
    return send(data, "st", RBANDS), send(data, "st", -RBANDS)


def lanes(shape):
    return lax.broadcasted_iota(jnp.int32, shape, len(shape) - 1)


def roll(x, by):
    return pltpu.roll(x, by, x.ndim - 1)


def frames_of(own, sibling, band):
    own = own.astype(F32)
    sibling = sibling.astype(F32)
    first = jnp.where(band == 0, own, sibling)
    second = jnp.where(band == 0, sibling, own)
    low = lanes(first.shape) < HALF
    return jnp.where(low, first, roll(second, HALF)), jnp.where(low, roll(first, HALF), second)


def tile_of(frame0, frame1, band):
    low = lanes(frame0.shape) < HALF
    upper = jnp.where(low, frame0, roll(frame1, HALF))
    lower = jnp.where(low, roll(frame0, HALF), frame1)
    return jnp.where(band == 0, upper, lower)


def time_pieces(own, before, after, m, n_x):
    own32 = own.astype(F32)
    before = jnp.where(m > 0, before.astype(F32), 0.0)
    after = jnp.where(m < n_x - 1, after.astype(F32), 0.0)
    low = lanes(own32.shape) < HALF
    earlier = roll(jnp.where(low, own32, before), HALF)
    later = roll(jnp.where(low, after, own32), HALF)
    return earlier.astype(BF), own, later.astype(BF)


def inside(dr, dc, shape):
    lane = lanes(shape)
    row = lane // W + dr
    col = lane % W + dc
    return (row >= 0) & (row < ROWS) & (col >= 0) & (col < W)


def spatial_forward(latents, mine, sibling, weight):
    n_ch, n_x = sizes()
    cb = latents.shape[0]
    channels = n_ch * cb

    def body(latents_ref, mine_ref, sibling_ref, w_ref, out_ref, field, acc):
        c, _, band = place()
        tap = pl.program_id(0)

        @pl.when(tap == 0)
        def _():
            for k in range(n_ch):
                at = pl.ds(pl.multiple_of(((c + n_ch - k) % n_ch) * cb, 16), cb)
                f0, f1 = frames_of(mine_ref[k], sibling_ref[k], band)
                field[at, :FRAME] = f0.astype(BF)
                field[at, FRAME:] = f1.astype(BF)
            acc[...] = jnp.zeros_like(acc)

        dr = tap // 3 - 1
        dc = tap % 3 - 1
        part = jnp.dot(w_ref[0], field[...], preferred_element_type=F32)
        by = (FRAME - (W * dr + dc)) % FRAME
        ok = inside(dr, dc, (cb, FRAME))
        acc[:, :FRAME] += jnp.where(ok, roll(part[:, :FRAME], by), 0.0)
        acc[:, FRAME:] += jnp.where(ok, roll(part[:, FRAME:], by), 0.0)

        @pl.when(tap == 8)
        def _():
            total = tile_of(acc[:, :FRAME], acc[:, FRAME:], band)
            out_ref[...] = (latents_ref[...].astype(F32) + total).astype(BF)

    whole = lambda shape: pl.BlockSpec(shape, lambda g: (0,) * len(shape))
    return pl.pallas_call(
        body,
        grid=(9,),
        in_specs=[
            whole((cb, TILE)),
            whole((n_ch, cb, TILE)),
            whole((n_ch, cb, TILE)),
            pl.BlockSpec((1, cb, channels), lambda g: (g, 0, 0)),
        ],
        out_specs=whole((cb, TILE)),
        out_shape=jax.ShapeDtypeStruct((cb, TILE), BF),
        scratch_shapes=[pltpu.VMEM((channels, 2 * FRAME), BF), pltpu.VMEM((cb, 2 * FRAME), F32)],
        compiler_params=pltpu.CompilerParams(vmem_limit_bytes=16 * MIB),
        name="spatial_forward",
    )(latents, mine, sibling, weight)


def temporal_forward(hidden, mine, before, after, weight):
    n_ch, n_x = sizes()
    cb = hidden.shape[0]
    channels = n_ch * cb

    def body(hidden_ref, mine_ref, before_ref, after_ref, w_ref, out_ref, field):
        c, m, _ = place()
        for k in range(n_ch):
            at = pl.ds(pl.multiple_of(((c + n_ch - k) % n_ch) * cb, 16), cb)
            pieces = time_pieces(mine_ref[k], before_ref[k], after_ref[k], m, n_x)
            for d in range(3):
                field[d, at, :] = pieces[d]
        total = hidden_ref[...].astype(F32)
        for d in range(3):
            total += jnp.dot(w_ref[d], field[d], preferred_element_type=F32)
        out_ref[...] = total.astype(BF)

    return pl.pallas_call(
        body,
        out_shape=jax.ShapeDtypeStruct((cb, TILE), BF),
        scratch_shapes=[pltpu.VMEM((3, channels, TILE), BF)],
        compiler_params=pltpu.CompilerParams(vmem_limit_bytes=16 * MIB),
        name="temporal_forward",
    )(hidden, mine, before, after, weight)


def emit_chunks(total, scratch, out_refs, c, n_ch, cb):
    scratch[...] = total.T
    for k in range(n_ch):
        at = pl.ds(pl.multiple_of(((c + k) % n_ch) * cb, 16), cb)
        out_refs[k][...] = scratch[at, :].astype(out_refs[k].dtype)


def chunk_shapes(n_ch, cb):
    return [jax.ShapeDtypeStruct((cb, TILE), BF if k else F32) for k in range(n_ch)]


def temporal_backward(field, before, after, weight):
    n_ch, n_x = sizes()
    cb = field.shape[0]
    channels = n_ch * cb

    def body(field_ref, before_ref, after_ref, w_ref, *rest):
        out_refs, scratch = rest[:n_ch], rest[n_ch]
        c, m, _ = place()
        pieces = time_pieces(field_ref[...], before_ref[...], after_ref[...], m, n_x)
        total = jnp.zeros((TILE, channels), F32)
        for d in range(3):
            left = pieces[2 - d].astype(F32).T.astype(BF)
            total += jnp.dot(left, w_ref[d], preferred_element_type=F32)
        emit_chunks(total, scratch, out_refs, c, n_ch, cb)

    return pl.pallas_call(
        body,
        out_shape=chunk_shapes(n_ch, cb),
        scratch_shapes=[pltpu.VMEM((channels, TILE), F32)],
        compiler_params=pltpu.CompilerParams(vmem_limit_bytes=16 * MIB),
        name="temporal_backward",
    )(field, before, after, weight)


def spatial_backward(field, sibling, weight):
    n_ch, _ = sizes()
    cb = field.shape[0]
    channels = n_ch * cb

    def body(field_ref, sibling_ref, w_ref, *rest):
        out_refs, (left, acc, scratch) = rest[:n_ch], rest[n_ch:]
        c, _, band = place()
        step = pl.program_id(0)

        @pl.when(step == 0)
        def _():
            f0, f1 = frames_of(field_ref[...], sibling_ref[...], band)
            left[...] = jnp.zeros_like(left)
            col = lax.broadcasted_iota(jnp.int32, (FRAME, cb), 0) % W
            for a, frame in enumerate((f0, f1)):
                cells = frame.T
                for q in range(3):
                    dc = q - 1
                    moved = pltpu.roll(cells, dc % FRAME, 0) if dc else cells
                    ok = (col - dc >= 0) & (col - dc < W)
                    left[a, W : W + FRAME, q * cb : (q + 1) * cb] = jnp.where(ok, moved, 0.0).astype(BF)
            acc[...] = jnp.zeros_like(acc)

        start = pl.multiple_of(W + HALF * band - W * (step - 1), W)
        rows = jnp.concatenate([left[0, pl.ds(start, HALF), :], left[1, pl.ds(start, HALF), :]], axis=0)
        acc[...] += jnp.dot(rows, w_ref[...], preferred_element_type=F32)

        @pl.when(step == 2)
        def _():
            emit_chunks(acc[...], scratch, out_refs, c, n_ch, cb)

    whole = lambda shape: pl.BlockSpec(shape, lambda g: (0,) * len(shape))
    return pl.pallas_call(
        body,
        grid=(3,),
        in_specs=[
            whole((cb, TILE)),
            whole((cb, TILE)),
            pl.BlockSpec((3 * cb, channels), lambda g: (g, 0)),
        ],
        out_specs=[whole((cb, TILE)) for _ in range(n_ch)],
        out_shape=chunk_shapes(n_ch, cb),
        scratch_shapes=[
            pltpu.VMEM((2, FRAME + 2 * W, 3 * cb), BF),
            pltpu.VMEM((TILE, channels), F32),
            pltpu.VMEM((channels, TILE), F32),
        ],
        compiler_params=pltpu.CompilerParams(vmem_limit_bytes=24 * MIB),
        name="spatial_backward",
    )(field, sibling, weight.reshape(9 * cb, channels))


def contract_cells(a, b):
    return lax.dot_general(a, b, (((1,), (1,)), ((), ())), preferred_element_type=F32)


def spatial_grads(grads, grads_sibling, fields, fields_sibling, scale):
    n_x, ob, _ = grads.shape
    ib = fields.shape[1]

    def body(g_ref, gs_ref, l_ref, ls_ref, out_ref, left, right):
        _, _, band = place()
        tap = pl.program_id(0)

        @pl.when(tap == 0)
        def _():
            for j in range(n_x):
                for a, frame in enumerate(frames_of(g_ref[j], gs_ref[j], band)):
                    left[:, (2 * j + a) * FRAME : (2 * j + a + 1) * FRAME] = frame.astype(BF)
                for a, frame in enumerate(frames_of(l_ref[j], ls_ref[j], band)):
                    right[2 * j + a] = frame

        dr = tap // 3 - 1
        dc = tap % 3 - 1
        by = (FRAME - (W * dr + dc)) % FRAME
        ok = inside(dr, dc, (ib, FRAME))
        moved = [jnp.where(ok, roll(right[f], by), 0.0).astype(BF) for f in range(2 * n_x)]
        out_ref[0] = contract_cells(left[...], jnp.concatenate(moved, axis=1)) * scale

    whole = lambda shape: pl.BlockSpec(shape, lambda g: (0,) * len(shape))
    return pl.pallas_call(
        body,
        grid=(9,),
        in_specs=[whole((n_x, ob, TILE))] * 2 + [whole((n_x, ib, TILE))] * 2,
        out_specs=pl.BlockSpec((1, ob, ib), lambda g: (g, 0, 0)),
        out_shape=jax.ShapeDtypeStruct((9, ob, ib), F32),
        scratch_shapes=[pltpu.VMEM((ob, 2 * n_x * FRAME), BF), pltpu.VMEM((2 * n_x, ib, FRAME), F32)],
        compiler_params=pltpu.CompilerParams(vmem_limit_bytes=24 * MIB),
        name="spatial_grads",
    )(grads, grads_sibling, fields, fields_sibling)


def temporal_grads(grads, grads_sibling, fields, fields_sibling, scale):
    n_x, ob, _ = grads.shape
    ib = fields.shape[1]
    span = 2 * n_x * FRAME

    def body(g_ref, gs_ref, h_ref, hs_ref, out_ref, left, right):
        _, m, band = place()
        step = pl.program_id(0)

        @pl.when(step == 0)
        def _():
            right[:, :FRAME] = jnp.zeros((ib, FRAME), BF)
            right[:, FRAME + span :] = jnp.zeros((ib, FRAME), BF)
            for j in range(n_x):
                block = (m + n_x - j) % n_x
                for a, frame in enumerate(frames_of(g_ref[j], gs_ref[j], band)):
                    at = pl.multiple_of((2 * block + a) * FRAME, FRAME)
                    left[:, pl.ds(at, FRAME)] = frame.astype(BF)
                for a, frame in enumerate(frames_of(h_ref[j], hs_ref[j], band)):
                    at = pl.multiple_of((2 * block + a + 1) * FRAME, FRAME)
                    right[:, pl.ds(at, FRAME)] = frame.astype(BF)

        moved = right[:, pl.ds(pl.multiple_of(step * FRAME, FRAME), span)]
        out_ref[0] = contract_cells(left[...], moved) * scale

    whole = lambda shape: pl.BlockSpec(shape, lambda g: (0,) * len(shape))
    return pl.pallas_call(
        body,
        grid=(3,),
        in_specs=[whole((n_x, ob, TILE))] * 2 + [whole((n_x, ib, TILE))] * 2,
        out_specs=pl.BlockSpec((1, ob, ib), lambda g: (g, 0, 0)),
        out_shape=jax.ShapeDtypeStruct((3, ob, ib), F32),
        scratch_shapes=[pltpu.VMEM((ob, span), BF), pltpu.VMEM((ib, span + 2 * FRAME), BF)],
        compiler_params=pltpu.CompilerParams(vmem_limit_bytes=24 * MIB),
        name="temporal_grads",
    )(grads, grads_sibling, fields, fields_sibling)


def reduce_ch(base, chunks):
    total = base.astype(F32) + chunks[0]
    for k in range(1, len(chunks)):
        total = total + send(chunks[k], "ch", k).astype(F32)
    return total.astype(BF)


def on_device(latents, spatial_weight, temporal_weight, cotangent):
    n_ch, n_x = sizes()
    assert n_ch == RBANDS * n_x
    c, m, band = place()
    scale = 1.0 / math.sqrt(TILE * RBANDS * n_x)

    def block(stack, b):
        return lax.dynamic_index_in_dim(stack, (c + n_ch - b) % n_ch, 0, keepdims=False)

    mine = gather_ch(latents)
    sibling = swap_band(mine)
    hidden = spatial_forward(latents, mine, sibling, spatial_weight)

    cot_ring = ring_blocks(cotangent)
    if n_x == 2:
        cot_before = cot_after = cot_ring[0]
    else:
        cot_before, cot_after = cot_ring[0], cot_ring[-1]
    hidden_grad = reduce_ch(
        cotangent, temporal_backward(cotangent, cot_before, cot_after, temporal_weight)
    )
    grad_sibling = swap_band(hidden_grad)
    latent_grad = reduce_ch(
        hidden_grad, spatial_backward(hidden_grad, grad_sibling, spatial_weight)
    )

    hidden_mine = gather_ch(hidden)
    before, after = neighbours(hidden_mine)
    temporal_out = temporal_forward(hidden, hidden_mine, before, after, temporal_weight)

    own_block = RBANDS * m + band
    sib_block = RBANDS * m + 1 - band

    cots = jnp.stack([cotangent] + cot_ring)
    cots_sibling = swap_band(cots)

    hid_own, hid_sib = [block(hidden_mine, own_block)], [block(hidden_mine, sib_block)]
    for j in range(1, n_x):
        if n_x == 2:
            hid_own.append(block(before, own_block))
            hid_sib.append(block(before, sib_block))
        else:
            target = RBANDS * ((m + j) % n_x)
            both = jnp.stack([block(hidden_mine, target + band), block(hidden_mine, target + 1 - band)])
            both = send(both, "st", RBANDS * j)
            hid_own.append(both[0])
            hid_sib.append(both[1])
    hids = jnp.stack(hid_own)
    hids_sibling = swap_band(jnp.stack(hid_sib))
    temporal_grad = temporal_grads(cots, cots_sibling, hids, hids_sibling, scale)

    lat_own, lat_sib = [block(mine, own_block)], [block(sibling, own_block)]
    grad_own, grad_sib = [hidden_grad], [grad_sibling]
    for j in range(1, n_x):
        target = RBANDS * ((m + j) % n_x) + band
        both = send(jnp.stack([block(mine, target), block(sibling, target)]), "st", RBANDS * j)
        lat_own.append(both[0])
        lat_sib.append(both[1])
        both = send(jnp.stack([hidden_grad, grad_sibling]), "st", RBANDS * j)
        grad_own.append(both[0])
        grad_sib.append(both[1])
    spatial_grad = spatial_grads(
        jnp.stack(grad_own), jnp.stack(grad_sib), jnp.stack(lat_own), jnp.stack(lat_sib), scale
    )
    return temporal_out, latent_grad, spatial_grad, temporal_grad


def solution(mesh):
    return jax.shard_map(
        on_device,
        mesh=mesh,
        in_specs=(
            P("ch", ("groups", "st")),
            P(None, "ch", None),
            P(None, "ch", None),
            P("ch", ("groups", "st")),
        ),
        out_specs=(
            P("ch", ("groups", "st")),
            P("ch", ("groups", "st")),
            P("groups", "ch", "st"),
            P("groups", "ch", "st"),
        ),
        check_vma=False,
    )
```

time: 659 us -> 77.9 us (0.12); the launches traced: 649 us -> 77.5 us
  local copies, waits for them, and re-layouts: 243 us -> 5.76 us
  blocking collectives: 154 us -> 0 us
  waiting for transfers between devices: 160 us -> 25.9 us
  matrix products: 37.1 us -> 0 us
  Pallas kernels: 0 us -> 18.8 us
  between operations: 15.2 us -> 0.86 us
  other arithmetic: 10.6 us -> 2.77 us
    unnamed x96 -> x10, local copies, waits for them, and re-layouts: 175 us -> 5.68 us
    all_gather x4 -> x0, blocking collectives: 154 us -> none  [circulate(): lax.all_gather(data, 'ch', axis=0, tiled=True)]
    all_to_all x2 -> x0, waiting for transfers between devices: 152 us -> none  [the longest x1 152 us: on_device(): lax.all_to_all(jnp.transpose(spatial_weight, (0, 2, 1)), 'ch', split_axis...]
    dot_general x36 -> x0, matrix products: 37.1 us -> none  [the longest x20 19.2 us: contract(): jnp.dot(weights[position], pieces[position], preferred_element_type=jnp.f...]
    squeeze x12 -> x0, local copies, waits for them, and re-layouts: 27.2 us -> none  [the longest x10 21.6 us: contract(): weights[position]]
    slice x8 -> x2, local copies, waits for them, and re-layouts: 20.7 us -> 0.02 us  [the longest x1 0.01 us: on_device(): lat_sib.append(both[1])]
    pallas_call x0 -> x6, Pallas kernels: none -> 18.8 us  [the longest x1 6.45 us: spatial_grads(): pl.pallas_call(body, grid=(9,), in_specs=[whole((n_x, ob, TILE))] * 2 + [...]
    ppermute x8 -> x20, waiting for transfers between devices: 7.46 us -> 25.9 us  [the longest x16 24.6 us: send(): return lax.ppermute(data, axis, [(i, (i + by) % n) for i in range(n)])]
  transfers between devices with their start and end apart: 12 -> 20, of which waited for: 5 -> 8; matrix products, arithmetic and copies ran while one was open for 31% -> 4% of each run, Pallas kernels for 0% -> 21%
where the time goes in v1:
time: 77.9 us; the launch traced here: 77.5 us
  waiting for transfers between devices  25.9 us (33%)
  starting transfers between devices  23.5 us (30%)
  Pallas kernels  18.8 us (24%)
  local copies, waits for them, and re-layouts  5.76 us (7%)
  other arithmetic  2.77 us (4%)
  between operations  0.86 us (1%)
    ppermute x16, waiting for transfers between devices, send(): return lax.ppermute(data, axis, [(i, (i + by) % n) for i in range(n)])  24.6 us
    ppermute x16, starting transfers between devices, send(): return lax.ppermute(data, axis, [(i, (i + by) % n) for i in range(n)])  23.2 us
    pallas_call x1, Pallas kernels, spatial_grads(): pl.pallas_call(body, grid=(9,), in_specs=[whole((n_x, ob, TILE))] * 2 + [...  6.45 us
    unnamed x10, local copies, waits for them, and re-layouts  5.68 us
    pallas_call x1, Pallas kernels, spatial_forward(): pl.pallas_call(body, grid=(9,), in_specs=[whole((cb, TILE)), whole((n_ch,...  4.79 us
    pallas_call x1, Pallas kernels, temporal_grads(): pl.pallas_call(body, grid=(3,), in_specs=[whole((n_x, ob, TILE))] * 2 + [...  2.65 us
    pallas_call x1, Pallas kernels, spatial_backward(): pl.pallas_call(body, grid=(3,), in_specs=[whole((cb, TILE)), whole((cb, T...  2.24 us
    pallas_call x1, Pallas kernels, temporal_forward(): pl.pallas_call(body, out_shape=jax.ShapeDtypeStruct((cb, TILE), BF), scra...  1.78 us
  transfers between devices with their start and end apart: 20, of which 8 were waited for; matrix products, arithmetic and copies ran while one was open for 4% of the time, Pallas kernels for 21%

profile of v1, /device:TPU:0, one launch (start us, length us, event | category | flops | bytes accessed | tf_op | source)
XLA Modules:
  0.0 77.5 jit_solution(10602757822827413683)
XLA Ops:
  0.6 3.0 %collective-permute-start.8 = (bf16[320,128]{1,0:T(8,128)(2,1)}, bf16[320,128]{1,0:T(8,128)(2,1)S(1)}, u32[]{:S(2)}, u32[]{:S(2)}) collective-permute-start(bf16[320,128]{1,0:T(8,128)(2,1)} %field_ref.1), channel_id=1, source_target_pairs={{0,8},{4,12},{8,0},{12,4},{1,9},{5,13},{9,1},{13,5},{2,10},{6,14},... | collective-permute-start | bytes 245768 | tf_op jit(solution)/shard_map/ppermute | solution.py:34
  3.6 2.6 %collective-permute-start.1 = (bf16[320,128]{1,0:T(8,128)(2,1)}, bf16[320,128]{1,0:T(8,128)(2,1)S(1)}, u32[]{:S(2)}, u32[]{:S(2)}) collective-permute-start(bf16[320,128]{1,0:T(8,128)(2,1)} %latents_ref.1), channel_id=1, source_target_pairs={{0,2},{1,3},{2,0},{3,1},{4,6},{5,7},{6,4},{7,5},{8,10},{9,11},{10,... | collective-permute-start | bytes 245768 | tf_op jit(solution)/shard_map/ppermute | solution.py:34
  6.2 1.6 %collective-permute-start = (bf16[320,128]{1,0:T(8,128)(2,1)}, bf16[320,128]{1,0:T(8,128)(2,1)S(1)}, u32[]{:S(2)}, u32[]{:S(2)}) collective-permute-start(bf16[320,128]{1,0:T(8,128)(2,1)} %latents_ref.1), channel_id=1, source_target_pairs={{0,1},{1,2},{2,3},{3,0},{4,5},{5,6},{6,7},{7,4},{8,9},{9,10},{10,1... | collective-permute-start | bytes 245768 | tf_op jit(solution)/shard_map/ppermute | solution.py:34
  7.8 2.2 %collective-permute-start.2 = (bf16[320,128]{1,0:T(8,128)(2,1)}, bf16[320,128]{1,0:T(8,128)(2,1)S(1)}, u32[]{:S(2)}, u32[]{:S(2)}) collective-permute-start(bf16[320,128]{1,0:T(8,128)(2,1)} %latents_ref.1), channel_id=1, source_target_pairs={{0,3},{1,0},{2,1},{3,2},{4,7},{5,4},{6,5},{7,6},{8,11},{9,8},{10,9... | collective-permute-start | bytes 245768 | tf_op jit(solution)/shard_map/ppermute | solution.py:34
  10.0 0.0 collective-permute-done.8.before_ref.after_ref
  10.1 0.9 %pad_maximum_fusion.8.g_ref = bf16[2,320,128]{2,1,0:T(8,128)(2,1)S(1)} fusion(bf16[1,320,128]{2,1,0:T(8,128)(2,1)S(1)} %bitcast.20, bf16[1,320,128]{2,1,0:T(8,128)(2,1)} %bitcast.19), kind=kLoop, calls=%fused_computation.8 | loop fusion | flops 81920 | bytes 327680 | tf_op jit(solution)/shard_map/stack | solution.py:382
  11.0 0.1 collective-permute-start.18
  11.0 0.0 copy-start.1
  11.0 1.7 %copy-done.1 = bf16[3,320,1280]{2,1,0:T(8,128)(2,1)S(1)} copy-done((bf16[3,320,1280]{2,1,0:T(8,128)(2,1)S(1)}, bf16[3,320,1280]{2,1,0:T(8,128)(2,1)}, u32[]{:S(2)}) %copy-start.1) | copy-done | bytes 2457624
  12.7 0.0 copy-start.3
  12.7 0.9 %copy-done.3 = bf16[320,128]{1,0:T(8,128)(2,1)S(1)} copy-done((bf16[320,128]{1,0:T(8,128)(2,1)S(1)}, bf16[320,128]{1,0:T(8,128)(2,1)}, u32[]{:S(2)}) %copy-start.3) | copy-done | bytes 81944
  13.6 0.9 %temporal_backward.1 = (f32[320,128]{1,0:T(8,128)S(1)}, bf16[320,128]{1,0:T(8,128)(2,1)S(1)}, bf16[320,128]{1,0:T(8,128)(2,1)S(1)}, bf16[320,128]{1,0:T(8,128)(2,1)S(1)}) custom-call(bf16[320,128]{1,0:T(8,128)(2,1)S(1)} %copy-done.3, bf16[320,128]{1,0:T(8,128)(2,1)S(1)} %collective-permute-done.8.before_ref.after_ref, ...), custom_call_target="tpu_custom_call" | custom-call | tf_op jit(solution)/shard_map/temporal_backward/pallas_call | solution.py:202
  14.5 0.1 collective-permute-start.9
  14.5 0.0 collective-permute-done.1
  14.6 0.9 %collective-permute-start.10 = (bf16[320,128]{1,0:T(8,128)(2,1)S(1)}, bf16[320,128]{1,0:T(8,128)(2,1)S(1)}, u32[]{:S(2)}, u32[]{:S(2)}) collective-permute-start(bf16[320,128]{1,0:T(8,128)(2,1)S(1)} %get-tuple-element.14), channel_id=1, source_target_pairs={{0,2},{1,3},{2,0},{3,1},{4,6},{5,7},{6,4},{7,5},{8,10},{9,11},{10,... | collective-permute-start | bytes 245768 | tf_op jit(solution)/shard_map/ppermute | solution.py:34
  15.5 0.0 collective-permute-done
  15.5 3.0 %collective-permute-start.11 = (bf16[320,128]{1,0:T(8,128)(2,1)S(1)}, bf16[320,128]{1,0:T(8,128)(2,1)S(1)}, u32[]{:S(2)}, u32[]{:S(2)}) collective-permute-start(bf16[320,128]{1,0:T(8,128)(2,1)S(1)} %get-tuple-element.15), channel_id=1, source_target_pairs={{0,3},{1,0},{2,1},{3,2},{4,7},{5,4},{6,5},{7,6},{8,11},{9,8},{10,9... | collective-permute-start | bytes 245768 | tf_op jit(solution)/shard_map/ppermute | solution.py:34
  18.4 0.0 collective-permute-done.2
  18.4 0.9 %pad_maximum_fusion.mine_ref = bf16[4,320,128]{2,1,0:T(8,128)(2,1)S(1)} fusion(bf16[1,320,128]{2,1,0:T(8,128)(2,1)S(1)} %bitcast.24, bf16[1,320,128]{2,1,0:T(8,128)(2,1)S(1)} %bitcast.22, bf16[1,320,128]{2,1,0:T(8,128)(2,1)S(1)} %bitcast.23, bf16[1,320,128]{2,1,0:T(8,128)(2,1)} %bitcast.21), kind=kLoop, calls=%fused_computation | loop fusion | flops 491520 | bytes 655360 | tf_op jit(solution)/shard_map/stack | solution.py:44
  19.4 0.1 collective-permute-start.3
  19.4 2.2 %collective-permute-done.9 = bf16[320,128]{1,0:T(8,128)(2,1)S(1)} collective-permute-done((bf16[320,128]{1,0:T(8,128)(2,1)S(1)}, bf16[320,128]{1,0:T(8,128)(2,1)S(1)}, u32[]{:S(2)}, u32[]{:S(2)}) %collective-permute-start.9) | collective-permute-done | bytes 81952 | tf_op jit(solution)/shard_map/ppermute | solution.py:34
  21.7 2.6 %collective-permute-done.10 = bf16[320,128]{1,0:T(8,128)(2,1)S(1)} collective-permute-done((bf16[320,128]{1,0:T(8,128)(2,1)S(1)}, bf16[320,128]{1,0:T(8,128)(2,1)S(1)}, u32[]{:S(2)}, u32[]{:S(2)}) %collective-permute-start.10) | collective-permute-done | bytes 81952 | tf_op jit(solution)/shard_map/ppermute | solution.py:34
  24.3 0.0 collective-permute-done.11
  24.3 0.1 add_convert_fusion.1.field_ref
  24.3 0.0 copy-start.4
  24.4 0.1 collective-permute-start.12
  24.5 1.2 %collective-permute-done.12.sibling_ref = bf16[320,128]{1,0:T(8,128)(2,1)S(1)} collective-permute-done((bf16[320,128]{1,0:T(8,128)(2,1)S(1)}, bf16[320,128]{1,0:T(8,128)(2,1)S(1)}, u32[]{:S(2)}, u32[]{:S(2)}) %collective-permute-start.12) | collective-permute-done | bytes 81952 | tf_op jit(solution)/shard_map/ppermute | solution.py:39
  25.7 0.0 copy-start
  25.7 3.1 %copy-done = bf16[9,320,1280]{2,1,0:T(8,128)(2,1)S(1)} copy-done((bf16[9,320,1280]{2,1,0:T(8,128)(2,1)S(1)}, bf16[9,320,1280]{2,1,0:T(8,128)(2,1)}, u32[]{:S(2)}) %copy-start) | copy-done | bytes 7372824
  28.8 2.2 %spatial_backward.1 = (f32[320,128]{1,0:T(8,128)S(1)}, bf16[320,128]{1,0:T(8,128)(2,1)S(1)}, bf16[320,128]{1,0:T(8,128)(2,1)S(1)}, bf16[320,128]{1,0:T(8,128)(2,1)S(1)}) custom-call(bf16[320,128]{1,0:T(8,128)(2,1)S(1)} %add_convert_fusion.1.field_ref, bf16[320,128]{1,0:T(8,128)(2,1)S(1)} %collective-permute-done.12.sibling_ref, bf16[2880,1280]{1,0:T(8,128)(2,1)S(1)} %bitcast.13), custom_call_target="tpu_custom_call" | custom-call | tf_op jit(solution)/shard_map/spatial_backward/pallas_call | solution.py:244
  31.0 2.0 %collective-permute-start.13 = (bf16[320,128]{1,0:T(8,128)(2,1)S(1)}, bf16[320,128]{1,0:T(8,128)(2,1)S(1)}, u32[]{:S(2)}, u32[]{:S(2)}) collective-permute-start(bf16[320,128]{1,0:T(8,128)(2,1)S(1)} %get-tuple-element.17), channel_id=1, source_target_pairs={{0,1},{1,2},{2,3},{3,0},{4,5},{5,6},{6,7},{7,4},{8,9},{9,10},{10,1... | collective-permute-start | bytes 245768 | tf_op jit(solution)/shard_map/ppermute | solution.py:34
  33.0 1.1 %collective-permute-start.14 = (bf16[320,128]{1,0:T(8,128)(2,1)S(1)}, bf16[320,128]{1,0:T(8,128)(2,1)S(1)}, u32[]{:S(2)}, u32[]{:S(2)}) collective-permute-start(bf16[320,128]{1,0:T(8,128)(2,1)S(1)} %get-tuple-element.18), channel_id=1, source_target_pairs={{0,2},{1,3},{2,0},{3,1},{4,6},{5,7},{6,4},{7,5},{8,10},{9,11},{10,... | collective-permute-start | bytes 245768 | tf_op jit(solution)/shard_map/ppermute | solution.py:34
  34.1 1.3 %collective-permute-start.15 = (bf16[320,128]{1,0:T(8,128)(2,1)S(1)}, bf16[320,128]{1,0:T(8,128)(2,1)S(1)}, u32[]{:S(2)}, u32[]{:S(2)}) collective-permute-start(bf16[320,128]{1,0:T(8,128)(2,1)S(1)} %get-tuple-element.19), channel_id=1, source_target_pairs={{0,3},{1,0},{2,1},{3,2},{4,7},{5,4},{6,5},{7,6},{8,11},{9,8},{10,9... | collective-permute-start | bytes 245768 | tf_op jit(solution)/shard_map/ppermute | solution.py:34
  35.5 2.8 %collective-permute-done.13 = bf16[320,128]{1,0:T(8,128)(2,1)S(1)} collective-permute-done((bf16[320,128]{1,0:T(8,128)(2,1)S(1)}, bf16[320,128]{1,0:T(8,128)(2,1)S(1)}, u32[]{:S(2)}, u32[]{:S(2)}) %collective-permute-start.13) | collective-permute-done | bytes 81952 | tf_op jit(solution)/shard_map/ppermute | solution.py:34
  38.3 0.5 collective-permute-start.16
  38.8 2.2 %collective-permute-done.14 = bf16[320,128]{1,0:T(8,128)(2,1)S(1)} collective-permute-done((bf16[320,128]{1,0:T(8,128)(2,1)S(1)}, bf16[320,128]{1,0:T(8,128)(2,1)S(1)}, u32[]{:S(2)}, u32[]{:S(2)}) %collective-permute-start.14) | collective-permute-done | bytes 81952 | tf_op jit(solution)/shard_map/ppermute | solution.py:34
  41.0 0.0 collective-permute-done.15
  41.0 0.7 add_convert_fusion
  41.7 0.0 collective-permute-done.3.sibling_ref
  41.7 0.0 copy-done.4
  41.7 4.8 %spatial_forward.1.hidden_ref = bf16[320,128]{1,0:T(8,128)(2,1)S(1)} custom-call(bf16[320,128]{1,0:T(8,128)(2,1)S(1)} %copy-done.4, bf16[4,320,128]{2,1,0:T(8,128)(2,1)S(1)} %pad_maximum_fusion.mine_ref, bf16[4,320,128]{2,1,0:T(8,128)(2,1)S(1)} %collective-permute-done.3.sibling_ref, bf16[9,320,1280]{2,1,0:T(8,128)(2,1)S(1)} %copy-done), custom_call_target="tpu_custom_call" | custom-call | tf_op jit(solution)/shard_map/spatial_forward/pallas_call | solution.py:133
  46.5 2.6 %collective-permute-start.6 = (bf16[320,128]{1,0:T(8,128)(2,1)S(1)}, bf16[320,128]{1,0:T(8,128)(2,1)S(1)}, u32[]{:S(2)}, u32[]{:S(2)}) collective-permute-start(bf16[320,128]{1,0:T(8,128)(2,1)S(1)} %spatial_forward.1.hidden_ref), channel_id=1, source_target_pairs={{0,3},{1,0},{2,1},{3,2},{4,7},{5,4},{6,5},{7,6},{8,11},{9,8},{10,9... | collective-permute-start | bytes 245768 | tf_op jit(solution)/shard_map/ppermute | solution.py:34
  49.1 1.1 %collective-permute-start.5 = (bf16[320,128]{1,0:T(8,128)(2,1)S(1)}, bf16[320,128]{1,0:T(8,128)(2,1)S(1)}, u32[]{:S(2)}, u32[]{:S(2)}) collective-permute-start(bf16[320,128]{1,0:T(8,128)(2,1)S(1)} %spatial_forward.1.hidden_ref), channel_id=1, source_target_pairs={{0,2},{1,3},{2,0},{3,1},{4,6},{5,7},{6,4},{7,5},{8,10},{9,11},{10,... | collective-permute-start | bytes 245768 | tf_op jit(solution)/shard_map/ppermute | solution.py:34
  50.2 0.0 collective-permute-start.4
  50.3 0.0 copy-start.2
  50.3 0.0 collective-permute-done.16
  50.3 0.6 collective-permute-start.17
  51.0 1.0 %collective-permute-done.6 = bf16[320,128]{1,0:T(8,128)(2,1)S(1)} collective-permute-done((bf16[320,128]{1,0:T(8,128)(2,1)S(1)}, bf16[320,128]{1,0:T(8,128)(2,1)S(1)}, u32[]{:S(2)}, u32[]{:S(2)}) %collective-permute-start.6) | collective-permute-done | bytes 81952 | tf_op jit(solution)/shard_map/ppermute | solution.py:34
  52.0 5.9 %collective-permute-done.5 = bf16[320,128]{1,0:T(8,128)(2,1)S(1)} collective-permute-done((bf16[320,128]{1,0:T(8,128)(2,1)S(1)}, bf16[320,128]{1,0:T(8,128)(2,1)S(1)}, u32[]{:S(2)}, u32[]{:S(2)}) %collective-permute-start.5) | collective-permute-done | bytes 81952 | tf_op jit(solution)/shard_map/ppermute | solution.py:34
  57.8 0.0 collective-permute-done.4
  57.9 0.6 collective-permute-start.7
  58.5 0.0 collective-permute-done.17
  58.5 7.9 %collective-permute-done.7.before_ref.after_ref = bf16[4,320,128]{2,1,0:T(8,128)(2,1)S(1)} collective-permute-done((bf16[4,320,128]{2,1,0:T(8,128)(2,1)S(1)}, bf16[4,320,128]{2,1,0:T(8,128)(2,1)S(1)}, u32[]{:S(2)}, u32[]{:S(2)}) %collective-permute-start.7) | collective-permute-done | bytes 327712 | tf_op jit(solution)/shard_map/ppermute | solution.py:34
  66.5 0.1 collective-permute-start.19
  66.6 6.4 %spatial_grads.1 = f32[9,320,320]{2,1,0:T(8,128)} custom-call(bf16[2,320,128]{2,1,0:T(8,128)(2,1)S(1)} %get-tuple-element.32.g_ref, bf16[2,320,128]{2,1,0:T(8,128)(2,1)S(1)} %get-tuple-element.33.gs_ref, bf16[2,320,128]{2,1,0:T(8,128)(2,1)S(1)} %get-tuple-element.34.l_ref, bf16[2,320,128]{2,1,0:T(8,128)(2,1)S(1)} %get-tuple-element.35.ls_ref), custom_call_target="tpu_custom_call" | custom-call | tf_op jit(solution)/shard_map/spatial_grads/pallas_call | solution.py:292
  73.1 0.0 copy-done.2
  73.1 1.8 %temporal_forward.1 = bf16[320,128]{1,0:T(8,128)(2,1)} custom-call(bf16[320,128]{1,0:T(8,128)(2,1)S(1)} %spatial_forward.1.hidden_ref, bf16[4,320,128]{2,1,0:T(8,128)(2,1)S(1)} %pad_maximum_fusion.1.mine_ref, bf16[4,320,128]{2,1,0:T(8,128)(2,1)S(1)} %collective-permute-done.7.before_ref.after_ref, ...), custom_call_target="tpu_custom_call" | custom-call | tf_op jit(solution)/shard_map/temporal_forward/pallas_call | solution.py:167
  74.9 0.0 collective-permute-done.18.gs_ref
  74.9 0.0 collective-permute-done.19.hs_ref
  74.9 2.6 %temporal_grads.1 = f32[3,320,320]{2,1,0:T(8,128)} custom-call(bf16[2,320,128]{2,1,0:T(8,128)(2,1)S(1)} %pad_maximum_fusion.8.g_ref, bf16[2,320,128]{2,1,0:T(8,128)(2,1)S(1)} %collective-permute-done.18.gs_ref, bf16[2,320,128]{2,1,0:T(8,128)(2,1)S(1)} %pad_maximum_fusion.9.h_ref, bf16[2,320,128]{2,1,0:T(8,128)(2,1)S(1)} %collective-permute-done.19.hs_ref), custom_call_target="tpu_custom_call" | custom-call | tf_op jit(solution)/shard_map/temporal_grads/pallas_call | solution.py:330
  (13 shorter events, 0.3 us)
Async XLA Ops:
  0.6 9.4 %collective-permute-start.8 = (bf16[320,128]{1,0:T(8,128)(2,1)}, bf16[320,128]{1,0:T(8,128)(2,1)S(1)}, u32[]{:S(2)}, u32[]{:S(2)}) collective-permute-start(bf16[320,128]{1,0:T(8,128)(2,1)} %field_ref.1), channel_id=1, source_target_pairs={{0,8},{4,12},{8,0},{12,4},{1,9},{5,13},{9,1},{13,5},{2,10},{6,14},... | collective-permute-start | bytes 245768 | tf_op jit(solution)/shard_map/ppermute | solution.py:34
  3.6 10.9 %collective-permute-start.1 = (bf16[320,128]{1,0:T(8,128)(2,1)}, bf16[320,128]{1,0:T(8,128)(2,1)S(1)}, u32[]{:S(2)}, u32[]{:S(2)}) collective-permute-start(bf16[320,128]{1,0:T(8,128)(2,1)} %latents_ref.1), channel_id=1, source_target_pairs={{0,2},{1,3},{2,0},{3,1},{4,6},{5,7},{6,4},{7,5},{8,10},{9,11},{10,... | collective-permute-start | bytes 245768 | tf_op jit(solution)/shard_map/ppermute | solution.py:34
  6.2 9.2 %collective-permute-start = (bf16[320,128]{1,0:T(8,128)(2,1)}, bf16[320,128]{1,0:T(8,128)(2,1)S(1)}, u32[]{:S(2)}, u32[]{:S(2)}) collective-permute-start(bf16[320,128]{1,0:T(8,128)(2,1)} %latents_ref.1), channel_id=1, source_target_pairs={{0,1},{1,2},{2,3},{3,0},{4,5},{5,6},{6,7},{7,4},{8,9},{9,10},{10,1... | collective-permute-start | bytes 245768 | tf_op jit(solution)/shard_map/ppermute | solution.py:34
  7.8 10.6 %collective-permute-start.2 = (bf16[320,128]{1,0:T(8,128)(2,1)}, bf16[320,128]{1,0:T(8,128)(2,1)S(1)}, u32[]{:S(2)}, u32[]{:S(2)}) collective-permute-start(bf16[320,128]{1,0:T(8,128)(2,1)} %latents_ref.1), channel_id=1, source_target_pairs={{0,3},{1,0},{2,1},{3,2},{4,7},{5,4},{6,5},{7,6},{8,11},{9,8},{10,9... | collective-permute-start | bytes 245768 | tf_op jit(solution)/shard_map/ppermute | solution.py:34
  11.0 63.9 %collective-permute-start.18 = (bf16[2,320,128]{2,1,0:T(8,128)(2,1)S(1)}, bf16[2,320,128]{2,1,0:T(8,128)(2,1)S(1)}, u32[]{:S(2)}, u32[]{:S(2)}) collective-permute-start(bf16[2,320,128]{2,1,0:T(8,128)(2,1)S(1)} %pad_maximum_fusion.8.g_ref), channel_id=1, source_target_pairs={{0,4},{4,0},{8,12},{12,8},{1,5},{5,1},{9,13},{13,9},{2,6},{6,2},{1... | collective-permute-start | bytes 491528 | tf_op jit(solution)/shard_map/ppermute | solution.py:39
  11.0 1.7 %copy-start.1 = (bf16[3,320,1280]{2,1,0:T(8,128)(2,1)S(1)}, bf16[3,320,1280]{2,1,0:T(8,128)(2,1)}, u32[]{:S(2)}) copy-start(bf16[3,320,1280]{2,1,0:T(8,128)(2,1)} %w_ref.5) | copy-start | bytes 7372804
  12.7 0.9 %copy-start.3 = (bf16[320,128]{1,0:T(8,128)(2,1)S(1)}, bf16[320,128]{1,0:T(8,128)(2,1)}, u32[]{:S(2)}) copy-start(bf16[320,128]{1,0:T(8,128)(2,1)} %field_ref.1) | copy-start | bytes 245764
  14.5 7.2 %collective-permute-start.9 = (bf16[320,128]{1,0:T(8,128)(2,1)S(1)}, bf16[320,128]{1,0:T(8,128)(2,1)S(1)}, u32[]{:S(2)}, u32[]{:S(2)}) collective-permute-start(bf16[320,128]{1,0:T(8,128)(2,1)S(1)} %get-tuple-element.13), channel_id=1, source_target_pairs={{0,1},{1,2},{2,3},{3,0},{4,5},{5,6},{6,7},{7,4},{8,9},{9,10},{10,1... | collective-permute-start | bytes 245768 | tf_op jit(solution)/shard_map/ppermute | solution.py:34
  14.6 9.7 %collective-permute-start.10 = (bf16[320,128]{1,0:T(8,128)(2,1)S(1)}, bf16[320,128]{1,0:T(8,128)(2,1)S(1)}, u32[]{:S(2)}, u32[]{:S(2)}) collective-permute-start(bf16[320,128]{1,0:T(8,128)(2,1)S(1)} %get-tuple-element.14), channel_id=1, source_target_pairs={{0,2},{1,3},{2,0},{3,1},{4,6},{5,7},{6,4},{7,5},{8,10},{9,11},{10,... | collective-permute-start | bytes 245768 | tf_op jit(solution)/shard_map/ppermute | solution.py:34
  15.5 8.8 %collective-permute-start.11 = (bf16[320,128]{1,0:T(8,128)(2,1)S(1)}, bf16[320,128]{1,0:T(8,128)(2,1)S(1)}, u32[]{:S(2)}, u32[]{:S(2)}) collective-permute-start(bf16[320,128]{1,0:T(8,128)(2,1)S(1)} %get-tuple-element.15), channel_id=1, source_target_pairs={{0,3},{1,0},{2,1},{3,2},{4,7},{5,4},{6,5},{7,6},{8,11},{9,8},{10,9... | collective-permute-start | bytes 245768 | tf_op jit(solution)/shard_map/ppermute | solution.py:34
  19.4 22.3 %collective-permute-start.3 = (bf16[4,320,128]{2,1,0:T(8,128)(2,1)S(1)}, bf16[4,320,128]{2,1,0:T(8,128)(2,1)S(1)}, u32[]{:S(2)}, u32[]{:S(2)}) collective-permute-start(bf16[4,320,128]{2,1,0:T(8,128)(2,1)S(1)} %pad_maximum_fusion.mine_ref), channel_id=1, source_target_pairs={{0,4},{4,0},{8,12},{12,8},{1,5},{5,1},{9,13},{13,9},{2,6},{6,2},{1... | collective-permute-start | bytes 983048 | tf_op jit(solution)/shard_map/ppermute | solution.py:39
  24.3 17.4 %copy-start.4 = (bf16[320,128]{1,0:T(8,128)(2,1)S(1)}, bf16[320,128]{1,0:T(8,128)(2,1)}, u32[]{:S(2)}) copy-start(bf16[320,128]{1,0:T(8,128)(2,1)} %latents_ref.1) | copy-start | bytes 245764
  24.4 1.3 %collective-permute-start.12 = (bf16[320,128]{1,0:T(8,128)(2,1)S(1)}, bf16[320,128]{1,0:T(8,128)(2,1)S(1)}, u32[]{:S(2)}, u32[]{:S(2)}) collective-permute-start(bf16[320,128]{1,0:T(8,128)(2,1)S(1)} %add_convert_fusion.1.field_ref), channel_id=1, source_target_pairs={{0,4},{4,0},{8,12},{12,8},{1,5},{5,1},{9,13},{13,9},{2,6},{6,2},{1... | collective-permute-start | bytes 245768 | tf_op jit(solution)/shard_map/ppermute | solution.py:39
  25.7 3.1 %copy-start = (bf16[9,320,1280]{2,1,0:T(8,128)(2,1)S(1)}, bf16[9,320,1280]{2,1,0:T(8,128)(2,1)}, u32[]{:S(2)}) copy-start(bf16[9,320,1280]{2,1,0:T(8,128)(2,1)} %w_ref.3) | copy-start | bytes 22118404
  31.0 7.2 %collective-permute-start.13 = (bf16[320,128]{1,0:T(8,128)(2,1)S(1)}, bf16[320,128]{1,0:T(8,128)(2,1)S(1)}, u32[]{:S(2)}, u32[]{:S(2)}) collective-permute-start(bf16[320,128]{1,0:T(8,128)(2,1)S(1)} %get-tuple-element.17), channel_id=1, source_target_pairs={{0,1},{1,2},{2,3},{3,0},{4,5},{5,6},{6,7},{7,4},{8,9},{9,10},{10,1... | collective-permute-start | bytes 245768 | tf_op jit(solution)/shard_map/ppermute | solution.py:34
  33.0 8.0 %collective-permute-start.14 = (bf16[320,128]{1,0:T(8,128)(2,1)S(1)}, bf16[320,128]{1,0:T(8,128)(2,1)S(1)}, u32[]{:S(2)}, u32[]{:S(2)}) collective-permute-start(bf16[320,128]{1,0:T(8,128)(2,1)S(1)} %get-tuple-element.18), channel_id=1, source_target_pairs={{0,2},{1,3},{2,0},{3,1},{4,6},{5,7},{6,4},{7,5},{8,10},{9,11},{10,... | collective-permute-start | bytes 245768 | tf_op jit(solution)/shard_map/ppermute | solution.py:34
  34.1 6.9 %collective-permute-start.15 = (bf16[320,128]{1,0:T(8,128)(2,1)S(1)}, bf16[320,128]{1,0:T(8,128)(2,1)S(1)}, u32[]{:S(2)}, u32[]{:S(2)}) collective-permute-start(bf16[320,128]{1,0:T(8,128)(2,1)S(1)} %get-tuple-element.19), channel_id=1, source_target_pairs={{0,3},{1,0},{2,1},{3,2},{4,7},{5,4},{6,5},{7,6},{8,11},{9,8},{10,9... | collective-permute-start | bytes 245768 | tf_op jit(solution)/shard_map/ppermute | solution.py:34
  38.3 12.0 %collective-permute-start.16 = (bf16[2,320,128]{2,1,0:T(8,128)(2,1)S(1)}, bf16[2,320,128]{2,1,0:T(8,128)(2,1)S(1)}, u32[]{:S(2)}, u32[]{:S(2)}) collective-permute-start(bf16[2,320,128]{2,1,0:T(8,128)(2,1)S(1)} %pad_maximum_fusion.2), channel_id=1, source_target_pairs={{0,8},{4,12},{8,0},{12,4},{1,9},{5,13},{9,1},{13,5},{2,10},{6,14},... | collective-permute-start | bytes 491528 | tf_op jit(solution)/shard_map/ppermute | solution.py:34
  46.5 5.5 %collective-permute-start.6 = (bf16[320,128]{1,0:T(8,128)(2,1)S(1)}, bf16[320,128]{1,0:T(8,128)(2,1)S(1)}, u32[]{:S(2)}, u32[]{:S(2)}) collective-permute-start(bf16[320,128]{1,0:T(8,128)(2,1)S(1)} %spatial_forward.1.hidden_ref), channel_id=1, source_target_pairs={{0,3},{1,0},{2,1},{3,2},{4,7},{5,4},{6,5},{7,6},{8,11},{9,8},{10,9... | collective-permute-start | bytes 245768 | tf_op jit(solution)/shard_map/ppermute | solution.py:34
  49.1 8.7 %collective-permute-start.5 = (bf16[320,128]{1,0:T(8,128)(2,1)S(1)}, bf16[320,128]{1,0:T(8,128)(2,1)S(1)}, u32[]{:S(2)}, u32[]{:S(2)}) collective-permute-start(bf16[320,128]{1,0:T(8,128)(2,1)S(1)} %spatial_forward.1.hidden_ref), channel_id=1, source_target_pairs={{0,2},{1,3},{2,0},{3,1},{4,6},{5,7},{6,4},{7,5},{8,10},{9,11},{10,... | collective-permute-start | bytes 245768 | tf_op jit(solution)/shard_map/ppermute | solution.py:34
  50.2 7.6 %collective-permute-start.4 = (bf16[320,128]{1,0:T(8,128)(2,1)S(1)}, bf16[320,128]{1,0:T(8,128)(2,1)S(1)}, u32[]{:S(2)}, u32[]{:S(2)}) collective-permute-start(bf16[320,128]{1,0:T(8,128)(2,1)S(1)} %spatial_forward.1.hidden_ref), channel_id=1, source_target_pairs={{0,1},{1,2},{2,3},{3,0},{4,5},{5,6},{6,7},{7,4},{8,9},{9,10},{10,1... | collective-permute-start | bytes 245768 | tf_op jit(solution)/shard_map/ppermute | solution.py:34
  50.3 22.8 %copy-start.2 = (bf16[3,320,1280]{2,1,0:T(8,128)(2,1)S(1)}, bf16[3,320,1280]{2,1,0:T(8,128)(2,1)}, u32[]{:S(2)}) copy-start(bf16[3,320,1280]{2,1,0:T(8,128)(2,1)} %w_ref.5) | copy-start | bytes 7372804
  50.3 8.2 %collective-permute-start.17 = (bf16[2,320,128]{2,1,0:T(8,128)(2,1)S(1)}, bf16[2,320,128]{2,1,0:T(8,128)(2,1)S(1)}, u32[]{:S(2)}, u32[]{:S(2)}) collective-permute-start(bf16[2,320,128]{2,1,0:T(8,128)(2,1)S(1)} %pad_maximum_fusion.5), channel_id=1, source_target_pairs={{0,8},{4,12},{8,0},{12,4},{1,9},{5,13},{9,1},{13,5},{2,10},{6,14},... | collective-permute-start | bytes 491528 | tf_op jit(solution)/shard_map/ppermute | solution.py:34
  57.9 8.6 %collective-permute-start.7 = (bf16[4,320,128]{2,1,0:T(8,128)(2,1)S(1)}, bf16[4,320,128]{2,1,0:T(8,128)(2,1)S(1)}, u32[]{:S(2)}, u32[]{:S(2)}) collective-permute-start(bf16[4,320,128]{2,1,0:T(8,128)(2,1)S(1)} %pad_maximum_fusion.1.mine_ref), channel_id=1, source_target_pairs={{0,8},{4,12},{8,0},{12,4},{1,9},{5,13},{9,1},{13,5},{2,10},{6,14},... | collective-permute-start | bytes 983048 | tf_op jit(solution)/shard_map/ppermute | solution.py:34
  66.5 8.4 %collective-permute-start.19 = (bf16[2,320,128]{2,1,0:T(8,128)(2,1)S(1)}, bf16[2,320,128]{2,1,0:T(8,128)(2,1)S(1)}, u32[]{:S(2)}, u32[]{:S(2)}) collective-permute-start(bf16[2,320,128]{2,1,0:T(8,128)(2,1)S(1)} %pad_maximum_fusion.10), channel_id=1, source_target_pairs={{0,4},{4,0},{8,12},{12,8},{1,5},{5,1},{9,13},{13,9},{2,6},{6,2},{1... | collective-permute-start | bytes 491528 | tf_op jit(solution)/shard_map/ppermute | solution.py:39

commit v2 on v1

v2 whole, which is shorter than its diff:
```python
import math

import jax
import jax.numpy as jnp
from jax import lax
from jax.experimental import pallas as pl
from jax.experimental.pallas import tpu as pltpu
from jax.sharding import PartitionSpec as P

FT = 2
RT = 2
W = 32
RBANDS = 2
TILE = FT * RT * W
HALF = RT * W
ROWS = RBANDS * RT
FRAME = ROWS * W
MIB = 1 << 20
BF = jnp.bfloat16
F32 = jnp.float32


def sizes():
    return lax.axis_size("ch"), lax.axis_size("st") // RBANDS


def place():
    st = lax.axis_index("st")
    return lax.axis_index("ch"), st // RBANDS, st % RBANDS


def send(data, axis, by):
    n = lax.axis_size(axis)
    return lax.ppermute(data, axis, [(i, (i + by) % n) for i in range(n)])


def swap_band(data):
    n = lax.axis_size("st")
    return lax.ppermute(data, "st", [(i, i ^ 1) for i in range(n)])


def gather_ch(shard):
    n_ch, _ = sizes()
    return [shard] + [send(shard, "ch", k) for k in range(1, n_ch)]


def ring_blocks(data):
    _, n_x = sizes()
    return [send(data, "st", RBANDS * j) for j in range(1, n_x)]


def neighbours(data):
    _, n_x = sizes()
    if n_x == 2:
        other = send(data, "st", RBANDS)
        return other, other
    return send(data, "st", RBANDS), send(data, "st", -RBANDS)


def lanes(shape):
    return lax.broadcasted_iota(jnp.int32, shape, len(shape) - 1)


def roll(x, by):
    return pltpu.roll(x, by, x.ndim - 1)


def frames_of(own, sibling, band):
    own = own.astype(F32)
    sibling = sibling.astype(F32)
    first = jnp.where(band == 0, own, sibling)
    second = jnp.where(band == 0, sibling, own)
    low = lanes(first.shape) < HALF
    return jnp.where(low, first, roll(second, HALF)), jnp.where(low, roll(first, HALF), second)


def tile_of(frame0, frame1, band):
    low = lanes(frame0.shape) < HALF
    upper = jnp.where(low, frame0, roll(frame1, HALF))
    lower = jnp.where(low, roll(frame0, HALF), frame1)
    return jnp.where(band == 0, upper, lower)


def time_pieces(own, before, after, m, n_x):
    own32 = own.astype(F32)
    before = jnp.where(m > 0, before.astype(F32), 0.0)
    after = jnp.where(m < n_x - 1, after.astype(F32), 0.0)
    low = lanes(own32.shape) < HALF
    earlier = roll(jnp.where(low, own32, before), HALF)
    later = roll(jnp.where(low, after, own32), HALF)
    return earlier.astype(BF), own, later.astype(BF)


def inside(dr, dc, shape):
    lane = lanes(shape)
    row = lane // W + dr
    col = lane % W + dc
    return (row >= 0) & (row < ROWS) & (col >= 0) & (col < W)


def spatial_forward(mine, siblings, weight):
    n_ch, n_x = sizes()
    cb = mine[0].shape[0]
    channels = n_ch * cb

    def body(*refs):
        mine_refs, sibling_refs = refs[:n_ch], refs[n_ch : 2 * n_ch]
        w_ref, out_ref, field, acc = refs[2 * n_ch :]
        c, _, band = place()
        for k in range(n_ch):
            at = pl.ds(pl.multiple_of(((c + n_ch - k) % n_ch) * cb, 16), cb)
            f0, f1 = frames_of(mine_refs[k][...], sibling_refs[k][...], band)
            field[at, :FRAME] = f0.astype(BF)
            field[at, FRAME:] = f1.astype(BF)
        for tap in range(9):
            dr, dc = tap // 3 - 1, tap % 3 - 1
            part = jnp.dot(w_ref[tap], field[...], preferred_element_type=F32)
            by = (-(W * dr + dc)) % FRAME
            ok = inside(dr, dc, (cb, FRAME))
            for a in range(FT):
                at = slice(a * FRAME, (a + 1) * FRAME)
                moved = part[:, at]
                if by:
                    moved = jnp.where(ok, roll(moved, by), 0.0)
                acc[:, at] = moved + acc[:, at] if tap else moved
        total = tile_of(acc[:, :FRAME], acc[:, FRAME:], band)
        out_ref[...] = (mine_refs[0][...].astype(F32) + total).astype(BF)

    return pl.pallas_call(
        body,
        out_shape=jax.ShapeDtypeStruct((cb, TILE), BF),
        scratch_shapes=[pltpu.VMEM((channels, FT * FRAME), BF), pltpu.VMEM((cb, FT * FRAME), F32)],
        compiler_params=pltpu.CompilerParams(vmem_limit_bytes=16 * MIB),
        name="spatial_forward",
    )(*mine, *siblings, weight)


def temporal_forward(mine, before, after, weight):
    n_ch, n_x = sizes()
    cb = mine[0].shape[0]
    channels = n_ch * cb

    def body(*refs):
        mine_refs = refs[:n_ch]
        before_ref, after_ref, w_ref, out_ref, field = refs[n_ch:]
        c, m, _ = place()
        for k in range(n_ch):
            at = pl.ds(pl.multiple_of(((c + n_ch - k) % n_ch) * cb, 16), cb)
            pieces = time_pieces(mine_refs[k][...], before_ref[k], after_ref[k], m, n_x)
            for d in range(3):
                field[d, at, :] = pieces[d]
        total = mine_refs[0][...].astype(F32)
        for d in range(3):
            total += jnp.dot(w_ref[d], field[d], preferred_element_type=F32)
        out_ref[...] = total.astype(BF)

    return pl.pallas_call(
        body,
        out_shape=jax.ShapeDtypeStruct((cb, TILE), BF),
        scratch_shapes=[pltpu.VMEM((3, channels, TILE), BF)],
        compiler_params=pltpu.CompilerParams(vmem_limit_bytes=16 * MIB),
        name="temporal_forward",
    )(*mine, before, after, weight)


def emit_chunks(total, scratch, out_refs, c, n_ch, cb):
    scratch[...] = total.T
    for k in range(n_ch):
        at = pl.ds(pl.multiple_of(((c + k) % n_ch) * cb, 16), cb)
        out_refs[k][...] = scratch[at, :].astype(out_refs[k].dtype)


def chunk_shapes(n_ch, cb):
    return [jax.ShapeDtypeStruct((cb, TILE), BF if k else F32) for k in range(n_ch)]


def temporal_backward(field, before, after, weight):
    n_ch, n_x = sizes()
    cb = field.shape[0]
    channels = n_ch * cb

    def body(field_ref, before_ref, after_ref, w_ref, *rest):
        out_refs, scratch = rest[:n_ch], rest[n_ch]
        c, m, _ = place()
        pieces = time_pieces(field_ref[...], before_ref[...], after_ref[...], m, n_x)
        total = jnp.zeros((TILE, channels), F32)
        for d in range(3):
            left = pieces[2 - d].astype(F32).T.astype(BF)
            total += jnp.dot(left, w_ref[d], preferred_element_type=F32)
        emit_chunks(total, scratch, out_refs, c, n_ch, cb)

    return pl.pallas_call(
        body,
        out_shape=chunk_shapes(n_ch, cb),
        scratch_shapes=[pltpu.VMEM((channels, TILE), F32)],
        compiler_params=pltpu.CompilerParams(vmem_limit_bytes=16 * MIB),
        name="temporal_backward",
    )(field, before, after, weight)


def shifted_columns(frame, toward):
    cells = frame.T
    col = lax.broadcasted_iota(jnp.int32, cells.shape, 0) % W
    out = []
    for dc in (-toward, 0, toward):
        moved = cells
        if dc:
            ok = (col + dc >= 0) & (col + dc < W)
            moved = jnp.where(ok, pltpu.roll(cells, (-dc) % FRAME, 0), 0.0)
        out.append(moved.astype(BF))
    return out


def spatial_backward(field, sibling, weight):
    n_ch, _ = sizes()
    cb = field.shape[0]
    channels = n_ch * cb

    def body(field_ref, sibling_ref, w_ref, *rest):
        out_refs, (left, scratch) = rest[:n_ch], rest[n_ch:]
        c, _, band = place()
        blank = jnp.zeros((W, 3 * cb), BF)
        for a, frame in enumerate(frames_of(field_ref[...], sibling_ref[...], band)):
            left[a, :W, :] = blank
            left[a, W + FRAME :, :] = blank
            for q, moved in enumerate(shifted_columns(frame, -1)):
                left[a, W : W + FRAME, q * cb : (q + 1) * cb] = moved
        total = jnp.zeros((TILE, channels), F32)
        for g in range(3):
            start = pl.multiple_of(HALF * band + W * (2 - g), W)
            rows = jnp.concatenate([left[a, pl.ds(start, HALF), :] for a in range(FT)], axis=0)
            total += jnp.dot(rows, w_ref[g], preferred_element_type=F32)
        emit_chunks(total, scratch, out_refs, c, n_ch, cb)

    return pl.pallas_call(
        body,
        out_shape=chunk_shapes(n_ch, cb),
        scratch_shapes=[
            pltpu.VMEM((FT, FRAME + 2 * W, 3 * cb), BF),
            pltpu.VMEM((channels, TILE), F32),
        ],
        compiler_params=pltpu.CompilerParams(vmem_limit_bytes=16 * MIB),
        name="spatial_backward",
    )(field, sibling, weight.reshape(3, 3 * cb, channels))


def pairs_from(own, sibling, rest):
    return [(own, sibling)] + [(both.at[0], both.at[1]) for both in rest]


def spatial_grads(grads, fields, scale):
    _, n_x = sizes()
    ob, ib = grads[0].shape[0], fields[0].shape[0]
    frames = FT * n_x
    n_in = n_x + 1

    def body(*refs):
        g_refs, l_refs = refs[:n_in], refs[n_in : 2 * n_in]
        out_ref, left, right = refs[2 * n_in :]
        _, _, band = place()
        step = pl.program_id(0)

        @pl.when(step == 0)
        def _():
            blank = jnp.zeros((W, ib), BF)
            g_pairs = pairs_from(g_refs[0], g_refs[1], g_refs[2:])
            l_pairs = pairs_from(l_refs[0], l_refs[1], l_refs[2:])
            for j in range(n_x):
                for a, frame in enumerate(frames_of(g_pairs[j][0][...], g_pairs[j][1][...], band)):
                    f = FT * j + a
                    left[:, f * FRAME : (f + 1) * FRAME] = frame.astype(BF)
                for a, frame in enumerate(frames_of(l_pairs[j][0][...], l_pairs[j][1][...], band)):
                    f = FT * j + a
                    for q, moved in enumerate(shifted_columns(frame, 1)):
                        right[q, f, :W, :] = blank
                        right[q, f, W + FRAME :, :] = blank
                        right[q, f, W : W + FRAME, :] = moved

        start = pl.multiple_of(W * (step // 3), W)
        moved = jnp.concatenate([right[step % 3, f, pl.ds(start, FRAME), :] for f in range(frames)], axis=0)
        out_ref[0] = jnp.dot(left[...], moved, preferred_element_type=F32) * scale

    whole = lambda x: pl.BlockSpec(x.shape, lambda g: (0,) * x.ndim)
    args = (*grads[:2], *grads[2], *fields[:2], *fields[2])
    return pl.pallas_call(
        body,
        grid=(9,),
        in_specs=[whole(x) for x in args],
        out_specs=pl.BlockSpec((1, ob, ib), lambda g: (g, 0, 0)),
        out_shape=jax.ShapeDtypeStruct((9, ob, ib), F32),
        scratch_shapes=[
            pltpu.VMEM((ob, frames * FRAME), BF),
            pltpu.VMEM((3, frames, FRAME + 2 * W, ib), BF),
        ],
        compiler_params=pltpu.CompilerParams(vmem_limit_bytes=24 * MIB),
        name="spatial_grads",
    )(*args)


def temporal_grads(grads, grads_sibling, fields, fields_sibling, scale):
    _, n_x = sizes()
    ob, ib = grads[0].shape[0], fields[0].shape[0]
    span = FT * n_x * FRAME

    def body(*refs):
        g_refs, gs_refs, h_refs, hs_refs = (refs[q * n_x : (q + 1) * n_x] for q in range(4))
        out_ref, left, right = refs[4 * n_x :]
        _, m, band = place()
        right[:FRAME, :] = jnp.zeros((FRAME, ib), BF)
        right[FRAME + span :, :] = jnp.zeros((FRAME, ib), BF)
        for j in range(n_x):
            block = (m + n_x - j) % n_x
            for a, frame in enumerate(frames_of(g_refs[j][...], gs_refs[j][...], band)):
                at = pl.multiple_of((FT * block + a) * FRAME, FRAME)
                left[:, pl.ds(at, FRAME)] = frame.astype(BF)
            for a, frame in enumerate(frames_of(h_refs[j][...], hs_refs[j][...], band)):
                at = pl.multiple_of((FT * block + a + 1) * FRAME, FRAME)
                right[pl.ds(at, FRAME), :] = frame.T.astype(BF)
        for d in range(3):
            moved = right[d * FRAME : d * FRAME + span, :]
            out_ref[d] = jnp.dot(left[...], moved, preferred_element_type=F32) * scale

    return pl.pallas_call(
        body,
        out_shape=jax.ShapeDtypeStruct((3, ob, ib), F32),
        scratch_shapes=[pltpu.VMEM((ob, span), BF), pltpu.VMEM((span + 2 * FRAME, ib), BF)],
        compiler_params=pltpu.CompilerParams(vmem_limit_bytes=24 * MIB),
        name="temporal_grads",
    )(*grads, *grads_sibling, *fields, *fields_sibling)


def reduce_ch(base, chunks):
    total = base.astype(F32) + chunks[0]
    for k in range(1, len(chunks)):
        total = total + send(chunks[k], "ch", k).astype(F32)
    return total.astype(BF)


def on_device(latents, spatial_weight, temporal_weight, cotangent):
    n_ch, n_x = sizes()
    assert n_ch == RBANDS * n_x
    c, m, band = place()
    scale = 1.0 / math.sqrt(TILE * RBANDS * n_x)

    def block(pieces, b):
        stack = jnp.stack(pieces) if isinstance(pieces, list) else pieces
        return lax.dynamic_index_in_dim(stack, (c + n_ch - b) % n_ch, 0, keepdims=False)

    cot_ring = ring_blocks(cotangent)
    mine = gather_ch(latents)
    chunks = temporal_backward(cotangent, cot_ring[0], cot_ring[-1], temporal_weight)

    siblings = [swap_band(piece) for piece in mine]
    hidden = spatial_forward(mine, siblings, spatial_weight)
    hidden, base = lax.optimization_barrier((hidden, cotangent))

    hidden_grad = reduce_ch(base, chunks)
    grad_sibling = swap_band(hidden_grad)
    chunks = spatial_backward(hidden_grad, grad_sibling, spatial_weight)
    latent_grad = reduce_ch(hidden_grad, chunks)

    hidden_mine = gather_ch(hidden)
    before, after = neighbours(jnp.stack(hidden_mine))
    temporal_out = temporal_forward(hidden_mine, before, after, temporal_weight)

    own_block = RBANDS * m + band
    sib_block = RBANDS * m + 1 - band

    hid_own, hid_sib = [block(hidden_mine, own_block)], [block(hidden_mine, sib_block)]
    for j in range(1, n_x):
        if n_x == 2:
            hid_own.append(block(before, own_block))
            hid_sib.append(block(before, sib_block))
        else:
            target = RBANDS * ((m + j) % n_x)
            both = jnp.stack([block(hidden_mine, target + band), block(hidden_mine, target + 1 - band)])
            both = send(both, "st", RBANDS * j)
            hid_own.append(both[0])
            hid_sib.append(both[1])
    cots = [cotangent] + cot_ring
    temporal_grad = temporal_grads(
        cots, [swap_band(x) for x in cots], hid_own, [swap_band(x) for x in hid_sib], scale
    )

    lat_rest, grad_rest = [], []
    for j in range(1, n_x):
        target = RBANDS * ((m + j) % n_x) + band
        both = jnp.stack([block(mine, target), block(siblings, target)])
        lat_rest.append(send(both, "st", RBANDS * j))
        grad_rest.append(send(jnp.stack([hidden_grad, grad_sibling]), "st", RBANDS * j))
    spatial_grad = spatial_grads(
        (hidden_grad, grad_sibling, grad_rest),
        (block(mine, own_block), block(siblings, own_block), lat_rest),
        scale,
    )
    return temporal_out, latent_grad, spatial_grad, temporal_grad


def solution(mesh):
    return jax.shard_map(
        on_device,
        mesh=mesh,
        in_specs=(
            P("ch", ("groups", "st")),
            P(None, "ch", None),
            P(None, "ch", None),
            P("ch", ("groups", "st")),
        ),
        out_specs=(
            P("ch", ("groups", "st")),
            P("ch", ("groups", "st")),
            P("groups", "ch", "st"),
            P("groups", "ch", "st"),
        ),
        check_vma=False,
    )
```

time: 77.9 us -> 66.8 us (0.86)
  waiting for transfers between devices: 25.9 us -> 11.2 us
  starting transfers between devices: 23.5 us -> 28.9 us
  Pallas kernels: 18.8 us -> 17.1 us
    ppermute x16, waiting for transfers between devices: 24.6 us -> 11.1 us  [send(): return lax.ppermute(data, axis, [(i, (i + by) % n) for i in range(n)])]
    ppermute x16, starting transfers between devices: 23.2 us -> 27.1 us  [send(): return lax.ppermute(data, axis, [(i, (i + by) % n) for i in range(n)])]
    pallas_call x4, Pallas kernels: 16.1 us -> 13.6 us  [the longest x1 6.13 us: spatial_grads(): pl.pallas_call(body, grid=(9,), in_specs=[whole(x) for x in args], out_sp...]
    ppermute x4 -> x9, starting transfers between devices: 0.28 us -> 1.81 us  [swap_band(): return lax.ppermute(data, 'st', [(i, i ^ 1) for i in range(n)])]
    ppermute x4 -> x9, waiting for transfers between devices: 1.24 us -> 0.02 us  [swap_band(): return lax.ppermute(data, 'st', [(i, i ^ 1) for i in range(n)])]
    another operation x9 -> x5, other arithmetic: 2.01 us -> 1.05 us  [the longest x2 0.97 us: block(): stack = jnp.stack(pieces) if isinstance(pieces, list) else pieces]
    pallas_call x1, Pallas kernels: 0.85 us -> 1.74 us  [temporal_backward(): pl.pallas_call(body, out_shape=chunk_shapes(n_ch, cb), scratch_shapes=[pl...]
    convert_element_type x2, other arithmetic: 0.76 us -> 1.63 us  [reduce_ch(): return total.astype(BF)]
  transfers between devices with their start and end apart: 20 -> 25, of which waited for: 8 -> 6; matrix products, arithmetic and copies ran while one was open for 4% -> 4% of each run, Pallas kernels for 21% -> 21%
where the time goes in v2:
time: 66.8 us; the launch traced here: 66.4 us
  starting transfers between devices  28.9 us (43%)
  Pallas kernels  17.1 us (26%)
  waiting for transfers between devices  11.2 us (17%)
  local copies, waits for them, and re-layouts  5.74 us (9%)
  other arithmetic  2.68 us (4%)
  between operations  0.79 us (1%)
    ppermute x16, starting transfers between devices, send(): return lax.ppermute(data, axis, [(i, (i + by) % n) for i in range(n)])  27.1 us
    ppermute x16, waiting for transfers between devices, send(): return lax.ppermute(data, axis, [(i, (i + by) % n) for i in range(n)])  11.1 us
    pallas_call x1, Pallas kernels, spatial_grads(): pl.pallas_call(body, grid=(9,), in_specs=[whole(x) for x in args], out_sp...  6.13 us
    unnamed x10, local copies, waits for them, and re-layouts  5.68 us
    pallas_call x1, Pallas kernels, temporal_grads(): pl.pallas_call(body, out_shape=jax.ShapeDtypeStruct((3, ob, ib), F32), sc...  3.1 us
    pallas_call x1, Pallas kernels, spatial_forward(): pl.pallas_call(body, out_shape=jax.ShapeDtypeStruct((cb, TILE), BF), scra...  2.68 us
    ppermute x9, starting transfers between devices, swap_band(): return lax.ppermute(data, 'st', [(i, i ^ 1) for i in range(n)])  1.81 us
    pallas_call x1, Pallas kernels, temporal_forward(): pl.pallas_call(body, out_shape=jax.ShapeDtypeStruct((cb, TILE), BF), scra...  1.78 us
  transfers between devices with their start and end apart: 25, of which 6 were waited for; matrix products, arithmetic and copies ran while one was open for 4% of the time, Pallas kernels for 21%

profile of v2, /device:TPU:0, one launch (start us, length us, event | category | flops | bytes accessed | tf_op | source)
XLA Modules:
  0.0 66.4 jit_solution(8763284429966976838)
XLA Ops:
  0.6 3.1 %collective-permute-start = (bf16[320,128]{1,0:T(8,128)(2,1)}, bf16[320,128]{1,0:T(8,128)(2,1)S(1)}, u32[]{:S(2)}, u32[]{:S(2)}) collective-permute-start(bf16[320,128]{1,0:T(8,128)(2,1)} %refs_0_.2), channel_id=1, source_target_pairs={{0,1},{1,2},{2,3},{3,0},{4,5},{5,6},{6,7},{7,4},{8,9},{9,10},{10,1... | collective-permute-start | bytes 245768 | tf_op jit(solution)/shard_map/ppermute | solution.py:34
  3.7 1.5 %collective-permute-start.11 = (bf16[320,128]{1,0:T(8,128)(2,1)}, bf16[320,128]{1,0:T(8,128)(2,1)S(1)}, u32[]{:S(2)}, u32[]{:S(2)}) collective-permute-start(bf16[320,128]{1,0:T(8,128)(2,1)} %refs_0_.3), channel_id=1, source_target_pairs={{0,8},{4,12},{8,0},{12,4},{1,9},{5,13},{9,1},{13,5},{2,10},{6,14},... | collective-permute-start | bytes 245768 | tf_op jit(solution)/shard_map/ppermute | solution.py:34
  5.2 2.6 %collective-permute-start.1 = (bf16[320,128]{1,0:T(8,128)(2,1)}, bf16[320,128]{1,0:T(8,128)(2,1)S(1)}, u32[]{:S(2)}, u32[]{:S(2)}) collective-permute-start(bf16[320,128]{1,0:T(8,128)(2,1)} %refs_0_.2), channel_id=1, source_target_pairs={{0,2},{1,3},{2,0},{3,1},{4,6},{5,7},{6,4},{7,5},{8,10},{9,11},{10,... | collective-permute-start | bytes 245768 | tf_op jit(solution)/shard_map/ppermute | solution.py:34
  7.8 1.3 %collective-permute-start.2 = (bf16[320,128]{1,0:T(8,128)(2,1)}, bf16[320,128]{1,0:T(8,128)(2,1)S(1)}, u32[]{:S(2)}, u32[]{:S(2)}) collective-permute-start(bf16[320,128]{1,0:T(8,128)(2,1)} %refs_0_.2), channel_id=1, source_target_pairs={{0,3},{1,0},{2,1},{3,2},{4,7},{5,4},{6,5},{7,6},{8,11},{9,8},{10,9... | collective-permute-start | bytes 245768 | tf_op jit(solution)/shard_map/ppermute | solution.py:34
  9.1 0.0 collective-permute-start.3
  9.1 0.0 collective-permute-done.refs_1_
  9.1 0.5 collective-permute-start.4
  9.7 0.0 collective-permute-done.11.before_ref.after_ref.refs_1_
  9.7 1.7 %copy-done.2 = bf16[3,320,1280]{2,1,0:T(8,128)(2,1)S(1)} copy-done((bf16[3,320,1280]{2,1,0:T(8,128)(2,1)S(1)}, bf16[3,320,1280]{2,1,0:T(8,128)(2,1)}, u32[]{:S(2)}) %copy-start.2) | copy-done | bytes 2457624
  11.3 1.7 %temporal_backward.1 = (f32[320,128]{1,0:T(8,128)S(1)}, bf16[320,128]{1,0:T(8,128)(2,1)S(1)}, bf16[320,128]{1,0:T(8,128)(2,1)S(1)}, bf16[320,128]{1,0:T(8,128)(2,1)S(1)}) custom-call(bf16[320,128]{1,0:T(8,128)(2,1)} %refs_0_.3, bf16[320,128]{1,0:T(8,128)(2,1)S(1)} %collective-permute-done.11.before_ref.after_ref.refs_1_, ...), custom_call_target="tpu_custom_call" | custom-call | tf_op jit(solution)/shard_map/temporal_backward/pallas_call | solution.py:192
  13.1 0.9 %collective-permute-start.14 = (bf16[320,128]{1,0:T(8,128)(2,1)S(1)}, bf16[320,128]{1,0:T(8,128)(2,1)S(1)}, u32[]{:S(2)}, u32[]{:S(2)}) collective-permute-start(bf16[320,128]{1,0:T(8,128)(2,1)S(1)} %get-tuple-element.19), channel_id=1, source_target_pairs={{0,3},{1,0},{2,1},{3,2},{4,7},{5,4},{6,5},{7,6},{8,11},{9,8},{10,9... | collective-permute-start | bytes 245768 | tf_op jit(solution)/shard_map/ppermute | solution.py:34
  14.0 0.0 collective-permute-done.1.refs_2_
  14.0 1.3 %collective-permute-start.13 = (bf16[320,128]{1,0:T(8,128)(2,1)S(1)}, bf16[320,128]{1,0:T(8,128)(2,1)S(1)}, u32[]{:S(2)}, u32[]{:S(2)}) collective-permute-start(bf16[320,128]{1,0:T(8,128)(2,1)S(1)} %get-tuple-element.18), channel_id=1, source_target_pairs={{0,2},{1,3},{2,0},{3,1},{4,6},{5,7},{6,4},{7,5},{8,10},{9,11},{10,... | collective-permute-start | bytes 245768 | tf_op jit(solution)/shard_map/ppermute | solution.py:34
  15.3 0.0 collective-permute-done.2.refs_3_
  15.3 1.3 %collective-permute-start.12 = (bf16[320,128]{1,0:T(8,128)(2,1)S(1)}, bf16[320,128]{1,0:T(8,128)(2,1)S(1)}, u32[]{:S(2)}, u32[]{:S(2)}) collective-permute-start(bf16[320,128]{1,0:T(8,128)(2,1)S(1)} %get-tuple-element.17), channel_id=1, source_target_pairs={{0,1},{1,2},{2,3},{3,0},{4,5},{5,6},{6,7},{7,4},{8,9},{9,10},{10,1... | collective-permute-start | bytes 245768 | tf_op jit(solution)/shard_map/ppermute | solution.py:34
  16.6 0.0 collective-permute-done.3.refs_4_
  16.6 0.0 collective-permute-start.5
  16.6 0.0 collective-permute-done.4.refs_5_
  16.6 0.5 collective-permute-start.6
  17.1 0.9 %pad_maximum_fusion.1 = bf16[4,320,128]{2,1,0:T(8,128)(2,1)S(1)} fusion(bf16[1,320,128]{2,1,0:T(8,128)(2,1)S(1)} %bitcast.36, bf16[1,320,128]{2,1,0:T(8,128)(2,1)S(1)} %bitcast.35, bf16[1,320,128]{2,1,0:T(8,128)(2,1)S(1)} %bitcast.34, bf16[1,320,128]{2,1,0:T(8,128)(2,1)} %bitcast.31), kind=kLoop, calls=%fused_computation.1 | loop fusion | flops 491520 | bytes 655360 | tf_op jit(solution)/shard_map/stack | solution.py:346
  18.1 0.0 collective-permute-done.5.refs_6_
  18.1 0.1 collective-permute-start.21
  18.2 0.0 collective-permute-done.6.refs_7_
  18.2 3.1 %copy-done = bf16[9,320,1280]{2,1,0:T(8,128)(2,1)S(1)} copy-done((bf16[9,320,1280]{2,1,0:T(8,128)(2,1)S(1)}, bf16[9,320,1280]{2,1,0:T(8,128)(2,1)}, u32[]{:S(2)}) %copy-start) | copy-done | bytes 7372824
  21.3 0.9 %copy-done.4 = bf16[320,128]{1,0:T(8,128)(2,1)S(1)} copy-done((bf16[320,128]{1,0:T(8,128)(2,1)S(1)}, bf16[320,128]{1,0:T(8,128)(2,1)}, u32[]{:S(2)}) %copy-start.4) | copy-done | bytes 81944
  22.2 2.7 %spatial_forward.1.refs_0_ = bf16[320,128]{1,0:T(8,128)(2,1)S(1)} custom-call(bf16[320,128]{1,0:T(8,128)(2,1)S(1)} %copy-done.4, bf16[320,128]{1,0:T(8,128)(2,1)S(1)} %collective-permute-done.refs_1_, bf16[320,128]{1,0:T(8,128)(2,1)S(1)} %collective-permute-done.1.refs_2_, bf16[320,128]{1,0:T(8,128)(2,1)S(1)} %collective-permute-done.2.refs_3_, ...), custom_call_target="tpu_custom_call" | custom-call | tf_op jit(solution)/shard_map/spatial_forward/pallas_call | solution.py:129
  24.9 0.9 %collective-permute-start.7 = (bf16[320,128]{1,0:T(8,128)(2,1)S(1)}, bf16[320,128]{1,0:T(8,128)(2,1)S(1)}, u32[]{:S(2)}, u32[]{:S(2)}) collective-permute-start(bf16[320,128]{1,0:T(8,128)(2,1)S(1)} %spatial_forward.1.refs_0_), channel_id=1, source_target_pairs={{0,1},{1,2},{2,3},{3,0},{4,5},{5,6},{6,7},{7,4},{8,9},{9,10},{10,1... | collective-permute-start | bytes 245768 | tf_op jit(solution)/shard_map/ppermute | solution.py:34
  25.8 0.0 collective-permute-done.14
  25.8 2.2 %collective-permute-start.8 = (bf16[320,128]{1,0:T(8,128)(2,1)S(1)}, bf16[320,128]{1,0:T(8,128)(2,1)S(1)}, u32[]{:S(2)}, u32[]{:S(2)}) collective-permute-start(bf16[320,128]{1,0:T(8,128)(2,1)S(1)} %spatial_forward.1.refs_0_), channel_id=1, source_target_pairs={{0,2},{1,3},{2,0},{3,1},{4,6},{5,7},{6,4},{7,5},{8,10},{9,11},{10,... | collective-permute-start | bytes 245768 | tf_op jit(solution)/shard_map/ppermute | solution.py:34
  28.0 0.0 collective-permute-done.13
  28.0 1.3 %collective-permute-start.9 = (bf16[320,128]{1,0:T(8,128)(2,1)S(1)}, bf16[320,128]{1,0:T(8,128)(2,1)S(1)}, u32[]{:S(2)}, u32[]{:S(2)}) collective-permute-start(bf16[320,128]{1,0:T(8,128)(2,1)S(1)} %spatial_forward.1.refs_0_), channel_id=1, source_target_pairs={{0,3},{1,0},{2,1},{3,2},{4,7},{5,4},{6,5},{7,6},{8,11},{9,8},{10,9... | collective-permute-start | bytes 245768 | tf_op jit(solution)/shard_map/ppermute | solution.py:34
  29.4 0.0 collective-permute-done.12
  29.4 0.9 %add_convert_fusion.1.field_ref.refs_0_ = bf16[320,128]{1,0:T(8,128)(2,1)S(1)} fusion(bf16[320,128]{1,0:T(8,128)(2,1)S(1)} %collective-permute-done.14, bf16[320,128]{1,0:T(8,128)(2,1)S(1)} %collective-permute-done.13, bf16[320,128]{1,0:T(8,128)(2,1)S(1)} %collective-permute-done.12, f32[320,128]{1,0:T(8,128)S(1)} %get-tuple-element.16, ...), kind=kLoop, calls=%fused_computation.6 | loop fusion | flops 368640 | bytes 573440 | tf_op jit(solution)/shard_map/convert_element_type | solution.py:336
  30.3 0.1 collective-permute-start.15
  30.5 1.6 %collective-permute-done.7.refs_1_ = bf16[320,128]{1,0:T(8,128)(2,1)S(1)} collective-permute-done((bf16[320,128]{1,0:T(8,128)(2,1)S(1)}, bf16[320,128]{1,0:T(8,128)(2,1)S(1)}, u32[]{:S(2)}, u32[]{:S(2)}) %collective-permute-start.7) | collective-permute-done | bytes 81952 | tf_op jit(solution)/shard_map/ppermute | solution.py:34
  32.1 3.0 %collective-permute-done.8.refs_2_ = bf16[320,128]{1,0:T(8,128)(2,1)S(1)} collective-permute-done((bf16[320,128]{1,0:T(8,128)(2,1)S(1)}, bf16[320,128]{1,0:T(8,128)(2,1)S(1)}, u32[]{:S(2)}, u32[]{:S(2)}) %collective-permute-start.8) | collective-permute-done | bytes 81952 | tf_op jit(solution)/shard_map/ppermute | solution.py:34
  35.1 0.0 collective-permute-done.9.refs_3_
  35.2 2.7 %collective-permute-start.10 = (bf16[4,320,128]{2,1,0:T(8,128)(2,1)S(1)}, bf16[4,320,128]{2,1,0:T(8,128)(2,1)S(1)}, u32[]{:S(2)}, u32[]{:S(2)}) collective-permute-start(bf16[4,320,128]{2,1,0:T(8,128)(2,1)S(1)} %pad_maximum_fusion), channel_id=1, source_target_pairs={{0,8},{4,12},{8,0},{12,4},{1,9},{5,13},{9,1},{13,5},{2,10},{6,14},... | collective-permute-start | bytes 983048 | tf_op jit(solution)/shard_map/ppermute | solution.py:34
  37.9 0.1 collective-permute-start.20
  38.0 0.0 collective-permute-done.15.sibling_ref.refs_1_
  38.0 0.0 copy-done.1
  38.0 1.6 %spatial_backward.1 = (f32[320,128]{1,0:T(8,128)S(1)}, bf16[320,128]{1,0:T(8,128)(2,1)S(1)}, bf16[320,128]{1,0:T(8,128)(2,1)S(1)}, bf16[320,128]{1,0:T(8,128)(2,1)S(1)}) custom-call(bf16[320,128]{1,0:T(8,128)(2,1)S(1)} %add_convert_fusion.1.field_ref.refs_0_, bf16[320,128]{1,0:T(8,128)(2,1)S(1)} %collective-permute-done.15.sibling_ref.refs_1_, ...), custom_call_target="tpu_custom_call" | custom-call | tf_op jit(solution)/shard_map/spatial_backward/pallas_call | solution.py:235
  39.7 0.0 copy-start.3
  39.7 2.6 %collective-permute-start.18 = (bf16[320,128]{1,0:T(8,128)(2,1)S(1)}, bf16[320,128]{1,0:T(8,128)(2,1)S(1)}, u32[]{:S(2)}, u32[]{:S(2)}) collective-permute-start(bf16[320,128]{1,0:T(8,128)(2,1)S(1)} %get-tuple-element.23), channel_id=1, source_target_pairs={{0,3},{1,0},{2,1},{3,2},{4,7},{5,4},{6,5},{7,6},{8,11},{9,8},{10,9... | collective-permute-start | bytes 245768 | tf_op jit(solution)/shard_map/ppermute | solution.py:34
  42.2 0.8 %collective-permute-start.17 = (bf16[320,128]{1,0:T(8,128)(2,1)S(1)}, bf16[320,128]{1,0:T(8,128)(2,1)S(1)}, u32[]{:S(2)}, u32[]{:S(2)}) collective-permute-start(bf16[320,128]{1,0:T(8,128)(2,1)S(1)} %get-tuple-element.22), channel_id=1, source_target_pairs={{0,2},{1,3},{2,0},{3,1},{4,6},{5,7},{6,4},{7,5},{8,10},{9,11},{10,... | collective-permute-start | bytes 245768 | tf_op jit(solution)/shard_map/ppermute | solution.py:34
  43.1 3.4 %collective-permute-done.10.refs_4_.refs_5_ = bf16[4,320,128]{2,1,0:T(8,128)(2,1)S(1)} collective-permute-done((bf16[4,320,128]{2,1,0:T(8,128)(2,1)S(1)}, bf16[4,320,128]{2,1,0:T(8,128)(2,1)S(1)}, u32[]{:S(2)}, u32[]{:S(2)}) %collective-permute-start.10) | collective-permute-done | bytes 327712 | tf_op jit(solution)/shard_map/ppermute | solution.py:34
  46.5 1.8 %collective-permute-start.16 = (bf16[320,128]{1,0:T(8,128)(2,1)S(1)}, bf16[320,128]{1,0:T(8,128)(2,1)S(1)}, u32[]{:S(2)}, u32[]{:S(2)}) collective-permute-start(bf16[320,128]{1,0:T(8,128)(2,1)S(1)} %get-tuple-element.21), channel_id=1, source_target_pairs={{0,1},{1,2},{2,3},{3,0},{4,5},{5,6},{6,7},{7,4},{8,9},{9,10},{10,1... | collective-permute-start | bytes 245768 | tf_op jit(solution)/shard_map/ppermute | solution.py:34
  48.3 0.0 collective-permute-done.18
  48.3 0.1 collective-permute-start.22
  48.4 0.2 collective-permute-done.17
  48.6 2.7 %collective-permute-start.19 = (bf16[2,320,128]{2,1,0:T(8,128)(2,1)S(1)}, bf16[2,320,128]{2,1,0:T(8,128)(2,1)S(1)}, u32[]{:S(2)}, u32[]{:S(2)}) collective-permute-start(bf16[2,320,128]{2,1,0:T(8,128)(2,1)S(1)} %pad_maximum_fusion.3), channel_id=1, source_target_pairs={{0,8},{4,12},{8,0},{12,4},{1,9},{5,13},{9,1},{13,5},{2,10},{6,14},... | collective-permute-start | bytes 491528 | tf_op jit(solution)/shard_map/ppermute | solution.py:34
  51.3 1.4 %collective-permute-done.16 = bf16[320,128]{1,0:T(8,128)(2,1)S(1)} collective-permute-done((bf16[320,128]{1,0:T(8,128)(2,1)S(1)}, bf16[320,128]{1,0:T(8,128)(2,1)S(1)}, u32[]{:S(2)}, u32[]{:S(2)}) %collective-permute-start.16) | collective-permute-done | bytes 81952 | tf_op jit(solution)/shard_map/ppermute | solution.py:34
  52.8 0.0 collective-permute-start.23
  52.8 0.0 collective-permute-done.20.refs_5_
  52.8 0.5 collective-permute-start.24
  53.3 0.7 %add_convert_fusion = bf16[320,128]{1,0:T(8,128)(2,1)} fusion(bf16[320,128]{1,0:T(8,128)(2,1)S(1)} %collective-permute-done.18, bf16[320,128]{1,0:T(8,128)(2,1)S(1)} %collective-permute-done.17, bf16[320,128]{1,0:T(8,128)(2,1)S(1)} %collective-permute-done.16, f32[320,128]{1,0:T(8,128)S(1)} %get-tuple-element.20, ...), kind=kLoop, calls=%fused_computation.5 | loop fusion | flops 368640 | bytes 573440 | tf_op jit(solution)/shard_map/convert_element_type | solution.py:336
  54.0 1.4 %collective-permute-done.19.refs_2_ = bf16[2,320,128]{2,1,0:T(8,128)(2,1)S(1)} collective-permute-done((bf16[2,320,128]{2,1,0:T(8,128)(2,1)S(1)}, bf16[2,320,128]{2,1,0:T(8,128)(2,1)S(1)}, u32[]{:S(2)}, u32[]{:S(2)}) %collective-permute-start.19) | collective-permute-done | bytes 163872 | tf_op jit(solution)/shard_map/ppermute | solution.py:34
  55.3 6.1 %spatial_grads.1 = f32[9,320,320]{2,1,0:T(8,128)} custom-call(bf16[320,128]{1,0:T(8,128)(2,1)S(1)} %add_convert_fusion.1.field_ref.refs_0_, bf16[320,128]{1,0:T(8,128)(2,1)S(1)} %collective-permute-done.15.sibling_ref.refs_1_, bf16[2,320,128]{2,1,0:T(8,128)(2,1)S(1)} %collective-permute-done.19.refs_2_, bf16[320,128]{1,0:T(8,128)(2,1)S(1)} %get-tuple-element.32.refs_3_, ...), custom_call_target="tpu_custom_call" | custom-call | tf_op jit(solution)/shard_map/spatial_grads/pallas_call | solution.py:285
  61.5 1.8 %temporal_forward.1 = bf16[320,128]{1,0:T(8,128)(2,1)} custom-call(bf16[320,128]{1,0:T(8,128)(2,1)S(1)} %spatial_forward.1.refs_0_, bf16[320,128]{1,0:T(8,128)(2,1)S(1)} %collective-permute-done.7.refs_1_, bf16[320,128]{1,0:T(8,128)(2,1)S(1)} %collective-permute-done.8.refs_2_, bf16[320,128]{1,0:T(8,128)(2,1)S(1)} %collective-permute-done.9.refs_3_, ...), custom_call_target="tpu_custom_call" | custom-call | tf_op jit(solution)/shard_map/temporal_forward/pallas_call | solution.py:157
  63.3 0.0 collective-permute-done.21.refs_2_
  63.3 0.0 collective-permute-done.22.refs_3_
  63.3 0.0 collective-permute-done.23.refs_6_
  63.3 0.0 collective-permute-done.24.refs_7_
  63.3 3.1 %temporal_grads.1 = f32[3,320,320]{2,1,0:T(8,128)} custom-call(bf16[320,128]{1,0:T(8,128)(2,1)} %refs_0_.3, bf16[320,128]{1,0:T(8,128)(2,1)S(1)} %collective-permute-done.11.before_ref.after_ref.refs_1_, bf16[320,128]{1,0:T(8,128)(2,1)S(1)} %collective-permute-done.21.refs_2_, bf16[320,128]{1,0:T(8,128)(2,1)S(1)} %collective-permute-done.22.refs_3_, ...), custom_call_target="tpu_custom_call" | custom-call | tf_op jit(solution)/shard_map/temporal_grads/pallas_call | solution.py:323
  (12 shorter events, 0.2 us)
Async XLA Ops:
  0.6 8.5 %collective-permute-start = (bf16[320,128]{1,0:T(8,128)(2,1)}, bf16[320,128]{1,0:T(8,128)(2,1)S(1)}, u32[]{:S(2)}, u32[]{:S(2)}) collective-permute-start(bf16[320,128]{1,0:T(8,128)(2,1)} %refs_0_.2), channel_id=1, source_target_pairs={{0,1},{1,2},{2,3},{3,0},{4,5},{5,6},{6,7},{7,4},{8,9},{9,10},{10,1... | collective-permute-start | bytes 245768 | tf_op jit(solution)/shard_map/ppermute | solution.py:34
  3.7 5.9 %collective-permute-start.11 = (bf16[320,128]{1,0:T(8,128)(2,1)}, bf16[320,128]{1,0:T(8,128)(2,1)S(1)}, u32[]{:S(2)}, u32[]{:S(2)}) collective-permute-start(bf16[320,128]{1,0:T(8,128)(2,1)} %refs_0_.3), channel_id=1, source_target_pairs={{0,8},{4,12},{8,0},{12,4},{1,9},{5,13},{9,1},{13,5},{2,10},{6,14},... | collective-permute-start | bytes 245768 | tf_op jit(solution)/shard_map/ppermute | solution.py:34
  5.2 8.8 %collective-permute-start.1 = (bf16[320,128]{1,0:T(8,128)(2,1)}, bf16[320,128]{1,0:T(8,128)(2,1)S(1)}, u32[]{:S(2)}, u32[]{:S(2)}) collective-permute-start(bf16[320,128]{1,0:T(8,128)(2,1)} %refs_0_.2), channel_id=1, source_target_pairs={{0,2},{1,3},{2,0},{3,1},{4,6},{5,7},{6,4},{7,5},{8,10},{9,11},{10,... | collective-permute-start | bytes 245768 | tf_op jit(solution)/shard_map/ppermute | solution.py:34
  7.8 7.5 %collective-permute-start.2 = (bf16[320,128]{1,0:T(8,128)(2,1)}, bf16[320,128]{1,0:T(8,128)(2,1)S(1)}, u32[]{:S(2)}, u32[]{:S(2)}) collective-permute-start(bf16[320,128]{1,0:T(8,128)(2,1)} %refs_0_.2), channel_id=1, source_target_pairs={{0,3},{1,0},{2,1},{3,2},{4,7},{5,4},{6,5},{7,6},{8,11},{9,8},{10,9... | collective-permute-start | bytes 245768 | tf_op jit(solution)/shard_map/ppermute | solution.py:34
  9.1 7.5 %collective-permute-start.3 = (bf16[320,128]{1,0:T(8,128)(2,1)}, bf16[320,128]{1,0:T(8,128)(2,1)S(1)}, u32[]{:S(2)}, u32[]{:S(2)}) collective-permute-start(bf16[320,128]{1,0:T(8,128)(2,1)} %refs_0_.2), channel_id=1, source_target_pairs={{0,4},{4,0},{8,12},{12,8},{1,5},{5,1},{9,13},{13,9},{2,6},{6,2},{1... | collective-permute-start | bytes 245768 | tf_op jit(solution)/shard_map/ppermute | solution.py:39
  9.1 7.5 %collective-permute-start.4 = (bf16[320,128]{1,0:T(8,128)(2,1)S(1)}, bf16[320,128]{1,0:T(8,128)(2,1)S(1)}, u32[]{:S(2)}, u32[]{:S(2)}) collective-permute-start(bf16[320,128]{1,0:T(8,128)(2,1)S(1)} %collective-permute-done.refs_1_), channel_id=1, source_target_pairs={{0,4},{4,0},{8,12},{12,8},{1,5},{5,1},{9,13},{13,9},{2,6},{6,2},{1... | collective-permute-start | bytes 245768 | tf_op jit(solution)/shard_map/ppermute | solution.py:39
  9.7 1.7 %copy-start.2 = (bf16[3,320,1280]{2,1,0:T(8,128)(2,1)S(1)}, bf16[3,320,1280]{2,1,0:T(8,128)(2,1)}, u32[]{:S(2)}) copy-start(bf16[3,320,1280]{2,1,0:T(8,128)(2,1)} %w_ref.1) | copy-start | bytes 7372804
  13.1 12.7 %collective-permute-start.14 = (bf16[320,128]{1,0:T(8,128)(2,1)S(1)}, bf16[320,128]{1,0:T(8,128)(2,1)S(1)}, u32[]{:S(2)}, u32[]{:S(2)}) collective-permute-start(bf16[320,128]{1,0:T(8,128)(2,1)S(1)} %get-tuple-element.19), channel_id=1, source_target_pairs={{0,3},{1,0},{2,1},{3,2},{4,7},{5,4},{6,5},{7,6},{8,11},{9,8},{10,9... | collective-permute-start | bytes 245768 | tf_op jit(solution)/shard_map/ppermute | solution.py:34
  14.0 14.1 %collective-permute-start.13 = (bf16[320,128]{1,0:T(8,128)(2,1)S(1)}, bf16[320,128]{1,0:T(8,128)(2,1)S(1)}, u32[]{:S(2)}, u32[]{:S(2)}) collective-permute-start(bf16[320,128]{1,0:T(8,128)(2,1)S(1)} %get-tuple-element.18), channel_id=1, source_target_pairs={{0,2},{1,3},{2,0},{3,1},{4,6},{5,7},{6,4},{7,5},{8,10},{9,11},{10,... | collective-permute-start | bytes 245768 | tf_op jit(solution)/shard_map/ppermute | solution.py:34
  15.3 14.1 %collective-permute-start.12 = (bf16[320,128]{1,0:T(8,128)(2,1)S(1)}, bf16[320,128]{1,0:T(8,128)(2,1)S(1)}, u32[]{:S(2)}, u32[]{:S(2)}) collective-permute-start(bf16[320,128]{1,0:T(8,128)(2,1)S(1)} %get-tuple-element.17), channel_id=1, source_target_pairs={{0,1},{1,2},{2,3},{3,0},{4,5},{5,6},{6,7},{7,4},{8,9},{9,10},{10,1... | collective-permute-start | bytes 245768 | tf_op jit(solution)/shard_map/ppermute | solution.py:34
  16.6 1.4 %collective-permute-start.5 = (bf16[320,128]{1,0:T(8,128)(2,1)S(1)}, bf16[320,128]{1,0:T(8,128)(2,1)S(1)}, u32[]{:S(2)}, u32[]{:S(2)}) collective-permute-start(bf16[320,128]{1,0:T(8,128)(2,1)S(1)} %collective-permute-done.1.refs_2_), channel_id=1, source_target_pairs={{0,4},{4,0},{8,12},{12,8},{1,5},{5,1},{9,13},{13,9},{2,6},{6,2},{1... | collective-permute-start | bytes 245768 | tf_op jit(solution)/shard_map/ppermute | solution.py:39
  16.6 1.6 %collective-permute-start.6 = (bf16[320,128]{1,0:T(8,128)(2,1)S(1)}, bf16[320,128]{1,0:T(8,128)(2,1)S(1)}, u32[]{:S(2)}, u32[]{:S(2)}) collective-permute-start(bf16[320,128]{1,0:T(8,128)(2,1)S(1)} %collective-permute-done.2.refs_3_), channel_id=1, source_target_pairs={{0,4},{4,0},{8,12},{12,8},{1,5},{5,1},{9,13},{13,9},{2,6},{6,2},{1... | collective-permute-start | bytes 245768 | tf_op jit(solution)/shard_map/ppermute | solution.py:39
  18.1 45.2 %collective-permute-start.21 = (bf16[320,128]{1,0:T(8,128)(2,1)}, bf16[320,128]{1,0:T(8,128)(2,1)S(1)}, u32[]{:S(2)}, u32[]{:S(2)}) collective-permute-start(bf16[320,128]{1,0:T(8,128)(2,1)} %refs_0_.3), channel_id=1, source_target_pairs={{0,4},{4,0},{8,12},{12,8},{1,5},{5,1},{9,13},{13,9},{2,6},{6,2},{1... | collective-permute-start | bytes 245768 | tf_op jit(solution)/shard_map/ppermute | solution.py:39
  18.2 3.1 %copy-start = (bf16[9,320,1280]{2,1,0:T(8,128)(2,1)S(1)}, bf16[9,320,1280]{2,1,0:T(8,128)(2,1)}, u32[]{:S(2)}) copy-start(bf16[9,320,1280]{2,1,0:T(8,128)(2,1)} %refs_8_.1) | copy-start | bytes 22118404
  21.3 0.9 %copy-start.4 = (bf16[320,128]{1,0:T(8,128)(2,1)S(1)}, bf16[320,128]{1,0:T(8,128)(2,1)}, u32[]{:S(2)}) copy-start(bf16[320,128]{1,0:T(8,128)(2,1)} %refs_0_.2) | copy-start | bytes 245764
  22.2 15.8 %copy-start.1 = (bf16[9,320,1280]{2,1,0:T(8,128)(2,1)S(1)}, bf16[9,320,1280]{2,1,0:T(8,128)(2,1)}, u32[]{:S(2)}) copy-start(bf16[9,320,1280]{2,1,0:T(8,128)(2,1)} %refs_8_.1) | copy-start | bytes 22118404
  24.9 7.2 %collective-permute-start.7 = (bf16[320,128]{1,0:T(8,128)(2,1)S(1)}, bf16[320,128]{1,0:T(8,128)(2,1)S(1)}, u32[]{:S(2)}, u32[]{:S(2)}) collective-permute-start(bf16[320,128]{1,0:T(8,128)(2,1)S(1)} %spatial_forward.1.refs_0_), channel_id=1, source_target_pairs={{0,1},{1,2},{2,3},{3,0},{4,5},{5,6},{6,7},{7,4},{8,9},{9,10},{10,1... | collective-permute-start | bytes 245768 | tf_op jit(solution)/shard_map/ppermute | solution.py:34
  25.8 9.3 %collective-permute-start.8 = (bf16[320,128]{1,0:T(8,128)(2,1)S(1)}, bf16[320,128]{1,0:T(8,128)(2,1)S(1)}, u32[]{:S(2)}, u32[]{:S(2)}) collective-permute-start(bf16[320,128]{1,0:T(8,128)(2,1)S(1)} %spatial_forward.1.refs_0_), channel_id=1, source_target_pairs={{0,2},{1,3},{2,0},{3,1},{4,6},{5,7},{6,4},{7,5},{8,10},{9,11},{10,... | collective-permute-start | bytes 245768 | tf_op jit(solution)/shard_map/ppermute | solution.py:34
  28.0 7.1 %collective-permute-start.9 = (bf16[320,128]{1,0:T(8,128)(2,1)S(1)}, bf16[320,128]{1,0:T(8,128)(2,1)S(1)}, u32[]{:S(2)}, u32[]{:S(2)}) collective-permute-start(bf16[320,128]{1,0:T(8,128)(2,1)S(1)} %spatial_forward.1.refs_0_), channel_id=1, source_target_pairs={{0,3},{1,0},{2,1},{3,2},{4,7},{5,4},{6,5},{7,6},{8,11},{9,8},{10,9... | collective-permute-start | bytes 245768 | tf_op jit(solution)/shard_map/ppermute | solution.py:34
  30.3 7.7 %collective-permute-start.15 = (bf16[320,128]{1,0:T(8,128)(2,1)S(1)}, bf16[320,128]{1,0:T(8,128)(2,1)S(1)}, u32[]{:S(2)}, u32[]{:S(2)}) collective-permute-start(bf16[320,128]{1,0:T(8,128)(2,1)S(1)} %add_convert_fusion.1.field_ref.refs_0_), channel_id=1, source_target_pairs={{0,4},{4,0},{8,12},{12,8},{1,5},{5,1},{9,13},{13,9},{2,6},{6,2},{1... | collective-permute-start | bytes 245768 | tf_op jit(solution)/shard_map/ppermute | solution.py:39
  35.2 11.4 %collective-permute-start.10 = (bf16[4,320,128]{2,1,0:T(8,128)(2,1)S(1)}, bf16[4,320,128]{2,1,0:T(8,128)(2,1)S(1)}, u32[]{:S(2)}, u32[]{:S(2)}) collective-permute-start(bf16[4,320,128]{2,1,0:T(8,128)(2,1)S(1)} %pad_maximum_fusion), channel_id=1, source_target_pairs={{0,8},{4,12},{8,0},{12,4},{1,9},{5,13},{9,1},{13,5},{2,10},{6,14},... | collective-permute-start | bytes 983048 | tf_op jit(solution)/shard_map/ppermute | solution.py:34
  37.9 14.9 %collective-permute-start.20 = (bf16[2,320,128]{2,1,0:T(8,128)(2,1)S(1)}, bf16[2,320,128]{2,1,0:T(8,128)(2,1)S(1)}, u32[]{:S(2)}, u32[]{:S(2)}) collective-permute-start(bf16[2,320,128]{2,1,0:T(8,128)(2,1)S(1)} %pad_maximum_fusion.4), channel_id=1, source_target_pairs={{0,8},{4,12},{8,0},{12,4},{1,9},{5,13},{9,1},{13,5},{2,10},{6,14},... | collective-permute-start | bytes 491528 | tf_op jit(solution)/shard_map/ppermute | solution.py:34
  39.7 21.8 %copy-start.3 = (bf16[3,320,1280]{2,1,0:T(8,128)(2,1)S(1)}, bf16[3,320,1280]{2,1,0:T(8,128)(2,1)}, u32[]{:S(2)}) copy-start(bf16[3,320,1280]{2,1,0:T(8,128)(2,1)} %w_ref.1) | copy-start | bytes 7372804
  39.7 8.7 %collective-permute-start.18 = (bf16[320,128]{1,0:T(8,128)(2,1)S(1)}, bf16[320,128]{1,0:T(8,128)(2,1)S(1)}, u32[]{:S(2)}, u32[]{:S(2)}) collective-permute-start(bf16[320,128]{1,0:T(8,128)(2,1)S(1)} %get-tuple-element.23), channel_id=1, source_target_pairs={{0,3},{1,0},{2,1},{3,2},{4,7},{5,4},{6,5},{7,6},{8,11},{9,8},{10,9... | collective-permute-start | bytes 245768 | tf_op jit(solution)/shard_map/ppermute | solution.py:34
  42.2 6.4 %collective-permute-start.17 = (bf16[320,128]{1,0:T(8,128)(2,1)S(1)}, bf16[320,128]{1,0:T(8,128)(2,1)S(1)}, u32[]{:S(2)}, u32[]{:S(2)}) collective-permute-start(bf16[320,128]{1,0:T(8,128)(2,1)S(1)} %get-tuple-element.22), channel_id=1, source_target_pairs={{0,2},{1,3},{2,0},{3,1},{4,6},{5,7},{6,4},{7,5},{8,10},{9,11},{10,... | collective-permute-start | bytes 245768 | tf_op jit(solution)/shard_map/ppermute | solution.py:34
  46.5 6.2 %collective-permute-start.16 = (bf16[320,128]{1,0:T(8,128)(2,1)S(1)}, bf16[320,128]{1,0:T(8,128)(2,1)S(1)}, u32[]{:S(2)}, u32[]{:S(2)}) collective-permute-start(bf16[320,128]{1,0:T(8,128)(2,1)S(1)} %get-tuple-element.21), channel_id=1, source_target_pairs={{0,1},{1,2},{2,3},{3,0},{4,5},{5,6},{6,7},{7,4},{8,9},{9,10},{10,1... | collective-permute-start | bytes 245768 | tf_op jit(solution)/shard_map/ppermute | solution.py:34
  48.3 14.9 %collective-permute-start.22 = (bf16[320,128]{1,0:T(8,128)(2,1)S(1)}, bf16[320,128]{1,0:T(8,128)(2,1)S(1)}, u32[]{:S(2)}, u32[]{:S(2)}) collective-permute-start(bf16[320,128]{1,0:T(8,128)(2,1)S(1)} %collective-permute-done.11.before_ref.after_ref.refs_1_), channel_id=1, source_target_pairs={{0,4},{4,0},{8,12},{12,8},{1,5},{5,1},{9,13},{13,9},{2,6},{6,2},{1... | collective-permute-start | bytes 245768 | tf_op jit(solution)/shard_map/ppermute | solution.py:39
  48.6 6.7 %collective-permute-start.19 = (bf16[2,320,128]{2,1,0:T(8,128)(2,1)S(1)}, bf16[2,320,128]{2,1,0:T(8,128)(2,1)S(1)}, u32[]{:S(2)}, u32[]{:S(2)}) collective-permute-start(bf16[2,320,128]{2,1,0:T(8,128)(2,1)S(1)} %pad_maximum_fusion.3), channel_id=1, source_target_pairs={{0,8},{4,12},{8,0},{12,4},{1,9},{5,13},{9,1},{13,5},{2,10},{6,14},... | collective-permute-start | bytes 491528 | tf_op jit(solution)/shard_map/ppermute | solution.py:34
  52.8 10.5 %collective-permute-start.23 = (bf16[320,128]{1,0:T(8,128)(2,1)S(1)}, bf16[320,128]{1,0:T(8,128)(2,1)S(1)}, u32[]{:S(2)}, u32[]{:S(2)}) collective-permute-start(bf16[320,128]{1,0:T(8,128)(2,1)S(1)} %get-tuple-element.26), channel_id=1, source_target_pairs={{0,4},{4,0},{8,12},{12,8},{1,5},{5,1},{9,13},{13,9},{2,6},{6,2},{1... | collective-permute-start | bytes 245768 | tf_op jit(solution)/shard_map/ppermute | solution.py:39
  52.8 10.5 %collective-permute-start.24 = (bf16[320,128]{1,0:T(8,128)(2,1)S(1)}, bf16[320,128]{1,0:T(8,128)(2,1)S(1)}, u32[]{:S(2)}, u32[]{:S(2)}) collective-permute-start(bf16[320,128]{1,0:T(8,128)(2,1)S(1)} %get-tuple-element.24), channel_id=1, source_target_pairs={{0,4},{4,0},{8,12},{12,8},{1,5},{5,1},{9,13},{13,9},{2,6},{6,2},{1... | collective-permute-start | bytes 245768 | tf_op jit(solution)/shard_map/ppermute | solution.py:39

commit v3 on v2

--- a/solution.py
+++ b/solution.py
@@ -39,6 +39,10 @@
     return lax.ppermute(data, "st", [(i, i ^ 1) for i in range(n)])
 
 
+def after_all(values, others):
+    return lax.optimization_barrier((values, others))[0]
+
+
 def gather_ch(shard):
     n_ch, _ = sizes()
     return [shard] + [send(shard, "ch", k) for k in range(1, n_ch)]
@@ -96,6 +100,19 @@
     row = lane // W + dr
     col = lane % W + dc
     return (row >= 0) & (row < ROWS) & (col >= 0) & (col < W)
+
+
+def bring_in(latents, cotangent):
+    def body(l_ref, t_ref, lo_ref, to_ref):
+        lo_ref[...] = l_ref[...]
+        to_ref[...] = t_ref[...]
+
+    return pl.pallas_call(
+        body,
+        out_shape=[jax.ShapeDtypeStruct(x.shape, x.dtype) for x in (latents, cotangent)],
+        cost_estimate=pl.CostEstimate(flops=8000000000, transcendentals=0, bytes_accessed=1_000_000),
+        name="bring_in",
+    )(latents, cotangent)
 
 
 def spatial_forward(mine, siblings, weight):
@@ -194,6 +211,7 @@
         out_shape=chunk_shapes(n_ch, cb),
         scratch_shapes=[pltpu.VMEM((channels, TILE), F32)],
         compiler_params=pltpu.CompilerParams(vmem_limit_bytes=16 * MIB),
+        cost_estimate=pl.CostEstimate(flops=4000000000, transcendentals=0, bytes_accessed=3_000_000),
         name="temporal_backward",
     )(field, before, after, weight)
 
@@ -256,41 +274,41 @@
 
     def body(*refs):
         g_refs, l_refs = refs[:n_in], refs[n_in : 2 * n_in]
-        out_ref, left, right = refs[2 * n_in :]
+        out_hbm, left, right, out, sems = refs[2 * n_in :]
         _, _, band = place()
-        step = pl.program_id(0)
-
-        @pl.when(step == 0)
-        def _():
-            blank = jnp.zeros((W, ib), BF)
-            g_pairs = pairs_from(g_refs[0], g_refs[1], g_refs[2:])
-            l_pairs = pairs_from(l_refs[0], l_refs[1], l_refs[2:])
-            for j in range(n_x):
-                for a, frame in enumerate(frames_of(g_pairs[j][0][...], g_pairs[j][1][...], band)):
-                    f = FT * j + a
-                    left[:, f * FRAME : (f + 1) * FRAME] = frame.astype(BF)
-                for a, frame in enumerate(frames_of(l_pairs[j][0][...], l_pairs[j][1][...], band)):
-                    f = FT * j + a
-                    for q, moved in enumerate(shifted_columns(frame, 1)):
-                        right[q, f, :W, :] = blank
-                        right[q, f, W + FRAME :, :] = blank
-                        right[q, f, W : W + FRAME, :] = moved
-
-        start = pl.multiple_of(W * (step // 3), W)
-        moved = jnp.concatenate([right[step % 3, f, pl.ds(start, FRAME), :] for f in range(frames)], axis=0)
-        out_ref[0] = jnp.dot(left[...], moved, preferred_element_type=F32) * scale
-
-    whole = lambda x: pl.BlockSpec(x.shape, lambda g: (0,) * x.ndim)
+        blank = jnp.zeros((W, ib), BF)
+        g_pairs = pairs_from(g_refs[0], g_refs[1], g_refs[2:])
+        l_pairs = pairs_from(l_refs[0], l_refs[1], l_refs[2:])
+        for j in range(n_x):
+            for a, frame in enumerate(frames_of(g_pairs[j][0][...], g_pairs[j][1][...], band)):
+                f = FT * j + a
+                left[:, f * FRAME : (f + 1) * FRAME] = frame.astype(BF)
+            for a, frame in enumerate(frames_of(l_pairs[j][0][...], l_pairs[j][1][...], band)):
+                f = FT * j + a
+                for q, moved in enumerate(shifted_columns(frame, 1)):
+                    right[q, f, :W, :] = blank
+                    right[q, f, W + FRAME :, :] = blank
+                    right[q, f, W : W + FRAME, :] = moved
+        copies = []
+        for tap in range(9):
+            at = slice(W * (tap // 3), W * (tap // 3) + FRAME)
+            moved = jnp.concatenate([right[tap % 3, f, at, :] for f in range(frames)], axis=0)
+            out[tap] = jnp.dot(left[...], moved, preferred_element_type=F32) * scale
+            copies.append(pltpu.make_async_copy(out.at[tap], out_hbm.at[tap], sems.at[tap]))
+            copies[-1].start()
+        for copy in copies:
+            copy.wait()
+
     args = (*grads[:2], *grads[2], *fields[:2], *fields[2])
     return pl.pallas_call(
         body,
-        grid=(9,),
-        in_specs=[whole(x) for x in args],
-        out_specs=pl.BlockSpec((1, ob, ib), lambda g: (g, 0, 0)),
+        out_specs=pl.BlockSpec(memory_space=pltpu.HBM),
         out_shape=jax.ShapeDtypeStruct((9, ob, ib), F32),
         scratch_shapes=[
             pltpu.VMEM((ob, frames * FRAME), BF),
             pltpu.VMEM((3, frames, FRAME + 2 * W, ib), BF),
+            pltpu.VMEM((9, ob, ib), F32),
+            pltpu.SemaphoreType.DMA((9,)),
         ],
         compiler_params=pltpu.CompilerParams(vmem_limit_bytes=24 * MIB),
         name="spatial_grads",
@@ -304,7 +322,7 @@
 
     def body(*refs):
         g_refs, gs_refs, h_refs, hs_refs = (refs[q * n_x : (q + 1) * n_x] for q in range(4))
-        out_ref, left, right = refs[4 * n_x :]
+        out_hbm, left, right, out, sems = refs[4 * n_x :]
         _, m, band = place()
         right[:FRAME, :] = jnp.zeros((FRAME, ib), BF)
         right[FRAME + span :, :] = jnp.zeros((FRAME, ib), BF)
@@ -316,14 +334,25 @@
             for a, frame in enumerate(frames_of(h_refs[j][...], hs_refs[j][...], band)):
                 at = pl.multiple_of((FT * block + a + 1) * FRAME, FRAME)
                 right[pl.ds(at, FRAME), :] = frame.T.astype(BF)
+        copies = []
         for d in range(3):
             moved = right[d * FRAME : d * FRAME + span, :]
-            out_ref[d] = jnp.dot(left[...], moved, preferred_element_type=F32) * scale
-
-    return pl.pallas_call(
-        body,
+            out[d] = jnp.dot(left[...], moved, preferred_element_type=F32) * scale
+            copies.append(pltpu.make_async_copy(out.at[d], out_hbm.at[d], sems.at[d]))
+            copies[-1].start()
+        for copy in copies:
+            copy.wait()
+
+    return pl.pallas_call(
+        body,
+        out_specs=pl.BlockSpec(memory_space=pltpu.HBM),
         out_shape=jax.ShapeDtypeStruct((3, ob, ib), F32),
-        scratch_shapes=[pltpu.VMEM((ob, span), BF), pltpu.VMEM((span + 2 * FRAME, ib), BF)],
+        scratch_shapes=[
+            pltpu.VMEM((ob, span), BF),
+            pltpu.VMEM((span + 2 * FRAME, ib), BF),
+            pltpu.VMEM((3, ob, ib), F32),
+            pltpu.SemaphoreType.DMA((3,)),
+        ],
         compiler_params=pltpu.CompilerParams(vmem_limit_bytes=24 * MIB),
         name="temporal_grads",
     )(*grads, *grads_sibling, *fields, *fields_sibling)
@@ -346,25 +375,44 @@
         stack = jnp.stack(pieces) if isinstance(pieces, list) else pieces
         return lax.dynamic_index_in_dim(stack, (c + n_ch - b) % n_ch, 0, keepdims=False)
 
+    latents, cotangent = bring_in(latents, cotangent)
+
     cot_ring = ring_blocks(cotangent)
     mine = gather_ch(latents)
     chunks = temporal_backward(cotangent, cot_ring[0], cot_ring[-1], temporal_weight)
 
     siblings = [swap_band(piece) for piece in mine]
+    cots = [cotangent] + cot_ring
+    cots_sibling = [swap_band(x) for x in cots]
+    siblings = after_all(siblings, cots_sibling)
     hidden = spatial_forward(mine, siblings, spatial_weight)
-    hidden, base = lax.optimization_barrier((hidden, cotangent))
+    base = after_all(cotangent, hidden)
 
     hidden_grad = reduce_ch(base, chunks)
     grad_sibling = swap_band(hidden_grad)
     chunks = spatial_backward(hidden_grad, grad_sibling, spatial_weight)
+    hidden_mine = gather_ch(hidden)
+    hidden_mine = after_all(hidden_mine, chunks)
     latent_grad = reduce_ch(hidden_grad, chunks)
 
-    hidden_mine = gather_ch(hidden)
     before, after = neighbours(jnp.stack(hidden_mine))
-    temporal_out = temporal_forward(hidden_mine, before, after, temporal_weight)
 
     own_block = RBANDS * m + band
     sib_block = RBANDS * m + 1 - band
+
+    lat_rest, grad_rest = [], []
+    for j in range(1, n_x):
+        target = RBANDS * ((m + j) % n_x) + band
+        both = jnp.stack([block(mine, target), block(siblings, target)])
+        lat_rest.append(send(both, "st", RBANDS * j))
+        grad_rest.append(send(jnp.stack([hidden_grad, grad_sibling]), "st", RBANDS * j))
+    spatial_grad = spatial_grads(
+        (hidden_grad, grad_sibling, grad_rest),
+        (block(mine, own_block), block(siblings, own_block), lat_rest),
+        scale,
+    )
+    before, after = after_all((before, after), (spatial_grad, latent_grad))
+    temporal_out = temporal_forward(hidden_mine, before, after, temporal_weight)
 
     hid_own, hid_sib = [block(hidden_mine, own_block)], [block(hidden_mine, sib_block)]
     for j in range(1, n_x):
@@ -377,22 +425,10 @@
             both = send(both, "st", RBANDS * j)
             hid_own.append(both[0])
             hid_sib.append(both[1])
-    cots = [cotangent] + cot_ring
     temporal_grad = temporal_grads(
-        cots, [swap_band(x) for x in cots], hid_own, [swap_band(x) for x in hid_sib], scale
+        cots, cots_sibling, hid_own, [swap_band(x) for x in hid_sib], scale
     )
 
-    lat_rest, grad_rest = [], []
-    for j in range(1, n_x):
-        target = RBANDS * ((m + j) % n_x) + band
-        both = jnp.stack([block(mine, target), block(siblings, target)])
-        lat_rest.append(send(both, "st", RBANDS * j))
-        grad_rest.append(send(jnp.stack([hidden_grad, grad_sibling]), "st", RBANDS * j))
-    spatial_grad = spatial_grads(
-        (hidden_grad, grad_sibling, grad_rest),
-        (block(mine, own_block), block(siblings, own_block), lat_rest),
-        scale,
-    )
     return temporal_out, latent_grad, spatial_grad, temporal_grad
 
 

time: 66.8 us -> 58.4 us (0.87)
  starting transfers between devices: 28.9 us -> 24.9 us
  Pallas kernels: 17.1 us -> 14.4 us
  waiting for transfers between devices: 11.2 us -> 13.9 us
  local copies, waits for them, and re-layouts: 5.74 us -> 3.14 us
  other arithmetic: 2.68 us -> 0.92 us
    ppermute x16, starting transfers between devices: 27.1 us -> 23.6 us  [send(): return lax.ppermute(data, axis, [(i, (i + by) % n) for i in range(n)])]
    unnamed x10 -> x14, local copies, waits for them, and re-layouts: 5.68 us -> 3.07 us
    ppermute x16, waiting for transfers between devices: 11.1 us -> 13.3 us  [send(): return lax.ppermute(data, axis, [(i, (i + by) % n) for i in range(n)])]
    pallas_call x2 -> x3, Pallas kernels: 9.24 us -> 7.46 us  [the longest x1 3.07 us: spatial_grads(): pl.pallas_call(body, out_specs=pl.BlockSpec(memory_space=pltpu.HBM), out_...]
    another operation x2, other arithmetic: 0.97 us -> 0.09 us  [block(): stack = jnp.stack(pieces) if isinstance(pieces, list) else pieces]
    pallas_call x1, Pallas kernels: 1.74 us -> 0.85 us  [temporal_backward(): pl.pallas_call(body, out_shape=chunk_shapes(n_ch, cb), scratch_shapes=[pl...]
    convert_element_type x2, other arithmetic: 1.63 us -> 0.75 us  [reduce_ch(): return total.astype(BF)]
  transfers between devices with their start and end apart: 25 -> 25, of which waited for: 6 -> 6; matrix products, arithmetic and copies ran while one was open for 4% -> 2% of each run, Pallas kernels for 21% -> 17%
where the time goes in v3:
time: 58.4 us; the launch traced here: 58.1 us
  starting transfers between devices  24.9 us (43%)
  Pallas kernels  14.4 us (25%)
  waiting for transfers between devices  13.9 us (24%)
  local copies, waits for them, and re-layouts  3.14 us (5%)
  other arithmetic  0.92 us (2%)
  between operations  0.86 us (1%)
    ppermute x16, starting transfers between devices, send(): return lax.ppermute(data, axis, [(i, (i + by) % n) for i in range(n)])  23.6 us
    ppermute x16, waiting for transfers between devices, send(): return lax.ppermute(data, axis, [(i, (i + by) % n) for i in range(n)])  13.3 us
    unnamed x14, local copies, waits for them, and re-layouts  3.07 us
    pallas_call x1, Pallas kernels, spatial_grads(): pl.pallas_call(body, out_specs=pl.BlockSpec(memory_space=pltpu.HBM), out_...  3.07 us
    pallas_call x1, Pallas kernels, temporal_grads(): pl.pallas_call(body, out_specs=pl.BlockSpec(memory_space=pltpu.HBM), out_...  2.79 us
    pallas_call x1, Pallas kernels, spatial_forward(): pl.pallas_call(body, out_shape=jax.ShapeDtypeStruct((cb, TILE), BF), scra...  2.69 us
    pallas_call x1, Pallas kernels, temporal_forward(): pl.pallas_call(body, out_shape=jax.ShapeDtypeStruct((cb, TILE), BF), scra...  1.79 us
    pallas_call x1, Pallas kernels, spatial_backward(): pl.pallas_call(body, out_shape=chunk_shapes(n_ch, cb), scratch_shapes=[pl...  1.62 us
  transfers between devices with their start and end apart: 25, of which 6 were waited for; matrix products, arithmetic and copies ran while one was open for 2% of the time, Pallas kernels for 17%

profile of v3, /device:TPU:0, one launch (start us, length us, event | category | flops | bytes accessed | tf_op | source)
XLA Modules:
  0.0 58.1 jit_solution(517037150785020944)
XLA Ops:
  0.6 1.6 %bring_in.1 = (bf16[320,128]{1,0:T(8,128)(2,1)}, bf16[320,128]{1,0:T(8,128)(2,1)}) custom-call(bf16[320,128]{1,0:T(8,128)(2,1)} %l_ref.1, bf16[320,128]{1,0:T(8,128)(2,1)} %t_ref.1), custom_call_target="tpu_custom_call" | custom-call | flops 8000000000 | bytes 1000000 | tf_op jit(solution)/shard_map/bring_in/pallas_call | solution.py:110
  2.2 2.9 %collective-permute-start.8 = (bf16[320,128]{1,0:T(8,128)(2,1)}, bf16[320,128]{1,0:T(8,128)(2,1)S(1)}, u32[]{:S(2)}, u32[]{:S(2)}) collective-permute-start(bf16[320,128]{1,0:T(8,128)(2,1)} %get-tuple-element.31.field_ref.refs_0_), channel_id=1, source_target_pairs={{0,8},{4,12},{8,0},{12,4},{1,9},{5,13},{9,1},{13,5},{2,10},{6,14},... | collective-permute-start | bytes 245768 | tf_op jit(solution)/shard_map/ppermute | solution.py:34
  5.2 0.0 collective-permute-start.7
  5.2 0.5 collective-permute-start.3
  5.7 3.6 %collective-permute-start.2 = (bf16[320,128]{1,0:T(8,128)(2,1)}, bf16[320,128]{1,0:T(8,128)(2,1)S(1)}, u32[]{:S(2)}, u32[]{:S(2)}) collective-permute-start(bf16[320,128]{1,0:T(8,128)(2,1)} %get-tuple-element.25.refs_0_), channel_id=1, source_target_pairs={{0,3},{1,0},{2,1},{3,2},{4,7},{5,4},{6,5},{7,6},{8,11},{9,8},{10,9... | collective-permute-start | bytes 245768 | tf_op jit(solution)/shard_map/ppermute | solution.py:34
  9.3 0.0 collective-permute-start.1
  9.3 0.0 collective-permute-done.8.before_ref.after_ref.refs_1_
  9.3 1.0 %collective-permute-start = (bf16[320,128]{1,0:T(8,128)(2,1)}, bf16[320,128]{1,0:T(8,128)(2,1)S(1)}, u32[]{:S(2)}, u32[]{:S(2)}) collective-permute-start(bf16[320,128]{1,0:T(8,128)(2,1)} %get-tuple-element.25.refs_0_), channel_id=1, source_target_pairs={{0,1},{1,2},{2,3},{3,0},{4,5},{5,6},{6,7},{7,4},{8,9},{9,10},{10,1... | collective-permute-start | bytes 245768 | tf_op jit(solution)/shard_map/ppermute | solution.py:34
  10.3 2.2 %copy-done = bf16[3,320,1280]{2,1,0:T(8,128)(2,1)S(1)} copy-done((bf16[3,320,1280]{2,1,0:T(8,128)(2,1)S(1)}, bf16[3,320,1280]{2,1,0:T(8,128)(2,1)}, u32[]{:S(2)}) %copy-start) | copy-done | bytes 2457624
  12.5 0.9 %copy-done.3 = bf16[320,128]{1,0:T(8,128)(2,1)S(1)} copy-done((bf16[320,128]{1,0:T(8,128)(2,1)S(1)}, bf16[320,128]{1,0:T(8,128)(2,1)}, u32[]{:S(2)}) %copy-start.3) | copy-done | bytes 81944
  13.4 0.9 %temporal_backward.1 = (f32[320,128]{1,0:T(8,128)S(1)}, bf16[320,128]{1,0:T(8,128)(2,1)S(1)}, bf16[320,128]{1,0:T(8,128)(2,1)S(1)}, bf16[320,128]{1,0:T(8,128)(2,1)S(1)}) custom-call(bf16[320,128]{1,0:T(8,128)(2,1)S(1)} %copy-done.3, bf16[320,128]{1,0:T(8,128)(2,1)S(1)} %collective-permute-done.8.before_ref.after_ref.refs_1_, ...), custom_call_target="tpu_custom_call" | custom-call | flops 4000000000 | bytes 3000000 | tf_op jit(solution)/shard_map/temporal_backward/pallas_call | solution.py:209
  14.2 0.0 collective-permute-done.2.refs_3_
  14.2 0.1 collective-permute-start.9
  14.3 3.0 %collective-permute-done.1.refs_2_ = bf16[320,128]{1,0:T(8,128)(2,1)S(1)} collective-permute-done((bf16[320,128]{1,0:T(8,128)(2,1)}, bf16[320,128]{1,0:T(8,128)(2,1)S(1)}, u32[]{:S(2)}, u32[]{:S(2)}) %collective-permute-start.1) | collective-permute-done | bytes 81952 | tf_op jit(solution)/shard_map/ppermute | solution.py:34
  17.3 0.0 collective-permute-start.6
  17.3 0.0 collective-permute-done.refs_1_
  17.3 0.5 collective-permute-start.5
  17.8 0.0 copy-done.2
  17.8 0.0 collective-permute-done.7.refs_2_
  17.8 0.1 collective-permute-start.4
  18.0 0.0 collective-permute-done.3.refs_4_
  18.0 0.2 collective-permute-start.13
  18.2 0.0 collective-permute-done.9.refs_3_
  18.2 2.4 %collective-permute-start.14 = (bf16[320,128]{1,0:T(8,128)(2,1)S(1)}, bf16[320,128]{1,0:T(8,128)(2,1)S(1)}, u32[]{:S(2)}, u32[]{:S(2)}) collective-permute-start(bf16[320,128]{1,0:T(8,128)(2,1)S(1)} %get-tuple-element.34), channel_id=1, source_target_pairs={{0,2},{1,3},{2,0},{3,1},{4,6},{5,7},{6,4},{7,5},{8,10},{9,11},{10,... | collective-permute-start | bytes 245768 | tf_op jit(solution)/shard_map/ppermute | solution.py:34
  20.6 0.0 collective-permute-done.6.refs_7_
  20.6 2.3 %collective-permute-start.15 = (bf16[320,128]{1,0:T(8,128)(2,1)S(1)}, bf16[320,128]{1,0:T(8,128)(2,1)S(1)}, u32[]{:S(2)}, u32[]{:S(2)}) collective-permute-start(bf16[320,128]{1,0:T(8,128)(2,1)S(1)} %get-tuple-element.35), channel_id=1, source_target_pairs={{0,3},{1,0},{2,1},{3,2},{4,7},{5,4},{6,5},{7,6},{8,11},{9,8},{10,9... | collective-permute-start | bytes 245768 | tf_op jit(solution)/shard_map/ppermute | solution.py:34
  22.9 0.0 collective-permute-done.5.refs_6_
  22.9 0.0 collective-permute-done.4.refs_5_
  23.0 2.7 %spatial_forward.1.refs_0_ = bf16[320,128]{1,0:T(8,128)(2,1)S(1)} custom-call(bf16[320,128]{1,0:T(8,128)(2,1)S(1)} %copy-done.2, bf16[320,128]{1,0:T(8,128)(2,1)S(1)} %collective-permute-done.refs_1_, bf16[320,128]{1,0:T(8,128)(2,1)S(1)} %collective-permute-done.1.refs_2_, bf16[320,128]{1,0:T(8,128)(2,1)S(1)} %collective-permute-done.2.refs_3_, ...), custom_call_target="tpu_custom_call" | custom-call | tf_op jit(solution)/shard_map/spatial_forward/pallas_call | solution.py:146
  25.7 0.1 collective-permute-start.12
  25.7 1.1 %collective-permute-start.11 = (bf16[320,128]{1,0:T(8,128)(2,1)S(1)}, bf16[320,128]{1,0:T(8,128)(2,1)S(1)}, u32[]{:S(2)}, u32[]{:S(2)}) collective-permute-start(bf16[320,128]{1,0:T(8,128)(2,1)S(1)} %spatial_forward.1.refs_0_), channel_id=1, source_target_pairs={{0,2},{1,3},{2,0},{3,1},{4,6},{5,7},{6,4},{7,5},{8,10},{9,11},{10,... | collective-permute-start | bytes 245768 | tf_op jit(solution)/shard_map/ppermute | solution.py:34
  26.9 0.0 collective-permute-done.13
  26.9 1.9 %collective-permute-start.10 = (bf16[320,128]{1,0:T(8,128)(2,1)S(1)}, bf16[320,128]{1,0:T(8,128)(2,1)S(1)}, u32[]{:S(2)}, u32[]{:S(2)}) collective-permute-start(bf16[320,128]{1,0:T(8,128)(2,1)S(1)} %spatial_forward.1.refs_0_), channel_id=1, source_target_pairs={{0,1},{1,2},{2,3},{3,0},{4,5},{5,6},{6,7},{7,4},{8,9},{9,10},{10,1... | collective-permute-start | bytes 245768 | tf_op jit(solution)/shard_map/ppermute | solution.py:34
  28.8 0.0 collective-permute-done.14
  28.8 0.0 collective-permute-done.15
  28.8 0.1 add_convert_fusion.1.field_ref.refs_0_
  28.9 0.1 collective-permute-start.16
  29.0 0.6 %collective-permute-start.19 = (bf16[2,320,128]{2,1,0:T(8,128)(2,1)S(1)}, bf16[2,320,128]{2,1,0:T(8,128)(2,1)S(1)}, u32[]{:S(2)}, u32[]{:S(2)}) collective-permute-start(bf16[2,320,128]{2,1,0:T(8,128)(2,1)S(1)} %pad_maximum_fusion.4), channel_id=1, source_target_pairs={{0,8},{4,12},{8,0},{12,4},{1,9},{5,13},{9,1},{13,5},{2,10},{6,14},... | collective-permute-start | bytes 491528 | tf_op jit(solution)/shard_map/ppermute | solution.py:34
  29.6 0.6 %collective-permute-done.16.sibling_ref.refs_1_ = bf16[320,128]{1,0:T(8,128)(2,1)S(1)} collective-permute-done((bf16[320,128]{1,0:T(8,128)(2,1)S(1)}, bf16[320,128]{1,0:T(8,128)(2,1)S(1)}, u32[]{:S(2)}, u32[]{:S(2)}) %collective-permute-start.16) | collective-permute-done | bytes 81952 | tf_op jit(solution)/shard_map/ppermute | solution.py:39
  30.2 1.6 %spatial_backward.1 = (f32[320,128]{1,0:T(8,128)S(1)}, bf16[320,128]{1,0:T(8,128)(2,1)S(1)}, bf16[320,128]{1,0:T(8,128)(2,1)S(1)}, bf16[320,128]{1,0:T(8,128)(2,1)S(1)}) custom-call(bf16[320,128]{1,0:T(8,128)(2,1)S(1)} %add_convert_fusion.1.field_ref.refs_0_, bf16[320,128]{1,0:T(8,128)(2,1)S(1)} %collective-permute-done.16.sibling_ref.refs_1_, ...), custom_call_target="tpu_custom_call" | custom-call | tf_op jit(solution)/shard_map/spatial_backward/pallas_call | solution.py:253
  31.9 0.0 copy-start.1
  31.9 2.0 %collective-permute-start.20 = (bf16[320,128]{1,0:T(8,128)(2,1)S(1)}, bf16[320,128]{1,0:T(8,128)(2,1)S(1)}, u32[]{:S(2)}, u32[]{:S(2)}) collective-permute-start(bf16[320,128]{1,0:T(8,128)(2,1)S(1)} %get-tuple-element.37), channel_id=1, source_target_pairs={{0,1},{1,2},{2,3},{3,0},{4,5},{5,6},{6,7},{7,4},{8,9},{9,10},{10,1... | collective-permute-start | bytes 245768 | tf_op jit(solution)/shard_map/ppermute | solution.py:34
  33.9 0.0 collective-permute-done.12.refs_3_
  33.9 3.6 %collective-permute-start.21 = (bf16[320,128]{1,0:T(8,128)(2,1)S(1)}, bf16[320,128]{1,0:T(8,128)(2,1)S(1)}, u32[]{:S(2)}, u32[]{:S(2)}) collective-permute-start(bf16[320,128]{1,0:T(8,128)(2,1)S(1)} %get-tuple-element.38), channel_id=1, source_target_pairs={{0,2},{1,3},{2,0},{3,1},{4,6},{5,7},{6,4},{7,5},{8,10},{9,11},{10,... | collective-permute-start | bytes 245768 | tf_op jit(solution)/shard_map/ppermute | solution.py:34
  37.5 0.0 collective-permute-done.11.refs_2_
  37.5 0.3 collective-permute-start.22
  37.8 0.0 collective-permute-done.10.refs_1_
  37.8 0.6 %collective-permute-start.17 = (bf16[4,320,128]{2,1,0:T(8,128)(2,1)S(1)}, bf16[4,320,128]{2,1,0:T(8,128)(2,1)S(1)}, u32[]{:S(2)}, u32[]{:S(2)}) collective-permute-start(bf16[4,320,128]{2,1,0:T(8,128)(2,1)S(1)} %pad_maximum_fusion), channel_id=1, source_target_pairs={{0,8},{4,12},{8,0},{12,4},{1,9},{5,13},{9,1},{13,5},{2,10},{6,14},... | collective-permute-start | bytes 983048 | tf_op jit(solution)/shard_map/ppermute | solution.py:34
  38.5 1.7 %collective-permute-done.20 = bf16[320,128]{1,0:T(8,128)(2,1)S(1)} collective-permute-done((bf16[320,128]{1,0:T(8,128)(2,1)S(1)}, bf16[320,128]{1,0:T(8,128)(2,1)S(1)}, u32[]{:S(2)}, u32[]{:S(2)}) %collective-permute-start.20) | collective-permute-done | bytes 81952 | tf_op jit(solution)/shard_map/ppermute | solution.py:34
  40.2 0.9 %collective-permute-start.18 = (bf16[2,320,128]{2,1,0:T(8,128)(2,1)S(1)}, bf16[2,320,128]{2,1,0:T(8,128)(2,1)S(1)}, u32[]{:S(2)}, u32[]{:S(2)}) collective-permute-start(bf16[2,320,128]{2,1,0:T(8,128)(2,1)S(1)} %pad_maximum_fusion.3), channel_id=1, source_target_pairs={{0,8},{4,12},{8,0},{12,4},{1,9},{5,13},{9,1},{13,5},{2,10},{6,14},... | collective-permute-start | bytes 491528 | tf_op jit(solution)/shard_map/ppermute | solution.py:34
  41.1 2.2 %collective-permute-done.21 = bf16[320,128]{1,0:T(8,128)(2,1)S(1)} collective-permute-done((bf16[320,128]{1,0:T(8,128)(2,1)S(1)}, bf16[320,128]{1,0:T(8,128)(2,1)S(1)}, u32[]{:S(2)}, u32[]{:S(2)}) %collective-permute-start.21) | collective-permute-done | bytes 81952 | tf_op jit(solution)/shard_map/ppermute | solution.py:34
  43.3 0.0 collective-permute-start.23
  43.3 0.3 collective-permute-done.22
  43.6 0.7 %add_convert_fusion = bf16[320,128]{1,0:T(8,128)(2,1)} fusion(bf16[320,128]{1,0:T(8,128)(2,1)S(1)} %collective-permute-done.22, bf16[320,128]{1,0:T(8,128)(2,1)S(1)} %collective-permute-done.21, bf16[320,128]{1,0:T(8,128)(2,1)S(1)} %collective-permute-done.20, f32[320,128]{1,0:T(8,128)S(1)} %get-tuple-element.36, ...), kind=kLoop, calls=%fused_computation.5 | loop fusion | flops 368640 | bytes 573440 | tf_op jit(solution)/shard_map/convert_element_type | solution.py:365
  44.3 0.0 collective-permute-done.19.refs_5_
  44.3 6.1 %collective-permute-done.18.refs_2_ = bf16[2,320,128]{2,1,0:T(8,128)(2,1)S(1)} collective-permute-done((bf16[2,320,128]{2,1,0:T(8,128)(2,1)S(1)}, bf16[2,320,128]{2,1,0:T(8,128)(2,1)S(1)}, u32[]{:S(2)}, u32[]{:S(2)}) %collective-permute-start.18) | collective-permute-done | bytes 163872 | tf_op jit(solution)/shard_map/ppermute | solution.py:34
  50.3 3.1 %spatial_grads.1 = f32[9,320,320]{2,1,0:T(8,128)} custom-call(bf16[320,128]{1,0:T(8,128)(2,1)S(1)} %add_convert_fusion.1.field_ref.refs_0_, bf16[320,128]{1,0:T(8,128)(2,1)S(1)} %collective-permute-done.16.sibling_ref.refs_1_, bf16[2,320,128]{2,1,0:T(8,128)(2,1)S(1)} %collective-permute-done.18.refs_2_, bf16[320,128]{1,0:T(8,128)(2,1)S(1)} %get-tuple-element.51.refs_3_, ...), custom_call_target="tpu_custom_call" | custom-call | tf_op jit(solution)/shard_map/spatial_grads/pallas_call | solution.py:303
  53.4 0.0 collective-permute-done.17.refs_4_.refs_5_
  53.4 0.1 collective-permute-start.24
  53.5 0.0 copy-done.1
  53.5 1.8 %temporal_forward.1 = bf16[320,128]{1,0:T(8,128)(2,1)} custom-call(bf16[320,128]{1,0:T(8,128)(2,1)S(1)} %spatial_forward.1.refs_0_, bf16[320,128]{1,0:T(8,128)(2,1)S(1)} %collective-permute-done.10.refs_1_, bf16[320,128]{1,0:T(8,128)(2,1)S(1)} %collective-permute-done.11.refs_2_, bf16[320,128]{1,0:T(8,128)(2,1)S(1)} %collective-permute-done.12.refs_3_, ...), custom_call_target="tpu_custom_call" | custom-call | tf_op jit(solution)/shard_map/temporal_forward/pallas_call | solution.py:174
  55.3 0.0 collective-permute-done.23.refs_6_
  55.3 0.0 collective-permute-done.24.refs_7_
  55.3 2.8 %temporal_grads.1 = f32[3,320,320]{2,1,0:T(8,128)} custom-call(bf16[320,128]{1,0:T(8,128)(2,1)S(1)} %copy-done.4, bf16[320,128]{1,0:T(8,128)(2,1)S(1)} %collective-permute-done.8.before_ref.after_ref.refs_1_, bf16[320,128]{1,0:T(8,128)(2,1)} %collective-permute-done.7.refs_2_, bf16[320,128]{1,0:T(8,128)(2,1)S(1)} %collective-permute-done.9.refs_3_, ...), custom_call_target="tpu_custom_call" | custom-call | tf_op jit(solution)/shard_map/temporal_grads/pallas_call | solution.py:346
  (19 shorter events, 0.3 us)
Async XLA Ops:
  2.2 7.1 %collective-permute-start.8 = (bf16[320,128]{1,0:T(8,128)(2,1)}, bf16[320,128]{1,0:T(8,128)(2,1)S(1)}, u32[]{:S(2)}, u32[]{:S(2)}) collective-permute-start(bf16[320,128]{1,0:T(8,128)(2,1)} %get-tuple-element.31.field_ref.refs_0_), channel_id=1, source_target_pairs={{0,8},{4,12},{8,0},{12,4},{1,9},{5,13},{9,1},{13,5},{2,10},{6,14},... | collective-permute-start | bytes 245768 | tf_op jit(solution)/shard_map/ppermute | solution.py:34
  5.2 12.7 %collective-permute-start.7 = (bf16[320,128]{1,0:T(8,128)(2,1)}, bf16[320,128]{1,0:T(8,128)(2,1)}, u32[]{:S(2)}, u32[]{:S(2)}) collective-permute-start(bf16[320,128]{1,0:T(8,128)(2,1)} %get-tuple-element.31.field_ref.refs_0_), channel_id=1, source_target_pairs={{0,4},{4,0},{8,12},{12,8},{1,5},{5,1},{9,13},{13,9},{2,6},{6,2},{1... | collective-permute-start | bytes 245768 | tf_op jit(solution)/shard_map/ppermute | solution.py:39
  5.2 12.8 %collective-permute-start.3 = (bf16[320,128]{1,0:T(8,128)(2,1)}, bf16[320,128]{1,0:T(8,128)(2,1)S(1)}, u32[]{:S(2)}, u32[]{:S(2)}) collective-permute-start(bf16[320,128]{1,0:T(8,128)(2,1)} %get-tuple-element.25.refs_0_), channel_id=1, source_target_pairs={{0,4},{4,0},{8,12},{12,8},{1,5},{5,1},{9,13},{13,9},{2,6},{6,2},{1... | collective-permute-start | bytes 245768 | tf_op jit(solution)/shard_map/ppermute | solution.py:39
  5.7 8.5 %collective-permute-start.2 = (bf16[320,128]{1,0:T(8,128)(2,1)}, bf16[320,128]{1,0:T(8,128)(2,1)S(1)}, u32[]{:S(2)}, u32[]{:S(2)}) collective-permute-start(bf16[320,128]{1,0:T(8,128)(2,1)} %get-tuple-element.25.refs_0_), channel_id=1, source_target_pairs={{0,3},{1,0},{2,1},{3,2},{4,7},{5,4},{6,5},{7,6},{8,11},{9,8},{10,9... | collective-permute-start | bytes 245768 | tf_op jit(solution)/shard_map/ppermute | solution.py:34
  9.3 8.0 %collective-permute-start.1 = (bf16[320,128]{1,0:T(8,128)(2,1)}, bf16[320,128]{1,0:T(8,128)(2,1)S(1)}, u32[]{:S(2)}, u32[]{:S(2)}) collective-permute-start(bf16[320,128]{1,0:T(8,128)(2,1)} %get-tuple-element.25.refs_0_), channel_id=1, source_target_pairs={{0,2},{1,3},{2,0},{3,1},{4,6},{5,7},{6,4},{7,5},{8,10},{9,11},{10,... | collective-permute-start | bytes 245768 | tf_op jit(solution)/shard_map/ppermute | solution.py:34
  9.3 13.7 %slice-start = ((s8[7372800]{0:T(1024)(128)(4,1)}), s8[3178496]{0:T(1024)(128)(4,1)S(1)}, s32[]{:S(2)}) async-start(s8[7372800]{0:T(1024)(128)(4,1)} %bitcast.27), calls=%async_computation | async-start | bytes 6356992
  9.3 13.7 %slice-start.1 = ((s8[7372800]{0:T(1024)(128)(4,1)}), s8[4194304]{0:T(1024)(128)(4,1)S(1)}, s32[]{:S(2)}) async-start(s8[7372800]{0:T(1024)(128)(4,1)} %bitcast.27), calls=%async_computation.1 | async-start | bytes 8388608
  9.3 8.0 %collective-permute-start = (bf16[320,128]{1,0:T(8,128)(2,1)}, bf16[320,128]{1,0:T(8,128)(2,1)S(1)}, u32[]{:S(2)}, u32[]{:S(2)}) collective-permute-start(bf16[320,128]{1,0:T(8,128)(2,1)} %get-tuple-element.25.refs_0_), channel_id=1, source_target_pairs={{0,1},{1,2},{2,3},{3,0},{4,5},{5,6},{6,7},{7,4},{8,9},{9,10},{10,1... | collective-permute-start | bytes 245768 | tf_op jit(solution)/shard_map/ppermute | solution.py:34
  10.3 2.2 %copy-start = (bf16[3,320,1280]{2,1,0:T(8,128)(2,1)S(1)}, bf16[3,320,1280]{2,1,0:T(8,128)(2,1)}, u32[]{:S(2)}) copy-start(bf16[3,320,1280]{2,1,0:T(8,128)(2,1)} %refs_6_.1) | copy-start | bytes 7372804
  12.5 0.9 %copy-start.3 = (bf16[320,128]{1,0:T(8,128)(2,1)S(1)}, bf16[320,128]{1,0:T(8,128)(2,1)}, u32[]{:S(2)}) copy-start(bf16[320,128]{1,0:T(8,128)(2,1)} %get-tuple-element.31.field_ref.refs_0_) | copy-start | bytes 245764
  13.3 4.4 %copy-start.2 = (bf16[320,128]{1,0:T(8,128)(2,1)S(1)}, bf16[320,128]{1,0:T(8,128)(2,1)}, u32[]{:S(2)}) copy-start(bf16[320,128]{1,0:T(8,128)(2,1)} %get-tuple-element.25.refs_0_) | copy-start | bytes 245764
  14.2 4.0 %collective-permute-start.9 = (bf16[320,128]{1,0:T(8,128)(2,1)S(1)}, bf16[320,128]{1,0:T(8,128)(2,1)S(1)}, u32[]{:S(2)}, u32[]{:S(2)}) collective-permute-start(bf16[320,128]{1,0:T(8,128)(2,1)S(1)} %collective-permute-done.8.before_ref.after_ref.refs_1_), channel_id=1, source_target_pairs={{0,4},{4,0},{8,12},{12,8},{1,5},{5,1},{9,13},{13,9},{2,6},{6,2},{1... | collective-permute-start | bytes 245768 | tf_op jit(solution)/shard_map/ppermute | solution.py:39
  17.3 3.3 %collective-permute-start.6 = (bf16[320,128]{1,0:T(8,128)(2,1)S(1)}, bf16[320,128]{1,0:T(8,128)(2,1)S(1)}, u32[]{:S(2)}, u32[]{:S(2)}) collective-permute-start(bf16[320,128]{1,0:T(8,128)(2,1)S(1)} %collective-permute-done.2.refs_3_), channel_id=1, source_target_pairs={{0,4},{4,0},{8,12},{12,8},{1,5},{5,1},{9,13},{13,9},{2,6},{6,2},{1... | collective-permute-start | bytes 245768 | tf_op jit(solution)/shard_map/ppermute | solution.py:39
  17.3 5.7 %collective-permute-start.5 = (bf16[320,128]{1,0:T(8,128)(2,1)S(1)}, bf16[320,128]{1,0:T(8,128)(2,1)S(1)}, u32[]{:S(2)}, u32[]{:S(2)}) collective-permute-start(bf16[320,128]{1,0:T(8,128)(2,1)S(1)} %collective-permute-done.1.refs_2_), channel_id=1, source_target_pairs={{0,4},{4,0},{8,12},{12,8},{1,5},{5,1},{9,13},{13,9},{2,6},{6,2},{1... | collective-permute-start | bytes 245768 | tf_op jit(solution)/shard_map/ppermute | solution.py:39
  17.8 5.1 %collective-permute-start.4 = (bf16[320,128]{1,0:T(8,128)(2,1)S(1)}, bf16[320,128]{1,0:T(8,128)(2,1)S(1)}, u32[]{:S(2)}, u32[]{:S(2)}) collective-permute-start(bf16[320,128]{1,0:T(8,128)(2,1)S(1)} %collective-permute-done.refs_1_), channel_id=1, source_target_pairs={{0,4},{4,0},{8,12},{12,8},{1,5},{5,1},{9,13},{13,9},{2,6},{6,2},{1... | collective-permute-start | bytes 245768 | tf_op jit(solution)/shard_map/ppermute | solution.py:39
  18.0 9.0 %collective-permute-start.13 = (bf16[320,128]{1,0:T(8,128)(2,1)S(1)}, bf16[320,128]{1,0:T(8,128)(2,1)S(1)}, u32[]{:S(2)}, u32[]{:S(2)}) collective-permute-start(bf16[320,128]{1,0:T(8,128)(2,1)S(1)} %get-tuple-element.33), channel_id=1, source_target_pairs={{0,1},{1,2},{2,3},{3,0},{4,5},{5,6},{6,7},{7,4},{8,9},{9,10},{10,1... | collective-permute-start | bytes 245768 | tf_op jit(solution)/shard_map/ppermute | solution.py:34
  18.2 10.6 %collective-permute-start.14 = (bf16[320,128]{1,0:T(8,128)(2,1)S(1)}, bf16[320,128]{1,0:T(8,128)(2,1)S(1)}, u32[]{:S(2)}, u32[]{:S(2)}) collective-permute-start(bf16[320,128]{1,0:T(8,128)(2,1)S(1)} %get-tuple-element.34), channel_id=1, source_target_pairs={{0,2},{1,3},{2,0},{3,1},{4,6},{5,7},{6,4},{7,5},{8,10},{9,11},{10,... | collective-permute-start | bytes 245768 | tf_op jit(solution)/shard_map/ppermute | solution.py:34
  20.6 8.2 %copy-start.4 = (bf16[320,128]{1,0:T(8,128)(2,1)S(1)}, bf16[320,128]{1,0:T(8,128)(2,1)}, u32[]{:S(2)}) copy-start(bf16[320,128]{1,0:T(8,128)(2,1)} %get-tuple-element.31.field_ref.refs_0_) | copy-start | bytes 245764
  20.6 8.2 %collective-permute-start.15 = (bf16[320,128]{1,0:T(8,128)(2,1)S(1)}, bf16[320,128]{1,0:T(8,128)(2,1)S(1)}, u32[]{:S(2)}, u32[]{:S(2)}) collective-permute-start(bf16[320,128]{1,0:T(8,128)(2,1)S(1)} %get-tuple-element.35), channel_id=1, source_target_pairs={{0,3},{1,0},{2,1},{3,2},{4,7},{5,4},{6,5},{7,6},{8,11},{9,8},{10,9... | collective-permute-start | bytes 245768 | tf_op jit(solution)/shard_map/ppermute | solution.py:34
  25.7 8.2 %collective-permute-start.12 = (bf16[320,128]{1,0:T(8,128)(2,1)S(1)}, bf16[320,128]{1,0:T(8,128)(2,1)S(1)}, u32[]{:S(2)}, u32[]{:S(2)}) collective-permute-start(bf16[320,128]{1,0:T(8,128)(2,1)S(1)} %spatial_forward.1.refs_0_), channel_id=1, source_target_pairs={{0,3},{1,0},{2,1},{3,2},{4,7},{5,4},{6,5},{7,6},{8,11},{9,8},{10,9... | collective-permute-start | bytes 245768 | tf_op jit(solution)/shard_map/ppermute | solution.py:34
  25.7 11.8 %collective-permute-start.11 = (bf16[320,128]{1,0:T(8,128)(2,1)S(1)}, bf16[320,128]{1,0:T(8,128)(2,1)S(1)}, u32[]{:S(2)}, u32[]{:S(2)}) collective-permute-start(bf16[320,128]{1,0:T(8,128)(2,1)S(1)} %spatial_forward.1.refs_0_), channel_id=1, source_target_pairs={{0,2},{1,3},{2,0},{3,1},{4,6},{5,7},{6,4},{7,5},{8,10},{9,11},{10,... | collective-permute-start | bytes 245768 | tf_op jit(solution)/shard_map/ppermute | solution.py:34
  26.9 10.9 %collective-permute-start.10 = (bf16[320,128]{1,0:T(8,128)(2,1)S(1)}, bf16[320,128]{1,0:T(8,128)(2,1)S(1)}, u32[]{:S(2)}, u32[]{:S(2)}) collective-permute-start(bf16[320,128]{1,0:T(8,128)(2,1)S(1)} %spatial_forward.1.refs_0_), channel_id=1, source_target_pairs={{0,1},{1,2},{2,3},{3,0},{4,5},{5,6},{6,7},{7,4},{8,9},{9,10},{10,1... | collective-permute-start | bytes 245768 | tf_op jit(solution)/shard_map/ppermute | solution.py:34
  28.9 1.3 %collective-permute-start.16 = (bf16[320,128]{1,0:T(8,128)(2,1)S(1)}, bf16[320,128]{1,0:T(8,128)(2,1)S(1)}, u32[]{:S(2)}, u32[]{:S(2)}) collective-permute-start(bf16[320,128]{1,0:T(8,128)(2,1)S(1)} %add_convert_fusion.1.field_ref.refs_0_), channel_id=1, source_target_pairs={{0,4},{4,0},{8,12},{12,8},{1,5},{5,1},{9,13},{13,9},{2,6},{6,2},{1... | collective-permute-start | bytes 245768 | tf_op jit(solution)/shard_map/ppermute | solution.py:39
  29.0 15.3 %collective-permute-start.19 = (bf16[2,320,128]{2,1,0:T(8,128)(2,1)S(1)}, bf16[2,320,128]{2,1,0:T(8,128)(2,1)S(1)}, u32[]{:S(2)}, u32[]{:S(2)}) collective-permute-start(bf16[2,320,128]{2,1,0:T(8,128)(2,1)S(1)} %pad_maximum_fusion.4), channel_id=1, source_target_pairs={{0,8},{4,12},{8,0},{12,4},{1,9},{5,13},{9,1},{13,5},{2,10},{6,14},... | collective-permute-start | bytes 491528 | tf_op jit(solution)/shard_map/ppermute | solution.py:34
  31.9 21.7 %copy-start.1 = (bf16[3,320,1280]{2,1,0:T(8,128)(2,1)S(1)}, bf16[3,320,1280]{2,1,0:T(8,128)(2,1)}, u32[]{:S(2)}) copy-start(bf16[3,320,1280]{2,1,0:T(8,128)(2,1)} %refs_6_.1) | copy-start | bytes 7372804
  31.9 8.4 %collective-permute-start.20 = (bf16[320,128]{1,0:T(8,128)(2,1)S(1)}, bf16[320,128]{1,0:T(8,128)(2,1)S(1)}, u32[]{:S(2)}, u32[]{:S(2)}) collective-permute-start(bf16[320,128]{1,0:T(8,128)(2,1)S(1)} %get-tuple-element.37), channel_id=1, source_target_pairs={{0,1},{1,2},{2,3},{3,0},{4,5},{5,6},{6,7},{7,4},{8,9},{9,10},{10,1... | collective-permute-start | bytes 245768 | tf_op jit(solution)/shard_map/ppermute | solution.py:34
  33.9 9.4 %collective-permute-start.21 = (bf16[320,128]{1,0:T(8,128)(2,1)S(1)}, bf16[320,128]{1,0:T(8,128)(2,1)S(1)}, u32[]{:S(2)}, u32[]{:S(2)}) collective-permute-start(bf16[320,128]{1,0:T(8,128)(2,1)S(1)} %get-tuple-element.38), channel_id=1, source_target_pairs={{0,2},{1,3},{2,0},{3,1},{4,6},{5,7},{6,4},{7,5},{8,10},{9,11},{10,... | collective-permute-start | bytes 245768 | tf_op jit(solution)/shard_map/ppermute | solution.py:34
  37.5 6.1 %collective-permute-start.22 = (bf16[320,128]{1,0:T(8,128)(2,1)S(1)}, bf16[320,128]{1,0:T(8,128)(2,1)S(1)}, u32[]{:S(2)}, u32[]{:S(2)}) collective-permute-start(bf16[320,128]{1,0:T(8,128)(2,1)S(1)} %get-tuple-element.39), channel_id=1, source_target_pairs={{0,3},{1,0},{2,1},{3,2},{4,7},{5,4},{6,5},{7,6},{8,11},{9,8},{10,9... | collective-permute-start | bytes 245768 | tf_op jit(solution)/shard_map/ppermute | solution.py:34
  37.8 15.6 %collective-permute-start.17 = (bf16[4,320,128]{2,1,0:T(8,128)(2,1)S(1)}, bf16[4,320,128]{2,1,0:T(8,128)(2,1)S(1)}, u32[]{:S(2)}, u32[]{:S(2)}) collective-permute-start(bf16[4,320,128]{2,1,0:T(8,128)(2,1)S(1)} %pad_maximum_fusion), channel_id=1, source_target_pairs={{0,8},{4,12},{8,0},{12,4},{1,9},{5,13},{9,1},{13,5},{2,10},{6,14},... | collective-permute-start | bytes 983048 | tf_op jit(solution)/shard_map/ppermute | solution.py:34
  40.2 10.1 %collective-permute-start.18 = (bf16[2,320,128]{2,1,0:T(8,128)(2,1)S(1)}, bf16[2,320,128]{2,1,0:T(8,128)(2,1)S(1)}, u32[]{:S(2)}, u32[]{:S(2)}) collective-permute-start(bf16[2,320,128]{2,1,0:T(8,128)(2,1)S(1)} %pad_maximum_fusion.3), channel_id=1, source_target_pairs={{0,8},{4,12},{8,0},{12,4},{1,9},{5,13},{9,1},{13,5},{2,10},{6,14},... | collective-permute-start | bytes 491528 | tf_op jit(solution)/shard_map/ppermute | solution.py:34
  43.3 12.0 %collective-permute-start.23 = (bf16[320,128]{1,0:T(8,128)(2,1)S(1)}, bf16[320,128]{1,0:T(8,128)(2,1)S(1)}, u32[]{:S(2)}, u32[]{:S(2)}) collective-permute-start(bf16[320,128]{1,0:T(8,128)(2,1)S(1)} %get-tuple-element.48), channel_id=1, source_target_pairs={{0,4},{4,0},{8,12},{12,8},{1,5},{5,1},{9,13},{13,9},{2,6},{6,2},{1... | collective-permute-start | bytes 245768 | tf_op jit(solution)/shard_map/ppermute | solution.py:39
  53.4 1.9 %collective-permute-start.24 = (bf16[320,128]{1,0:T(8,128)(2,1)S(1)}, bf16[320,128]{1,0:T(8,128)(2,1)S(1)}, u32[]{:S(2)}, u32[]{:S(2)}) collective-permute-start(bf16[320,128]{1,0:T(8,128)(2,1)S(1)} %get-tuple-element.46), channel_id=1, source_target_pairs={{0,4},{4,0},{8,12},{12,8},{1,5},{5,1},{9,13},{13,9},{2,6},{6,2},{1... | collective-permute-start | bytes 245768 | tf_op jit(solution)/shard_map/ppermute | solution.py:39

commit v4 on v3

--- a/solution.py
+++ b/solution.py
@@ -100,19 +100,6 @@
     row = lane // W + dr
     col = lane % W + dc
     return (row >= 0) & (row < ROWS) & (col >= 0) & (col < W)
-
-
-def bring_in(latents, cotangent):
-    def body(l_ref, t_ref, lo_ref, to_ref):
-        lo_ref[...] = l_ref[...]
-        to_ref[...] = t_ref[...]
-
-    return pl.pallas_call(
-        body,
-        out_shape=[jax.ShapeDtypeStruct(x.shape, x.dtype) for x in (latents, cotangent)],
-        cost_estimate=pl.CostEstimate(flops=8000000000, transcendentals=0, bytes_accessed=1_000_000),
-        name="bring_in",
-    )(latents, cotangent)
 
 
 def spatial_forward(mine, siblings, weight):
@@ -262,28 +249,21 @@
     )(field, sibling, weight.reshape(3, 3 * cb, channels))
 
 
-def pairs_from(own, sibling, rest):
-    return [(own, sibling)] + [(both.at[0], both.at[1]) for both in rest]
-
-
-def spatial_grads(grads, fields, scale):
+def spatial_grads(grads, grads_sibling, fields, fields_sibling, scale):
     _, n_x = sizes()
     ob, ib = grads[0].shape[0], fields[0].shape[0]
     frames = FT * n_x
-    n_in = n_x + 1
 
     def body(*refs):
-        g_refs, l_refs = refs[:n_in], refs[n_in : 2 * n_in]
-        out_hbm, left, right, out, sems = refs[2 * n_in :]
+        g_refs, gs_refs, l_refs, ls_refs = (refs[q * n_x : (q + 1) * n_x] for q in range(4))
+        out_hbm, left, right, out, sems = refs[4 * n_x :]
         _, _, band = place()
         blank = jnp.zeros((W, ib), BF)
-        g_pairs = pairs_from(g_refs[0], g_refs[1], g_refs[2:])
-        l_pairs = pairs_from(l_refs[0], l_refs[1], l_refs[2:])
         for j in range(n_x):
-            for a, frame in enumerate(frames_of(g_pairs[j][0][...], g_pairs[j][1][...], band)):
+            for a, frame in enumerate(frames_of(g_refs[j][...], gs_refs[j][...], band)):
                 f = FT * j + a
                 left[:, f * FRAME : (f + 1) * FRAME] = frame.astype(BF)
-            for a, frame in enumerate(frames_of(l_pairs[j][0][...], l_pairs[j][1][...], band)):
+            for a, frame in enumerate(frames_of(l_refs[j][...], ls_refs[j][...], band)):
                 f = FT * j + a
                 for q, moved in enumerate(shifted_columns(frame, 1)):
                     right[q, f, :W, :] = blank
@@ -299,7 +279,6 @@
         for copy in copies:
             copy.wait()
 
-    args = (*grads[:2], *grads[2], *fields[:2], *fields[2])
     return pl.pallas_call(
         body,
         out_specs=pl.BlockSpec(memory_space=pltpu.HBM),
@@ -312,7 +291,7 @@
         ],
         compiler_params=pltpu.CompilerParams(vmem_limit_bytes=24 * MIB),
         name="spatial_grads",
-    )(*args)
+    )(*grads, *grads_sibling, *fields, *fields_sibling)
 
 
 def temporal_grads(grads, grads_sibling, fields, fields_sibling, scale):
@@ -358,10 +337,14 @@
     )(*grads, *grads_sibling, *fields, *fields_sibling)
 
 
-def reduce_ch(base, chunks):
-    total = base.astype(F32) + chunks[0]
-    for k in range(1, len(chunks)):
-        total = total + send(chunks[k], "ch", k).astype(F32)
+def scatter_ch(chunks):
+    return [send(chunks[k], "ch", k) for k in range(1, len(chunks))]
+
+
+def total_of(base, own, received):
+    total = base.astype(F32) + own
+    for chunk in received:
+        total = total + chunk.astype(F32)
     return total.astype(BF)
 
 
@@ -375,43 +358,44 @@
         stack = jnp.stack(pieces) if isinstance(pieces, list) else pieces
         return lax.dynamic_index_in_dim(stack, (c + n_ch - b) % n_ch, 0, keepdims=False)
 
-    latents, cotangent = bring_in(latents, cotangent)
-
+    own_block = RBANDS * m + band
+    sib_block = RBANDS * m + 1 - band
+
+    siblings = [swap_band(latents)]
+    mine = gather_ch(latents)
+    cotangent = after_all(cotangent, siblings[0])
     cot_ring = ring_blocks(cotangent)
-    mine = gather_ch(latents)
     chunks = temporal_backward(cotangent, cot_ring[0], cot_ring[-1], temporal_weight)
-
-    siblings = [swap_band(piece) for piece in mine]
+    partials = scatter_ch(chunks)
+    mine = after_all(mine, chunks)
+
+    siblings += [swap_band(piece) for piece in mine[1:]]
     cots = [cotangent] + cot_ring
     cots_sibling = [swap_band(x) for x in cots]
     siblings = after_all(siblings, cots_sibling)
     hidden = spatial_forward(mine, siblings, spatial_weight)
-    base = after_all(cotangent, hidden)
-
-    hidden_grad = reduce_ch(base, chunks)
+    hidden_mine = gather_ch(hidden)
+
+    hidden_grad = total_of(after_all(cotangent, hidden), chunks[0], partials)
+    grad_ring = ring_blocks(hidden_grad)
     grad_sibling = swap_band(hidden_grad)
     chunks = spatial_backward(hidden_grad, grad_sibling, spatial_weight)
-    hidden_mine = gather_ch(hidden)
-    hidden_mine = after_all(hidden_mine, chunks)
-    latent_grad = reduce_ch(hidden_grad, chunks)
-
-    before, after = neighbours(jnp.stack(hidden_mine))
-
-    own_block = RBANDS * m + band
-    sib_block = RBANDS * m + 1 - band
-
-    lat_rest, grad_rest = [], []
+    partials = scatter_ch(chunks)
+
+    lat_own, lat_sib = [block(mine, own_block)], [block(siblings, own_block)]
     for j in range(1, n_x):
         target = RBANDS * ((m + j) % n_x) + band
-        both = jnp.stack([block(mine, target), block(siblings, target)])
-        lat_rest.append(send(both, "st", RBANDS * j))
-        grad_rest.append(send(jnp.stack([hidden_grad, grad_sibling]), "st", RBANDS * j))
-    spatial_grad = spatial_grads(
-        (hidden_grad, grad_sibling, grad_rest),
-        (block(mine, own_block), block(siblings, own_block), lat_rest),
-        scale,
-    )
-    before, after = after_all((before, after), (spatial_grad, latent_grad))
+        both = send(jnp.stack([block(mine, target), block(siblings, target)]), "st", RBANDS * j)
+        lat_own.append(both[0])
+        lat_sib.append(both[1])
+    grads = [hidden_grad] + grad_ring
+    grads_sibling = [grad_sibling] + [swap_band(x) for x in grad_ring]
+    lat_own = after_all(lat_own, partials[0])
+    spatial_grad = spatial_grads(grads, grads_sibling, lat_own, lat_sib, scale)
+
+    hidden_mine = after_all(hidden_mine, chunks)
+    before, after = neighbours(jnp.stack(hidden_mine))
+    before, after = after_all((before, after), (spatial_grad, partials[1]))
     temporal_out = temporal_forward(hidden_mine, before, after, temporal_weight)
 
     hid_own, hid_sib = [block(hidden_mine, own_block)], [block(hidden_mine, sib_block)]
@@ -425,10 +409,10 @@
             both = send(both, "st", RBANDS * j)
             hid_own.append(both[0])
             hid_sib.append(both[1])
-    temporal_grad = temporal_grads(
-        cots, cots_sibling, hid_own, [swap_band(x) for x in hid_sib], scale
-    )
-
+    hid_own = after_all(hid_own, partials[2:])
+    temporal_grad = temporal_grads(cots, cots_sibling, hid_own, [swap_band(x) for x in hid_sib], scale)
+
+    latent_grad = total_of(hidden_grad, chunks[0], partials)
     return temporal_out, latent_grad, spatial_grad, temporal_grad
 
 

time: 58.4 us -> 53.5 us (0.916)
  waiting for transfers between devices: 13.9 us -> 9.99 us
  starting transfers between devices: 24.9 us -> 24.2 us
  Pallas kernels: 14.4 us -> 13.8 us
    ppermute x16, waiting for transfers between devices: 13.3 us -> 7.66 us  [send(): return lax.ppermute(data, axis, [(i, (i + by) % n) for i in range(n)])]
    ppermute x9 -> x10, waiting for transfers between devices: 0.66 us -> 2.33 us  [swap_band(): return lax.ppermute(data, 'st', [(i, i ^ 1) for i in range(n)])]
    pallas_call x1 -> x0, Pallas kernels: 1.6 us -> none  [bring_in(): pl.pallas_call(body, out_shape=[jax.ShapeDtypeStruct(x.shape, x.dtype) fo...]
    ppermute x16, starting transfers between devices: 23.6 us -> 22.5 us  [send(): return lax.ppermute(data, axis, [(i, (i + by) % n) for i in range(n)])]
    pallas_call x1, Pallas kernels: 0.85 us -> 1.81 us  [temporal_backward(): pl.pallas_call(body, out_shape=chunk_shapes(n_ch, cb), scratch_shapes=[pl...]
    ppermute x9 -> x10, starting transfers between devices: 1.31 us -> 1.69 us  [swap_band(): return lax.ppermute(data, 'st', [(i, i ^ 1) for i in range(n)])]
  transfers between devices with their start and end apart: 25 -> 26, of which waited for: 6 -> 6; matrix products, arithmetic and copies ran while one was open for 2% -> 2% of each run, Pallas kernels for 17% -> 21%
where the time goes in v4:
time: 53.5 us; the launch traced here: 53.3 us
  starting transfers between devices  24.2 us (45%)
  Pallas kernels  13.8 us (26%)
  waiting for transfers between devices  9.99 us (19%)
  local copies, waits for them, and re-layouts  3.57 us (7%)
  other arithmetic  0.89 us (2%)
  between operations  0.88 us (2%)
    ppermute x16, starting transfers between devices, send(): return lax.ppermute(data, axis, [(i, (i + by) % n) for i in range(n)])  22.5 us
    ppermute x16, waiting for transfers between devices, send(): return lax.ppermute(data, axis, [(i, (i + by) % n) for i in range(n)])  7.66 us
    unnamed x14, local copies, waits for them, and re-layouts  3.5 us
    pallas_call x1, Pallas kernels, spatial_grads(): pl.pallas_call(body, out_specs=pl.BlockSpec(memory_space=pltpu.HBM), out_...  3.08 us
    pallas_call x1, Pallas kernels, temporal_grads(): pl.pallas_call(body, out_specs=pl.BlockSpec(memory_space=pltpu.HBM), out_...  2.79 us
    pallas_call x1, Pallas kernels, spatial_forward(): pl.pallas_call(body, out_shape=jax.ShapeDtypeStruct((cb, TILE), BF), scra...  2.69 us
    ppermute x10, waiting for transfers between devices, swap_band(): return lax.ppermute(data, 'st', [(i, i ^ 1) for i in range(n)])  2.33 us
    pallas_call x1, Pallas kernels, temporal_backward(): pl.pallas_call(body, out_shape=chunk_shapes(n_ch, cb), scratch_shapes=[pl...  1.81 us
  transfers between devices with their start and end apart: 26, of which 6 were waited for; matrix products, arithmetic and copies ran while one was open for 2% of the time, Pallas kernels for 21%

profile of v4, /device:TPU:0, one launch (start us, length us, event | category | flops | bytes accessed | tf_op | source)
XLA Modules:
  0.0 53.3 jit_solution(2627048609566248408)
XLA Ops:
  0.6 0.5 collective-permute-start.3
  1.1 1.1 %collective-permute-done.3.refs_4_ = bf16[320,128]{1,0:T(8,128)(2,1)S(1)} collective-permute-done((bf16[320,128]{1,0:T(8,128)(2,1)}, bf16[320,128]{1,0:T(8,128)(2,1)S(1)}, u32[]{:S(2)}, u32[]{:S(2)}) %collective-permute-start.3) | collective-permute-done | bytes 81952 | tf_op jit(solution)/shard_map/ppermute | solution.py:39
  2.3 2.8 %collective-permute-start.4 = (bf16[320,128]{1,0:T(8,128)(2,1)}, bf16[320,128]{1,0:T(8,128)(2,1)}, u32[]{:S(2)}, u32[]{:S(2)}) collective-permute-start(bf16[320,128]{1,0:T(8,128)(2,1)} %refs_0_.1), channel_id=1, source_target_pairs={{0,8},{4,12},{8,0},{12,4},{1,9},{5,13},{9,1},{13,5},{2,10},{6,14},... | collective-permute-start | bytes 245768 | tf_op jit(solution)/shard_map/ppermute | solution.py:34
  5.1 3.6 %collective-permute-start.2 = (bf16[320,128]{1,0:T(8,128)(2,1)}, bf16[320,128]{1,0:T(8,128)(2,1)S(1)}, u32[]{:S(2)}, u32[]{:S(2)}) collective-permute-start(bf16[320,128]{1,0:T(8,128)(2,1)} %refs_0_), channel_id=1, source_target_pairs={{0,3},{1,0},{2,1},{3,2},{4,7},{5,4},{6,5},{7,6},{8,11},{9,8},{10,9... | collective-permute-start | bytes 245768 | tf_op jit(solution)/shard_map/ppermute | solution.py:34
  8.7 0.0 collective-permute-start.1
  8.7 1.0 %collective-permute-start = (bf16[320,128]{1,0:T(8,128)(2,1)}, bf16[320,128]{1,0:T(8,128)(2,1)S(1)}, u32[]{:S(2)}, u32[]{:S(2)}) collective-permute-start(bf16[320,128]{1,0:T(8,128)(2,1)} %refs_0_), channel_id=1, source_target_pairs={{0,1},{1,2},{2,3},{3,0},{4,5},{5,6},{6,7},{7,4},{8,9},{9,10},{10,1... | collective-permute-start | bytes 245768 | tf_op jit(solution)/shard_map/ppermute | solution.py:34
  9.7 0.0 collective-permute-start.8
  9.7 0.0 collective-permute-done.4.before_ref.after_ref.refs_1_
  9.8 0.0 copy-start
  9.8 1.8 %copy-done = bf16[3,320,1280]{2,1,0:T(8,128)(2,1)S(1)} copy-done((bf16[3,320,1280]{2,1,0:T(8,128)(2,1)S(1)}, bf16[3,320,1280]{2,1,0:T(8,128)(2,1)}, u32[]{:S(2)}) %copy-start) | copy-done | bytes 2457624
  11.6 1.6 %copy-done.3 = bf16[320,128]{1,0:T(8,128)(2,1)S(1)} copy-done((bf16[320,128]{1,0:T(8,128)(2,1)S(1)}, bf16[320,128]{1,0:T(8,128)(2,1)}, u32[]{:S(2)}) %copy-start.3) | copy-done | bytes 81944
  13.2 1.8 %temporal_backward.1 = (f32[320,128]{1,0:T(8,128)S(1)}, bf16[320,128]{1,0:T(8,128)(2,1)S(1)}, bf16[320,128]{1,0:T(8,128)(2,1)S(1)}, bf16[320,128]{1,0:T(8,128)(2,1)S(1)}) custom-call(bf16[320,128]{1,0:T(8,128)(2,1)S(1)} %copy-done.3, bf16[320,128]{1,0:T(8,128)(2,1)} %collective-permute-done.4.before_ref.after_ref.refs_1_, ...), custom_call_target="tpu_custom_call" | custom-call | flops 4000000000 | bytes 3000000 | tf_op jit(solution)/shard_map/temporal_backward/pallas_call | solution.py:196
  15.1 0.0 collective-permute-done.2.refs_3_
  15.1 1.4 %collective-permute-done.1.refs_2_ = bf16[320,128]{1,0:T(8,128)(2,1)S(1)} collective-permute-done((bf16[320,128]{1,0:T(8,128)(2,1)}, bf16[320,128]{1,0:T(8,128)(2,1)S(1)}, u32[]{:S(2)}, u32[]{:S(2)}) %collective-permute-start.1) | collective-permute-done | bytes 81952 | tf_op jit(solution)/shard_map/ppermute | solution.py:34
  16.5 0.0 collective-permute-done.refs_1_
  16.5 0.0 collective-permute-start.5
  16.5 0.5 collective-permute-start.6
  17.0 0.0 collective-permute-start.7
  17.0 0.5 collective-permute-start.9
  17.6 0.0 collective-permute-done.8.refs_2_
  17.6 1.2 %collective-permute-start.13 = (bf16[320,128]{1,0:T(8,128)(2,1)S(1)}, bf16[320,128]{1,0:T(8,128)(2,1)S(1)}, u32[]{:S(2)}, u32[]{:S(2)}) collective-permute-start(bf16[320,128]{1,0:T(8,128)(2,1)S(1)} %get-tuple-element.34), channel_id=1, source_target_pairs={{0,1},{1,2},{2,3},{3,0},{4,5},{5,6},{6,7},{7,4},{8,9},{9,10},{10,1... | collective-permute-start | bytes 245768 | tf_op jit(solution)/shard_map/ppermute | solution.py:34
  18.8 0.0 collective-permute-done.9.refs_3_
  18.8 2.0 %collective-permute-start.14 = (bf16[320,128]{1,0:T(8,128)(2,1)S(1)}, bf16[320,128]{1,0:T(8,128)(2,1)S(1)}, u32[]{:S(2)}, u32[]{:S(2)}) collective-permute-start(bf16[320,128]{1,0:T(8,128)(2,1)S(1)} %get-tuple-element.35), channel_id=1, source_target_pairs={{0,2},{1,3},{2,0},{3,1},{4,6},{5,7},{6,4},{7,5},{8,10},{9,11},{10,... | collective-permute-start | bytes 245768 | tf_op jit(solution)/shard_map/ppermute | solution.py:34
  20.8 0.0 collective-permute-done.5.refs_5_
  20.8 1.9 %collective-permute-start.15 = (bf16[320,128]{1,0:T(8,128)(2,1)S(1)}, bf16[320,128]{1,0:T(8,128)(2,1)S(1)}, u32[]{:S(2)}, u32[]{:S(2)}) collective-permute-start(bf16[320,128]{1,0:T(8,128)(2,1)S(1)} %get-tuple-element.36), channel_id=1, source_target_pairs={{0,3},{1,0},{2,1},{3,2},{4,7},{5,4},{6,5},{7,6},{8,11},{9,8},{10,9... | collective-permute-start | bytes 245768 | tf_op jit(solution)/shard_map/ppermute | solution.py:34
  22.7 0.0 collective-permute-done.6.refs_6_
  22.7 0.0 collective-permute-done.7.refs_7_
  22.7 2.7 %spatial_forward.1.refs_0_ = bf16[320,128]{1,0:T(8,128)(2,1)S(1)} custom-call(bf16[320,128]{1,0:T(8,128)(2,1)S(1)} %copy-done.2, bf16[320,128]{1,0:T(8,128)(2,1)S(1)} %collective-permute-done.refs_1_, bf16[320,128]{1,0:T(8,128)(2,1)S(1)} %collective-permute-done.1.refs_2_, bf16[320,128]{1,0:T(8,128)(2,1)S(1)} %collective-permute-done.2.refs_3_, ...), custom_call_target="tpu_custom_call" | custom-call | tf_op jit(solution)/shard_map/spatial_forward/pallas_call | solution.py:133
  25.4 0.6 %collective-permute-start.12 = (bf16[320,128]{1,0:T(8,128)(2,1)S(1)}, bf16[320,128]{1,0:T(8,128)(2,1)S(1)}, u32[]{:S(2)}, u32[]{:S(2)}) collective-permute-start(bf16[320,128]{1,0:T(8,128)(2,1)S(1)} %spatial_forward.1.refs_0_), channel_id=1, source_target_pairs={{0,3},{1,0},{2,1},{3,2},{4,7},{5,4},{6,5},{7,6},{8,11},{9,8},{10,9... | collective-permute-start | bytes 245768 | tf_op jit(solution)/shard_map/ppermute | solution.py:34
  26.0 1.1 %collective-permute-start.11 = (bf16[320,128]{1,0:T(8,128)(2,1)S(1)}, bf16[320,128]{1,0:T(8,128)(2,1)S(1)}, u32[]{:S(2)}, u32[]{:S(2)}) collective-permute-start(bf16[320,128]{1,0:T(8,128)(2,1)S(1)} %spatial_forward.1.refs_0_), channel_id=1, source_target_pairs={{0,2},{1,3},{2,0},{3,1},{4,6},{5,7},{6,4},{7,5},{8,10},{9,11},{10,... | collective-permute-start | bytes 245768 | tf_op jit(solution)/shard_map/ppermute | solution.py:34
  27.1 0.0 collective-permute-done.13
  27.1 1.3 %collective-permute-start.10 = (bf16[320,128]{1,0:T(8,128)(2,1)S(1)}, bf16[320,128]{1,0:T(8,128)(2,1)S(1)}, u32[]{:S(2)}, u32[]{:S(2)}) collective-permute-start(bf16[320,128]{1,0:T(8,128)(2,1)S(1)} %spatial_forward.1.refs_0_), channel_id=1, source_target_pairs={{0,1},{1,2},{2,3},{3,0},{4,5},{5,6},{6,7},{7,4},{8,9},{9,10},{10,1... | collective-permute-start | bytes 245768 | tf_op jit(solution)/shard_map/ppermute | solution.py:34
  28.4 0.0 collective-permute-done.14
  28.4 0.0 collective-permute-done.15
  28.4 0.1 add_convert_fusion.1.field_ref.refs_0_
  28.4 0.6 %collective-permute-start.18 = (bf16[320,128]{1,0:T(8,128)(2,1)S(1)}, bf16[320,128]{1,0:T(8,128)(2,1)S(1)}, u32[]{:S(2)}, u32[]{:S(2)}) collective-permute-start(bf16[320,128]{1,0:T(8,128)(2,1)S(1)} %add_convert_fusion.1.field_ref.refs_0_), channel_id=1, source_target_pairs={{0,8},{4,12},{8,0},{12,4},{1,9},{5,13},{9,1},{13,5},{2,10},{6,14},... | collective-permute-start | bytes 245768 | tf_op jit(solution)/shard_map/ppermute | solution.py:34
  29.0 0.0 collective-permute-start.16
  29.1 1.2 %collective-permute-done.16.sibling_ref.refs_2_ = bf16[320,128]{1,0:T(8,128)(2,1)S(1)} collective-permute-done((bf16[320,128]{1,0:T(8,128)(2,1)S(1)}, bf16[320,128]{1,0:T(8,128)(2,1)S(1)}, u32[]{:S(2)}, u32[]{:S(2)}) %collective-permute-start.16) | collective-permute-done | bytes 81952 | tf_op jit(solution)/shard_map/ppermute | solution.py:39
  30.3 1.5 %collective-permute-start.20 = (bf16[2,320,128]{2,1,0:T(8,128)(2,1)S(1)}, bf16[2,320,128]{2,1,0:T(8,128)(2,1)S(1)}, u32[]{:S(2)}, u32[]{:S(2)}) collective-permute-start(bf16[2,320,128]{2,1,0:T(8,128)(2,1)S(1)} %pad_maximum_fusion.3), channel_id=1, source_target_pairs={{0,8},{4,12},{8,0},{12,4},{1,9},{5,13},{9,1},{13,5},{2,10},{6,14},... | collective-permute-start | bytes 491528 | tf_op jit(solution)/shard_map/ppermute | solution.py:34
  31.8 1.6 %spatial_backward.1 = (f32[320,128]{1,0:T(8,128)S(1)}, bf16[320,128]{1,0:T(8,128)(2,1)S(1)}, bf16[320,128]{1,0:T(8,128)(2,1)S(1)}, bf16[320,128]{1,0:T(8,128)(2,1)S(1)}) custom-call(bf16[320,128]{1,0:T(8,128)(2,1)S(1)} %add_convert_fusion.1.field_ref.refs_0_, bf16[320,128]{1,0:T(8,128)(2,1)S(1)} %collective-permute-done.16.sibling_ref.refs_2_, ...), custom_call_target="tpu_custom_call" | custom-call | tf_op jit(solution)/shard_map/spatial_backward/pallas_call | solution.py:240
  33.4 0.0 copy-start.1
  33.4 0.0 collective-permute-done.12.refs_3_
  33.4 1.6 %collective-permute-start.21 = (bf16[320,128]{1,0:T(8,128)(2,1)S(1)}, bf16[320,128]{1,0:T(8,128)(2,1)S(1)}, u32[]{:S(2)}, u32[]{:S(2)}) collective-permute-start(bf16[320,128]{1,0:T(8,128)(2,1)S(1)} %get-tuple-element.47), channel_id=1, source_target_pairs={{0,1},{1,2},{2,3},{3,0},{4,5},{5,6},{6,7},{7,4},{8,9},{9,10},{10,1... | collective-permute-start | bytes 245768 | tf_op jit(solution)/shard_map/ppermute | solution.py:34
  35.0 1.1 %collective-permute-done.11.refs_2_ = bf16[320,128]{1,0:T(8,128)(2,1)S(1)} collective-permute-done((bf16[320,128]{1,0:T(8,128)(2,1)S(1)}, bf16[320,128]{1,0:T(8,128)(2,1)S(1)}, u32[]{:S(2)}, u32[]{:S(2)}) %collective-permute-start.11) | collective-permute-done | bytes 81952 | tf_op jit(solution)/shard_map/ppermute | solution.py:34
  36.1 2.8 %collective-permute-start.22 = (bf16[320,128]{1,0:T(8,128)(2,1)S(1)}, bf16[320,128]{1,0:T(8,128)(2,1)S(1)}, u32[]{:S(2)}, u32[]{:S(2)}) collective-permute-start(bf16[320,128]{1,0:T(8,128)(2,1)S(1)} %get-tuple-element.48), channel_id=1, source_target_pairs={{0,2},{1,3},{2,0},{3,1},{4,6},{5,7},{6,4},{7,5},{8,10},{9,11},{10,... | collective-permute-start | bytes 245768 | tf_op jit(solution)/shard_map/ppermute | solution.py:34
  38.9 0.0 collective-permute-done.10.refs_1_
  38.9 0.6 %collective-permute-start.17 = (bf16[4,320,128]{2,1,0:T(8,128)(2,1)S(1)}, bf16[4,320,128]{2,1,0:T(8,128)(2,1)S(1)}, u32[]{:S(2)}, u32[]{:S(2)}) collective-permute-start(bf16[4,320,128]{2,1,0:T(8,128)(2,1)S(1)} %pad_maximum_fusion), channel_id=1, source_target_pairs={{0,8},{4,12},{8,0},{12,4},{1,9},{5,13},{9,1},{13,5},{2,10},{6,14},... | collective-permute-start | bytes 983048 | tf_op jit(solution)/shard_map/ppermute | solution.py:34
  39.5 0.0 collective-permute-done.18.refs_1_
  39.5 0.1 collective-permute-start.23
  39.6 0.0 collective-permute-done.20
  39.6 0.1 collective-permute-start.19
  39.7 2.0 %collective-permute-done.21 = bf16[320,128]{1,0:T(8,128)(2,1)S(1)} collective-permute-done((bf16[320,128]{1,0:T(8,128)(2,1)S(1)}, bf16[320,128]{1,0:T(8,128)(2,1)S(1)}, u32[]{:S(2)}, u32[]{:S(2)}) %collective-permute-start.21) | collective-permute-done | bytes 81952 | tf_op jit(solution)/shard_map/ppermute | solution.py:34
  41.7 0.0 collective-permute-start.24
  41.7 0.0 collective-permute-done.19.refs_3_
  41.7 3.1 %spatial_grads.1 = f32[9,320,320]{2,1,0:T(8,128)} custom-call(bf16[320,128]{1,0:T(8,128)(2,1)S(1)} %add_convert_fusion.1.field_ref.refs_0_, bf16[320,128]{1,0:T(8,128)(2,1)S(1)} %collective-permute-done.18.refs_1_, bf16[320,128]{1,0:T(8,128)(2,1)S(1)} %collective-permute-done.16.sibling_ref.refs_2_, bf16[320,128]{1,0:T(8,128)(2,1)S(1)} %collective-permute-done.19.refs_3_, ...), custom_call_target="tpu_custom_call" | custom-call | tf_op jit(solution)/shard_map/spatial_grads/pallas_call | solution.py:282
  44.8 0.0 collective-permute-done.22
  44.8 3.1 %collective-permute-done.17.refs_4_.refs_5_ = bf16[4,320,128]{2,1,0:T(8,128)(2,1)S(1)} collective-permute-done((bf16[4,320,128]{2,1,0:T(8,128)(2,1)S(1)}, bf16[4,320,128]{2,1,0:T(8,128)(2,1)S(1)}, u32[]{:S(2)}, u32[]{:S(2)}) %collective-permute-start.17) | collective-permute-done | bytes 327712 | tf_op jit(solution)/shard_map/ppermute | solution.py:34
  47.9 0.1 collective-permute-start.25
  48.0 0.0 collective-permute-done.23
  48.0 0.7 %add_convert_fusion = bf16[320,128]{1,0:T(8,128)(2,1)} fusion(bf16[320,128]{1,0:T(8,128)(2,1)S(1)} %collective-permute-done.23, bf16[320,128]{1,0:T(8,128)(2,1)S(1)} %collective-permute-done.22, bf16[320,128]{1,0:T(8,128)(2,1)S(1)} %collective-permute-done.21, f32[320,128]{1,0:T(8,128)S(1)} %get-tuple-element.46, ...), kind=kLoop, calls=%fused_computation.4 | loop fusion | flops 368640 | bytes 573440 | tf_op jit(solution)/shard_map/convert_element_type | solution.py:348
  48.7 1.8 %temporal_forward.1 = bf16[320,128]{1,0:T(8,128)(2,1)} custom-call(bf16[320,128]{1,0:T(8,128)(2,1)S(1)} %spatial_forward.1.refs_0_, bf16[320,128]{1,0:T(8,128)(2,1)S(1)} %collective-permute-done.10.refs_1_, bf16[320,128]{1,0:T(8,128)(2,1)S(1)} %collective-permute-done.11.refs_2_, bf16[320,128]{1,0:T(8,128)(2,1)S(1)} %collective-permute-done.12.refs_3_, ...), custom_call_target="tpu_custom_call" | custom-call | tf_op jit(solution)/shard_map/temporal_forward/pallas_call | solution.py:161
  50.5 0.0 collective-permute-done.24.refs_6_
  50.5 0.0 collective-permute-done.25.refs_7_
  50.5 2.8 %temporal_grads.1 = f32[3,320,320]{2,1,0:T(8,128)} custom-call(bf16[320,128]{1,0:T(8,128)(2,1)S(1)} %copy-done.4, bf16[320,128]{1,0:T(8,128)(2,1)} %collective-permute-done.4.before_ref.after_ref.refs_1_, bf16[320,128]{1,0:T(8,128)(2,1)S(1)} %collective-permute-done.8.refs_2_, bf16[320,128]{1,0:T(8,128)(2,1)S(1)} %collective-permute-done.9.refs_3_, ...), custom_call_target="tpu_custom_call" | custom-call | tf_op jit(solution)/shard_map/temporal_grads/pallas_call | solution.py:325
  (20 shorter events, 0.2 us)
Async XLA Ops:
  0.6 1.7 %collective-permute-start.3 = (bf16[320,128]{1,0:T(8,128)(2,1)}, bf16[320,128]{1,0:T(8,128)(2,1)S(1)}, u32[]{:S(2)}, u32[]{:S(2)}) collective-permute-start(bf16[320,128]{1,0:T(8,128)(2,1)} %refs_0_), channel_id=1, source_target_pairs={{0,4},{4,0},{8,12},{12,8},{1,5},{5,1},{9,13},{13,9},{2,6},{6,2},{1... | collective-permute-start | bytes 245768 | tf_op jit(solution)/shard_map/ppermute | solution.py:39
  2.3 7.5 %collective-permute-start.4 = (bf16[320,128]{1,0:T(8,128)(2,1)}, bf16[320,128]{1,0:T(8,128)(2,1)}, u32[]{:S(2)}, u32[]{:S(2)}) collective-permute-start(bf16[320,128]{1,0:T(8,128)(2,1)} %refs_0_.1), channel_id=1, source_target_pairs={{0,8},{4,12},{8,0},{12,4},{1,9},{5,13},{9,1},{13,5},{2,10},{6,14},... | collective-permute-start | bytes 245768 | tf_op jit(solution)/shard_map/ppermute | solution.py:34
  5.1 9.9 %collective-permute-start.2 = (bf16[320,128]{1,0:T(8,128)(2,1)}, bf16[320,128]{1,0:T(8,128)(2,1)S(1)}, u32[]{:S(2)}, u32[]{:S(2)}) collective-permute-start(bf16[320,128]{1,0:T(8,128)(2,1)} %refs_0_), channel_id=1, source_target_pairs={{0,3},{1,0},{2,1},{3,2},{4,7},{5,4},{6,5},{7,6},{8,11},{9,8},{10,9... | collective-permute-start | bytes 245768 | tf_op jit(solution)/shard_map/ppermute | solution.py:34
  8.7 7.8 %collective-permute-start.1 = (bf16[320,128]{1,0:T(8,128)(2,1)}, bf16[320,128]{1,0:T(8,128)(2,1)S(1)}, u32[]{:S(2)}, u32[]{:S(2)}) collective-permute-start(bf16[320,128]{1,0:T(8,128)(2,1)} %refs_0_), channel_id=1, source_target_pairs={{0,2},{1,3},{2,0},{3,1},{4,6},{5,7},{6,4},{7,5},{8,10},{9,11},{10,... | collective-permute-start | bytes 245768 | tf_op jit(solution)/shard_map/ppermute | solution.py:34
  8.7 7.8 %collective-permute-start = (bf16[320,128]{1,0:T(8,128)(2,1)}, bf16[320,128]{1,0:T(8,128)(2,1)S(1)}, u32[]{:S(2)}, u32[]{:S(2)}) collective-permute-start(bf16[320,128]{1,0:T(8,128)(2,1)} %refs_0_), channel_id=1, source_target_pairs={{0,1},{1,2},{2,3},{3,0},{4,5},{5,6},{6,7},{7,4},{8,9},{9,10},{10,1... | collective-permute-start | bytes 245768 | tf_op jit(solution)/shard_map/ppermute | solution.py:34
  9.7 13.0 %slice-start = ((s8[7372800]{0:T(1024)(128)(4,1)}), s8[3178496]{0:T(1024)(128)(4,1)S(1)}, s32[]{:S(2)}) async-start(s8[7372800]{0:T(1024)(128)(4,1)} %bitcast.29), calls=%async_computation | async-start | bytes 6356992
  9.7 13.0 %slice-start.1 = ((s8[7372800]{0:T(1024)(128)(4,1)}), s8[4194304]{0:T(1024)(128)(4,1)S(1)}, s32[]{:S(2)}) async-start(s8[7372800]{0:T(1024)(128)(4,1)} %bitcast.29), calls=%async_computation.1 | async-start | bytes 8388608
  9.7 7.9 %collective-permute-start.8 = (bf16[320,128]{1,0:T(8,128)(2,1)}, bf16[320,128]{1,0:T(8,128)(2,1)S(1)}, u32[]{:S(2)}, u32[]{:S(2)}) collective-permute-start(bf16[320,128]{1,0:T(8,128)(2,1)} %refs_0_.1), channel_id=1, source_target_pairs={{0,4},{4,0},{8,12},{12,8},{1,5},{5,1},{9,13},{13,9},{2,6},{6,2},{1... | collective-permute-start | bytes 245768 | tf_op jit(solution)/shard_map/ppermute | solution.py:39
  9.8 1.8 %copy-start = (bf16[3,320,1280]{2,1,0:T(8,128)(2,1)S(1)}, bf16[3,320,1280]{2,1,0:T(8,128)(2,1)}, u32[]{:S(2)}) copy-start(bf16[3,320,1280]{2,1,0:T(8,128)(2,1)} %refs_6_.1) | copy-start | bytes 7372804
  11.6 1.6 %copy-start.3 = (bf16[320,128]{1,0:T(8,128)(2,1)S(1)}, bf16[320,128]{1,0:T(8,128)(2,1)}, u32[]{:S(2)}) copy-start(bf16[320,128]{1,0:T(8,128)(2,1)} %refs_0_.1) | copy-start | bytes 245764
  13.2 4.3 %copy-start.2 = (bf16[320,128]{1,0:T(8,128)(2,1)S(1)}, bf16[320,128]{1,0:T(8,128)(2,1)}, u32[]{:S(2)}) copy-start(bf16[320,128]{1,0:T(8,128)(2,1)} %refs_0_) | copy-start | bytes 245764
  16.5 4.2 %collective-permute-start.5 = (bf16[320,128]{1,0:T(8,128)(2,1)S(1)}, bf16[320,128]{1,0:T(8,128)(2,1)S(1)}, u32[]{:S(2)}, u32[]{:S(2)}) collective-permute-start(bf16[320,128]{1,0:T(8,128)(2,1)S(1)} %collective-permute-done.refs_1_), channel_id=1, source_target_pairs={{0,4},{4,0},{8,12},{12,8},{1,5},{5,1},{9,13},{13,9},{2,6},{6,2},{1... | collective-permute-start | bytes 245768 | tf_op jit(solution)/shard_map/ppermute | solution.py:39
  16.5 6.2 %collective-permute-start.6 = (bf16[320,128]{1,0:T(8,128)(2,1)S(1)}, bf16[320,128]{1,0:T(8,128)(2,1)S(1)}, u32[]{:S(2)}, u32[]{:S(2)}) collective-permute-start(bf16[320,128]{1,0:T(8,128)(2,1)S(1)} %collective-permute-done.1.refs_2_), channel_id=1, source_target_pairs={{0,4},{4,0},{8,12},{12,8},{1,5},{5,1},{9,13},{13,9},{2,6},{6,2},{1... | collective-permute-start | bytes 245768 | tf_op jit(solution)/shard_map/ppermute | solution.py:39
  17.0 5.7 %collective-permute-start.7 = (bf16[320,128]{1,0:T(8,128)(2,1)S(1)}, bf16[320,128]{1,0:T(8,128)(2,1)S(1)}, u32[]{:S(2)}, u32[]{:S(2)}) collective-permute-start(bf16[320,128]{1,0:T(8,128)(2,1)S(1)} %collective-permute-done.2.refs_3_), channel_id=1, source_target_pairs={{0,4},{4,0},{8,12},{12,8},{1,5},{5,1},{9,13},{13,9},{2,6},{6,2},{1... | collective-permute-start | bytes 245768 | tf_op jit(solution)/shard_map/ppermute | solution.py:39
  17.0 1.7 %collective-permute-start.9 = (bf16[320,128]{1,0:T(8,128)(2,1)}, bf16[320,128]{1,0:T(8,128)(2,1)S(1)}, u32[]{:S(2)}, u32[]{:S(2)}) collective-permute-start(bf16[320,128]{1,0:T(8,128)(2,1)} %collective-permute-done.4.before_ref.after_ref.refs_1_), channel_id=1, source_target_pairs={{0,4},{4,0},{8,12},{12,8},{1,5},{5,1},{9,13},{13,9},{2,6},{6,2},{1... | collective-permute-start | bytes 245768 | tf_op jit(solution)/shard_map/ppermute | solution.py:39
  17.6 9.5 %collective-permute-start.13 = (bf16[320,128]{1,0:T(8,128)(2,1)S(1)}, bf16[320,128]{1,0:T(8,128)(2,1)S(1)}, u32[]{:S(2)}, u32[]{:S(2)}) collective-permute-start(bf16[320,128]{1,0:T(8,128)(2,1)S(1)} %get-tuple-element.34), channel_id=1, source_target_pairs={{0,1},{1,2},{2,3},{3,0},{4,5},{5,6},{6,7},{7,4},{8,9},{9,10},{10,1... | collective-permute-start | bytes 245768 | tf_op jit(solution)/shard_map/ppermute | solution.py:34
  18.8 9.6 %collective-permute-start.14 = (bf16[320,128]{1,0:T(8,128)(2,1)S(1)}, bf16[320,128]{1,0:T(8,128)(2,1)S(1)}, u32[]{:S(2)}, u32[]{:S(2)}) collective-permute-start(bf16[320,128]{1,0:T(8,128)(2,1)S(1)} %get-tuple-element.35), channel_id=1, source_target_pairs={{0,2},{1,3},{2,0},{3,1},{4,6},{5,7},{6,4},{7,5},{8,10},{9,11},{10,... | collective-permute-start | bytes 245768 | tf_op jit(solution)/shard_map/ppermute | solution.py:34
  20.8 7.6 %collective-permute-start.15 = (bf16[320,128]{1,0:T(8,128)(2,1)S(1)}, bf16[320,128]{1,0:T(8,128)(2,1)S(1)}, u32[]{:S(2)}, u32[]{:S(2)}) collective-permute-start(bf16[320,128]{1,0:T(8,128)(2,1)S(1)} %get-tuple-element.36), channel_id=1, source_target_pairs={{0,3},{1,0},{2,1},{3,2},{4,7},{5,4},{6,5},{7,6},{8,11},{9,8},{10,9... | collective-permute-start | bytes 245768 | tf_op jit(solution)/shard_map/ppermute | solution.py:34
  25.4 8.0 %collective-permute-start.12 = (bf16[320,128]{1,0:T(8,128)(2,1)S(1)}, bf16[320,128]{1,0:T(8,128)(2,1)S(1)}, u32[]{:S(2)}, u32[]{:S(2)}) collective-permute-start(bf16[320,128]{1,0:T(8,128)(2,1)S(1)} %spatial_forward.1.refs_0_), channel_id=1, source_target_pairs={{0,3},{1,0},{2,1},{3,2},{4,7},{5,4},{6,5},{7,6},{8,11},{9,8},{10,9... | collective-permute-start | bytes 245768 | tf_op jit(solution)/shard_map/ppermute | solution.py:34
  26.0 10.1 %collective-permute-start.11 = (bf16[320,128]{1,0:T(8,128)(2,1)S(1)}, bf16[320,128]{1,0:T(8,128)(2,1)S(1)}, u32[]{:S(2)}, u32[]{:S(2)}) collective-permute-start(bf16[320,128]{1,0:T(8,128)(2,1)S(1)} %spatial_forward.1.refs_0_), channel_id=1, source_target_pairs={{0,2},{1,3},{2,0},{3,1},{4,6},{5,7},{6,4},{7,5},{8,10},{9,11},{10,... | collective-permute-start | bytes 245768 | tf_op jit(solution)/shard_map/ppermute | solution.py:34
  27.1 11.8 %collective-permute-start.10 = (bf16[320,128]{1,0:T(8,128)(2,1)S(1)}, bf16[320,128]{1,0:T(8,128)(2,1)S(1)}, u32[]{:S(2)}, u32[]{:S(2)}) collective-permute-start(bf16[320,128]{1,0:T(8,128)(2,1)S(1)} %spatial_forward.1.refs_0_), channel_id=1, source_target_pairs={{0,1},{1,2},{2,3},{3,0},{4,5},{5,6},{6,7},{7,4},{8,9},{9,10},{10,1... | collective-permute-start | bytes 245768 | tf_op jit(solution)/shard_map/ppermute | solution.py:34
  28.4 11.1 %collective-permute-start.18 = (bf16[320,128]{1,0:T(8,128)(2,1)S(1)}, bf16[320,128]{1,0:T(8,128)(2,1)S(1)}, u32[]{:S(2)}, u32[]{:S(2)}) collective-permute-start(bf16[320,128]{1,0:T(8,128)(2,1)S(1)} %add_convert_fusion.1.field_ref.refs_0_), channel_id=1, source_target_pairs={{0,8},{4,12},{8,0},{12,4},{1,9},{5,13},{9,1},{13,5},{2,10},{6,14},... | collective-permute-start | bytes 245768 | tf_op jit(solution)/shard_map/ppermute | solution.py:34
  29.0 1.3 %collective-permute-start.16 = (bf16[320,128]{1,0:T(8,128)(2,1)S(1)}, bf16[320,128]{1,0:T(8,128)(2,1)S(1)}, u32[]{:S(2)}, u32[]{:S(2)}) collective-permute-start(bf16[320,128]{1,0:T(8,128)(2,1)S(1)} %add_convert_fusion.1.field_ref.refs_0_), channel_id=1, source_target_pairs={{0,4},{4,0},{8,12},{12,8},{1,5},{5,1},{9,13},{13,9},{2,6},{6,2},{1... | collective-permute-start | bytes 245768 | tf_op jit(solution)/shard_map/ppermute | solution.py:39
  30.3 9.3 %collective-permute-start.20 = (bf16[2,320,128]{2,1,0:T(8,128)(2,1)S(1)}, bf16[2,320,128]{2,1,0:T(8,128)(2,1)S(1)}, u32[]{:S(2)}, u32[]{:S(2)}) collective-permute-start(bf16[2,320,128]{2,1,0:T(8,128)(2,1)S(1)} %pad_maximum_fusion.3), channel_id=1, source_target_pairs={{0,8},{4,12},{8,0},{12,4},{1,9},{5,13},{9,1},{13,5},{2,10},{6,14},... | collective-permute-start | bytes 491528 | tf_op jit(solution)/shard_map/ppermute | solution.py:34
  33.4 15.3 %copy-start.1 = (bf16[3,320,1280]{2,1,0:T(8,128)(2,1)S(1)}, bf16[3,320,1280]{2,1,0:T(8,128)(2,1)}, u32[]{:S(2)}) copy-start(bf16[3,320,1280]{2,1,0:T(8,128)(2,1)} %refs_6_.1) | copy-start | bytes 7372804
  33.4 8.2 %collective-permute-start.21 = (bf16[320,128]{1,0:T(8,128)(2,1)S(1)}, bf16[320,128]{1,0:T(8,128)(2,1)S(1)}, u32[]{:S(2)}, u32[]{:S(2)}) collective-permute-start(bf16[320,128]{1,0:T(8,128)(2,1)S(1)} %get-tuple-element.47), channel_id=1, source_target_pairs={{0,1},{1,2},{2,3},{3,0},{4,5},{5,6},{6,7},{7,4},{8,9},{9,10},{10,1... | collective-permute-start | bytes 245768 | tf_op jit(solution)/shard_map/ppermute | solution.py:34
  36.1 8.7 %collective-permute-start.22 = (bf16[320,128]{1,0:T(8,128)(2,1)S(1)}, bf16[320,128]{1,0:T(8,128)(2,1)S(1)}, u32[]{:S(2)}, u32[]{:S(2)}) collective-permute-start(bf16[320,128]{1,0:T(8,128)(2,1)S(1)} %get-tuple-element.48), channel_id=1, source_target_pairs={{0,2},{1,3},{2,0},{3,1},{4,6},{5,7},{6,4},{7,5},{8,10},{9,11},{10,... | collective-permute-start | bytes 245768 | tf_op jit(solution)/shard_map/ppermute | solution.py:34
  38.9 9.0 %collective-permute-start.17 = (bf16[4,320,128]{2,1,0:T(8,128)(2,1)S(1)}, bf16[4,320,128]{2,1,0:T(8,128)(2,1)S(1)}, u32[]{:S(2)}, u32[]{:S(2)}) collective-permute-start(bf16[4,320,128]{2,1,0:T(8,128)(2,1)S(1)} %pad_maximum_fusion), channel_id=1, source_target_pairs={{0,8},{4,12},{8,0},{12,4},{1,9},{5,13},{9,1},{13,5},{2,10},{6,14},... | collective-permute-start | bytes 983048 | tf_op jit(solution)/shard_map/ppermute | solution.py:34
  39.5 8.5 %collective-permute-start.23 = (bf16[320,128]{1,0:T(8,128)(2,1)S(1)}, bf16[320,128]{1,0:T(8,128)(2,1)S(1)}, u32[]{:S(2)}, u32[]{:S(2)}) collective-permute-start(bf16[320,128]{1,0:T(8,128)(2,1)S(1)} %get-tuple-element.49), channel_id=1, source_target_pairs={{0,3},{1,0},{2,1},{3,2},{4,7},{5,4},{6,5},{7,6},{8,11},{9,8},{10,9... | collective-permute-start | bytes 245768 | tf_op jit(solution)/shard_map/ppermute | solution.py:34
  39.6 2.1 %collective-permute-start.19 = (bf16[320,128]{1,0:T(8,128)(2,1)S(1)}, bf16[320,128]{1,0:T(8,128)(2,1)S(1)}, u32[]{:S(2)}, u32[]{:S(2)}) collective-permute-start(bf16[320,128]{1,0:T(8,128)(2,1)S(1)} %collective-permute-done.18.refs_1_), channel_id=1, source_target_pairs={{0,4},{4,0},{8,12},{12,8},{1,5},{5,1},{9,13},{13,9},{2,6},{6,2},{1... | collective-permute-start | bytes 245768 | tf_op jit(solution)/shard_map/ppermute | solution.py:39
  41.7 8.8 %collective-permute-start.24 = (bf16[320,128]{1,0:T(8,128)(2,1)S(1)}, bf16[320,128]{1,0:T(8,128)(2,1)S(1)}, u32[]{:S(2)}, u32[]{:S(2)}) collective-permute-start(bf16[320,128]{1,0:T(8,128)(2,1)S(1)} %get-tuple-element.62), channel_id=1, source_target_pairs={{0,4},{4,0},{8,12},{12,8},{1,5},{5,1},{9,13},{13,9},{2,6},{6,2},{1... | collective-permute-start | bytes 245768 | tf_op jit(solution)/shard_map/ppermute | solution.py:39
  41.7 8.8 %copy-start.4 = (bf16[320,128]{1,0:T(8,128)(2,1)S(1)}, bf16[320,128]{1,0:T(8,128)(2,1)}, u32[]{:S(2)}) copy-start(bf16[320,128]{1,0:T(8,128)(2,1)} %refs_0_.1) | copy-start | bytes 245764
  47.9 2.6 %collective-permute-start.25 = (bf16[320,128]{1,0:T(8,128)(2,1)S(1)}, bf16[320,128]{1,0:T(8,128)(2,1)S(1)}, u32[]{:S(2)}, u32[]{:S(2)}) collective-permute-start(bf16[320,128]{1,0:T(8,128)(2,1)S(1)} %get-tuple-element.60), channel_id=1, source_target_pairs={{0,4},{4,0},{8,12},{12,8},{1,5},{5,1},{9,13},{13,9},{2,6},{6,2},{1... | collective-permute-start | bytes 245768 | tf_op jit(solution)/shard_map/ppermute | solution.py:39

commit v5 on v4

--- a/solution.py
+++ b/solution.py
@@ -363,7 +363,6 @@
 
     siblings = [swap_band(latents)]
     mine = gather_ch(latents)
-    cotangent = after_all(cotangent, siblings[0])
     cot_ring = ring_blocks(cotangent)
     chunks = temporal_backward(cotangent, cot_ring[0], cot_ring[-1], temporal_weight)
     partials = scatter_ch(chunks)
@@ -373,21 +372,21 @@
     cots = [cotangent] + cot_ring
     cots_sibling = [swap_band(x) for x in cots]
     siblings = after_all(siblings, cots_sibling)
-    hidden = spatial_forward(mine, siblings, spatial_weight)
-    hidden_mine = gather_ch(hidden)
-
-    hidden_grad = total_of(after_all(cotangent, hidden), chunks[0], partials)
-    grad_ring = ring_blocks(hidden_grad)
-    grad_sibling = swap_band(hidden_grad)
-    chunks = spatial_backward(hidden_grad, grad_sibling, spatial_weight)
-    partials = scatter_ch(chunks)
-
     lat_own, lat_sib = [block(mine, own_block)], [block(siblings, own_block)]
     for j in range(1, n_x):
         target = RBANDS * ((m + j) % n_x) + band
         both = send(jnp.stack([block(mine, target), block(siblings, target)]), "st", RBANDS * j)
         lat_own.append(both[0])
         lat_sib.append(both[1])
+    hidden = spatial_forward(mine, siblings, spatial_weight)
+    hidden_mine = gather_ch(hidden)
+
+    hidden_grad = total_of(after_all(cotangent, hidden), chunks[0], partials)
+    grad_ring = ring_blocks(hidden_grad)
+    grad_sibling = swap_band(hidden_grad)
+    chunks = spatial_backward(hidden_grad, grad_sibling, spatial_weight)
+    partials = scatter_ch(chunks)
+
     grads = [hidden_grad] + grad_ring
     grads_sibling = [grad_sibling] + [swap_band(x) for x in grad_ring]
     lat_own = after_all(lat_own, partials[0])

time: 53.5 us -> 49.6 us (0.927)
  waiting for transfers between devices: 9.99 us -> 6.27 us
    ppermute x16, waiting for transfers between devices: 7.66 us -> 5.07 us  [send(): return lax.ppermute(data, axis, [(i, (i + by) % n) for i in range(n)])]
    ppermute x10, waiting for transfers between devices: 2.33 us -> 1.2 us  [swap_band(): return lax.ppermute(data, 'st', [(i, i ^ 1) for i in range(n)])]
  transfers between devices with their start and end apart: 26 -> 26, of which waited for: 6 -> 5; matrix products, arithmetic and copies ran while one was open for 2% -> 2% of each run, Pallas kernels for 21% -> 22%
where the time goes in v5:
time: 49.6 us; the launch traced here: 49.4 us
  starting transfers between devices  24.3 us (49%)
  Pallas kernels  13.8 us (28%)
  waiting for transfers between devices  6.27 us (13%)
  local copies, waits for them, and re-layouts  3.35 us (7%)
  other arithmetic  0.89 us (2%)
  between operations  0.85 us (2%)
    ppermute x16, starting transfers between devices, send(): return lax.ppermute(data, axis, [(i, (i + by) % n) for i in range(n)])  22.6 us
    ppermute x16, waiting for transfers between devices, send(): return lax.ppermute(data, axis, [(i, (i + by) % n) for i in range(n)])  5.07 us
    unnamed x14, local copies, waits for them, and re-layouts  3.28 us
    pallas_call x1, Pallas kernels, spatial_grads(): pl.pallas_call(body, out_specs=pl.BlockSpec(memory_space=pltpu.HBM), out_...  3.08 us
    pallas_call x1, Pallas kernels, temporal_grads(): pl.pallas_call(body, out_specs=pl.BlockSpec(memory_space=pltpu.HBM), out_...  2.79 us
    pallas_call x1, Pallas kernels, spatial_forward(): pl.pallas_call(body, out_shape=jax.ShapeDtypeStruct((cb, TILE), BF), scra...  2.69 us
    pallas_call x1, Pallas kernels, temporal_backward(): pl.pallas_call(body, out_shape=chunk_shapes(n_ch, cb), scratch_shapes=[pl...  1.81 us
    pallas_call x1, Pallas kernels, temporal_forward(): pl.pallas_call(body, out_shape=jax.ShapeDtypeStruct((cb, TILE), BF), scra...  1.78 us
  transfers between devices with their start and end apart: 26, of which 5 were waited for; matrix products, arithmetic and copies ran while one was open for 2% of the time, Pallas kernels for 22%

profile of v5, /device:TPU:0, one launch (start us, length us, event | category | flops | bytes accessed | tf_op | source)
XLA Modules:
  0.0 49.4 jit_solution(4500700854408128965)
XLA Ops:
  0.6 3.0 %collective-permute-start.3 = (bf16[320,128]{1,0:T(8,128)(2,1)}, bf16[320,128]{1,0:T(8,128)(2,1)}, u32[]{:S(2)}, u32[]{:S(2)}) collective-permute-start(bf16[320,128]{1,0:T(8,128)(2,1)} %refs_0_.2), channel_id=1, source_target_pairs={{0,8},{4,12},{8,0},{12,4},{1,9},{5,13},{9,1},{13,5},{2,10},{6,14},... | collective-permute-start | bytes 245768 | tf_op jit(solution)/shard_map/ppermute | solution.py:34
  3.6 3.6 %collective-permute-start.2 = (bf16[320,128]{1,0:T(8,128)(2,1)}, bf16[320,128]{1,0:T(8,128)(2,1)S(1)}, u32[]{:S(2)}, u32[]{:S(2)}) collective-permute-start(bf16[320,128]{1,0:T(8,128)(2,1)} %refs_0_.1), channel_id=1, source_target_pairs={{0,3},{1,0},{2,1},{3,2},{4,7},{5,4},{6,5},{7,6},{8,11},{9,8},{10,9... | collective-permute-start | bytes 245768 | tf_op jit(solution)/shard_map/ppermute | solution.py:34
  7.2 0.0 collective-permute-start.1
  7.2 1.0 %collective-permute-start = (bf16[320,128]{1,0:T(8,128)(2,1)}, bf16[320,128]{1,0:T(8,128)(2,1)S(1)}, u32[]{:S(2)}, u32[]{:S(2)}) collective-permute-start(bf16[320,128]{1,0:T(8,128)(2,1)} %refs_0_.1), channel_id=1, source_target_pairs={{0,1},{1,2},{2,3},{3,0},{4,5},{5,6},{6,7},{7,4},{8,9},{9,10},{10,1... | collective-permute-start | bytes 245768 | tf_op jit(solution)/shard_map/ppermute | solution.py:34
  8.3 0.0 collective-permute-start.4
  8.3 0.0 collective-permute-done.3.before_ref.after_ref.refs_1_
  8.3 0.5 %collective-permute-start.8 = (bf16[320,128]{1,0:T(8,128)(2,1)}, bf16[320,128]{1,0:T(8,128)(2,1)S(1)}, u32[]{:S(2)}, u32[]{:S(2)}) collective-permute-start(bf16[320,128]{1,0:T(8,128)(2,1)} %refs_0_.2), channel_id=1, source_target_pairs={{0,4},{4,0},{8,12},{12,8},{1,5},{5,1},{9,13},{13,9},{2,6},{6,2},{1... | collective-permute-start | bytes 245768 | tf_op jit(solution)/shard_map/ppermute | solution.py:39
  8.8 1.9 %copy-done = bf16[3,320,1280]{2,1,0:T(8,128)(2,1)S(1)} copy-done((bf16[3,320,1280]{2,1,0:T(8,128)(2,1)S(1)}, bf16[3,320,1280]{2,1,0:T(8,128)(2,1)}, u32[]{:S(2)}) %copy-start) | copy-done | bytes 2457624
  10.7 1.3 %copy-done.3 = bf16[320,128]{1,0:T(8,128)(2,1)S(1)} copy-done((bf16[320,128]{1,0:T(8,128)(2,1)S(1)}, bf16[320,128]{1,0:T(8,128)(2,1)}, u32[]{:S(2)}) %copy-start.3) | copy-done | bytes 81944
  12.0 1.8 %temporal_backward.1 = (f32[320,128]{1,0:T(8,128)S(1)}, bf16[320,128]{1,0:T(8,128)(2,1)S(1)}, bf16[320,128]{1,0:T(8,128)(2,1)S(1)}, bf16[320,128]{1,0:T(8,128)(2,1)S(1)}) custom-call(bf16[320,128]{1,0:T(8,128)(2,1)S(1)} %copy-done.3, bf16[320,128]{1,0:T(8,128)(2,1)} %collective-permute-done.3.before_ref.after_ref.refs_1_, ...), custom_call_target="tpu_custom_call" | custom-call | flops 4000000000 | bytes 3000000 | tf_op jit(solution)/shard_map/temporal_backward/pallas_call | solution.py:196
  13.9 0.0 collective-permute-done.2.refs_3_
  13.9 0.7 %collective-permute-done.1.refs_2_ = bf16[320,128]{1,0:T(8,128)(2,1)S(1)} collective-permute-done((bf16[320,128]{1,0:T(8,128)(2,1)}, bf16[320,128]{1,0:T(8,128)(2,1)S(1)}, u32[]{:S(2)}, u32[]{:S(2)}) %collective-permute-start.1) | collective-permute-done | bytes 81952 | tf_op jit(solution)/shard_map/ppermute | solution.py:34
  14.6 0.0 collective-permute-done.refs_1_
  14.6 0.0 collective-permute-start.5
  14.6 0.5 %collective-permute-start.6 = (bf16[320,128]{1,0:T(8,128)(2,1)S(1)}, bf16[320,128]{1,0:T(8,128)(2,1)S(1)}, u32[]{:S(2)}, u32[]{:S(2)}) collective-permute-start(bf16[320,128]{1,0:T(8,128)(2,1)S(1)} %collective-permute-done.1.refs_2_), channel_id=1, source_target_pairs={{0,4},{4,0},{8,12},{12,8},{1,5},{5,1},{9,13},{13,9},{2,6},{6,2},{1... | collective-permute-start | bytes 245768 | tf_op jit(solution)/shard_map/ppermute | solution.py:39
  15.1 0.0 collective-permute-start.9
  15.1 0.0 copy-done.2
  15.2 0.0 collective-permute-done.4.refs_4_
  15.2 0.6 %collective-permute-start.7 = (bf16[320,128]{1,0:T(8,128)(2,1)S(1)}, bf16[320,128]{1,0:T(8,128)(2,1)S(1)}, u32[]{:S(2)}, u32[]{:S(2)}) collective-permute-start(bf16[320,128]{1,0:T(8,128)(2,1)S(1)} %collective-permute-done.2.refs_3_), channel_id=1, source_target_pairs={{0,4},{4,0},{8,12},{12,8},{1,5},{5,1},{9,13},{13,9},{2,6},{6,2},{1... | collective-permute-start | bytes 245768 | tf_op jit(solution)/shard_map/ppermute | solution.py:39
  15.8 0.0 collective-permute-done.8.refs_2_
  15.8 1.8 %collective-permute-start.13 = (bf16[320,128]{1,0:T(8,128)(2,1)S(1)}, bf16[320,128]{1,0:T(8,128)(2,1)S(1)}, u32[]{:S(2)}, u32[]{:S(2)}) collective-permute-start(bf16[320,128]{1,0:T(8,128)(2,1)S(1)} %get-tuple-element.32), channel_id=1, source_target_pairs={{0,1},{1,2},{2,3},{3,0},{4,5},{5,6},{6,7},{7,4},{8,9},{9,10},{10,1... | collective-permute-start | bytes 245768 | tf_op jit(solution)/shard_map/ppermute | solution.py:34
  17.6 0.0 collective-permute-done.9.refs_3_
  17.6 1.2 %collective-permute-start.14 = (bf16[320,128]{1,0:T(8,128)(2,1)S(1)}, bf16[320,128]{1,0:T(8,128)(2,1)S(1)}, u32[]{:S(2)}, u32[]{:S(2)}) collective-permute-start(bf16[320,128]{1,0:T(8,128)(2,1)S(1)} %get-tuple-element.33), channel_id=1, source_target_pairs={{0,2},{1,3},{2,0},{3,1},{4,6},{5,7},{6,4},{7,5},{8,10},{9,11},{10,... | collective-permute-start | bytes 245768 | tf_op jit(solution)/shard_map/ppermute | solution.py:34
  18.8 0.0 collective-permute-done.5.refs_5_
  18.8 2.1 %collective-permute-start.15 = (bf16[320,128]{1,0:T(8,128)(2,1)S(1)}, bf16[320,128]{1,0:T(8,128)(2,1)S(1)}, u32[]{:S(2)}, u32[]{:S(2)}) collective-permute-start(bf16[320,128]{1,0:T(8,128)(2,1)S(1)} %get-tuple-element.34), channel_id=1, source_target_pairs={{0,3},{1,0},{2,1},{3,2},{4,7},{5,4},{6,5},{7,6},{8,11},{9,8},{10,9... | collective-permute-start | bytes 245768 | tf_op jit(solution)/shard_map/ppermute | solution.py:34
  20.9 0.0 collective-permute-done.6.refs_6_
  20.9 0.0 collective-permute-done.7.refs_7_
  20.9 2.7 %spatial_forward.1.refs_0_ = bf16[320,128]{1,0:T(8,128)(2,1)S(1)} custom-call(bf16[320,128]{1,0:T(8,128)(2,1)S(1)} %copy-done.2, bf16[320,128]{1,0:T(8,128)(2,1)S(1)} %collective-permute-done.refs_1_, bf16[320,128]{1,0:T(8,128)(2,1)S(1)} %collective-permute-done.1.refs_2_, bf16[320,128]{1,0:T(8,128)(2,1)S(1)} %collective-permute-done.2.refs_3_, ...), custom_call_target="tpu_custom_call" | custom-call | tf_op jit(solution)/shard_map/spatial_forward/pallas_call | solution.py:133
  23.6 1.2 %collective-permute-start.12 = (bf16[320,128]{1,0:T(8,128)(2,1)S(1)}, bf16[320,128]{1,0:T(8,128)(2,1)S(1)}, u32[]{:S(2)}, u32[]{:S(2)}) collective-permute-start(bf16[320,128]{1,0:T(8,128)(2,1)S(1)} %spatial_forward.1.refs_0_), channel_id=1, source_target_pairs={{0,3},{1,0},{2,1},{3,2},{4,7},{5,4},{6,5},{7,6},{8,11},{9,8},{10,9... | collective-permute-start | bytes 245768 | tf_op jit(solution)/shard_map/ppermute | solution.py:34
  24.8 0.3 collective-permute-start.11
  25.1 0.0 collective-permute-done.13
  25.1 1.4 %collective-permute-start.10 = (bf16[320,128]{1,0:T(8,128)(2,1)S(1)}, bf16[320,128]{1,0:T(8,128)(2,1)S(1)}, u32[]{:S(2)}, u32[]{:S(2)}) collective-permute-start(bf16[320,128]{1,0:T(8,128)(2,1)S(1)} %spatial_forward.1.refs_0_), channel_id=1, source_target_pairs={{0,1},{1,2},{2,3},{3,0},{4,5},{5,6},{6,7},{7,4},{8,9},{9,10},{10,1... | collective-permute-start | bytes 245768 | tf_op jit(solution)/shard_map/ppermute | solution.py:34
  26.5 0.0 collective-permute-done.14
  26.5 0.0 collective-permute-done.15
  26.5 0.1 add_convert_fusion.1.field_ref.refs_0_
  26.5 0.6 %collective-permute-start.18 = (bf16[320,128]{1,0:T(8,128)(2,1)S(1)}, bf16[320,128]{1,0:T(8,128)(2,1)S(1)}, u32[]{:S(2)}, u32[]{:S(2)}) collective-permute-start(bf16[320,128]{1,0:T(8,128)(2,1)S(1)} %add_convert_fusion.1.field_ref.refs_0_), channel_id=1, source_target_pairs={{0,8},{4,12},{8,0},{12,4},{1,9},{5,13},{9,1},{13,5},{2,10},{6,14},... | collective-permute-start | bytes 245768 | tf_op jit(solution)/shard_map/ppermute | solution.py:34
  27.1 0.0 collective-permute-start.16
  27.2 1.2 %collective-permute-done.16.sibling_ref.refs_2_ = bf16[320,128]{1,0:T(8,128)(2,1)S(1)} collective-permute-done((bf16[320,128]{1,0:T(8,128)(2,1)S(1)}, bf16[320,128]{1,0:T(8,128)(2,1)S(1)}, u32[]{:S(2)}, u32[]{:S(2)}) %collective-permute-start.16) | collective-permute-done | bytes 81952 | tf_op jit(solution)/shard_map/ppermute | solution.py:39
  28.4 1.5 %collective-permute-start.20 = (bf16[2,320,128]{2,1,0:T(8,128)(2,1)S(1)}, bf16[2,320,128]{2,1,0:T(8,128)(2,1)S(1)}, u32[]{:S(2)}, u32[]{:S(2)}) collective-permute-start(bf16[2,320,128]{2,1,0:T(8,128)(2,1)S(1)} %pad_maximum_fusion.3), channel_id=1, source_target_pairs={{0,8},{4,12},{8,0},{12,4},{1,9},{5,13},{9,1},{13,5},{2,10},{6,14},... | collective-permute-start | bytes 491528 | tf_op jit(solution)/shard_map/ppermute | solution.py:34
  29.9 1.6 %spatial_backward.1 = (f32[320,128]{1,0:T(8,128)S(1)}, bf16[320,128]{1,0:T(8,128)(2,1)S(1)}, bf16[320,128]{1,0:T(8,128)(2,1)S(1)}, bf16[320,128]{1,0:T(8,128)(2,1)S(1)}) custom-call(bf16[320,128]{1,0:T(8,128)(2,1)S(1)} %add_convert_fusion.1.field_ref.refs_0_, bf16[320,128]{1,0:T(8,128)(2,1)S(1)} %collective-permute-done.16.sibling_ref.refs_2_, ...), custom_call_target="tpu_custom_call" | custom-call | tf_op jit(solution)/shard_map/spatial_backward/pallas_call | solution.py:240
  31.5 0.0 copy-start.1
  31.5 0.0 collective-permute-done.12.refs_3_
  31.5 1.9 %collective-permute-start.21 = (bf16[320,128]{1,0:T(8,128)(2,1)S(1)}, bf16[320,128]{1,0:T(8,128)(2,1)S(1)}, u32[]{:S(2)}, u32[]{:S(2)}) collective-permute-start(bf16[320,128]{1,0:T(8,128)(2,1)S(1)} %get-tuple-element.45), channel_id=1, source_target_pairs={{0,1},{1,2},{2,3},{3,0},{4,5},{5,6},{6,7},{7,4},{8,9},{9,10},{10,1... | collective-permute-start | bytes 245768 | tf_op jit(solution)/shard_map/ppermute | solution.py:34
  33.4 0.8 %collective-permute-done.11.refs_2_ = bf16[320,128]{1,0:T(8,128)(2,1)S(1)} collective-permute-done((bf16[320,128]{1,0:T(8,128)(2,1)S(1)}, bf16[320,128]{1,0:T(8,128)(2,1)S(1)}, u32[]{:S(2)}, u32[]{:S(2)}) %collective-permute-start.11) | collective-permute-done | bytes 81952 | tf_op jit(solution)/shard_map/ppermute | solution.py:34
  34.3 0.4 collective-permute-start.22
  34.6 0.0 collective-permute-done.10.refs_1_
  34.7 0.6 %collective-permute-start.17 = (bf16[4,320,128]{2,1,0:T(8,128)(2,1)S(1)}, bf16[4,320,128]{2,1,0:T(8,128)(2,1)S(1)}, u32[]{:S(2)}, u32[]{:S(2)}) collective-permute-start(bf16[4,320,128]{2,1,0:T(8,128)(2,1)S(1)} %pad_maximum_fusion), channel_id=1, source_target_pairs={{0,8},{4,12},{8,0},{12,4},{1,9},{5,13},{9,1},{13,5},{2,10},{6,14},... | collective-permute-start | bytes 983048 | tf_op jit(solution)/shard_map/ppermute | solution.py:34
  35.3 0.0 collective-permute-done.18.refs_1_
  35.3 2.1 %collective-permute-start.23 = (bf16[320,128]{1,0:T(8,128)(2,1)S(1)}, bf16[320,128]{1,0:T(8,128)(2,1)S(1)}, u32[]{:S(2)}, u32[]{:S(2)}) collective-permute-start(bf16[320,128]{1,0:T(8,128)(2,1)S(1)} %get-tuple-element.47), channel_id=1, source_target_pairs={{0,3},{1,0},{2,1},{3,2},{4,7},{5,4},{6,5},{7,6},{8,11},{9,8},{10,9... | collective-permute-start | bytes 245768 | tf_op jit(solution)/shard_map/ppermute | solution.py:34
  37.4 0.0 collective-permute-done.20
  37.4 0.0 collective-permute-start.19
  37.5 1.3 %collective-permute-done.21 = bf16[320,128]{1,0:T(8,128)(2,1)S(1)} collective-permute-done((bf16[320,128]{1,0:T(8,128)(2,1)S(1)}, bf16[320,128]{1,0:T(8,128)(2,1)S(1)}, u32[]{:S(2)}, u32[]{:S(2)}) %collective-permute-start.21) | collective-permute-done | bytes 81952 | tf_op jit(solution)/shard_map/ppermute | solution.py:34
  38.7 0.0 collective-permute-start.24
  38.7 0.0 collective-permute-done.19.refs_3_
  38.7 3.1 %spatial_grads.1 = f32[9,320,320]{2,1,0:T(8,128)} custom-call(bf16[320,128]{1,0:T(8,128)(2,1)S(1)} %add_convert_fusion.1.field_ref.refs_0_, bf16[320,128]{1,0:T(8,128)(2,1)S(1)} %collective-permute-done.18.refs_1_, bf16[320,128]{1,0:T(8,128)(2,1)S(1)} %collective-permute-done.16.sibling_ref.refs_2_, bf16[320,128]{1,0:T(8,128)(2,1)S(1)} %collective-permute-done.19.refs_3_, ...), custom_call_target="tpu_custom_call" | custom-call | tf_op jit(solution)/shard_map/spatial_grads/pallas_call | solution.py:282
  41.8 0.0 collective-permute-done.22
  41.8 2.2 %collective-permute-done.17.refs_4_.refs_5_ = bf16[4,320,128]{2,1,0:T(8,128)(2,1)S(1)} collective-permute-done((bf16[4,320,128]{2,1,0:T(8,128)(2,1)S(1)}, bf16[4,320,128]{2,1,0:T(8,128)(2,1)S(1)}, u32[]{:S(2)}, u32[]{:S(2)}) %collective-permute-start.17) | collective-permute-done | bytes 327712 | tf_op jit(solution)/shard_map/ppermute | solution.py:34
  44.0 0.1 collective-permute-start.25
  44.1 0.0 collective-permute-done.23
  44.1 0.7 %add_convert_fusion = bf16[320,128]{1,0:T(8,128)(2,1)} fusion(bf16[320,128]{1,0:T(8,128)(2,1)S(1)} %collective-permute-done.23, bf16[320,128]{1,0:T(8,128)(2,1)S(1)} %collective-permute-done.22, bf16[320,128]{1,0:T(8,128)(2,1)S(1)} %collective-permute-done.21, f32[320,128]{1,0:T(8,128)S(1)} %get-tuple-element.44, ...), kind=kLoop, calls=%fused_computation.4 | loop fusion | flops 368640 | bytes 573440 | tf_op jit(solution)/shard_map/convert_element_type | solution.py:348
  44.8 1.8 %temporal_forward.1 = bf16[320,128]{1,0:T(8,128)(2,1)} custom-call(bf16[320,128]{1,0:T(8,128)(2,1)S(1)} %spatial_forward.1.refs_0_, bf16[320,128]{1,0:T(8,128)(2,1)S(1)} %collective-permute-done.10.refs_1_, bf16[320,128]{1,0:T(8,128)(2,1)S(1)} %collective-permute-done.11.refs_2_, bf16[320,128]{1,0:T(8,128)(2,1)S(1)} %collective-permute-done.12.refs_3_, ...), custom_call_target="tpu_custom_call" | custom-call | tf_op jit(solution)/shard_map/temporal_forward/pallas_call | solution.py:161
  46.6 0.0 collective-permute-done.24.refs_6_
  46.6 0.0 collective-permute-done.25.refs_7_
  46.6 2.8 %temporal_grads.1 = f32[3,320,320]{2,1,0:T(8,128)} custom-call(bf16[320,128]{1,0:T(8,128)(2,1)S(1)} %copy-done.4, bf16[320,128]{1,0:T(8,128)(2,1)} %collective-permute-done.3.before_ref.after_ref.refs_1_, bf16[320,128]{1,0:T(8,128)(2,1)S(1)} %collective-permute-done.8.refs_2_, bf16[320,128]{1,0:T(8,128)(2,1)S(1)} %collective-permute-done.9.refs_3_, ...), custom_call_target="tpu_custom_call" | custom-call | tf_op jit(solution)/shard_map/temporal_grads/pallas_call | solution.py:325
  (20 shorter events, 0.2 us)
Async XLA Ops:
  0.6 7.6 %collective-permute-start.3 = (bf16[320,128]{1,0:T(8,128)(2,1)}, bf16[320,128]{1,0:T(8,128)(2,1)}, u32[]{:S(2)}, u32[]{:S(2)}) collective-permute-start(bf16[320,128]{1,0:T(8,128)(2,1)} %refs_0_.2), channel_id=1, source_target_pairs={{0,8},{4,12},{8,0},{12,4},{1,9},{5,13},{9,1},{13,5},{2,10},{6,14},... | collective-permute-start | bytes 245768 | tf_op jit(solution)/shard_map/ppermute | solution.py:34
  3.6 10.2 %collective-permute-start.2 = (bf16[320,128]{1,0:T(8,128)(2,1)}, bf16[320,128]{1,0:T(8,128)(2,1)S(1)}, u32[]{:S(2)}, u32[]{:S(2)}) collective-permute-start(bf16[320,128]{1,0:T(8,128)(2,1)} %refs_0_.1), channel_id=1, source_target_pairs={{0,3},{1,0},{2,1},{3,2},{4,7},{5,4},{6,5},{7,6},{8,11},{9,8},{10,9... | collective-permute-start | bytes 245768 | tf_op jit(solution)/shard_map/ppermute | solution.py:34
  7.2 7.4 %collective-permute-start.1 = (bf16[320,128]{1,0:T(8,128)(2,1)}, bf16[320,128]{1,0:T(8,128)(2,1)S(1)}, u32[]{:S(2)}, u32[]{:S(2)}) collective-permute-start(bf16[320,128]{1,0:T(8,128)(2,1)} %refs_0_.1), channel_id=1, source_target_pairs={{0,2},{1,3},{2,0},{3,1},{4,6},{5,7},{6,4},{7,5},{8,10},{9,11},{10,... | collective-permute-start | bytes 245768 | tf_op jit(solution)/shard_map/ppermute | solution.py:34
  7.2 7.4 %collective-permute-start = (bf16[320,128]{1,0:T(8,128)(2,1)}, bf16[320,128]{1,0:T(8,128)(2,1)S(1)}, u32[]{:S(2)}, u32[]{:S(2)}) collective-permute-start(bf16[320,128]{1,0:T(8,128)(2,1)} %refs_0_.1), channel_id=1, source_target_pairs={{0,1},{1,2},{2,3},{3,0},{4,5},{5,6},{6,7},{7,4},{8,9},{9,10},{10,1... | collective-permute-start | bytes 245768 | tf_op jit(solution)/shard_map/ppermute | solution.py:34
  8.3 6.9 %collective-permute-start.4 = (bf16[320,128]{1,0:T(8,128)(2,1)}, bf16[320,128]{1,0:T(8,128)(2,1)S(1)}, u32[]{:S(2)}, u32[]{:S(2)}) collective-permute-start(bf16[320,128]{1,0:T(8,128)(2,1)} %refs_0_.1), channel_id=1, source_target_pairs={{0,4},{4,0},{8,12},{12,8},{1,5},{5,1},{9,13},{13,9},{2,6},{6,2},{1... | collective-permute-start | bytes 245768 | tf_op jit(solution)/shard_map/ppermute | solution.py:39
  8.3 12.7 %slice-start = ((s8[7372800]{0:T(1024)(128)(4,1)}), s8[3178496]{0:T(1024)(128)(4,1)S(1)}, s32[]{:S(2)}) async-start(s8[7372800]{0:T(1024)(128)(4,1)} %bitcast.29), calls=%async_computation | async-start | bytes 6356992
  8.3 12.7 %slice-start.1 = ((s8[7372800]{0:T(1024)(128)(4,1)}), s8[4194304]{0:T(1024)(128)(4,1)S(1)}, s32[]{:S(2)}) async-start(s8[7372800]{0:T(1024)(128)(4,1)} %bitcast.29), calls=%async_computation.1 | async-start | bytes 8388608
  8.3 7.5 %collective-permute-start.8 = (bf16[320,128]{1,0:T(8,128)(2,1)}, bf16[320,128]{1,0:T(8,128)(2,1)S(1)}, u32[]{:S(2)}, u32[]{:S(2)}) collective-permute-start(bf16[320,128]{1,0:T(8,128)(2,1)} %refs_0_.2), channel_id=1, source_target_pairs={{0,4},{4,0},{8,12},{12,8},{1,5},{5,1},{9,13},{13,9},{2,6},{6,2},{1... | collective-permute-start | bytes 245768 | tf_op jit(solution)/shard_map/ppermute | solution.py:39
  8.8 1.9 %copy-start = (bf16[3,320,1280]{2,1,0:T(8,128)(2,1)S(1)}, bf16[3,320,1280]{2,1,0:T(8,128)(2,1)}, u32[]{:S(2)}) copy-start(bf16[3,320,1280]{2,1,0:T(8,128)(2,1)} %refs_6_.1) | copy-start | bytes 7372804
  10.7 1.3 %copy-start.3 = (bf16[320,128]{1,0:T(8,128)(2,1)S(1)}, bf16[320,128]{1,0:T(8,128)(2,1)}, u32[]{:S(2)}) copy-start(bf16[320,128]{1,0:T(8,128)(2,1)} %refs_0_.2) | copy-start | bytes 245764
  12.0 3.1 %copy-start.2 = (bf16[320,128]{1,0:T(8,128)(2,1)S(1)}, bf16[320,128]{1,0:T(8,128)(2,1)}, u32[]{:S(2)}) copy-start(bf16[320,128]{1,0:T(8,128)(2,1)} %refs_0_.1) | copy-start | bytes 245764
  14.6 4.2 %collective-permute-start.5 = (bf16[320,128]{1,0:T(8,128)(2,1)S(1)}, bf16[320,128]{1,0:T(8,128)(2,1)S(1)}, u32[]{:S(2)}, u32[]{:S(2)}) collective-permute-start(bf16[320,128]{1,0:T(8,128)(2,1)S(1)} %collective-permute-done.refs_1_), channel_id=1, source_target_pairs={{0,4},{4,0},{8,12},{12,8},{1,5},{5,1},{9,13},{13,9},{2,6},{6,2},{1... | collective-permute-start | bytes 245768 | tf_op jit(solution)/shard_map/ppermute | solution.py:39
  14.6 6.3 %collective-permute-start.6 = (bf16[320,128]{1,0:T(8,128)(2,1)S(1)}, bf16[320,128]{1,0:T(8,128)(2,1)S(1)}, u32[]{:S(2)}, u32[]{:S(2)}) collective-permute-start(bf16[320,128]{1,0:T(8,128)(2,1)S(1)} %collective-permute-done.1.refs_2_), channel_id=1, source_target_pairs={{0,4},{4,0},{8,12},{12,8},{1,5},{5,1},{9,13},{13,9},{2,6},{6,2},{1... | collective-permute-start | bytes 245768 | tf_op jit(solution)/shard_map/ppermute | solution.py:39
  15.1 2.5 %collective-permute-start.9 = (bf16[320,128]{1,0:T(8,128)(2,1)}, bf16[320,128]{1,0:T(8,128)(2,1)S(1)}, u32[]{:S(2)}, u32[]{:S(2)}) collective-permute-start(bf16[320,128]{1,0:T(8,128)(2,1)} %collective-permute-done.3.before_ref.after_ref.refs_1_), channel_id=1, source_target_pairs={{0,4},{4,0},{8,12},{12,8},{1,5},{5,1},{9,13},{13,9},{2,6},{6,2},{1... | collective-permute-start | bytes 245768 | tf_op jit(solution)/shard_map/ppermute | solution.py:39
  15.2 5.7 %collective-permute-start.7 = (bf16[320,128]{1,0:T(8,128)(2,1)S(1)}, bf16[320,128]{1,0:T(8,128)(2,1)S(1)}, u32[]{:S(2)}, u32[]{:S(2)}) collective-permute-start(bf16[320,128]{1,0:T(8,128)(2,1)S(1)} %collective-permute-done.2.refs_3_), channel_id=1, source_target_pairs={{0,4},{4,0},{8,12},{12,8},{1,5},{5,1},{9,13},{13,9},{2,6},{6,2},{1... | collective-permute-start | bytes 245768 | tf_op jit(solution)/shard_map/ppermute | solution.py:39
  15.8 9.3 %collective-permute-start.13 = (bf16[320,128]{1,0:T(8,128)(2,1)S(1)}, bf16[320,128]{1,0:T(8,128)(2,1)S(1)}, u32[]{:S(2)}, u32[]{:S(2)}) collective-permute-start(bf16[320,128]{1,0:T(8,128)(2,1)S(1)} %get-tuple-element.32), channel_id=1, source_target_pairs={{0,1},{1,2},{2,3},{3,0},{4,5},{5,6},{6,7},{7,4},{8,9},{9,10},{10,1... | collective-permute-start | bytes 245768 | tf_op jit(solution)/shard_map/ppermute | solution.py:34
  17.6 8.9 %collective-permute-start.14 = (bf16[320,128]{1,0:T(8,128)(2,1)S(1)}, bf16[320,128]{1,0:T(8,128)(2,1)S(1)}, u32[]{:S(2)}, u32[]{:S(2)}) collective-permute-start(bf16[320,128]{1,0:T(8,128)(2,1)S(1)} %get-tuple-element.33), channel_id=1, source_target_pairs={{0,2},{1,3},{2,0},{3,1},{4,6},{5,7},{6,4},{7,5},{8,10},{9,11},{10,... | collective-permute-start | bytes 245768 | tf_op jit(solution)/shard_map/ppermute | solution.py:34
  18.8 7.7 %collective-permute-start.15 = (bf16[320,128]{1,0:T(8,128)(2,1)S(1)}, bf16[320,128]{1,0:T(8,128)(2,1)S(1)}, u32[]{:S(2)}, u32[]{:S(2)}) collective-permute-start(bf16[320,128]{1,0:T(8,128)(2,1)S(1)} %get-tuple-element.34), channel_id=1, source_target_pairs={{0,3},{1,0},{2,1},{3,2},{4,7},{5,4},{6,5},{7,6},{8,11},{9,8},{10,9... | collective-permute-start | bytes 245768 | tf_op jit(solution)/shard_map/ppermute | solution.py:34
  23.6 7.9 %collective-permute-start.12 = (bf16[320,128]{1,0:T(8,128)(2,1)S(1)}, bf16[320,128]{1,0:T(8,128)(2,1)S(1)}, u32[]{:S(2)}, u32[]{:S(2)}) collective-permute-start(bf16[320,128]{1,0:T(8,128)(2,1)S(1)} %spatial_forward.1.refs_0_), channel_id=1, source_target_pairs={{0,3},{1,0},{2,1},{3,2},{4,7},{5,4},{6,5},{7,6},{8,11},{9,8},{10,9... | collective-permute-start | bytes 245768 | tf_op jit(solution)/shard_map/ppermute | solution.py:34
  24.8 9.5 %collective-permute-start.11 = (bf16[320,128]{1,0:T(8,128)(2,1)S(1)}, bf16[320,128]{1,0:T(8,128)(2,1)S(1)}, u32[]{:S(2)}, u32[]{:S(2)}) collective-permute-start(bf16[320,128]{1,0:T(8,128)(2,1)S(1)} %spatial_forward.1.refs_0_), channel_id=1, source_target_pairs={{0,2},{1,3},{2,0},{3,1},{4,6},{5,7},{6,4},{7,5},{8,10},{9,11},{10,... | collective-permute-start | bytes 245768 | tf_op jit(solution)/shard_map/ppermute | solution.py:34
  25.1 9.5 %collective-permute-start.10 = (bf16[320,128]{1,0:T(8,128)(2,1)S(1)}, bf16[320,128]{1,0:T(8,128)(2,1)S(1)}, u32[]{:S(2)}, u32[]{:S(2)}) collective-permute-start(bf16[320,128]{1,0:T(8,128)(2,1)S(1)} %spatial_forward.1.refs_0_), channel_id=1, source_target_pairs={{0,1},{1,2},{2,3},{3,0},{4,5},{5,6},{6,7},{7,4},{8,9},{9,10},{10,1... | collective-permute-start | bytes 245768 | tf_op jit(solution)/shard_map/ppermute | solution.py:34
  26.5 8.8 %collective-permute-start.18 = (bf16[320,128]{1,0:T(8,128)(2,1)S(1)}, bf16[320,128]{1,0:T(8,128)(2,1)S(1)}, u32[]{:S(2)}, u32[]{:S(2)}) collective-permute-start(bf16[320,128]{1,0:T(8,128)(2,1)S(1)} %add_convert_fusion.1.field_ref.refs_0_), channel_id=1, source_target_pairs={{0,8},{4,12},{8,0},{12,4},{1,9},{5,13},{9,1},{13,5},{2,10},{6,14},... | collective-permute-start | bytes 245768 | tf_op jit(solution)/shard_map/ppermute | solution.py:34
  27.1 1.3 %collective-permute-start.16 = (bf16[320,128]{1,0:T(8,128)(2,1)S(1)}, bf16[320,128]{1,0:T(8,128)(2,1)S(1)}, u32[]{:S(2)}, u32[]{:S(2)}) collective-permute-start(bf16[320,128]{1,0:T(8,128)(2,1)S(1)} %add_convert_fusion.1.field_ref.refs_0_), channel_id=1, source_target_pairs={{0,4},{4,0},{8,12},{12,8},{1,5},{5,1},{9,13},{13,9},{2,6},{6,2},{1... | collective-permute-start | bytes 245768 | tf_op jit(solution)/shard_map/ppermute | solution.py:39
  28.4 9.0 %collective-permute-start.20 = (bf16[2,320,128]{2,1,0:T(8,128)(2,1)S(1)}, bf16[2,320,128]{2,1,0:T(8,128)(2,1)S(1)}, u32[]{:S(2)}, u32[]{:S(2)}) collective-permute-start(bf16[2,320,128]{2,1,0:T(8,128)(2,1)S(1)} %pad_maximum_fusion.3), channel_id=1, source_target_pairs={{0,8},{4,12},{8,0},{12,4},{1,9},{5,13},{9,1},{13,5},{2,10},{6,14},... | collective-permute-start | bytes 491528 | tf_op jit(solution)/shard_map/ppermute | solution.py:34
  31.5 13.3 %copy-start.1 = (bf16[3,320,1280]{2,1,0:T(8,128)(2,1)S(1)}, bf16[3,320,1280]{2,1,0:T(8,128)(2,1)}, u32[]{:S(2)}) copy-start(bf16[3,320,1280]{2,1,0:T(8,128)(2,1)} %refs_6_.1) | copy-start | bytes 7372804
  31.5 7.2 %collective-permute-start.21 = (bf16[320,128]{1,0:T(8,128)(2,1)S(1)}, bf16[320,128]{1,0:T(8,128)(2,1)S(1)}, u32[]{:S(2)}, u32[]{:S(2)}) collective-permute-start(bf16[320,128]{1,0:T(8,128)(2,1)S(1)} %get-tuple-element.45), channel_id=1, source_target_pairs={{0,1},{1,2},{2,3},{3,0},{4,5},{5,6},{6,7},{7,4},{8,9},{9,10},{10,1... | collective-permute-start | bytes 245768 | tf_op jit(solution)/shard_map/ppermute | solution.py:34
  34.3 7.6 %collective-permute-start.22 = (bf16[320,128]{1,0:T(8,128)(2,1)S(1)}, bf16[320,128]{1,0:T(8,128)(2,1)S(1)}, u32[]{:S(2)}, u32[]{:S(2)}) collective-permute-start(bf16[320,128]{1,0:T(8,128)(2,1)S(1)} %get-tuple-element.46), channel_id=1, source_target_pairs={{0,2},{1,3},{2,0},{3,1},{4,6},{5,7},{6,4},{7,5},{8,10},{9,11},{10,... | collective-permute-start | bytes 245768 | tf_op jit(solution)/shard_map/ppermute | solution.py:34
  34.7 9.3 %collective-permute-start.17 = (bf16[4,320,128]{2,1,0:T(8,128)(2,1)S(1)}, bf16[4,320,128]{2,1,0:T(8,128)(2,1)S(1)}, u32[]{:S(2)}, u32[]{:S(2)}) collective-permute-start(bf16[4,320,128]{2,1,0:T(8,128)(2,1)S(1)} %pad_maximum_fusion), channel_id=1, source_target_pairs={{0,8},{4,12},{8,0},{12,4},{1,9},{5,13},{9,1},{13,5},{2,10},{6,14},... | collective-permute-start | bytes 983048 | tf_op jit(solution)/shard_map/ppermute | solution.py:34
  35.3 8.8 %collective-permute-start.23 = (bf16[320,128]{1,0:T(8,128)(2,1)S(1)}, bf16[320,128]{1,0:T(8,128)(2,1)S(1)}, u32[]{:S(2)}, u32[]{:S(2)}) collective-permute-start(bf16[320,128]{1,0:T(8,128)(2,1)S(1)} %get-tuple-element.47), channel_id=1, source_target_pairs={{0,3},{1,0},{2,1},{3,2},{4,7},{5,4},{6,5},{7,6},{8,11},{9,8},{10,9... | collective-permute-start | bytes 245768 | tf_op jit(solution)/shard_map/ppermute | solution.py:34
  37.4 1.3 %collective-permute-start.19 = (bf16[320,128]{1,0:T(8,128)(2,1)S(1)}, bf16[320,128]{1,0:T(8,128)(2,1)S(1)}, u32[]{:S(2)}, u32[]{:S(2)}) collective-permute-start(bf16[320,128]{1,0:T(8,128)(2,1)S(1)} %collective-permute-done.18.refs_1_), channel_id=1, source_target_pairs={{0,4},{4,0},{8,12},{12,8},{1,5},{5,1},{9,13},{13,9},{2,6},{6,2},{1... | collective-permute-start | bytes 245768 | tf_op jit(solution)/shard_map/ppermute | solution.py:39
  38.7 7.9 %collective-permute-start.24 = (bf16[320,128]{1,0:T(8,128)(2,1)S(1)}, bf16[320,128]{1,0:T(8,128)(2,1)S(1)}, u32[]{:S(2)}, u32[]{:S(2)}) collective-permute-start(bf16[320,128]{1,0:T(8,128)(2,1)S(1)} %get-tuple-element.60), channel_id=1, source_target_pairs={{0,4},{4,0},{8,12},{12,8},{1,5},{5,1},{9,13},{13,9},{2,6},{6,2},{1... | collective-permute-start | bytes 245768 | tf_op jit(solution)/shard_map/ppermute | solution.py:39
  38.7 7.9 %copy-start.4 = (bf16[320,128]{1,0:T(8,128)(2,1)S(1)}, bf16[320,128]{1,0:T(8,128)(2,1)}, u32[]{:S(2)}) copy-start(bf16[320,128]{1,0:T(8,128)(2,1)} %refs_0_.2) | copy-start | bytes 245764
  44.0 2.6 %collective-permute-start.25 = (bf16[320,128]{1,0:T(8,128)(2,1)S(1)}, bf16[320,128]{1,0:T(8,128)(2,1)S(1)}, u32[]{:S(2)}, u32[]{:S(2)}) collective-permute-start(bf16[320,128]{1,0:T(8,128)(2,1)S(1)} %get-tuple-element.58), channel_id=1, source_target_pairs={{0,4},{4,0},{8,12},{12,8},{1,5},{5,1},{9,13},{13,9},{2,6},{6,2},{1... | collective-permute-start | bytes 245768 | tf_op jit(solution)/shard_map/ppermute | solution.py:39

commit v6 on v5

--- a/solution.py
+++ b/solution.py
@@ -34,6 +34,10 @@
     return lax.ppermute(data, axis, [(i, (i + by) % n) for i in range(n)])
 
 
+def swap_ch(data, k):
+    return lax.ppermute(data, "ch", [(i, i ^ k) for i in range(lax.axis_size("ch"))])
+
+
 def swap_band(data):
     n = lax.axis_size("st")
     return lax.ppermute(data, "st", [(i, i ^ 1) for i in range(n)])
@@ -45,7 +49,7 @@
 
 def gather_ch(shard):
     n_ch, _ = sizes()
-    return [shard] + [send(shard, "ch", k) for k in range(1, n_ch)]
+    return [shard] + [swap_ch(shard, k) for k in range(1, n_ch)]
 
 
 def ring_blocks(data):
@@ -112,7 +116,7 @@
         w_ref, out_ref, field, acc = refs[2 * n_ch :]
         c, _, band = place()
         for k in range(n_ch):
-            at = pl.ds(pl.multiple_of(((c + n_ch - k) % n_ch) * cb, 16), cb)
+            at = pl.ds(pl.multiple_of((c ^ k) * cb, 16), cb)
             f0, f1 = frames_of(mine_refs[k][...], sibling_refs[k][...], band)
             field[at, :FRAME] = f0.astype(BF)
             field[at, FRAME:] = f1.astype(BF)
@@ -149,7 +153,7 @@
         before_ref, after_ref, w_ref, out_ref, field = refs[n_ch:]
         c, m, _ = place()
         for k in range(n_ch):
-            at = pl.ds(pl.multiple_of(((c + n_ch - k) % n_ch) * cb, 16), cb)
+            at = pl.ds(pl.multiple_of((c ^ k) * cb, 16), cb)
             pieces = time_pieces(mine_refs[k][...], before_ref[k], after_ref[k], m, n_x)
             for d in range(3):
                 field[d, at, :] = pieces[d]
@@ -170,7 +174,7 @@
 def emit_chunks(total, scratch, out_refs, c, n_ch, cb):
     scratch[...] = total.T
     for k in range(n_ch):
-        at = pl.ds(pl.multiple_of(((c + k) % n_ch) * cb, 16), cb)
+        at = pl.ds(pl.multiple_of((c ^ k) * cb, 16), cb)
         out_refs[k][...] = scratch[at, :].astype(out_refs[k].dtype)
 
 
@@ -183,24 +187,41 @@
     cb = field.shape[0]
     channels = n_ch * cb
 
-    def body(field_ref, before_ref, after_ref, w_ref, *rest):
-        out_refs, scratch = rest[:n_ch], rest[n_ch]
+    def body(field_hbm, before_ref, after_ref, w_hbm, *rest):
+        out_refs, (field_ref, w_ref, scratch, sems) = rest[:n_ch], rest[n_ch:]
+        first = pltpu.make_async_copy(field_hbm, field_ref, sems.at[3])
+        first.start()
+        copies = [pltpu.make_async_copy(w_hbm.at[d], w_ref.at[d], sems.at[d]) for d in range(3)]
+        for copy in copies:
+            copy.start()
         c, m, _ = place()
+        first.wait()
         pieces = time_pieces(field_ref[...], before_ref[...], after_ref[...], m, n_x)
         total = jnp.zeros((TILE, channels), F32)
         for d in range(3):
             left = pieces[2 - d].astype(F32).T.astype(BF)
+            copies[d].wait()
             total += jnp.dot(left, w_ref[d], preferred_element_type=F32)
         emit_chunks(total, scratch, out_refs, c, n_ch, cb)
 
-    return pl.pallas_call(
-        body,
+    vmem = pl.BlockSpec(memory_space=pltpu.VMEM)
+    hbm = pl.BlockSpec(memory_space=pltpu.HBM)
+    in_hbm = lambda x: pltpu.with_memory_space_constraint(x, pltpu.HBM)
+    return pl.pallas_call(
+        body,
+        in_specs=[hbm, vmem, vmem, hbm],
+        out_specs=[vmem] * n_ch,
         out_shape=chunk_shapes(n_ch, cb),
-        scratch_shapes=[pltpu.VMEM((channels, TILE), F32)],
+        scratch_shapes=[
+            pltpu.VMEM(field.shape, BF),
+            pltpu.VMEM(weight.shape, BF),
+            pltpu.VMEM((channels, TILE), F32),
+            pltpu.SemaphoreType.DMA((4,)),
+        ],
         compiler_params=pltpu.CompilerParams(vmem_limit_bytes=16 * MIB),
-        cost_estimate=pl.CostEstimate(flops=4000000000, transcendentals=0, bytes_accessed=3_000_000),
+        cost_estimate=pl.CostEstimate(flops=4_000_000_000, transcendentals=0, bytes_accessed=3_000_000),
         name="temporal_backward",
-    )(field, before, after, weight)
+    )(in_hbm(field), before, after, in_hbm(weight))
 
 
 def shifted_columns(frame, toward):
@@ -338,7 +359,7 @@
 
 
 def scatter_ch(chunks):
-    return [send(chunks[k], "ch", k) for k in range(1, len(chunks))]
+    return [swap_ch(chunks[k], k) for k in range(1, len(chunks))]
 
 
 def total_of(base, own, received):
@@ -350,13 +371,13 @@
 
 def on_device(latents, spatial_weight, temporal_weight, cotangent):
     n_ch, n_x = sizes()
-    assert n_ch == RBANDS * n_x
+    assert n_ch == RBANDS * n_x and n_ch & (n_ch - 1) == 0
     c, m, band = place()
     scale = 1.0 / math.sqrt(TILE * RBANDS * n_x)
 
     def block(pieces, b):
         stack = jnp.stack(pieces) if isinstance(pieces, list) else pieces
-        return lax.dynamic_index_in_dim(stack, (c + n_ch - b) % n_ch, 0, keepdims=False)
+        return lax.dynamic_index_in_dim(stack, c ^ b, 0, keepdims=False)
 
     own_block = RBANDS * m + band
     sib_block = RBANDS * m + 1 - band

time: 49.6 us -> 52.4 us (1.056)
  starting transfers between devices: 24.3 us -> 28.3 us
  local copies, waits for them, and re-layouts: 3.35 us -> 0.09 us
  Pallas kernels: 13.8 us -> 16.1 us
    ppermute x0 -> x12, starting transfers between devices: none -> 20.3 us  [swap_ch(): lax.ppermute(data, 'ch', [(i, i ^ k) for i in range(lax.axis_size('ch'))])]
    ppermute x16 -> x4, starting transfers between devices: 22.6 us -> 5.69 us  [send(): return lax.ppermute(data, axis, [(i, (i + by) % n) for i in range(n)])]
    ppermute x16 -> x4, waiting for transfers between devices: 5.07 us -> 1.3 us  [send(): return lax.ppermute(data, axis, [(i, (i + by) % n) for i in range(n)])]
    unnamed x14 -> x10, local copies, waits for them, and re-layouts: 3.28 us -> 0.02 us
    ppermute x0 -> x12, waiting for transfers between devices: none -> 2.86 us  [swap_ch(): lax.ppermute(data, 'ch', [(i, i ^ k) for i in range(lax.axis_size('ch'))])]
    pallas_call x1, Pallas kernels: 1.81 us -> 4.1 us  [temporal_backward(): pl.pallas_call(body, in_specs=[hbm, vmem, vmem, hbm], out_specs=[vmem] *...]
    ppermute x10, waiting for transfers between devices: 1.2 us -> 1.87 us  [swap_band(): return lax.ppermute(data, 'st', [(i, i ^ 1) for i in range(n)])]
    ppermute x10, starting transfers between devices: 1.67 us -> 2.3 us  [swap_band(): return lax.ppermute(data, 'st', [(i, i ^ 1) for i in range(n)])]
  transfers between devices with their start and end apart: 26 -> 26, of which waited for: 5 -> 5; matrix products, arithmetic and copies ran while one was open for 2% -> 2% of each run, Pallas kernels for 22% -> 25%
where the time goes in v6:
time: 52.4 us; the launch traced here: 52.2 us
  starting transfers between devices  28.3 us (54%)
  Pallas kernels  16.1 us (31%)
  waiting for transfers between devices  6.03 us (12%)
  other arithmetic  0.89 us (2%)
  between operations  0.86 us (2%)
    ppermute x12, starting transfers between devices, swap_ch(): lax.ppermute(data, 'ch', [(i, i ^ k) for i in range(lax.axis_size('ch'))])  20.3 us
    ppermute x4, starting transfers between devices, send(): return lax.ppermute(data, axis, [(i, (i + by) % n) for i in range(n)])  5.69 us
    pallas_call x1, Pallas kernels, temporal_backward(): pl.pallas_call(body, in_specs=[hbm, vmem, vmem, hbm], out_specs=[vmem] *...  4.1 us
    pallas_call x1, Pallas kernels, spatial_grads(): pl.pallas_call(body, out_specs=pl.BlockSpec(memory_space=pltpu.HBM), out_...  3.06 us
    ppermute x12, waiting for transfers between devices, swap_ch(): lax.ppermute(data, 'ch', [(i, i ^ k) for i in range(lax.axis_size('ch'))])  2.86 us
    pallas_call x1, Pallas kernels, temporal_grads(): pl.pallas_call(body, out_specs=pl.BlockSpec(memory_space=pltpu.HBM), out_...  2.79 us
    pallas_call x1, Pallas kernels, spatial_forward(): pl.pallas_call(body, out_shape=jax.ShapeDtypeStruct((cb, TILE), BF), scra...  2.68 us
    ppermute x10, starting transfers between devices, swap_band(): return lax.ppermute(data, 'st', [(i, i ^ 1) for i in range(n)])  2.3 us
  transfers between devices with their start and end apart: 26, of which 5 were waited for; matrix products, arithmetic and copies ran while one was open for 2% of the time, Pallas kernels for 25%

profile of v6, /device:TPU:0, one launch (start us, length us, event | category | flops | bytes accessed | tf_op | source)
XLA Modules:
  0.0 52.2 jit_solution(9612900244597497984)
XLA Ops:
  0.6 3.0 %collective-permute-start.3 = (bf16[320,128]{1,0:T(8,128)(2,1)}, bf16[320,128]{1,0:T(8,128)(2,1)}, u32[]{:S(2)}, u32[]{:S(2)}) collective-permute-start(bf16[320,128]{1,0:T(8,128)(2,1)} %refs_0_.2), channel_id=1, source_target_pairs={{0,8},{4,12},{8,0},{12,4},{1,9},{5,13},{9,1},{13,5},{2,10},{6,14},... | collective-permute-start | bytes 245768 | tf_op jit(solution)/shard_map/ppermute | solution.py:34
  3.6 3.6 %collective-permute-start.2 = (bf16[320,128]{1,0:T(8,128)(2,1)}, bf16[320,128]{1,0:T(8,128)(2,1)S(1)}, u32[]{:S(2)}, u32[]{:S(2)}) collective-permute-start(bf16[320,128]{1,0:T(8,128)(2,1)} %refs_0_.1), channel_id=1, source_target_pairs={{0,3},{1,2},{2,1},{3,0},{4,7},{5,6},{6,5},{7,4},{8,11},{9,10},{10,... | collective-permute-start | bytes 245768 | tf_op jit(solution)/shard_map/ppermute | solution.py:38
  7.2 0.0 collective-permute-start.1
  7.2 0.8 %collective-permute-start = (bf16[320,128]{1,0:T(8,128)(2,1)}, bf16[320,128]{1,0:T(8,128)(2,1)S(1)}, u32[]{:S(2)}, u32[]{:S(2)}) collective-permute-start(bf16[320,128]{1,0:T(8,128)(2,1)} %refs_0_.1), channel_id=1, source_target_pairs={{0,1},{1,0},{2,3},{3,2},{4,5},{5,4},{6,7},{7,6},{8,9},{9,8},{10,11... | collective-permute-start | bytes 245768 | tf_op jit(solution)/shard_map/ppermute | solution.py:38
  8.0 0.0 collective-permute-start.4
  8.0 0.0 collective-permute-done.3.before_ref.after_ref.refs_1_
  8.0 0.6 %collective-permute-start.8 = (bf16[320,128]{1,0:T(8,128)(2,1)}, bf16[320,128]{1,0:T(8,128)(2,1)S(1)}, u32[]{:S(2)}, u32[]{:S(2)}) collective-permute-start(bf16[320,128]{1,0:T(8,128)(2,1)} %refs_0_.2), channel_id=1, source_target_pairs={{0,4},{4,0},{8,12},{12,8},{1,5},{5,1},{9,13},{13,9},{2,6},{6,2},{1... | collective-permute-start | bytes 245768 | tf_op jit(solution)/shard_map/ppermute | solution.py:43
  8.6 4.1 %temporal_backward.1 = (f32[320,128]{1,0:T(8,128)S(1)}, bf16[320,128]{1,0:T(8,128)(2,1)S(1)}, bf16[320,128]{1,0:T(8,128)(2,1)S(1)}, bf16[320,128]{1,0:T(8,128)(2,1)S(1)}) custom-call(bf16[320,128]{1,0:T(8,128)(2,1)} %refs_0_.2, bf16[320,128]{1,0:T(8,128)(2,1)} %collective-permute-done.3.before_ref.after_ref.refs_1_, ...), custom_call_target="tpu_custom_call" | custom-call | flops 4000000000 | bytes 3000000 | tf_op jit(solution)/shard_map/temporal_backward/pallas_call | solution.py:210
  12.7 0.0 collective-permute-done.2.refs_3_
  12.7 1.3 %collective-permute-done.1.refs_2_ = bf16[320,128]{1,0:T(8,128)(2,1)S(1)} collective-permute-done((bf16[320,128]{1,0:T(8,128)(2,1)}, bf16[320,128]{1,0:T(8,128)(2,1)S(1)}, u32[]{:S(2)}, u32[]{:S(2)}) %collective-permute-start.1) | collective-permute-done | bytes 81952 | tf_op jit(solution)/shard_map/ppermute | solution.py:38
  14.0 0.0 collective-permute-done.refs_1_
  14.0 0.0 collective-permute-start.5
  14.0 0.5 collective-permute-start.6
  14.5 0.0 collective-permute-start.9
  14.5 0.0 copy-done.1
  14.6 0.0 collective-permute-done.4.refs_4_
  14.6 0.6 %collective-permute-start.7 = (bf16[320,128]{1,0:T(8,128)(2,1)S(1)}, bf16[320,128]{1,0:T(8,128)(2,1)S(1)}, u32[]{:S(2)}, u32[]{:S(2)}) collective-permute-start(bf16[320,128]{1,0:T(8,128)(2,1)S(1)} %collective-permute-done.2.refs_3_), channel_id=1, source_target_pairs={{0,4},{4,0},{8,12},{12,8},{1,5},{5,1},{9,13},{13,9},{2,6},{6,2},{1... | collective-permute-start | bytes 245768 | tf_op jit(solution)/shard_map/ppermute | solution.py:43
  15.2 0.0 collective-permute-done.8.refs_2_
  15.2 0.9 %collective-permute-start.13 = (bf16[320,128]{1,0:T(8,128)(2,1)S(1)}, bf16[320,128]{1,0:T(8,128)(2,1)S(1)}, u32[]{:S(2)}, u32[]{:S(2)}) collective-permute-start(bf16[320,128]{1,0:T(8,128)(2,1)S(1)} %get-tuple-element.32), channel_id=1, source_target_pairs={{0,1},{1,0},{2,3},{3,2},{4,5},{5,4},{6,7},{7,6},{8,9},{9,8},{10,11... | collective-permute-start | bytes 245768 | tf_op jit(solution)/shard_map/ppermute | solution.py:38
  16.1 0.0 collective-permute-done.9.refs_3_
  16.1 2.3 %collective-permute-start.14 = (bf16[320,128]{1,0:T(8,128)(2,1)S(1)}, bf16[320,128]{1,0:T(8,128)(2,1)S(1)}, u32[]{:S(2)}, u32[]{:S(2)}) collective-permute-start(bf16[320,128]{1,0:T(8,128)(2,1)S(1)} %get-tuple-element.33), channel_id=1, source_target_pairs={{0,2},{1,3},{2,0},{3,1},{4,6},{5,7},{6,4},{7,5},{8,10},{9,11},{10,... | collective-permute-start | bytes 245768 | tf_op jit(solution)/shard_map/ppermute | solution.py:38
  18.4 0.0 collective-permute-done.5.refs_5_
  18.4 1.2 %collective-permute-start.15 = (bf16[320,128]{1,0:T(8,128)(2,1)S(1)}, bf16[320,128]{1,0:T(8,128)(2,1)S(1)}, u32[]{:S(2)}, u32[]{:S(2)}) collective-permute-start(bf16[320,128]{1,0:T(8,128)(2,1)S(1)} %get-tuple-element.34), channel_id=1, source_target_pairs={{0,3},{1,2},{2,1},{3,0},{4,7},{5,6},{6,5},{7,4},{8,11},{9,10},{10,... | collective-permute-start | bytes 245768 | tf_op jit(solution)/shard_map/ppermute | solution.py:38
  19.6 0.0 collective-permute-done.6.refs_6_
  19.6 0.0 collective-permute-done.7.refs_7_
  19.6 0.0 slice-done
  19.6 0.0 slice-done.1
  19.6 2.7 %spatial_forward.1.refs_0_ = bf16[320,128]{1,0:T(8,128)(2,1)S(1)} custom-call(bf16[320,128]{1,0:T(8,128)(2,1)S(1)} %copy-done.1, bf16[320,128]{1,0:T(8,128)(2,1)S(1)} %collective-permute-done.refs_1_, bf16[320,128]{1,0:T(8,128)(2,1)S(1)} %collective-permute-done.1.refs_2_, bf16[320,128]{1,0:T(8,128)(2,1)S(1)} %collective-permute-done.2.refs_3_, ...), custom_call_target="tpu_custom_call" | custom-call | tf_op jit(solution)/shard_map/spatial_forward/pallas_call | solution.py:137
  22.3 2.7 %collective-permute-start.12 = (bf16[320,128]{1,0:T(8,128)(2,1)S(1)}, bf16[320,128]{1,0:T(8,128)(2,1)S(1)}, u32[]{:S(2)}, u32[]{:S(2)}) collective-permute-start(bf16[320,128]{1,0:T(8,128)(2,1)S(1)} %spatial_forward.1.refs_0_), channel_id=1, source_target_pairs={{0,3},{1,2},{2,1},{3,0},{4,7},{5,6},{6,5},{7,4},{8,11},{9,10},{10,... | collective-permute-start | bytes 245768 | tf_op jit(solution)/shard_map/ppermute | solution.py:38
  25.0 0.0 collective-permute-start.11
  25.0 0.0 collective-permute-done.13
  25.0 1.8 %collective-permute-start.10 = (bf16[320,128]{1,0:T(8,128)(2,1)S(1)}, bf16[320,128]{1,0:T(8,128)(2,1)S(1)}, u32[]{:S(2)}, u32[]{:S(2)}) collective-permute-start(bf16[320,128]{1,0:T(8,128)(2,1)S(1)} %spatial_forward.1.refs_0_), channel_id=1, source_target_pairs={{0,1},{1,0},{2,3},{3,2},{4,5},{5,4},{6,7},{7,6},{8,9},{9,8},{10,11... | collective-permute-start | bytes 245768 | tf_op jit(solution)/shard_map/ppermute | solution.py:38
  26.8 0.0 collective-permute-done.14
  26.8 0.0 collective-permute-done.15
  26.8 0.1 add_convert_fusion.1.field_ref.refs_0_
  26.9 0.6 %collective-permute-start.18 = (bf16[320,128]{1,0:T(8,128)(2,1)S(1)}, bf16[320,128]{1,0:T(8,128)(2,1)S(1)}, u32[]{:S(2)}, u32[]{:S(2)}) collective-permute-start(bf16[320,128]{1,0:T(8,128)(2,1)S(1)} %add_convert_fusion.1.field_ref.refs_0_), channel_id=1, source_target_pairs={{0,8},{4,12},{8,0},{12,4},{1,9},{5,13},{9,1},{13,5},{2,10},{6,14},... | collective-permute-start | bytes 245768 | tf_op jit(solution)/shard_map/ppermute | solution.py:34
  27.5 0.0 collective-permute-start.16
  27.6 1.2 %collective-permute-done.16.sibling_ref.refs_2_ = bf16[320,128]{1,0:T(8,128)(2,1)S(1)} collective-permute-done((bf16[320,128]{1,0:T(8,128)(2,1)S(1)}, bf16[320,128]{1,0:T(8,128)(2,1)S(1)}, u32[]{:S(2)}, u32[]{:S(2)}) %collective-permute-start.16) | collective-permute-done | bytes 81952 | tf_op jit(solution)/shard_map/ppermute | solution.py:43
  28.7 1.5 %collective-permute-start.20 = (bf16[2,320,128]{2,1,0:T(8,128)(2,1)S(1)}, bf16[2,320,128]{2,1,0:T(8,128)(2,1)S(1)}, u32[]{:S(2)}, u32[]{:S(2)}) collective-permute-start(bf16[2,320,128]{2,1,0:T(8,128)(2,1)S(1)} %pad_maximum_fusion.3), channel_id=1, source_target_pairs={{0,8},{4,12},{8,0},{12,4},{1,9},{5,13},{9,1},{13,5},{2,10},{6,14},... | collective-permute-start | bytes 491528 | tf_op jit(solution)/shard_map/ppermute | solution.py:34
  30.2 1.6 %spatial_backward.1 = (f32[320,128]{1,0:T(8,128)S(1)}, bf16[320,128]{1,0:T(8,128)(2,1)S(1)}, bf16[320,128]{1,0:T(8,128)(2,1)S(1)}, bf16[320,128]{1,0:T(8,128)(2,1)S(1)}) custom-call(bf16[320,128]{1,0:T(8,128)(2,1)S(1)} %add_convert_fusion.1.field_ref.refs_0_, bf16[320,128]{1,0:T(8,128)(2,1)S(1)} %collective-permute-done.16.sibling_ref.refs_2_, ...), custom_call_target="tpu_custom_call" | custom-call | tf_op jit(solution)/shard_map/spatial_backward/pallas_call | solution.py:261
  31.9 0.0 copy-start
  31.9 0.0 collective-permute-done.12.refs_3_
  31.9 4.6 %collective-permute-start.21 = (bf16[320,128]{1,0:T(8,128)(2,1)S(1)}, bf16[320,128]{1,0:T(8,128)(2,1)S(1)}, u32[]{:S(2)}, u32[]{:S(2)}) collective-permute-start(bf16[320,128]{1,0:T(8,128)(2,1)S(1)} %get-tuple-element.45), channel_id=1, source_target_pairs={{0,1},{1,0},{2,3},{3,2},{4,5},{5,4},{6,7},{7,6},{8,9},{9,8},{10,11... | collective-permute-start | bytes 245768 | tf_op jit(solution)/shard_map/ppermute | solution.py:38
  36.5 0.0 collective-permute-done.11.refs_2_
  36.5 1.0 %collective-permute-start.22 = (bf16[320,128]{1,0:T(8,128)(2,1)S(1)}, bf16[320,128]{1,0:T(8,128)(2,1)S(1)}, u32[]{:S(2)}, u32[]{:S(2)}) collective-permute-start(bf16[320,128]{1,0:T(8,128)(2,1)S(1)} %get-tuple-element.46), channel_id=1, source_target_pairs={{0,2},{1,3},{2,0},{3,1},{4,6},{5,7},{6,4},{7,5},{8,10},{9,11},{10,... | collective-permute-start | bytes 245768 | tf_op jit(solution)/shard_map/ppermute | solution.py:38
  37.5 0.0 collective-permute-done.10.refs_1_
  37.6 0.6 %collective-permute-start.17 = (bf16[4,320,128]{2,1,0:T(8,128)(2,1)S(1)}, bf16[4,320,128]{2,1,0:T(8,128)(2,1)S(1)}, u32[]{:S(2)}, u32[]{:S(2)}) collective-permute-start(bf16[4,320,128]{2,1,0:T(8,128)(2,1)S(1)} %pad_maximum_fusion), channel_id=1, source_target_pairs={{0,8},{4,12},{8,0},{12,4},{1,9},{5,13},{9,1},{13,5},{2,10},{6,14},... | collective-permute-start | bytes 983048 | tf_op jit(solution)/shard_map/ppermute | solution.py:34
  38.2 0.0 collective-permute-done.18.refs_1_
  38.2 1.5 %collective-permute-start.23 = (bf16[320,128]{1,0:T(8,128)(2,1)S(1)}, bf16[320,128]{1,0:T(8,128)(2,1)S(1)}, u32[]{:S(2)}, u32[]{:S(2)}) collective-permute-start(bf16[320,128]{1,0:T(8,128)(2,1)S(1)} %get-tuple-element.47), channel_id=1, source_target_pairs={{0,3},{1,2},{2,1},{3,0},{4,7},{5,6},{6,5},{7,4},{8,11},{9,10},{10,... | collective-permute-start | bytes 245768 | tf_op jit(solution)/shard_map/ppermute | solution.py:38
  39.7 0.0 collective-permute-done.20
  39.7 0.0 collective-permute-start.19
  39.7 0.0 collective-permute-done.21
  39.7 0.6 %collective-permute-start.24 = (bf16[320,128]{1,0:T(8,128)(2,1)S(1)}, bf16[320,128]{1,0:T(8,128)(2,1)S(1)}, u32[]{:S(2)}, u32[]{:S(2)}) collective-permute-start(bf16[320,128]{1,0:T(8,128)(2,1)S(1)} %get-tuple-element.60), channel_id=1, source_target_pairs={{0,4},{4,0},{8,12},{12,8},{1,5},{5,1},{9,13},{13,9},{2,6},{6,2},{1... | collective-permute-start | bytes 245768 | tf_op jit(solution)/shard_map/ppermute | solution.py:43
  40.3 0.7 %collective-permute-done.19.refs_3_ = bf16[320,128]{1,0:T(8,128)(2,1)S(1)} collective-permute-done((bf16[320,128]{1,0:T(8,128)(2,1)S(1)}, bf16[320,128]{1,0:T(8,128)(2,1)S(1)}, u32[]{:S(2)}, u32[]{:S(2)}) %collective-permute-start.19) | collective-permute-done | bytes 81952 | tf_op jit(solution)/shard_map/ppermute | solution.py:43
  40.9 3.1 %spatial_grads.1 = f32[9,320,320]{2,1,0:T(8,128)} custom-call(bf16[320,128]{1,0:T(8,128)(2,1)S(1)} %add_convert_fusion.1.field_ref.refs_0_, bf16[320,128]{1,0:T(8,128)(2,1)S(1)} %collective-permute-done.18.refs_1_, bf16[320,128]{1,0:T(8,128)(2,1)S(1)} %collective-permute-done.16.sibling_ref.refs_2_, bf16[320,128]{1,0:T(8,128)(2,1)S(1)} %collective-permute-done.19.refs_3_, ...), custom_call_target="tpu_custom_call" | custom-call | tf_op jit(solution)/shard_map/spatial_grads/pallas_call | solution.py:303
  44.0 1.5 %collective-permute-done.22 = bf16[320,128]{1,0:T(8,128)(2,1)S(1)} collective-permute-done((bf16[320,128]{1,0:T(8,128)(2,1)S(1)}, bf16[320,128]{1,0:T(8,128)(2,1)S(1)}, u32[]{:S(2)}, u32[]{:S(2)}) %collective-permute-start.22) | collective-permute-done | bytes 81952 | tf_op jit(solution)/shard_map/ppermute | solution.py:38
  45.6 1.3 %collective-permute-done.17.refs_4_.refs_5_ = bf16[4,320,128]{2,1,0:T(8,128)(2,1)S(1)} collective-permute-done((bf16[4,320,128]{2,1,0:T(8,128)(2,1)S(1)}, bf16[4,320,128]{2,1,0:T(8,128)(2,1)S(1)}, u32[]{:S(2)}, u32[]{:S(2)}) %collective-permute-start.17) | collective-permute-done | bytes 327712 | tf_op jit(solution)/shard_map/ppermute | solution.py:34
  46.9 0.1 collective-permute-start.25
  46.9 0.0 collective-permute-done.23
  47.0 0.7 %add_convert_fusion = bf16[320,128]{1,0:T(8,128)(2,1)} fusion(bf16[320,128]{1,0:T(8,128)(2,1)S(1)} %collective-permute-done.23, bf16[320,128]{1,0:T(8,128)(2,1)S(1)} %collective-permute-done.22, bf16[320,128]{1,0:T(8,128)(2,1)S(1)} %collective-permute-done.21, f32[320,128]{1,0:T(8,128)S(1)} %get-tuple-element.44, ...), kind=kLoop, calls=%fused_computation.4 | loop fusion | flops 368640 | bytes 573440 | tf_op jit(solution)/shard_map/convert_element_type | solution.py:369
  47.6 1.8 %temporal_forward.1 = bf16[320,128]{1,0:T(8,128)(2,1)} custom-call(bf16[320,128]{1,0:T(8,128)(2,1)S(1)} %spatial_forward.1.refs_0_, bf16[320,128]{1,0:T(8,128)(2,1)S(1)} %collective-permute-done.10.refs_1_, bf16[320,128]{1,0:T(8,128)(2,1)S(1)} %collective-permute-done.11.refs_2_, bf16[320,128]{1,0:T(8,128)(2,1)S(1)} %collective-permute-done.12.refs_3_, ...), custom_call_target="tpu_custom_call" | custom-call | tf_op jit(solution)/shard_map/temporal_forward/pallas_call | solution.py:165
  49.4 0.0 collective-permute-done.24.refs_6_
  49.4 0.0 collective-permute-done.25.refs_7_
  49.4 2.8 %temporal_grads.1 = f32[3,320,320]{2,1,0:T(8,128)} custom-call(bf16[320,128]{1,0:T(8,128)(2,1)S(1)} %copy-done.2, bf16[320,128]{1,0:T(8,128)(2,1)} %collective-permute-done.3.before_ref.after_ref.refs_1_, bf16[320,128]{1,0:T(8,128)(2,1)S(1)} %collective-permute-done.8.refs_2_, bf16[320,128]{1,0:T(8,128)(2,1)S(1)} %collective-permute-done.9.refs_3_, ...), custom_call_target="tpu_custom_call" | custom-call | tf_op jit(solution)/shard_map/temporal_grads/pallas_call | solution.py:346
  (16 shorter events, 0.2 us)
Async XLA Ops:
  0.6 7.4 %collective-permute-start.3 = (bf16[320,128]{1,0:T(8,128)(2,1)}, bf16[320,128]{1,0:T(8,128)(2,1)}, u32[]{:S(2)}, u32[]{:S(2)}) collective-permute-start(bf16[320,128]{1,0:T(8,128)(2,1)} %refs_0_.2), channel_id=1, source_target_pairs={{0,8},{4,12},{8,0},{12,4},{1,9},{5,13},{9,1},{13,5},{2,10},{6,14},... | collective-permute-start | bytes 245768 | tf_op jit(solution)/shard_map/ppermute | solution.py:34
  3.6 9.1 %collective-permute-start.2 = (bf16[320,128]{1,0:T(8,128)(2,1)}, bf16[320,128]{1,0:T(8,128)(2,1)S(1)}, u32[]{:S(2)}, u32[]{:S(2)}) collective-permute-start(bf16[320,128]{1,0:T(8,128)(2,1)} %refs_0_.1), channel_id=1, source_target_pairs={{0,3},{1,2},{2,1},{3,0},{4,7},{5,6},{6,5},{7,4},{8,11},{9,10},{10,... | collective-permute-start | bytes 245768 | tf_op jit(solution)/shard_map/ppermute | solution.py:38
  7.2 6.8 %collective-permute-start.1 = (bf16[320,128]{1,0:T(8,128)(2,1)}, bf16[320,128]{1,0:T(8,128)(2,1)S(1)}, u32[]{:S(2)}, u32[]{:S(2)}) collective-permute-start(bf16[320,128]{1,0:T(8,128)(2,1)} %refs_0_.1), channel_id=1, source_target_pairs={{0,2},{1,3},{2,0},{3,1},{4,6},{5,7},{6,4},{7,5},{8,10},{9,11},{10,... | collective-permute-start | bytes 245768 | tf_op jit(solution)/shard_map/ppermute | solution.py:38
  7.2 6.8 %collective-permute-start = (bf16[320,128]{1,0:T(8,128)(2,1)}, bf16[320,128]{1,0:T(8,128)(2,1)S(1)}, u32[]{:S(2)}, u32[]{:S(2)}) collective-permute-start(bf16[320,128]{1,0:T(8,128)(2,1)} %refs_0_.1), channel_id=1, source_target_pairs={{0,1},{1,0},{2,3},{3,2},{4,5},{5,4},{6,7},{7,6},{8,9},{9,8},{10,11... | collective-permute-start | bytes 245768 | tf_op jit(solution)/shard_map/ppermute | solution.py:38
  8.0 6.6 %collective-permute-start.4 = (bf16[320,128]{1,0:T(8,128)(2,1)}, bf16[320,128]{1,0:T(8,128)(2,1)S(1)}, u32[]{:S(2)}, u32[]{:S(2)}) collective-permute-start(bf16[320,128]{1,0:T(8,128)(2,1)} %refs_0_.1), channel_id=1, source_target_pairs={{0,4},{4,0},{8,12},{12,8},{1,5},{5,1},{9,13},{13,9},{2,6},{6,2},{1... | collective-permute-start | bytes 245768 | tf_op jit(solution)/shard_map/ppermute | solution.py:43
  8.0 11.6 %slice-start = ((s8[7372800]{0:T(1024)(128)(4,1)}), s8[3178496]{0:T(1024)(128)(4,1)S(1)}, s32[]{:S(2)}) async-start(s8[7372800]{0:T(1024)(128)(4,1)} %bitcast.29), calls=%async_computation | async-start | bytes 6356992
  8.0 6.5 %copy-start.1 = (bf16[320,128]{1,0:T(8,128)(2,1)S(1)}, bf16[320,128]{1,0:T(8,128)(2,1)}, u32[]{:S(2)}) copy-start(bf16[320,128]{1,0:T(8,128)(2,1)} %refs_0_.1) | copy-start | bytes 245764
  8.0 11.6 %slice-start.1 = ((s8[7372800]{0:T(1024)(128)(4,1)}), s8[4194304]{0:T(1024)(128)(4,1)S(1)}, s32[]{:S(2)}) async-start(s8[7372800]{0:T(1024)(128)(4,1)} %bitcast.29), calls=%async_computation.1 | async-start | bytes 8388608
  8.0 7.1 %collective-permute-start.8 = (bf16[320,128]{1,0:T(8,128)(2,1)}, bf16[320,128]{1,0:T(8,128)(2,1)S(1)}, u32[]{:S(2)}, u32[]{:S(2)}) collective-permute-start(bf16[320,128]{1,0:T(8,128)(2,1)} %refs_0_.2), channel_id=1, source_target_pairs={{0,4},{4,0},{8,12},{12,8},{1,5},{5,1},{9,13},{13,9},{2,6},{6,2},{1... | collective-permute-start | bytes 245768 | tf_op jit(solution)/shard_map/ppermute | solution.py:43
  14.0 4.3 %collective-permute-start.5 = (bf16[320,128]{1,0:T(8,128)(2,1)S(1)}, bf16[320,128]{1,0:T(8,128)(2,1)S(1)}, u32[]{:S(2)}, u32[]{:S(2)}) collective-permute-start(bf16[320,128]{1,0:T(8,128)(2,1)S(1)} %collective-permute-done.refs_1_), channel_id=1, source_target_pairs={{0,4},{4,0},{8,12},{12,8},{1,5},{5,1},{9,13},{13,9},{2,6},{6,2},{1... | collective-permute-start | bytes 245768 | tf_op jit(solution)/shard_map/ppermute | solution.py:43
  14.0 5.6 %collective-permute-start.6 = (bf16[320,128]{1,0:T(8,128)(2,1)S(1)}, bf16[320,128]{1,0:T(8,128)(2,1)S(1)}, u32[]{:S(2)}, u32[]{:S(2)}) collective-permute-start(bf16[320,128]{1,0:T(8,128)(2,1)S(1)} %collective-permute-done.1.refs_2_), channel_id=1, source_target_pairs={{0,4},{4,0},{8,12},{12,8},{1,5},{5,1},{9,13},{13,9},{2,6},{6,2},{1... | collective-permute-start | bytes 245768 | tf_op jit(solution)/shard_map/ppermute | solution.py:43
  14.5 1.5 %collective-permute-start.9 = (bf16[320,128]{1,0:T(8,128)(2,1)}, bf16[320,128]{1,0:T(8,128)(2,1)S(1)}, u32[]{:S(2)}, u32[]{:S(2)}) collective-permute-start(bf16[320,128]{1,0:T(8,128)(2,1)} %collective-permute-done.3.before_ref.after_ref.refs_1_), channel_id=1, source_target_pairs={{0,4},{4,0},{8,12},{12,8},{1,5},{5,1},{9,13},{13,9},{2,6},{6,2},{1... | collective-permute-start | bytes 245768 | tf_op jit(solution)/shard_map/ppermute | solution.py:43
  14.6 12.3 %copy-start.2 = (bf16[320,128]{1,0:T(8,128)(2,1)S(1)}, bf16[320,128]{1,0:T(8,128)(2,1)}, u32[]{:S(2)}) copy-start(bf16[320,128]{1,0:T(8,128)(2,1)} %refs_0_.2) | copy-start | bytes 245764
  14.6 5.0 %collective-permute-start.7 = (bf16[320,128]{1,0:T(8,128)(2,1)S(1)}, bf16[320,128]{1,0:T(8,128)(2,1)S(1)}, u32[]{:S(2)}, u32[]{:S(2)}) collective-permute-start(bf16[320,128]{1,0:T(8,128)(2,1)S(1)} %collective-permute-done.2.refs_3_), channel_id=1, source_target_pairs={{0,4},{4,0},{8,12},{12,8},{1,5},{5,1},{9,13},{13,9},{2,6},{6,2},{1... | collective-permute-start | bytes 245768 | tf_op jit(solution)/shard_map/ppermute | solution.py:43
  15.2 9.8 %collective-permute-start.13 = (bf16[320,128]{1,0:T(8,128)(2,1)S(1)}, bf16[320,128]{1,0:T(8,128)(2,1)S(1)}, u32[]{:S(2)}, u32[]{:S(2)}) collective-permute-start(bf16[320,128]{1,0:T(8,128)(2,1)S(1)} %get-tuple-element.32), channel_id=1, source_target_pairs={{0,1},{1,0},{2,3},{3,2},{4,5},{5,4},{6,7},{7,6},{8,9},{9,8},{10,11... | collective-permute-start | bytes 245768 | tf_op jit(solution)/shard_map/ppermute | solution.py:38
  16.1 10.7 %collective-permute-start.14 = (bf16[320,128]{1,0:T(8,128)(2,1)S(1)}, bf16[320,128]{1,0:T(8,128)(2,1)S(1)}, u32[]{:S(2)}, u32[]{:S(2)}) collective-permute-start(bf16[320,128]{1,0:T(8,128)(2,1)S(1)} %get-tuple-element.33), channel_id=1, source_target_pairs={{0,2},{1,3},{2,0},{3,1},{4,6},{5,7},{6,4},{7,5},{8,10},{9,11},{10,... | collective-permute-start | bytes 245768 | tf_op jit(solution)/shard_map/ppermute | solution.py:38
  18.4 8.4 %collective-permute-start.15 = (bf16[320,128]{1,0:T(8,128)(2,1)S(1)}, bf16[320,128]{1,0:T(8,128)(2,1)S(1)}, u32[]{:S(2)}, u32[]{:S(2)}) collective-permute-start(bf16[320,128]{1,0:T(8,128)(2,1)S(1)} %get-tuple-element.34), channel_id=1, source_target_pairs={{0,3},{1,2},{2,1},{3,0},{4,7},{5,6},{6,5},{7,4},{8,11},{9,10},{10,... | collective-permute-start | bytes 245768 | tf_op jit(solution)/shard_map/ppermute | solution.py:38
  22.3 9.6 %collective-permute-start.12 = (bf16[320,128]{1,0:T(8,128)(2,1)S(1)}, bf16[320,128]{1,0:T(8,128)(2,1)S(1)}, u32[]{:S(2)}, u32[]{:S(2)}) collective-permute-start(bf16[320,128]{1,0:T(8,128)(2,1)S(1)} %spatial_forward.1.refs_0_), channel_id=1, source_target_pairs={{0,3},{1,2},{2,1},{3,0},{4,7},{5,6},{6,5},{7,4},{8,11},{9,10},{10,... | collective-permute-start | bytes 245768 | tf_op jit(solution)/shard_map/ppermute | solution.py:38
  25.0 11.5 %collective-permute-start.11 = (bf16[320,128]{1,0:T(8,128)(2,1)S(1)}, bf16[320,128]{1,0:T(8,128)(2,1)S(1)}, u32[]{:S(2)}, u32[]{:S(2)}) collective-permute-start(bf16[320,128]{1,0:T(8,128)(2,1)S(1)} %spatial_forward.1.refs_0_), channel_id=1, source_target_pairs={{0,2},{1,3},{2,0},{3,1},{4,6},{5,7},{6,4},{7,5},{8,10},{9,11},{10,... | collective-permute-start | bytes 245768 | tf_op jit(solution)/shard_map/ppermute | solution.py:38
  25.0 12.5 %collective-permute-start.10 = (bf16[320,128]{1,0:T(8,128)(2,1)S(1)}, bf16[320,128]{1,0:T(8,128)(2,1)S(1)}, u32[]{:S(2)}, u32[]{:S(2)}) collective-permute-start(bf16[320,128]{1,0:T(8,128)(2,1)S(1)} %spatial_forward.1.refs_0_), channel_id=1, source_target_pairs={{0,1},{1,0},{2,3},{3,2},{4,5},{5,4},{6,7},{7,6},{8,9},{9,8},{10,11... | collective-permute-start | bytes 245768 | tf_op jit(solution)/shard_map/ppermute | solution.py:38
  26.9 11.3 %collective-permute-start.18 = (bf16[320,128]{1,0:T(8,128)(2,1)S(1)}, bf16[320,128]{1,0:T(8,128)(2,1)S(1)}, u32[]{:S(2)}, u32[]{:S(2)}) collective-permute-start(bf16[320,128]{1,0:T(8,128)(2,1)S(1)} %add_convert_fusion.1.field_ref.refs_0_), channel_id=1, source_target_pairs={{0,8},{4,12},{8,0},{12,4},{1,9},{5,13},{9,1},{13,5},{2,10},{6,14},... | collective-permute-start | bytes 245768 | tf_op jit(solution)/shard_map/ppermute | solution.py:34
  27.5 1.3 %collective-permute-start.16 = (bf16[320,128]{1,0:T(8,128)(2,1)S(1)}, bf16[320,128]{1,0:T(8,128)(2,1)S(1)}, u32[]{:S(2)}, u32[]{:S(2)}) collective-permute-start(bf16[320,128]{1,0:T(8,128)(2,1)S(1)} %add_convert_fusion.1.field_ref.refs_0_), channel_id=1, source_target_pairs={{0,4},{4,0},{8,12},{12,8},{1,5},{5,1},{9,13},{13,9},{2,6},{6,2},{1... | collective-permute-start | bytes 245768 | tf_op jit(solution)/shard_map/ppermute | solution.py:43
  28.7 10.9 %collective-permute-start.20 = (bf16[2,320,128]{2,1,0:T(8,128)(2,1)S(1)}, bf16[2,320,128]{2,1,0:T(8,128)(2,1)S(1)}, u32[]{:S(2)}, u32[]{:S(2)}) collective-permute-start(bf16[2,320,128]{2,1,0:T(8,128)(2,1)S(1)} %pad_maximum_fusion.3), channel_id=1, source_target_pairs={{0,8},{4,12},{8,0},{12,4},{1,9},{5,13},{9,1},{13,5},{2,10},{6,14},... | collective-permute-start | bytes 491528 | tf_op jit(solution)/shard_map/ppermute | solution.py:34
  31.9 15.8 %copy-start = (bf16[3,320,1280]{2,1,0:T(8,128)(2,1)S(1)}, bf16[3,320,1280]{2,1,0:T(8,128)(2,1)}, u32[]{:S(2)}) copy-start(bf16[3,320,1280]{2,1,0:T(8,128)(2,1)} %refs_6_.1) | copy-start | bytes 7372804
  31.9 7.8 %collective-permute-start.21 = (bf16[320,128]{1,0:T(8,128)(2,1)S(1)}, bf16[320,128]{1,0:T(8,128)(2,1)S(1)}, u32[]{:S(2)}, u32[]{:S(2)}) collective-permute-start(bf16[320,128]{1,0:T(8,128)(2,1)S(1)} %get-tuple-element.45), channel_id=1, source_target_pairs={{0,1},{1,0},{2,3},{3,2},{4,5},{5,4},{6,7},{7,6},{8,9},{9,8},{10,11... | collective-permute-start | bytes 245768 | tf_op jit(solution)/shard_map/ppermute | solution.py:38
  36.5 9.1 %collective-permute-start.22 = (bf16[320,128]{1,0:T(8,128)(2,1)S(1)}, bf16[320,128]{1,0:T(8,128)(2,1)S(1)}, u32[]{:S(2)}, u32[]{:S(2)}) collective-permute-start(bf16[320,128]{1,0:T(8,128)(2,1)S(1)} %get-tuple-element.46), channel_id=1, source_target_pairs={{0,2},{1,3},{2,0},{3,1},{4,6},{5,7},{6,4},{7,5},{8,10},{9,11},{10,... | collective-permute-start | bytes 245768 | tf_op jit(solution)/shard_map/ppermute | solution.py:38
  37.6 9.3 %collective-permute-start.17 = (bf16[4,320,128]{2,1,0:T(8,128)(2,1)S(1)}, bf16[4,320,128]{2,1,0:T(8,128)(2,1)S(1)}, u32[]{:S(2)}, u32[]{:S(2)}) collective-permute-start(bf16[4,320,128]{2,1,0:T(8,128)(2,1)S(1)} %pad_maximum_fusion), channel_id=1, source_target_pairs={{0,8},{4,12},{8,0},{12,4},{1,9},{5,13},{9,1},{13,5},{2,10},{6,14},... | collective-permute-start | bytes 983048 | tf_op jit(solution)/shard_map/ppermute | solution.py:34
  38.2 8.8 %collective-permute-start.23 = (bf16[320,128]{1,0:T(8,128)(2,1)S(1)}, bf16[320,128]{1,0:T(8,128)(2,1)S(1)}, u32[]{:S(2)}, u32[]{:S(2)}) collective-permute-start(bf16[320,128]{1,0:T(8,128)(2,1)S(1)} %get-tuple-element.47), channel_id=1, source_target_pairs={{0,3},{1,2},{2,1},{3,0},{4,7},{5,6},{6,5},{7,4},{8,11},{9,10},{10,... | collective-permute-start | bytes 245768 | tf_op jit(solution)/shard_map/ppermute | solution.py:38
  39.7 1.3 %collective-permute-start.19 = (bf16[320,128]{1,0:T(8,128)(2,1)S(1)}, bf16[320,128]{1,0:T(8,128)(2,1)S(1)}, u32[]{:S(2)}, u32[]{:S(2)}) collective-permute-start(bf16[320,128]{1,0:T(8,128)(2,1)S(1)} %collective-permute-done.18.refs_1_), channel_id=1, source_target_pairs={{0,4},{4,0},{8,12},{12,8},{1,5},{5,1},{9,13},{13,9},{2,6},{6,2},{1... | collective-permute-start | bytes 245768 | tf_op jit(solution)/shard_map/ppermute | solution.py:43
  39.7 9.7 %collective-permute-start.24 = (bf16[320,128]{1,0:T(8,128)(2,1)S(1)}, bf16[320,128]{1,0:T(8,128)(2,1)S(1)}, u32[]{:S(2)}, u32[]{:S(2)}) collective-permute-start(bf16[320,128]{1,0:T(8,128)(2,1)S(1)} %get-tuple-element.60), channel_id=1, source_target_pairs={{0,4},{4,0},{8,12},{12,8},{1,5},{5,1},{9,13},{13,9},{2,6},{6,2},{1... | collective-permute-start | bytes 245768 | tf_op jit(solution)/shard_map/ppermute | solution.py:43
  46.9 2.6 %collective-permute-start.25 = (bf16[320,128]{1,0:T(8,128)(2,1)S(1)}, bf16[320,128]{1,0:T(8,128)(2,1)S(1)}, u32[]{:S(2)}, u32[]{:S(2)}) collective-permute-start(bf16[320,128]{1,0:T(8,128)(2,1)S(1)} %get-tuple-element.58), channel_id=1, source_target_pairs={{0,4},{4,0},{8,12},{12,8},{1,5},{5,1},{9,13},{13,9},{2,6},{6,2},{1... | collective-permute-start | bytes 245768 | tf_op jit(solution)/shard_map/ppermute | solution.py:43

commit v7 on v5

--- a/solution.py
+++ b/solution.py
@@ -178,14 +178,19 @@
     return [jax.ShapeDtypeStruct((cb, TILE), BF if k else F32) for k in range(n_ch)]
 
 
-def temporal_backward(field, before, after, weight):
+def temporal_backward(ring, weight):
     n_ch, n_x = sizes()
+    field = ring[0]
     cb = field.shape[0]
     channels = n_ch * cb
 
-    def body(field_ref, before_ref, after_ref, w_ref, *rest):
-        out_refs, scratch = rest[:n_ch], rest[n_ch]
+    def body(*refs):
+        ring_refs, w_ref, out_refs = refs[:n_x], refs[n_x], refs[n_x + 1 : n_x + 1 + n_ch]
+        stack_ref, scratch = refs[n_x + 1 + n_ch :]
+        field_ref, before_ref, after_ref = ring_refs[0], ring_refs[1], ring_refs[-1]
         c, m, _ = place()
+        for j in range(n_x):
+            stack_ref[j] = ring_refs[j][...]
         pieces = time_pieces(field_ref[...], before_ref[...], after_ref[...], m, n_x)
         total = jnp.zeros((TILE, channels), F32)
         for d in range(3):
@@ -193,14 +198,15 @@
             total += jnp.dot(left, w_ref[d], preferred_element_type=F32)
         emit_chunks(total, scratch, out_refs, c, n_ch, cb)
 
-    return pl.pallas_call(
-        body,
-        out_shape=chunk_shapes(n_ch, cb),
+    *chunks, stack = pl.pallas_call(
+        body,
+        out_shape=chunk_shapes(n_ch, cb) + [jax.ShapeDtypeStruct((n_x, cb, TILE), BF)],
         scratch_shapes=[pltpu.VMEM((channels, TILE), F32)],
         compiler_params=pltpu.CompilerParams(vmem_limit_bytes=16 * MIB),
-        cost_estimate=pl.CostEstimate(flops=4000000000, transcendentals=0, bytes_accessed=3_000_000),
+        cost_estimate=pl.CostEstimate(flops=2000000000, transcendentals=0, bytes_accessed=3_000_000),
         name="temporal_backward",
-    )(field, before, after, weight)
+    )(*ring, weight)
+    return chunks, stack
 
 
 def shifted_columns(frame, toward):
@@ -296,18 +302,19 @@
 
 def temporal_grads(grads, grads_sibling, fields, fields_sibling, scale):
     _, n_x = sizes()
-    ob, ib = grads[0].shape[0], fields[0].shape[0]
+    ob, ib = grads.shape[1], fields[0].shape[0]
     span = FT * n_x * FRAME
 
     def body(*refs):
-        g_refs, gs_refs, h_refs, hs_refs = (refs[q * n_x : (q + 1) * n_x] for q in range(4))
-        out_hbm, left, right, out, sems = refs[4 * n_x :]
+        g_ref, gs_ref = refs[:2]
+        h_refs, hs_refs = refs[2 : 2 + n_x], refs[2 + n_x : 2 + 2 * n_x]
+        out_hbm, left, right, out, sems = refs[2 + 2 * n_x :]
         _, m, band = place()
         right[:FRAME, :] = jnp.zeros((FRAME, ib), BF)
         right[FRAME + span :, :] = jnp.zeros((FRAME, ib), BF)
         for j in range(n_x):
             block = (m + n_x - j) % n_x
-            for a, frame in enumerate(frames_of(g_refs[j][...], gs_refs[j][...], band)):
+            for a, frame in enumerate(frames_of(g_ref[j], gs_ref[j], band)):
                 at = pl.multiple_of((FT * block + a) * FRAME, FRAME)
                 left[:, pl.ds(at, FRAME)] = frame.astype(BF)
             for a, frame in enumerate(frames_of(h_refs[j][...], hs_refs[j][...], band)):
@@ -334,7 +341,7 @@
         ],
         compiler_params=pltpu.CompilerParams(vmem_limit_bytes=24 * MIB),
         name="temporal_grads",
-    )(*grads, *grads_sibling, *fields, *fields_sibling)
+    )(grads, grads_sibling, *fields, *fields_sibling)
 
 
 def scatter_ch(chunks):
@@ -364,14 +371,12 @@
     siblings = [swap_band(latents)]
     mine = gather_ch(latents)
     cot_ring = ring_blocks(cotangent)
-    chunks = temporal_backward(cotangent, cot_ring[0], cot_ring[-1], temporal_weight)
+    chunks, cots = temporal_backward([cotangent] + cot_ring, temporal_weight)
     partials = scatter_ch(chunks)
     mine = after_all(mine, chunks)
 
     siblings += [swap_band(piece) for piece in mine[1:]]
-    cots = [cotangent] + cot_ring
-    cots_sibling = [swap_band(x) for x in cots]
-    siblings = after_all(siblings, cots_sibling)
+    cots_sibling = swap_band(cots)
     lat_own, lat_sib = [block(mine, own_block)], [block(siblings, own_block)]
     for j in range(1, n_x):
         target = RBANDS * ((m + j) % n_x) + band

time: 49.6 us -> 47.9 us (0.966)
  waiting for transfers between devices: 6.27 us -> 8.78 us
  starting transfers between devices: 24.3 us -> 22.2 us
  Pallas kernels: 13.8 us -> 11.9 us
    ppermute x16, waiting for transfers between devices: 5.07 us -> 7.61 us  [send(): return lax.ppermute(data, axis, [(i, (i + by) % n) for i in range(n)])]
    ppermute x16, starting transfers between devices: 22.6 us -> 20.7 us  [send(): return lax.ppermute(data, axis, [(i, (i + by) % n) for i in range(n)])]
    pallas_call x1, Pallas kernels: 1.81 us -> 0.85 us  [temporal_backward(): pl.pallas_call(body, out_shape=chunk_shapes(n_ch, cb) + [jax.ShapeDtypeSt...]
    pallas_call x1, Pallas kernels: 2.79 us -> 1.91 us  [temporal_grads(): pl.pallas_call(body, out_specs=pl.BlockSpec(memory_space=pltpu.HBM), out_...]
    unnamed x14 -> x10, local copies, waits for them, and re-layouts: 3.28 us -> 2.99 us
    ppermute x10 -> x9, starting transfers between devices: 1.67 us -> 1.49 us  [swap_band(): return lax.ppermute(data, 'st', [(i, i ^ 1) for i in range(n)])]
    ppermute x10 -> x9, waiting for transfers between devices: 1.2 us -> 1.18 us  [swap_band(): return lax.ppermute(data, 'st', [(i, i ^ 1) for i in range(n)])]
  transfers between devices with their start and end apart: 26 -> 25, of which waited for: 5 -> 4; matrix products, arithmetic and copies ran while one was open for 2% -> 2% of each run, Pallas kernels for 22% -> 21%
where the time goes in v7:
time: 47.9 us; the launch traced here: 47.8 us
  starting transfers between devices  22.2 us (46%)
  Pallas kernels  11.9 us (25%)
  waiting for transfers between devices  8.78 us (18%)
  local copies, waits for them, and re-layouts  3.06 us (6%)
  other arithmetic  0.89 us (2%)
  between operations  0.86 us (2%)
    ppermute x16, starting transfers between devices, send(): return lax.ppermute(data, axis, [(i, (i + by) % n) for i in range(n)])  20.7 us
    ppermute x16, waiting for transfers between devices, send(): return lax.ppermute(data, axis, [(i, (i + by) % n) for i in range(n)])  7.61 us
    pallas_call x1, Pallas kernels, spatial_grads(): pl.pallas_call(body, out_specs=pl.BlockSpec(memory_space=pltpu.HBM), out_...  3.08 us
    unnamed x10, local copies, waits for them, and re-layouts  2.99 us
    pallas_call x1, Pallas kernels, spatial_forward(): pl.pallas_call(body, out_shape=jax.ShapeDtypeStruct((cb, TILE), BF), scra...  2.69 us
    pallas_call x1, Pallas kernels, temporal_grads(): pl.pallas_call(body, out_specs=pl.BlockSpec(memory_space=pltpu.HBM), out_...  1.91 us
    pallas_call x1, Pallas kernels, temporal_forward(): pl.pallas_call(body, out_shape=jax.ShapeDtypeStruct((cb, TILE), BF), scra...  1.79 us
    pallas_call x1, Pallas kernels, spatial_backward(): pl.pallas_call(body, out_shape=chunk_shapes(n_ch, cb), scratch_shapes=[pl...  1.62 us
  transfers between devices with their start and end apart: 25, of which 4 were waited for; matrix products, arithmetic and copies ran while one was open for 2% of the time, Pallas kernels for 21%

profile of v7, /device:TPU:0, one launch (start us, length us, event | category | flops | bytes accessed | tf_op | source)
XLA Modules:
  0.0 47.8 jit_solution(14085992175230954633)
XLA Ops:
  0.6 0.0 copy-start.3
  0.6 3.0 %collective-permute-start.3 = (bf16[320,128]{1,0:T(8,128)(2,1)}, bf16[320,128]{1,0:T(8,128)(2,1)S(1)}, u32[]{:S(2)}, u32[]{:S(2)}) collective-permute-start(bf16[320,128]{1,0:T(8,128)(2,1)} %refs_0_.1), channel_id=1, source_target_pairs={{0,8},{4,12},{8,0},{12,4},{1,9},{5,13},{9,1},{13,5},{2,10},{6,14},... | collective-permute-start | bytes 245768 | tf_op jit(solution)/shard_map/ppermute | solution.py:34
  3.6 3.6 %collective-permute-start.2 = (bf16[320,128]{1,0:T(8,128)(2,1)}, bf16[320,128]{1,0:T(8,128)(2,1)S(1)}, u32[]{:S(2)}, u32[]{:S(2)}) collective-permute-start(bf16[320,128]{1,0:T(8,128)(2,1)} %refs_0_.2), channel_id=1, source_target_pairs={{0,3},{1,0},{2,1},{3,2},{4,7},{5,4},{6,5},{7,6},{8,11},{9,8},{10,9... | collective-permute-start | bytes 245768 | tf_op jit(solution)/shard_map/ppermute | solution.py:34
  7.2 0.0 collective-permute-start.1
  7.2 1.0 %collective-permute-start = (bf16[320,128]{1,0:T(8,128)(2,1)}, bf16[320,128]{1,0:T(8,128)(2,1)S(1)}, u32[]{:S(2)}, u32[]{:S(2)}) collective-permute-start(bf16[320,128]{1,0:T(8,128)(2,1)} %refs_0_.2), channel_id=1, source_target_pairs={{0,1},{1,2},{2,3},{3,0},{4,5},{5,6},{6,7},{7,4},{8,9},{9,10},{10,1... | collective-permute-start | bytes 245768 | tf_op jit(solution)/shard_map/ppermute | solution.py:34
  8.3 0.0 collective-permute-start.4
  8.3 0.0 collective-permute-done.3.refs_1_
  8.3 0.0 copy-start.1
  8.3 1.8 %copy-done.1 = bf16[3,320,1280]{2,1,0:T(8,128)(2,1)S(1)} copy-done((bf16[3,320,1280]{2,1,0:T(8,128)(2,1)S(1)}, bf16[3,320,1280]{2,1,0:T(8,128)(2,1)}, u32[]{:S(2)}) %copy-start.1) | copy-done | bytes 2457624
  10.1 1.1 %copy-done.4 = bf16[320,128]{1,0:T(8,128)(2,1)S(1)} copy-done((bf16[320,128]{1,0:T(8,128)(2,1)S(1)}, bf16[320,128]{1,0:T(8,128)(2,1)}, u32[]{:S(2)}) %copy-start.4) | copy-done | bytes 81944
  11.3 0.9 %temporal_backward.1 = (f32[320,128]{1,0:T(8,128)S(1)}, bf16[320,128]{1,0:T(8,128)(2,1)S(1)}, bf16[320,128]{1,0:T(8,128)(2,1)S(1)}, bf16[320,128]{1,0:T(8,128)(2,1)S(1)}, bf16[2,320,128]{2,1,0:T(8,128)(2,1)S(1)}) custom-call(bf16[320,128]{1,0:T(8,128)(2,1)S(1)} %copy-done.4, bf16[320,128]{1,0:T(8,128)(2,1)S(1)} %collective-permute-done.3.refs_1_, ...), custom_call_target="tpu_custom_call" | custom-call | flops 2000000000 | bytes 3000000 | tf_op jit(solution)/shard_map/temporal_backward/pallas_call | solution.py:201
  12.1 2.5 %collective-permute-start.11 = (bf16[320,128]{1,0:T(8,128)(2,1)S(1)}, bf16[320,128]{1,0:T(8,128)(2,1)S(1)}, u32[]{:S(2)}, u32[]{:S(2)}) collective-permute-start(bf16[320,128]{1,0:T(8,128)(2,1)S(1)} %get-tuple-element.29), channel_id=1, source_target_pairs={{0,1},{1,2},{2,3},{3,0},{4,5},{5,6},{6,7},{7,4},{8,9},{9,10},{10,1... | collective-permute-start | bytes 245768 | tf_op jit(solution)/shard_map/ppermute | solution.py:34
  14.7 0.0 collective-permute-done.2.refs_3_
  14.7 0.0 collective-permute-done.1.refs_2_
  14.7 0.0 collective-permute-done.refs_1_
  14.7 0.3 collective-permute-start.5
  14.9 0.3 collective-permute-start.6
  15.2 0.2 collective-permute-start.7
  15.4 0.0 copy-done.3
  15.5 0.0 collective-permute-done.4.refs_4_
  15.5 1.9 %collective-permute-start.12 = (bf16[320,128]{1,0:T(8,128)(2,1)S(1)}, bf16[320,128]{1,0:T(8,128)(2,1)S(1)}, u32[]{:S(2)}, u32[]{:S(2)}) collective-permute-start(bf16[320,128]{1,0:T(8,128)(2,1)S(1)} %get-tuple-element.30), channel_id=1, source_target_pairs={{0,2},{1,3},{2,0},{3,1},{4,6},{5,7},{6,4},{7,5},{8,10},{9,11},{10,... | collective-permute-start | bytes 245768 | tf_op jit(solution)/shard_map/ppermute | solution.py:34
  17.4 0.0 collective-permute-done.5.refs_5_
  17.4 0.8 %collective-permute-start.13 = (bf16[320,128]{1,0:T(8,128)(2,1)S(1)}, bf16[320,128]{1,0:T(8,128)(2,1)S(1)}, u32[]{:S(2)}, u32[]{:S(2)}) collective-permute-start(bf16[320,128]{1,0:T(8,128)(2,1)S(1)} %get-tuple-element.31), channel_id=1, source_target_pairs={{0,3},{1,0},{2,1},{3,2},{4,7},{5,4},{6,5},{7,6},{8,11},{9,8},{10,9... | collective-permute-start | bytes 245768 | tf_op jit(solution)/shard_map/ppermute | solution.py:34
  18.3 0.0 collective-permute-done.6.refs_6_
  18.3 0.1 collective-permute-start.22
  18.4 0.0 collective-permute-done.7.refs_7_
  18.4 2.7 %spatial_forward.1.refs_0_ = bf16[320,128]{1,0:T(8,128)(2,1)S(1)} custom-call(bf16[320,128]{1,0:T(8,128)(2,1)S(1)} %copy-done.3, bf16[320,128]{1,0:T(8,128)(2,1)S(1)} %collective-permute-done.refs_1_, bf16[320,128]{1,0:T(8,128)(2,1)S(1)} %collective-permute-done.1.refs_2_, bf16[320,128]{1,0:T(8,128)(2,1)S(1)} %collective-permute-done.2.refs_3_, ...), custom_call_target="tpu_custom_call" | custom-call | tf_op jit(solution)/shard_map/spatial_forward/pallas_call | solution.py:133
  21.1 1.8 %collective-permute-start.10 = (bf16[320,128]{1,0:T(8,128)(2,1)S(1)}, bf16[320,128]{1,0:T(8,128)(2,1)S(1)}, u32[]{:S(2)}, u32[]{:S(2)}) collective-permute-start(bf16[320,128]{1,0:T(8,128)(2,1)S(1)} %spatial_forward.1.refs_0_), channel_id=1, source_target_pairs={{0,3},{1,0},{2,1},{3,2},{4,7},{5,4},{6,5},{7,6},{8,11},{9,8},{10,9... | collective-permute-start | bytes 245768 | tf_op jit(solution)/shard_map/ppermute | solution.py:34
  22.8 0.0 collective-permute-done.11
  22.8 1.0 %collective-permute-start.9 = (bf16[320,128]{1,0:T(8,128)(2,1)S(1)}, bf16[320,128]{1,0:T(8,128)(2,1)S(1)}, u32[]{:S(2)}, u32[]{:S(2)}) collective-permute-start(bf16[320,128]{1,0:T(8,128)(2,1)S(1)} %spatial_forward.1.refs_0_), channel_id=1, source_target_pairs={{0,2},{1,3},{2,0},{3,1},{4,6},{5,7},{6,4},{7,5},{8,10},{9,11},{10,... | collective-permute-start | bytes 245768 | tf_op jit(solution)/shard_map/ppermute | solution.py:34
  23.8 0.0 collective-permute-done.12
  23.8 0.6 %collective-permute-start.8 = (bf16[320,128]{1,0:T(8,128)(2,1)S(1)}, bf16[320,128]{1,0:T(8,128)(2,1)S(1)}, u32[]{:S(2)}, u32[]{:S(2)}) collective-permute-start(bf16[320,128]{1,0:T(8,128)(2,1)S(1)} %spatial_forward.1.refs_0_), channel_id=1, source_target_pairs={{0,1},{1,2},{2,3},{3,0},{4,5},{5,6},{6,7},{7,4},{8,9},{9,10},{10,1... | collective-permute-start | bytes 245768 | tf_op jit(solution)/shard_map/ppermute | solution.py:34
  24.4 0.0 collective-permute-done.13
  24.4 0.1 add_convert_fusion.1.field_ref.refs_0_
  24.5 0.1 collective-permute-start.14
  24.6 1.2 %collective-permute-done.14.sibling_ref.refs_2_ = bf16[320,128]{1,0:T(8,128)(2,1)S(1)} collective-permute-done((bf16[320,128]{1,0:T(8,128)(2,1)S(1)}, bf16[320,128]{1,0:T(8,128)(2,1)S(1)}, u32[]{:S(2)}, u32[]{:S(2)}) %collective-permute-start.14) | collective-permute-done | bytes 81952 | tf_op jit(solution)/shard_map/ppermute | solution.py:39
  25.8 0.5 %collective-permute-start.16 = (bf16[320,128]{1,0:T(8,128)(2,1)S(1)}, bf16[320,128]{1,0:T(8,128)(2,1)S(1)}, u32[]{:S(2)}, u32[]{:S(2)}) collective-permute-start(bf16[320,128]{1,0:T(8,128)(2,1)S(1)} %add_convert_fusion.1.field_ref.refs_0_), channel_id=1, source_target_pairs={{0,8},{4,12},{8,0},{12,4},{1,9},{5,13},{9,1},{13,5},{2,10},{6,14},... | collective-permute-start | bytes 245768 | tf_op jit(solution)/shard_map/ppermute | solution.py:34
  26.3 1.6 %spatial_backward.1 = (f32[320,128]{1,0:T(8,128)S(1)}, bf16[320,128]{1,0:T(8,128)(2,1)S(1)}, bf16[320,128]{1,0:T(8,128)(2,1)S(1)}, bf16[320,128]{1,0:T(8,128)(2,1)S(1)}) custom-call(bf16[320,128]{1,0:T(8,128)(2,1)S(1)} %add_convert_fusion.1.field_ref.refs_0_, bf16[320,128]{1,0:T(8,128)(2,1)S(1)} %collective-permute-done.14.sibling_ref.refs_2_, ...), custom_call_target="tpu_custom_call" | custom-call | tf_op jit(solution)/shard_map/spatial_backward/pallas_call | solution.py:246
  28.0 0.0 copy-start.2
  28.0 0.0 collective-permute-done.10.refs_3_
  28.0 1.6 %collective-permute-start.18 = (bf16[2,320,128]{2,1,0:T(8,128)(2,1)S(1)}, bf16[2,320,128]{2,1,0:T(8,128)(2,1)S(1)}, u32[]{:S(2)}, u32[]{:S(2)}) collective-permute-start(bf16[2,320,128]{2,1,0:T(8,128)(2,1)S(1)} %pad_maximum_fusion.3), channel_id=1, source_target_pairs={{0,8},{4,12},{8,0},{12,4},{1,9},{5,13},{9,1},{13,5},{2,10},{6,14},... | collective-permute-start | bytes 491528 | tf_op jit(solution)/shard_map/ppermute | solution.py:34
  29.5 2.3 %collective-permute-done.9.refs_2_ = bf16[320,128]{1,0:T(8,128)(2,1)S(1)} collective-permute-done((bf16[320,128]{1,0:T(8,128)(2,1)S(1)}, bf16[320,128]{1,0:T(8,128)(2,1)S(1)}, u32[]{:S(2)}, u32[]{:S(2)}) %collective-permute-start.9) | collective-permute-done | bytes 81952 | tf_op jit(solution)/shard_map/ppermute | solution.py:34
  31.9 0.0 collective-permute-start.19
  31.9 0.0 collective-permute-done.8.refs_1_
  31.9 1.1 %collective-permute-start.15 = (bf16[4,320,128]{2,1,0:T(8,128)(2,1)S(1)}, bf16[4,320,128]{2,1,0:T(8,128)(2,1)S(1)}, u32[]{:S(2)}, u32[]{:S(2)}) collective-permute-start(bf16[4,320,128]{2,1,0:T(8,128)(2,1)S(1)} %pad_maximum_fusion), channel_id=1, source_target_pairs={{0,8},{4,12},{8,0},{12,4},{1,9},{5,13},{9,1},{13,5},{2,10},{6,14},... | collective-permute-start | bytes 983048 | tf_op jit(solution)/shard_map/ppermute | solution.py:34
  33.0 0.0 collective-permute-done.16.refs_1_
  33.0 1.4 %collective-permute-start.20 = (bf16[320,128]{1,0:T(8,128)(2,1)S(1)}, bf16[320,128]{1,0:T(8,128)(2,1)S(1)}, u32[]{:S(2)}, u32[]{:S(2)}) collective-permute-start(bf16[320,128]{1,0:T(8,128)(2,1)S(1)} %get-tuple-element.39), channel_id=1, source_target_pairs={{0,2},{1,3},{2,0},{3,1},{4,6},{5,7},{6,4},{7,5},{8,10},{9,11},{10,... | collective-permute-start | bytes 245768 | tf_op jit(solution)/shard_map/ppermute | solution.py:34
  34.4 0.0 collective-permute-done.18
  34.4 0.0 collective-permute-start.17
  34.4 4.5 %collective-permute-done.19 = bf16[320,128]{1,0:T(8,128)(2,1)S(1)} collective-permute-done((bf16[320,128]{1,0:T(8,128)(2,1)S(1)}, bf16[320,128]{1,0:T(8,128)(2,1)S(1)}, u32[]{:S(2)}, u32[]{:S(2)}) %collective-permute-start.19) | collective-permute-done | bytes 81952 | tf_op jit(solution)/shard_map/ppermute | solution.py:34
  38.9 0.0 collective-permute-start.21
  38.9 0.0 collective-permute-done.17.refs_3_
  38.9 0.0 collective-permute-start.23
  38.9 3.1 %spatial_grads.1 = f32[9,320,320]{2,1,0:T(8,128)} custom-call(bf16[320,128]{1,0:T(8,128)(2,1)S(1)} %add_convert_fusion.1.field_ref.refs_0_, bf16[320,128]{1,0:T(8,128)(2,1)S(1)} %collective-permute-done.16.refs_1_, bf16[320,128]{1,0:T(8,128)(2,1)S(1)} %collective-permute-done.14.sibling_ref.refs_2_, bf16[320,128]{1,0:T(8,128)(2,1)S(1)} %collective-permute-done.17.refs_3_, ...), custom_call_target="tpu_custom_call" | custom-call | tf_op jit(solution)/shard_map/spatial_grads/pallas_call | solution.py:288
  42.0 0.0 collective-permute-done.20
  42.0 0.0 collective-permute-done.15.refs_4_.refs_5_
  42.1 0.6 %collective-permute-start.24 = (bf16[320,128]{1,0:T(8,128)(2,1)S(1)}, bf16[320,128]{1,0:T(8,128)(2,1)S(1)}, u32[]{:S(2)}, u32[]{:S(2)}) collective-permute-start(bf16[320,128]{1,0:T(8,128)(2,1)S(1)} %get-tuple-element.52), channel_id=1, source_target_pairs={{0,4},{4,0},{8,12},{12,8},{1,5},{5,1},{9,13},{13,9},{2,6},{6,2},{1... | collective-permute-start | bytes 245768 | tf_op jit(solution)/shard_map/ppermute | solution.py:39
  42.6 0.7 %collective-permute-done.21 = bf16[320,128]{1,0:T(8,128)(2,1)S(1)} collective-permute-done((bf16[320,128]{1,0:T(8,128)(2,1)S(1)}, bf16[320,128]{1,0:T(8,128)(2,1)S(1)}, u32[]{:S(2)}, u32[]{:S(2)}) %collective-permute-start.21) | collective-permute-done | bytes 81952 | tf_op jit(solution)/shard_map/ppermute | solution.py:34
  43.4 0.7 %add_convert_fusion = bf16[320,128]{1,0:T(8,128)(2,1)} fusion(bf16[320,128]{1,0:T(8,128)(2,1)S(1)} %collective-permute-done.21, bf16[320,128]{1,0:T(8,128)(2,1)S(1)} %collective-permute-done.20, bf16[320,128]{1,0:T(8,128)(2,1)S(1)} %collective-permute-done.19, f32[320,128]{1,0:T(8,128)S(1)} %get-tuple-element.37, ...), kind=kLoop, calls=%fused_computation.4 | loop fusion | flops 368640 | bytes 573440 | tf_op jit(solution)/shard_map/convert_element_type | solution.py:355
  44.1 1.8 %temporal_forward.1 = bf16[320,128]{1,0:T(8,128)(2,1)} custom-call(bf16[320,128]{1,0:T(8,128)(2,1)S(1)} %spatial_forward.1.refs_0_, bf16[320,128]{1,0:T(8,128)(2,1)S(1)} %collective-permute-done.8.refs_1_, bf16[320,128]{1,0:T(8,128)(2,1)S(1)} %collective-permute-done.9.refs_2_, bf16[320,128]{1,0:T(8,128)(2,1)S(1)} %collective-permute-done.10.refs_3_, ...), custom_call_target="tpu_custom_call" | custom-call | tf_op jit(solution)/shard_map/temporal_forward/pallas_call | solution.py:161
  45.8 0.0 collective-permute-done.22.refs_1_
  45.8 0.0 collective-permute-done.23.refs_4_
  45.8 0.0 collective-permute-done.24.refs_5_
  45.9 1.9 %temporal_grads.1 = f32[3,320,320]{2,1,0:T(8,128)} custom-call(bf16[2,320,128]{2,1,0:T(8,128)(2,1)S(1)} %get-tuple-element.49.refs_0_, bf16[2,320,128]{2,1,0:T(8,128)(2,1)S(1)} %collective-permute-done.22.refs_1_, bf16[320,128]{1,0:T(8,128)(2,1)S(1)} %get-tuple-element.50.refs_2_, bf16[320,128]{1,0:T(8,128)(2,1)S(1)} %get-tuple-element.51.refs_3_, ...), custom_call_target="tpu_custom_call" | custom-call | tf_op jit(solution)/shard_map/temporal_grads/pallas_call | solution.py:332
  (13 shorter events, 0.2 us)
Async XLA Ops:
  0.6 14.8 %copy-start.3 = (bf16[320,128]{1,0:T(8,128)(2,1)S(1)}, bf16[320,128]{1,0:T(8,128)(2,1)}, u32[]{:S(2)}) copy-start(bf16[320,128]{1,0:T(8,128)(2,1)} %refs_0_.2) | copy-start | bytes 245764
  0.6 7.6 %collective-permute-start.3 = (bf16[320,128]{1,0:T(8,128)(2,1)}, bf16[320,128]{1,0:T(8,128)(2,1)S(1)}, u32[]{:S(2)}, u32[]{:S(2)}) collective-permute-start(bf16[320,128]{1,0:T(8,128)(2,1)} %refs_0_.1), channel_id=1, source_target_pairs={{0,8},{4,12},{8,0},{12,4},{1,9},{5,13},{9,1},{13,5},{2,10},{6,14},... | collective-permute-start | bytes 245768 | tf_op jit(solution)/shard_map/ppermute | solution.py:34
  3.6 11.0 %collective-permute-start.2 = (bf16[320,128]{1,0:T(8,128)(2,1)}, bf16[320,128]{1,0:T(8,128)(2,1)S(1)}, u32[]{:S(2)}, u32[]{:S(2)}) collective-permute-start(bf16[320,128]{1,0:T(8,128)(2,1)} %refs_0_.2), channel_id=1, source_target_pairs={{0,3},{1,0},{2,1},{3,2},{4,7},{5,4},{6,5},{7,6},{8,11},{9,8},{10,9... | collective-permute-start | bytes 245768 | tf_op jit(solution)/shard_map/ppermute | solution.py:34
  7.2 7.4 %collective-permute-start.1 = (bf16[320,128]{1,0:T(8,128)(2,1)}, bf16[320,128]{1,0:T(8,128)(2,1)S(1)}, u32[]{:S(2)}, u32[]{:S(2)}) collective-permute-start(bf16[320,128]{1,0:T(8,128)(2,1)} %refs_0_.2), channel_id=1, source_target_pairs={{0,2},{1,3},{2,0},{3,1},{4,6},{5,7},{6,4},{7,5},{8,10},{9,11},{10,... | collective-permute-start | bytes 245768 | tf_op jit(solution)/shard_map/ppermute | solution.py:34
  7.2 7.4 %collective-permute-start = (bf16[320,128]{1,0:T(8,128)(2,1)}, bf16[320,128]{1,0:T(8,128)(2,1)S(1)}, u32[]{:S(2)}, u32[]{:S(2)}) collective-permute-start(bf16[320,128]{1,0:T(8,128)(2,1)} %refs_0_.2), channel_id=1, source_target_pairs={{0,1},{1,2},{2,3},{3,0},{4,5},{5,6},{6,7},{7,4},{8,9},{9,10},{10,1... | collective-permute-start | bytes 245768 | tf_op jit(solution)/shard_map/ppermute | solution.py:34
  8.3 7.2 %collective-permute-start.4 = (bf16[320,128]{1,0:T(8,128)(2,1)}, bf16[320,128]{1,0:T(8,128)(2,1)S(1)}, u32[]{:S(2)}, u32[]{:S(2)}) collective-permute-start(bf16[320,128]{1,0:T(8,128)(2,1)} %refs_0_.2), channel_id=1, source_target_pairs={{0,4},{4,0},{8,12},{12,8},{1,5},{5,1},{9,13},{13,9},{2,6},{6,2},{1... | collective-permute-start | bytes 245768 | tf_op jit(solution)/shard_map/ppermute | solution.py:39
  8.3 10.1 %copy-start = (bf16[9,320,1280]{2,1,0:T(8,128)(2,1)S(1)}, bf16[9,320,1280]{2,1,0:T(8,128)(2,1)}, u32[]{:S(2)}) copy-start(bf16[9,320,1280]{2,1,0:T(8,128)(2,1)} %refs_8_.1) | copy-start | bytes 22118404
  8.3 1.8 %copy-start.1 = (bf16[3,320,1280]{2,1,0:T(8,128)(2,1)S(1)}, bf16[3,320,1280]{2,1,0:T(8,128)(2,1)}, u32[]{:S(2)}) copy-start(bf16[3,320,1280]{2,1,0:T(8,128)(2,1)} %refs_6_.1) | copy-start | bytes 7372804
  10.1 1.1 %copy-start.4 = (bf16[320,128]{1,0:T(8,128)(2,1)S(1)}, bf16[320,128]{1,0:T(8,128)(2,1)}, u32[]{:S(2)}) copy-start(bf16[320,128]{1,0:T(8,128)(2,1)} %refs_0_.1) | copy-start | bytes 245764
  12.1 10.7 %collective-permute-start.11 = (bf16[320,128]{1,0:T(8,128)(2,1)S(1)}, bf16[320,128]{1,0:T(8,128)(2,1)S(1)}, u32[]{:S(2)}, u32[]{:S(2)}) collective-permute-start(bf16[320,128]{1,0:T(8,128)(2,1)S(1)} %get-tuple-element.29), channel_id=1, source_target_pairs={{0,1},{1,2},{2,3},{3,0},{4,5},{5,6},{6,7},{7,4},{8,9},{9,10},{10,1... | collective-permute-start | bytes 245768 | tf_op jit(solution)/shard_map/ppermute | solution.py:34
  14.7 2.8 %collective-permute-start.5 = (bf16[320,128]{1,0:T(8,128)(2,1)S(1)}, bf16[320,128]{1,0:T(8,128)(2,1)S(1)}, u32[]{:S(2)}, u32[]{:S(2)}) collective-permute-start(bf16[320,128]{1,0:T(8,128)(2,1)S(1)} %collective-permute-done.refs_1_), channel_id=1, source_target_pairs={{0,4},{4,0},{8,12},{12,8},{1,5},{5,1},{9,13},{13,9},{2,6},{6,2},{1... | collective-permute-start | bytes 245768 | tf_op jit(solution)/shard_map/ppermute | solution.py:39
  14.9 3.3 %collective-permute-start.6 = (bf16[320,128]{1,0:T(8,128)(2,1)S(1)}, bf16[320,128]{1,0:T(8,128)(2,1)S(1)}, u32[]{:S(2)}, u32[]{:S(2)}) collective-permute-start(bf16[320,128]{1,0:T(8,128)(2,1)S(1)} %collective-permute-done.1.refs_2_), channel_id=1, source_target_pairs={{0,4},{4,0},{8,12},{12,8},{1,5},{5,1},{9,13},{13,9},{2,6},{6,2},{1... | collective-permute-start | bytes 245768 | tf_op jit(solution)/shard_map/ppermute | solution.py:39
  15.2 3.1 %collective-permute-start.7 = (bf16[320,128]{1,0:T(8,128)(2,1)S(1)}, bf16[320,128]{1,0:T(8,128)(2,1)S(1)}, u32[]{:S(2)}, u32[]{:S(2)}) collective-permute-start(bf16[320,128]{1,0:T(8,128)(2,1)S(1)} %collective-permute-done.2.refs_3_), channel_id=1, source_target_pairs={{0,4},{4,0},{8,12},{12,8},{1,5},{5,1},{9,13},{13,9},{2,6},{6,2},{1... | collective-permute-start | bytes 245768 | tf_op jit(solution)/shard_map/ppermute | solution.py:39
  15.5 8.3 %collective-permute-start.12 = (bf16[320,128]{1,0:T(8,128)(2,1)S(1)}, bf16[320,128]{1,0:T(8,128)(2,1)S(1)}, u32[]{:S(2)}, u32[]{:S(2)}) collective-permute-start(bf16[320,128]{1,0:T(8,128)(2,1)S(1)} %get-tuple-element.30), channel_id=1, source_target_pairs={{0,2},{1,3},{2,0},{3,1},{4,6},{5,7},{6,4},{7,5},{8,10},{9,11},{10,... | collective-permute-start | bytes 245768 | tf_op jit(solution)/shard_map/ppermute | solution.py:34
  17.4 7.0 %collective-permute-start.13 = (bf16[320,128]{1,0:T(8,128)(2,1)S(1)}, bf16[320,128]{1,0:T(8,128)(2,1)S(1)}, u32[]{:S(2)}, u32[]{:S(2)}) collective-permute-start(bf16[320,128]{1,0:T(8,128)(2,1)S(1)} %get-tuple-element.31), channel_id=1, source_target_pairs={{0,3},{1,0},{2,1},{3,2},{4,7},{5,4},{6,5},{7,6},{8,11},{9,8},{10,9... | collective-permute-start | bytes 245768 | tf_op jit(solution)/shard_map/ppermute | solution.py:34
  18.3 27.6 %collective-permute-start.22 = (bf16[2,320,128]{2,1,0:T(8,128)(2,1)S(1)}, bf16[2,320,128]{2,1,0:T(8,128)(2,1)S(1)}, u32[]{:S(2)}, u32[]{:S(2)}) collective-permute-start(bf16[2,320,128]{2,1,0:T(8,128)(2,1)S(1)} %get-tuple-element.49.refs_0_), channel_id=1, source_target_pairs={{0,4},{4,0},{8,12},{12,8},{1,5},{5,1},{9,13},{13,9},{2,6},{6,2},{1... | collective-permute-start | bytes 491528 | tf_op jit(solution)/shard_map/ppermute | solution.py:39
  21.1 6.9 %collective-permute-start.10 = (bf16[320,128]{1,0:T(8,128)(2,1)S(1)}, bf16[320,128]{1,0:T(8,128)(2,1)S(1)}, u32[]{:S(2)}, u32[]{:S(2)}) collective-permute-start(bf16[320,128]{1,0:T(8,128)(2,1)S(1)} %spatial_forward.1.refs_0_), channel_id=1, source_target_pairs={{0,3},{1,0},{2,1},{3,2},{4,7},{5,4},{6,5},{7,6},{8,11},{9,8},{10,9... | collective-permute-start | bytes 245768 | tf_op jit(solution)/shard_map/ppermute | solution.py:34
  22.8 9.0 %collective-permute-start.9 = (bf16[320,128]{1,0:T(8,128)(2,1)S(1)}, bf16[320,128]{1,0:T(8,128)(2,1)S(1)}, u32[]{:S(2)}, u32[]{:S(2)}) collective-permute-start(bf16[320,128]{1,0:T(8,128)(2,1)S(1)} %spatial_forward.1.refs_0_), channel_id=1, source_target_pairs={{0,2},{1,3},{2,0},{3,1},{4,6},{5,7},{6,4},{7,5},{8,10},{9,11},{10,... | collective-permute-start | bytes 245768 | tf_op jit(solution)/shard_map/ppermute | solution.py:34
  23.8 8.1 %collective-permute-start.8 = (bf16[320,128]{1,0:T(8,128)(2,1)S(1)}, bf16[320,128]{1,0:T(8,128)(2,1)S(1)}, u32[]{:S(2)}, u32[]{:S(2)}) collective-permute-start(bf16[320,128]{1,0:T(8,128)(2,1)S(1)} %spatial_forward.1.refs_0_), channel_id=1, source_target_pairs={{0,1},{1,2},{2,3},{3,0},{4,5},{5,6},{6,7},{7,4},{8,9},{9,10},{10,1... | collective-permute-start | bytes 245768 | tf_op jit(solution)/shard_map/ppermute | solution.py:34
  24.5 1.3 %collective-permute-start.14 = (bf16[320,128]{1,0:T(8,128)(2,1)S(1)}, bf16[320,128]{1,0:T(8,128)(2,1)S(1)}, u32[]{:S(2)}, u32[]{:S(2)}) collective-permute-start(bf16[320,128]{1,0:T(8,128)(2,1)S(1)} %add_convert_fusion.1.field_ref.refs_0_), channel_id=1, source_target_pairs={{0,4},{4,0},{8,12},{12,8},{1,5},{5,1},{9,13},{13,9},{2,6},{6,2},{1... | collective-permute-start | bytes 245768 | tf_op jit(solution)/shard_map/ppermute | solution.py:39
  25.8 7.2 %collective-permute-start.16 = (bf16[320,128]{1,0:T(8,128)(2,1)S(1)}, bf16[320,128]{1,0:T(8,128)(2,1)S(1)}, u32[]{:S(2)}, u32[]{:S(2)}) collective-permute-start(bf16[320,128]{1,0:T(8,128)(2,1)S(1)} %add_convert_fusion.1.field_ref.refs_0_), channel_id=1, source_target_pairs={{0,8},{4,12},{8,0},{12,4},{1,9},{5,13},{9,1},{13,5},{2,10},{6,14},... | collective-permute-start | bytes 245768 | tf_op jit(solution)/shard_map/ppermute | solution.py:34
  28.0 16.1 %copy-start.2 = (bf16[3,320,1280]{2,1,0:T(8,128)(2,1)S(1)}, bf16[3,320,1280]{2,1,0:T(8,128)(2,1)}, u32[]{:S(2)}) copy-start(bf16[3,320,1280]{2,1,0:T(8,128)(2,1)} %refs_6_.1) | copy-start | bytes 7372804
  28.0 6.4 %collective-permute-start.18 = (bf16[2,320,128]{2,1,0:T(8,128)(2,1)S(1)}, bf16[2,320,128]{2,1,0:T(8,128)(2,1)S(1)}, u32[]{:S(2)}, u32[]{:S(2)}) collective-permute-start(bf16[2,320,128]{2,1,0:T(8,128)(2,1)S(1)} %pad_maximum_fusion.3), channel_id=1, source_target_pairs={{0,8},{4,12},{8,0},{12,4},{1,9},{5,13},{9,1},{13,5},{2,10},{6,14},... | collective-permute-start | bytes 491528 | tf_op jit(solution)/shard_map/ppermute | solution.py:34
  31.9 7.1 %collective-permute-start.19 = (bf16[320,128]{1,0:T(8,128)(2,1)S(1)}, bf16[320,128]{1,0:T(8,128)(2,1)S(1)}, u32[]{:S(2)}, u32[]{:S(2)}) collective-permute-start(bf16[320,128]{1,0:T(8,128)(2,1)S(1)} %get-tuple-element.38), channel_id=1, source_target_pairs={{0,1},{1,2},{2,3},{3,0},{4,5},{5,6},{6,7},{7,4},{8,9},{9,10},{10,1... | collective-permute-start | bytes 245768 | tf_op jit(solution)/shard_map/ppermute | solution.py:34
  31.9 10.1 %collective-permute-start.15 = (bf16[4,320,128]{2,1,0:T(8,128)(2,1)S(1)}, bf16[4,320,128]{2,1,0:T(8,128)(2,1)S(1)}, u32[]{:S(2)}, u32[]{:S(2)}) collective-permute-start(bf16[4,320,128]{2,1,0:T(8,128)(2,1)S(1)} %pad_maximum_fusion), channel_id=1, source_target_pairs={{0,8},{4,12},{8,0},{12,4},{1,9},{5,13},{9,1},{13,5},{2,10},{6,14},... | collective-permute-start | bytes 983048 | tf_op jit(solution)/shard_map/ppermute | solution.py:34
  33.0 9.0 %collective-permute-start.20 = (bf16[320,128]{1,0:T(8,128)(2,1)S(1)}, bf16[320,128]{1,0:T(8,128)(2,1)S(1)}, u32[]{:S(2)}, u32[]{:S(2)}) collective-permute-start(bf16[320,128]{1,0:T(8,128)(2,1)S(1)} %get-tuple-element.39), channel_id=1, source_target_pairs={{0,2},{1,3},{2,0},{3,1},{4,6},{5,7},{6,4},{7,5},{8,10},{9,11},{10,... | collective-permute-start | bytes 245768 | tf_op jit(solution)/shard_map/ppermute | solution.py:34
  34.4 4.5 %collective-permute-start.17 = (bf16[320,128]{1,0:T(8,128)(2,1)S(1)}, bf16[320,128]{1,0:T(8,128)(2,1)S(1)}, u32[]{:S(2)}, u32[]{:S(2)}) collective-permute-start(bf16[320,128]{1,0:T(8,128)(2,1)S(1)} %collective-permute-done.16.refs_1_), channel_id=1, source_target_pairs={{0,4},{4,0},{8,12},{12,8},{1,5},{5,1},{9,13},{13,9},{2,6},{6,2},{1... | collective-permute-start | bytes 245768 | tf_op jit(solution)/shard_map/ppermute | solution.py:39
  38.9 4.4 %collective-permute-start.21 = (bf16[320,128]{1,0:T(8,128)(2,1)S(1)}, bf16[320,128]{1,0:T(8,128)(2,1)S(1)}, u32[]{:S(2)}, u32[]{:S(2)}) collective-permute-start(bf16[320,128]{1,0:T(8,128)(2,1)S(1)} %get-tuple-element.40), channel_id=1, source_target_pairs={{0,3},{1,0},{2,1},{3,2},{4,7},{5,4},{6,5},{7,6},{8,11},{9,8},{10,9... | collective-permute-start | bytes 245768 | tf_op jit(solution)/shard_map/ppermute | solution.py:34
  38.9 6.9 %collective-permute-start.23 = (bf16[320,128]{1,0:T(8,128)(2,1)S(1)}, bf16[320,128]{1,0:T(8,128)(2,1)S(1)}, u32[]{:S(2)}, u32[]{:S(2)}) collective-permute-start(bf16[320,128]{1,0:T(8,128)(2,1)S(1)} %get-tuple-element.54), channel_id=1, source_target_pairs={{0,4},{4,0},{8,12},{12,8},{1,5},{5,1},{9,13},{13,9},{2,6},{6,2},{1... | collective-permute-start | bytes 245768 | tf_op jit(solution)/shard_map/ppermute | solution.py:39
  42.1 3.8 %collective-permute-start.24 = (bf16[320,128]{1,0:T(8,128)(2,1)S(1)}, bf16[320,128]{1,0:T(8,128)(2,1)S(1)}, u32[]{:S(2)}, u32[]{:S(2)}) collective-permute-start(bf16[320,128]{1,0:T(8,128)(2,1)S(1)} %get-tuple-element.52), channel_id=1, source_target_pairs={{0,4},{4,0},{8,12},{12,8},{1,5},{5,1},{9,13},{13,9},{2,6},{6,2},{1... | collective-permute-start | bytes 245768 | tf_op jit(solution)/shard_map/ppermute | solution.py:39

commit v8 on v7

--- a/solution.py
+++ b/solution.py
@@ -255,14 +255,22 @@
     )(field, sibling, weight.reshape(3, 3 * cb, channels))
 
 
-def spatial_grads(grads, grads_sibling, fields, fields_sibling, scale):
+def spatial_grads(grads, grads_sibling, fields, fields_sibling, own_sum, partials, scale):
     _, n_x = sizes()
     ob, ib = grads[0].shape[0], fields[0].shape[0]
     frames = FT * n_x
+    n_p = len(partials)
 
     def body(*refs):
         g_refs, gs_refs, l_refs, ls_refs = (refs[q * n_x : (q + 1) * n_x] for q in range(4))
-        out_hbm, left, right, out, sems = refs[4 * n_x :]
+        own_ref, partial_refs = refs[4 * n_x], refs[4 * n_x + 1 : 4 * n_x + 1 + n_p]
+        out_hbm, latent_hbm, left, right, out, latent, sems = refs[4 * n_x + 1 + n_p :]
+        total = g_refs[0][...].astype(F32) + own_ref[...]
+        for partial_ref in partial_refs:
+            total += partial_ref[...].astype(F32)
+        latent[...] = total.astype(BF)
+        latent_copy = pltpu.make_async_copy(latent, latent_hbm, sems.at[9])
+        latent_copy.start()
         _, _, band = place()
         blank = jnp.zeros((W, ib), BF)
         for j in range(n_x):
@@ -284,20 +292,22 @@
             copies[-1].start()
         for copy in copies:
             copy.wait()
+        latent_copy.wait()
 
     return pl.pallas_call(
         body,
-        out_specs=pl.BlockSpec(memory_space=pltpu.HBM),
-        out_shape=jax.ShapeDtypeStruct((9, ob, ib), F32),
+        out_specs=[pl.BlockSpec(memory_space=pltpu.HBM)] * 2,
+        out_shape=[jax.ShapeDtypeStruct((9, ob, ib), F32), jax.ShapeDtypeStruct((ob, TILE), BF)],
         scratch_shapes=[
             pltpu.VMEM((ob, frames * FRAME), BF),
             pltpu.VMEM((3, frames, FRAME + 2 * W, ib), BF),
             pltpu.VMEM((9, ob, ib), F32),
-            pltpu.SemaphoreType.DMA((9,)),
+            pltpu.VMEM((ob, TILE), BF),
+            pltpu.SemaphoreType.DMA((10,)),
         ],
         compiler_params=pltpu.CompilerParams(vmem_limit_bytes=24 * MIB),
         name="spatial_grads",
-    )(*grads, *grads_sibling, *fields, *fields_sibling)
+    )(*grads, *grads_sibling, *fields, *fields_sibling, own_sum, *partials)
 
 
 def temporal_grads(grads, grads_sibling, fields, fields_sibling, scale):
@@ -394,12 +404,14 @@
 
     grads = [hidden_grad] + grad_ring
     grads_sibling = [grad_sibling] + [swap_band(x) for x in grad_ring]
-    lat_own = after_all(lat_own, partials[0])
-    spatial_grad = spatial_grads(grads, grads_sibling, lat_own, lat_sib, scale)
+    lat_own = after_all(lat_own, partials)
+    spatial_grad, latent_grad = spatial_grads(
+        grads, grads_sibling, lat_own, lat_sib, chunks[0], partials, scale
+    )
 
     hidden_mine = after_all(hidden_mine, chunks)
     before, after = neighbours(jnp.stack(hidden_mine))
-    before, after = after_all((before, after), (spatial_grad, partials[1]))
+    before, after = after_all((before, after), spatial_grad)
     temporal_out = temporal_forward(hidden_mine, before, after, temporal_weight)
 
     hid_own, hid_sib = [block(hidden_mine, own_block)], [block(hidden_mine, sib_block)]
@@ -413,10 +425,8 @@
             both = send(both, "st", RBANDS * j)
             hid_own.append(both[0])
             hid_sib.append(both[1])
-    hid_own = after_all(hid_own, partials[2:])
     temporal_grad = temporal_grads(cots, cots_sibling, hid_own, [swap_band(x) for x in hid_sib], scale)
 
-    latent_grad = total_of(hidden_grad, chunks[0], partials)
     return temporal_out, latent_grad, spatial_grad, temporal_grad
 
 

time: 47.9 us -> 46.7 us (0.975)
  waiting for transfers between devices: 8.78 us -> 5.98 us
  starting transfers between devices: 22.2 us -> 24.5 us
  other arithmetic: 0.89 us -> 0.2 us
    ppermute x16, starting transfers between devices: 20.7 us -> 23.6 us  [send(): return lax.ppermute(data, axis, [(i, (i + by) % n) for i in range(n)])]
    ppermute x16, waiting for transfers between devices: 7.61 us -> 4.78 us  [send(): return lax.ppermute(data, axis, [(i, (i + by) % n) for i in range(n)])]
    convert_element_type x2 -> x1, other arithmetic: 0.74 us -> 0.05 us  [total_of(): return total.astype(BF)]
    ppermute x9, starting transfers between devices: 1.49 us -> 0.9 us  [swap_band(): return lax.ppermute(data, 'st', [(i, i ^ 1) for i in range(n)])]
  transfers between devices with their start and end apart: 25 -> 25, of which waited for: 4 -> 4; matrix products, arithmetic and copies ran while one was open for 2% -> 1% of each run, Pallas kernels for 21% -> 22%
where the time goes in v8:
time: 46.7 us; the launch traced here: 46.5 us
  starting transfers between devices  24.5 us (52%)
  Pallas kernels  12 us (26%)
  waiting for transfers between devices  5.98 us (13%)
  local copies, waits for them, and re-layouts  3.06 us (7%)
  between operations  0.82 us (2%)
    ppermute x16, starting transfers between devices, send(): return lax.ppermute(data, axis, [(i, (i + by) % n) for i in range(n)])  23.6 us
    ppermute x16, waiting for transfers between devices, send(): return lax.ppermute(data, axis, [(i, (i + by) % n) for i in range(n)])  4.78 us
    pallas_call x1, Pallas kernels, spatial_grads(): pl.pallas_call(body, out_specs=[pl.BlockSpec(memory_space=pltpu.HBM)] * 2...  3.11 us
    unnamed x10, local copies, waits for them, and re-layouts  2.99 us
    pallas_call x1, Pallas kernels, spatial_forward(): pl.pallas_call(body, out_shape=jax.ShapeDtypeStruct((cb, TILE), BF), scra...  2.69 us
    pallas_call x1, Pallas kernels, temporal_grads(): pl.pallas_call(body, out_specs=pl.BlockSpec(memory_space=pltpu.HBM), out_...  1.91 us
    pallas_call x1, Pallas kernels, temporal_forward(): pl.pallas_call(body, out_shape=jax.ShapeDtypeStruct((cb, TILE), BF), scra...  1.78 us
    pallas_call x1, Pallas kernels, spatial_backward(): pl.pallas_call(body, out_shape=chunk_shapes(n_ch, cb), scratch_shapes=[pl...  1.62 us
  transfers between devices with their start and end apart: 25, of which 4 were waited for; matrix products, arithmetic and copies ran while one was open for 1% of the time, Pallas kernels for 22%

profile of v8, /device:TPU:0, one launch (start us, length us, event | category | flops | bytes accessed | tf_op | source)
XLA Modules:
  0.0 46.5 jit_solution(4248500459606754691)
XLA Ops:
  0.6 0.0 copy-start.3
  0.6 3.0 %collective-permute-start.3 = (bf16[320,128]{1,0:T(8,128)(2,1)}, bf16[320,128]{1,0:T(8,128)(2,1)S(1)}, u32[]{:S(2)}, u32[]{:S(2)}) collective-permute-start(bf16[320,128]{1,0:T(8,128)(2,1)} %refs_0_.1), channel_id=1, source_target_pairs={{0,8},{4,12},{8,0},{12,4},{1,9},{5,13},{9,1},{13,5},{2,10},{6,14},... | collective-permute-start | bytes 245768 | tf_op jit(solution)/shard_map/ppermute | solution.py:34
  3.6 3.6 %collective-permute-start.2 = (bf16[320,128]{1,0:T(8,128)(2,1)}, bf16[320,128]{1,0:T(8,128)(2,1)S(1)}, u32[]{:S(2)}, u32[]{:S(2)}) collective-permute-start(bf16[320,128]{1,0:T(8,128)(2,1)} %refs_0_.2), channel_id=1, source_target_pairs={{0,3},{1,0},{2,1},{3,2},{4,7},{5,4},{6,5},{7,6},{8,11},{9,8},{10,9... | collective-permute-start | bytes 245768 | tf_op jit(solution)/shard_map/ppermute | solution.py:34
  7.2 0.0 collective-permute-start.1
  7.2 1.0 %collective-permute-start = (bf16[320,128]{1,0:T(8,128)(2,1)}, bf16[320,128]{1,0:T(8,128)(2,1)S(1)}, u32[]{:S(2)}, u32[]{:S(2)}) collective-permute-start(bf16[320,128]{1,0:T(8,128)(2,1)} %refs_0_.2), channel_id=1, source_target_pairs={{0,1},{1,2},{2,3},{3,0},{4,5},{5,6},{6,7},{7,4},{8,9},{9,10},{10,1... | collective-permute-start | bytes 245768 | tf_op jit(solution)/shard_map/ppermute | solution.py:34
  8.3 0.0 collective-permute-start.4
  8.3 0.0 collective-permute-done.3.refs_1_
  8.3 0.0 copy-start.1
  8.3 1.8 %copy-done.1 = bf16[3,320,1280]{2,1,0:T(8,128)(2,1)S(1)} copy-done((bf16[3,320,1280]{2,1,0:T(8,128)(2,1)S(1)}, bf16[3,320,1280]{2,1,0:T(8,128)(2,1)}, u32[]{:S(2)}) %copy-start.1) | copy-done | bytes 2457624
  10.1 1.1 %copy-done.4 = bf16[320,128]{1,0:T(8,128)(2,1)S(1)} copy-done((bf16[320,128]{1,0:T(8,128)(2,1)S(1)}, bf16[320,128]{1,0:T(8,128)(2,1)}, u32[]{:S(2)}) %copy-start.4) | copy-done | bytes 81944
  11.3 0.9 %temporal_backward.1 = (f32[320,128]{1,0:T(8,128)S(1)}, bf16[320,128]{1,0:T(8,128)(2,1)S(1)}, bf16[320,128]{1,0:T(8,128)(2,1)S(1)}, bf16[320,128]{1,0:T(8,128)(2,1)S(1)}, bf16[2,320,128]{2,1,0:T(8,128)(2,1)S(1)}) custom-call(bf16[320,128]{1,0:T(8,128)(2,1)S(1)} %copy-done.4, bf16[320,128]{1,0:T(8,128)(2,1)S(1)} %collective-permute-done.3.refs_1_, ...), custom_call_target="tpu_custom_call" | custom-call | flops 2000000000 | bytes 3000000 | tf_op jit(solution)/shard_map/temporal_backward/pallas_call | solution.py:201
  12.1 2.5 %collective-permute-start.11 = (bf16[320,128]{1,0:T(8,128)(2,1)S(1)}, bf16[320,128]{1,0:T(8,128)(2,1)S(1)}, u32[]{:S(2)}, u32[]{:S(2)}) collective-permute-start(bf16[320,128]{1,0:T(8,128)(2,1)S(1)} %get-tuple-element.29), channel_id=1, source_target_pairs={{0,1},{1,2},{2,3},{3,0},{4,5},{5,6},{6,7},{7,4},{8,9},{9,10},{10,1... | collective-permute-start | bytes 245768 | tf_op jit(solution)/shard_map/ppermute | solution.py:34
  14.7 0.0 collective-permute-done.2.refs_3_
  14.7 0.0 collective-permute-done.1.refs_2_
  14.7 0.0 collective-permute-done.refs_1_
  14.7 0.3 collective-permute-start.5
  14.9 0.3 collective-permute-start.6
  15.2 0.2 collective-permute-start.7
  15.4 0.0 copy-done.3
  15.5 0.0 collective-permute-done.4.refs_4_
  15.5 1.9 %collective-permute-start.12 = (bf16[320,128]{1,0:T(8,128)(2,1)S(1)}, bf16[320,128]{1,0:T(8,128)(2,1)S(1)}, u32[]{:S(2)}, u32[]{:S(2)}) collective-permute-start(bf16[320,128]{1,0:T(8,128)(2,1)S(1)} %get-tuple-element.30), channel_id=1, source_target_pairs={{0,2},{1,3},{2,0},{3,1},{4,6},{5,7},{6,4},{7,5},{8,10},{9,11},{10,... | collective-permute-start | bytes 245768 | tf_op jit(solution)/shard_map/ppermute | solution.py:34
  17.4 0.0 collective-permute-done.5.refs_5_
  17.4 0.8 %collective-permute-start.13 = (bf16[320,128]{1,0:T(8,128)(2,1)S(1)}, bf16[320,128]{1,0:T(8,128)(2,1)S(1)}, u32[]{:S(2)}, u32[]{:S(2)}) collective-permute-start(bf16[320,128]{1,0:T(8,128)(2,1)S(1)} %get-tuple-element.31), channel_id=1, source_target_pairs={{0,3},{1,0},{2,1},{3,2},{4,7},{5,4},{6,5},{7,6},{8,11},{9,8},{10,9... | collective-permute-start | bytes 245768 | tf_op jit(solution)/shard_map/ppermute | solution.py:34
  18.3 0.0 collective-permute-done.6.refs_6_
  18.3 0.0 collective-permute-done.7.refs_7_
  18.3 0.0 copy-done
  18.3 2.7 %spatial_forward.1.refs_0_ = bf16[320,128]{1,0:T(8,128)(2,1)S(1)} custom-call(bf16[320,128]{1,0:T(8,128)(2,1)S(1)} %copy-done.3, bf16[320,128]{1,0:T(8,128)(2,1)S(1)} %collective-permute-done.refs_1_, bf16[320,128]{1,0:T(8,128)(2,1)S(1)} %collective-permute-done.1.refs_2_, bf16[320,128]{1,0:T(8,128)(2,1)S(1)} %collective-permute-done.2.refs_3_, ...), custom_call_target="tpu_custom_call" | custom-call | tf_op jit(solution)/shard_map/spatial_forward/pallas_call | solution.py:133
  21.0 1.8 %collective-permute-start.10 = (bf16[320,128]{1,0:T(8,128)(2,1)S(1)}, bf16[320,128]{1,0:T(8,128)(2,1)S(1)}, u32[]{:S(2)}, u32[]{:S(2)}) collective-permute-start(bf16[320,128]{1,0:T(8,128)(2,1)S(1)} %spatial_forward.1.refs_0_), channel_id=1, source_target_pairs={{0,3},{1,0},{2,1},{3,2},{4,7},{5,4},{6,5},{7,6},{8,11},{9,8},{10,9... | collective-permute-start | bytes 245768 | tf_op jit(solution)/shard_map/ppermute | solution.py:34
  22.8 1.0 %collective-permute-start.9 = (bf16[320,128]{1,0:T(8,128)(2,1)S(1)}, bf16[320,128]{1,0:T(8,128)(2,1)S(1)}, u32[]{:S(2)}, u32[]{:S(2)}) collective-permute-start(bf16[320,128]{1,0:T(8,128)(2,1)S(1)} %spatial_forward.1.refs_0_), channel_id=1, source_target_pairs={{0,2},{1,3},{2,0},{3,1},{4,6},{5,7},{6,4},{7,5},{8,10},{9,11},{10,... | collective-permute-start | bytes 245768 | tf_op jit(solution)/shard_map/ppermute | solution.py:34
  23.7 0.0 collective-permute-done.11
  23.7 0.6 %collective-permute-start.8 = (bf16[320,128]{1,0:T(8,128)(2,1)S(1)}, bf16[320,128]{1,0:T(8,128)(2,1)S(1)}, u32[]{:S(2)}, u32[]{:S(2)}) collective-permute-start(bf16[320,128]{1,0:T(8,128)(2,1)S(1)} %spatial_forward.1.refs_0_), channel_id=1, source_target_pairs={{0,1},{1,2},{2,3},{3,0},{4,5},{5,6},{6,7},{7,4},{8,9},{9,10},{10,1... | collective-permute-start | bytes 245768 | tf_op jit(solution)/shard_map/ppermute | solution.py:34
  24.3 0.0 collective-permute-done.12
  24.3 0.0 collective-permute-done.13
  24.3 0.1 add_convert_fusion.field_ref.refs_0_
  24.4 0.6 %collective-permute-start.16 = (bf16[320,128]{1,0:T(8,128)(2,1)S(1)}, bf16[320,128]{1,0:T(8,128)(2,1)S(1)}, u32[]{:S(2)}, u32[]{:S(2)}) collective-permute-start(bf16[320,128]{1,0:T(8,128)(2,1)S(1)} %add_convert_fusion.field_ref.refs_0_), channel_id=1, source_target_pairs={{0,8},{4,12},{8,0},{12,4},{1,9},{5,13},{9,1},{13,5},{2,10},{6,14},... | collective-permute-start | bytes 245768 | tf_op jit(solution)/shard_map/ppermute | solution.py:34
  25.0 0.0 collective-permute-start.14
  25.1 1.2 %collective-permute-done.14.sibling_ref.refs_2_ = bf16[320,128]{1,0:T(8,128)(2,1)S(1)} collective-permute-done((bf16[320,128]{1,0:T(8,128)(2,1)S(1)}, bf16[320,128]{1,0:T(8,128)(2,1)S(1)}, u32[]{:S(2)}, u32[]{:S(2)}) %collective-permute-start.14) | collective-permute-done | bytes 81952 | tf_op jit(solution)/shard_map/ppermute | solution.py:39
  26.3 1.5 %collective-permute-start.18 = (bf16[2,320,128]{2,1,0:T(8,128)(2,1)S(1)}, bf16[2,320,128]{2,1,0:T(8,128)(2,1)S(1)}, u32[]{:S(2)}, u32[]{:S(2)}) collective-permute-start(bf16[2,320,128]{2,1,0:T(8,128)(2,1)S(1)} %pad_maximum_fusion.3), channel_id=1, source_target_pairs={{0,8},{4,12},{8,0},{12,4},{1,9},{5,13},{9,1},{13,5},{2,10},{6,14},... | collective-permute-start | bytes 491528 | tf_op jit(solution)/shard_map/ppermute | solution.py:34
  27.8 1.6 %spatial_backward.1 = (f32[320,128]{1,0:T(8,128)S(1)}, bf16[320,128]{1,0:T(8,128)(2,1)S(1)}, bf16[320,128]{1,0:T(8,128)(2,1)S(1)}, bf16[320,128]{1,0:T(8,128)(2,1)S(1)}) custom-call(bf16[320,128]{1,0:T(8,128)(2,1)S(1)} %add_convert_fusion.field_ref.refs_0_, bf16[320,128]{1,0:T(8,128)(2,1)S(1)} %collective-permute-done.14.sibling_ref.refs_2_, ...), custom_call_target="tpu_custom_call" | custom-call | tf_op jit(solution)/shard_map/spatial_backward/pallas_call | solution.py:246
  29.4 0.0 collective-permute-done.10.refs_3_
  29.4 2.0 %collective-permute-start.19 = (bf16[320,128]{1,0:T(8,128)(2,1)S(1)}, bf16[320,128]{1,0:T(8,128)(2,1)S(1)}, u32[]{:S(2)}, u32[]{:S(2)}) collective-permute-start(bf16[320,128]{1,0:T(8,128)(2,1)S(1)} %get-tuple-element.38), channel_id=1, source_target_pairs={{0,1},{1,2},{2,3},{3,0},{4,5},{5,6},{6,7},{7,4},{8,9},{9,10},{10,1... | collective-permute-start | bytes 245768 | tf_op jit(solution)/shard_map/ppermute | solution.py:34
  31.4 0.0 collective-permute-done.9.refs_2_
  31.4 1.8 %collective-permute-start.20 = (bf16[320,128]{1,0:T(8,128)(2,1)S(1)}, bf16[320,128]{1,0:T(8,128)(2,1)S(1)}, u32[]{:S(2)}, u32[]{:S(2)}) collective-permute-start(bf16[320,128]{1,0:T(8,128)(2,1)S(1)} %get-tuple-element.39), channel_id=1, source_target_pairs={{0,2},{1,3},{2,0},{3,1},{4,6},{5,7},{6,4},{7,5},{8,10},{9,11},{10,... | collective-permute-start | bytes 245768 | tf_op jit(solution)/shard_map/ppermute | solution.py:34
  33.2 0.0 collective-permute-done.8.refs_1_
  33.3 0.6 %collective-permute-start.15 = (bf16[4,320,128]{2,1,0:T(8,128)(2,1)S(1)}, bf16[4,320,128]{2,1,0:T(8,128)(2,1)S(1)}, u32[]{:S(2)}, u32[]{:S(2)}) collective-permute-start(bf16[4,320,128]{2,1,0:T(8,128)(2,1)S(1)} %pad_maximum_fusion), channel_id=1, source_target_pairs={{0,8},{4,12},{8,0},{12,4},{1,9},{5,13},{9,1},{13,5},{2,10},{6,14},... | collective-permute-start | bytes 983048 | tf_op jit(solution)/shard_map/ppermute | solution.py:34
  33.9 0.0 collective-permute-done.16.refs_1_
  33.9 0.9 %collective-permute-start.21 = (bf16[320,128]{1,0:T(8,128)(2,1)S(1)}, bf16[320,128]{1,0:T(8,128)(2,1)S(1)}, u32[]{:S(2)}, u32[]{:S(2)}) collective-permute-start(bf16[320,128]{1,0:T(8,128)(2,1)S(1)} %get-tuple-element.40), channel_id=1, source_target_pairs={{0,3},{1,0},{2,1},{3,2},{4,7},{5,4},{6,5},{7,6},{8,11},{9,8},{10,9... | collective-permute-start | bytes 245768 | tf_op jit(solution)/shard_map/ppermute | solution.py:34
  34.8 0.0 collective-permute-done.18
  34.8 0.0 collective-permute-start.17
  34.8 1.9 %collective-permute-done.19.refs_9_ = bf16[320,128]{1,0:T(8,128)(2,1)S(1)} collective-permute-done((bf16[320,128]{1,0:T(8,128)(2,1)S(1)}, bf16[320,128]{1,0:T(8,128)(2,1)S(1)}, u32[]{:S(2)}, u32[]{:S(2)}) %collective-permute-start.19) | collective-permute-done | bytes 81952 | tf_op jit(solution)/shard_map/ppermute | solution.py:34
  36.7 0.0 collective-permute-start.22
  36.7 2.4 %collective-permute-done.20.refs_10_ = bf16[320,128]{1,0:T(8,128)(2,1)S(1)} collective-permute-done((bf16[320,128]{1,0:T(8,128)(2,1)S(1)}, bf16[320,128]{1,0:T(8,128)(2,1)S(1)}, u32[]{:S(2)}, u32[]{:S(2)}) %collective-permute-start.20) | collective-permute-done | bytes 81952 | tf_op jit(solution)/shard_map/ppermute | solution.py:34
  39.1 0.0 collective-permute-start.23
  39.1 0.5 %collective-permute-done.21.refs_11_ = bf16[320,128]{1,0:T(8,128)(2,1)S(1)} collective-permute-done((bf16[320,128]{1,0:T(8,128)(2,1)S(1)}, bf16[320,128]{1,0:T(8,128)(2,1)S(1)}, u32[]{:S(2)}, u32[]{:S(2)}) %collective-permute-start.21) | collective-permute-done | bytes 81952 | tf_op jit(solution)/shard_map/ppermute | solution.py:34
  39.6 0.0 collective-permute-done.17.refs_3_
  39.6 3.1 %spatial_grads.1 = (f32[9,320,320]{2,1,0:T(8,128)}, bf16[320,128]{1,0:T(8,128)(2,1)}) custom-call(bf16[320,128]{1,0:T(8,128)(2,1)S(1)} %add_convert_fusion.field_ref.refs_0_, bf16[320,128]{1,0:T(8,128)(2,1)S(1)} %collective-permute-done.16.refs_1_, bf16[320,128]{1,0:T(8,128)(2,1)S(1)} %collective-permute-done.14.sibling_ref.refs_2_, ...), custom_call_target="tpu_custom_call" | custom-call | tf_op jit(solution)/shard_map/spatial_grads/pallas_call | solution.py:297
  42.7 0.0 collective-permute-done.15.refs_4_.refs_5_
  42.7 0.1 collective-permute-start.24
  42.8 0.0 copy-done.2
  42.8 1.8 %temporal_forward.1 = bf16[320,128]{1,0:T(8,128)(2,1)} custom-call(bf16[320,128]{1,0:T(8,128)(2,1)S(1)} %spatial_forward.1.refs_0_, bf16[320,128]{1,0:T(8,128)(2,1)S(1)} %collective-permute-done.8.refs_1_, bf16[320,128]{1,0:T(8,128)(2,1)S(1)} %collective-permute-done.9.refs_2_, bf16[320,128]{1,0:T(8,128)(2,1)S(1)} %collective-permute-done.10.refs_3_, ...), custom_call_target="tpu_custom_call" | custom-call | tf_op jit(solution)/shard_map/temporal_forward/pallas_call | solution.py:161
  44.6 0.0 collective-permute-done.22.refs_1_
  44.6 0.0 collective-permute-done.23.refs_4_
  44.6 0.0 collective-permute-done.24.refs_5_
  44.6 1.9 %temporal_grads.1 = f32[3,320,320]{2,1,0:T(8,128)} custom-call(bf16[2,320,128]{2,1,0:T(8,128)(2,1)S(1)} %get-tuple-element.51.refs_0_, bf16[2,320,128]{2,1,0:T(8,128)(2,1)S(1)} %collective-permute-done.22.refs_1_, bf16[320,128]{1,0:T(8,128)(2,1)S(1)} %get-tuple-element.55.refs_2_, bf16[320,128]{1,0:T(8,128)(2,1)S(1)} %get-tuple-element.53.refs_3_, ...), custom_call_target="tpu_custom_call" | custom-call | tf_op jit(solution)/shard_map/temporal_grads/pallas_call | solution.py:342
  (12 shorter events, 0.2 us)
Async XLA Ops:
  0.6 14.8 %copy-start.3 = (bf16[320,128]{1,0:T(8,128)(2,1)S(1)}, bf16[320,128]{1,0:T(8,128)(2,1)}, u32[]{:S(2)}) copy-start(bf16[320,128]{1,0:T(8,128)(2,1)} %refs_0_.2) | copy-start | bytes 245764
  0.6 7.6 %collective-permute-start.3 = (bf16[320,128]{1,0:T(8,128)(2,1)}, bf16[320,128]{1,0:T(8,128)(2,1)S(1)}, u32[]{:S(2)}, u32[]{:S(2)}) collective-permute-start(bf16[320,128]{1,0:T(8,128)(2,1)} %refs_0_.1), channel_id=1, source_target_pairs={{0,8},{4,12},{8,0},{12,4},{1,9},{5,13},{9,1},{13,5},{2,10},{6,14},... | collective-permute-start | bytes 245768 | tf_op jit(solution)/shard_map/ppermute | solution.py:34
  3.6 11.0 %collective-permute-start.2 = (bf16[320,128]{1,0:T(8,128)(2,1)}, bf16[320,128]{1,0:T(8,128)(2,1)S(1)}, u32[]{:S(2)}, u32[]{:S(2)}) collective-permute-start(bf16[320,128]{1,0:T(8,128)(2,1)} %refs_0_.2), channel_id=1, source_target_pairs={{0,3},{1,0},{2,1},{3,2},{4,7},{5,4},{6,5},{7,6},{8,11},{9,8},{10,9... | collective-permute-start | bytes 245768 | tf_op jit(solution)/shard_map/ppermute | solution.py:34
  7.2 7.4 %collective-permute-start.1 = (bf16[320,128]{1,0:T(8,128)(2,1)}, bf16[320,128]{1,0:T(8,128)(2,1)S(1)}, u32[]{:S(2)}, u32[]{:S(2)}) collective-permute-start(bf16[320,128]{1,0:T(8,128)(2,1)} %refs_0_.2), channel_id=1, source_target_pairs={{0,2},{1,3},{2,0},{3,1},{4,6},{5,7},{6,4},{7,5},{8,10},{9,11},{10,... | collective-permute-start | bytes 245768 | tf_op jit(solution)/shard_map/ppermute | solution.py:34
  7.2 7.4 %collective-permute-start = (bf16[320,128]{1,0:T(8,128)(2,1)}, bf16[320,128]{1,0:T(8,128)(2,1)S(1)}, u32[]{:S(2)}, u32[]{:S(2)}) collective-permute-start(bf16[320,128]{1,0:T(8,128)(2,1)} %refs_0_.2), channel_id=1, source_target_pairs={{0,1},{1,2},{2,3},{3,0},{4,5},{5,6},{6,7},{7,4},{8,9},{9,10},{10,1... | collective-permute-start | bytes 245768 | tf_op jit(solution)/shard_map/ppermute | solution.py:34
  8.3 7.2 %collective-permute-start.4 = (bf16[320,128]{1,0:T(8,128)(2,1)}, bf16[320,128]{1,0:T(8,128)(2,1)S(1)}, u32[]{:S(2)}, u32[]{:S(2)}) collective-permute-start(bf16[320,128]{1,0:T(8,128)(2,1)} %refs_0_.2), channel_id=1, source_target_pairs={{0,4},{4,0},{8,12},{12,8},{1,5},{5,1},{9,13},{13,9},{2,6},{6,2},{1... | collective-permute-start | bytes 245768 | tf_op jit(solution)/shard_map/ppermute | solution.py:39
  8.3 10.0 %copy-start = (bf16[9,320,1280]{2,1,0:T(8,128)(2,1)S(1)}, bf16[9,320,1280]{2,1,0:T(8,128)(2,1)}, u32[]{:S(2)}) copy-start(bf16[9,320,1280]{2,1,0:T(8,128)(2,1)} %refs_8_.1) | copy-start | bytes 22118404
  8.3 1.8 %copy-start.1 = (bf16[3,320,1280]{2,1,0:T(8,128)(2,1)S(1)}, bf16[3,320,1280]{2,1,0:T(8,128)(2,1)}, u32[]{:S(2)}) copy-start(bf16[3,320,1280]{2,1,0:T(8,128)(2,1)} %refs_6_.1) | copy-start | bytes 7372804
  10.1 1.1 %copy-start.4 = (bf16[320,128]{1,0:T(8,128)(2,1)S(1)}, bf16[320,128]{1,0:T(8,128)(2,1)}, u32[]{:S(2)}) copy-start(bf16[320,128]{1,0:T(8,128)(2,1)} %refs_0_.1) | copy-start | bytes 245764
  12.1 11.6 %collective-permute-start.11 = (bf16[320,128]{1,0:T(8,128)(2,1)S(1)}, bf16[320,128]{1,0:T(8,128)(2,1)S(1)}, u32[]{:S(2)}, u32[]{:S(2)}) collective-permute-start(bf16[320,128]{1,0:T(8,128)(2,1)S(1)} %get-tuple-element.29), channel_id=1, source_target_pairs={{0,1},{1,2},{2,3},{3,0},{4,5},{5,6},{6,7},{7,4},{8,9},{9,10},{10,1... | collective-permute-start | bytes 245768 | tf_op jit(solution)/shard_map/ppermute | solution.py:34
  14.7 2.8 %collective-permute-start.5 = (bf16[320,128]{1,0:T(8,128)(2,1)S(1)}, bf16[320,128]{1,0:T(8,128)(2,1)S(1)}, u32[]{:S(2)}, u32[]{:S(2)}) collective-permute-start(bf16[320,128]{1,0:T(8,128)(2,1)S(1)} %collective-permute-done.refs_1_), channel_id=1, source_target_pairs={{0,4},{4,0},{8,12},{12,8},{1,5},{5,1},{9,13},{13,9},{2,6},{6,2},{1... | collective-permute-start | bytes 245768 | tf_op jit(solution)/shard_map/ppermute | solution.py:39
  14.9 3.3 %collective-permute-start.6 = (bf16[320,128]{1,0:T(8,128)(2,1)S(1)}, bf16[320,128]{1,0:T(8,128)(2,1)S(1)}, u32[]{:S(2)}, u32[]{:S(2)}) collective-permute-start(bf16[320,128]{1,0:T(8,128)(2,1)S(1)} %collective-permute-done.1.refs_2_), channel_id=1, source_target_pairs={{0,4},{4,0},{8,12},{12,8},{1,5},{5,1},{9,13},{13,9},{2,6},{6,2},{1... | collective-permute-start | bytes 245768 | tf_op jit(solution)/shard_map/ppermute | solution.py:39
  15.2 3.0 %collective-permute-start.7 = (bf16[320,128]{1,0:T(8,128)(2,1)S(1)}, bf16[320,128]{1,0:T(8,128)(2,1)S(1)}, u32[]{:S(2)}, u32[]{:S(2)}) collective-permute-start(bf16[320,128]{1,0:T(8,128)(2,1)S(1)} %collective-permute-done.2.refs_3_), channel_id=1, source_target_pairs={{0,4},{4,0},{8,12},{12,8},{1,5},{5,1},{9,13},{13,9},{2,6},{6,2},{1... | collective-permute-start | bytes 245768 | tf_op jit(solution)/shard_map/ppermute | solution.py:39
  15.5 8.8 %collective-permute-start.12 = (bf16[320,128]{1,0:T(8,128)(2,1)S(1)}, bf16[320,128]{1,0:T(8,128)(2,1)S(1)}, u32[]{:S(2)}, u32[]{:S(2)}) collective-permute-start(bf16[320,128]{1,0:T(8,128)(2,1)S(1)} %get-tuple-element.30), channel_id=1, source_target_pairs={{0,2},{1,3},{2,0},{3,1},{4,6},{5,7},{6,4},{7,5},{8,10},{9,11},{10,... | collective-permute-start | bytes 245768 | tf_op jit(solution)/shard_map/ppermute | solution.py:34
  17.4 6.9 %collective-permute-start.13 = (bf16[320,128]{1,0:T(8,128)(2,1)S(1)}, bf16[320,128]{1,0:T(8,128)(2,1)S(1)}, u32[]{:S(2)}, u32[]{:S(2)}) collective-permute-start(bf16[320,128]{1,0:T(8,128)(2,1)S(1)} %get-tuple-element.31), channel_id=1, source_target_pairs={{0,3},{1,0},{2,1},{3,2},{4,7},{5,4},{6,5},{7,6},{8,11},{9,8},{10,9... | collective-permute-start | bytes 245768 | tf_op jit(solution)/shard_map/ppermute | solution.py:34
  21.0 8.4 %collective-permute-start.10 = (bf16[320,128]{1,0:T(8,128)(2,1)S(1)}, bf16[320,128]{1,0:T(8,128)(2,1)S(1)}, u32[]{:S(2)}, u32[]{:S(2)}) collective-permute-start(bf16[320,128]{1,0:T(8,128)(2,1)S(1)} %spatial_forward.1.refs_0_), channel_id=1, source_target_pairs={{0,3},{1,0},{2,1},{3,2},{4,7},{5,4},{6,5},{7,6},{8,11},{9,8},{10,9... | collective-permute-start | bytes 245768 | tf_op jit(solution)/shard_map/ppermute | solution.py:34
  22.8 8.6 %collective-permute-start.9 = (bf16[320,128]{1,0:T(8,128)(2,1)S(1)}, bf16[320,128]{1,0:T(8,128)(2,1)S(1)}, u32[]{:S(2)}, u32[]{:S(2)}) collective-permute-start(bf16[320,128]{1,0:T(8,128)(2,1)S(1)} %spatial_forward.1.refs_0_), channel_id=1, source_target_pairs={{0,2},{1,3},{2,0},{3,1},{4,6},{5,7},{6,4},{7,5},{8,10},{9,11},{10,... | collective-permute-start | bytes 245768 | tf_op jit(solution)/shard_map/ppermute | solution.py:34
  23.7 9.5 %collective-permute-start.8 = (bf16[320,128]{1,0:T(8,128)(2,1)S(1)}, bf16[320,128]{1,0:T(8,128)(2,1)S(1)}, u32[]{:S(2)}, u32[]{:S(2)}) collective-permute-start(bf16[320,128]{1,0:T(8,128)(2,1)S(1)} %spatial_forward.1.refs_0_), channel_id=1, source_target_pairs={{0,1},{1,2},{2,3},{3,0},{4,5},{5,6},{6,7},{7,4},{8,9},{9,10},{10,1... | collective-permute-start | bytes 245768 | tf_op jit(solution)/shard_map/ppermute | solution.py:34
  24.4 9.5 %collective-permute-start.16 = (bf16[320,128]{1,0:T(8,128)(2,1)S(1)}, bf16[320,128]{1,0:T(8,128)(2,1)S(1)}, u32[]{:S(2)}, u32[]{:S(2)}) collective-permute-start(bf16[320,128]{1,0:T(8,128)(2,1)S(1)} %add_convert_fusion.field_ref.refs_0_), channel_id=1, source_target_pairs={{0,8},{4,12},{8,0},{12,4},{1,9},{5,13},{9,1},{13,5},{2,10},{6,14},... | collective-permute-start | bytes 245768 | tf_op jit(solution)/shard_map/ppermute | solution.py:34
  25.0 1.3 %collective-permute-start.14 = (bf16[320,128]{1,0:T(8,128)(2,1)S(1)}, bf16[320,128]{1,0:T(8,128)(2,1)S(1)}, u32[]{:S(2)}, u32[]{:S(2)}) collective-permute-start(bf16[320,128]{1,0:T(8,128)(2,1)S(1)} %add_convert_fusion.field_ref.refs_0_), channel_id=1, source_target_pairs={{0,4},{4,0},{8,12},{12,8},{1,5},{5,1},{9,13},{13,9},{2,6},{6,2},{1... | collective-permute-start | bytes 245768 | tf_op jit(solution)/shard_map/ppermute | solution.py:39
  26.3 8.5 %collective-permute-start.18 = (bf16[2,320,128]{2,1,0:T(8,128)(2,1)S(1)}, bf16[2,320,128]{2,1,0:T(8,128)(2,1)S(1)}, u32[]{:S(2)}, u32[]{:S(2)}) collective-permute-start(bf16[2,320,128]{2,1,0:T(8,128)(2,1)S(1)} %pad_maximum_fusion.3), channel_id=1, source_target_pairs={{0,8},{4,12},{8,0},{12,4},{1,9},{5,13},{9,1},{13,5},{2,10},{6,14},... | collective-permute-start | bytes 491528 | tf_op jit(solution)/shard_map/ppermute | solution.py:34
  27.8 15.1 %copy-start.2 = (bf16[3,320,1280]{2,1,0:T(8,128)(2,1)S(1)}, bf16[3,320,1280]{2,1,0:T(8,128)(2,1)}, u32[]{:S(2)}) copy-start(bf16[3,320,1280]{2,1,0:T(8,128)(2,1)} %refs_6_.1) | copy-start | bytes 7372804
  29.4 7.3 %collective-permute-start.19 = (bf16[320,128]{1,0:T(8,128)(2,1)S(1)}, bf16[320,128]{1,0:T(8,128)(2,1)S(1)}, u32[]{:S(2)}, u32[]{:S(2)}) collective-permute-start(bf16[320,128]{1,0:T(8,128)(2,1)S(1)} %get-tuple-element.38), channel_id=1, source_target_pairs={{0,1},{1,2},{2,3},{3,0},{4,5},{5,6},{6,7},{7,4},{8,9},{9,10},{10,1... | collective-permute-start | bytes 245768 | tf_op jit(solution)/shard_map/ppermute | solution.py:34
  31.4 7.7 %collective-permute-start.20 = (bf16[320,128]{1,0:T(8,128)(2,1)S(1)}, bf16[320,128]{1,0:T(8,128)(2,1)S(1)}, u32[]{:S(2)}, u32[]{:S(2)}) collective-permute-start(bf16[320,128]{1,0:T(8,128)(2,1)S(1)} %get-tuple-element.39), channel_id=1, source_target_pairs={{0,2},{1,3},{2,0},{3,1},{4,6},{5,7},{6,4},{7,5},{8,10},{9,11},{10,... | collective-permute-start | bytes 245768 | tf_op jit(solution)/shard_map/ppermute | solution.py:34
  33.3 9.4 %collective-permute-start.15 = (bf16[4,320,128]{2,1,0:T(8,128)(2,1)S(1)}, bf16[4,320,128]{2,1,0:T(8,128)(2,1)S(1)}, u32[]{:S(2)}, u32[]{:S(2)}) collective-permute-start(bf16[4,320,128]{2,1,0:T(8,128)(2,1)S(1)} %pad_maximum_fusion), channel_id=1, source_target_pairs={{0,8},{4,12},{8,0},{12,4},{1,9},{5,13},{9,1},{13,5},{2,10},{6,14},... | collective-permute-start | bytes 983048 | tf_op jit(solution)/shard_map/ppermute | solution.py:34
  33.9 5.6 %collective-permute-start.21 = (bf16[320,128]{1,0:T(8,128)(2,1)S(1)}, bf16[320,128]{1,0:T(8,128)(2,1)S(1)}, u32[]{:S(2)}, u32[]{:S(2)}) collective-permute-start(bf16[320,128]{1,0:T(8,128)(2,1)S(1)} %get-tuple-element.40), channel_id=1, source_target_pairs={{0,3},{1,0},{2,1},{3,2},{4,7},{5,4},{6,5},{7,6},{8,11},{9,8},{10,9... | collective-permute-start | bytes 245768 | tf_op jit(solution)/shard_map/ppermute | solution.py:34
  34.8 4.8 %collective-permute-start.17 = (bf16[320,128]{1,0:T(8,128)(2,1)S(1)}, bf16[320,128]{1,0:T(8,128)(2,1)S(1)}, u32[]{:S(2)}, u32[]{:S(2)}) collective-permute-start(bf16[320,128]{1,0:T(8,128)(2,1)S(1)} %collective-permute-done.16.refs_1_), channel_id=1, source_target_pairs={{0,4},{4,0},{8,12},{12,8},{1,5},{5,1},{9,13},{13,9},{2,6},{6,2},{1... | collective-permute-start | bytes 245768 | tf_op jit(solution)/shard_map/ppermute | solution.py:39
  36.7 7.9 %collective-permute-start.22 = (bf16[2,320,128]{2,1,0:T(8,128)(2,1)S(1)}, bf16[2,320,128]{2,1,0:T(8,128)(2,1)S(1)}, u32[]{:S(2)}, u32[]{:S(2)}) collective-permute-start(bf16[2,320,128]{2,1,0:T(8,128)(2,1)S(1)} %get-tuple-element.51.refs_0_), channel_id=1, source_target_pairs={{0,4},{4,0},{8,12},{12,8},{1,5},{5,1},{9,13},{13,9},{2,6},{6,2},{1... | collective-permute-start | bytes 491528 | tf_op jit(solution)/shard_map/ppermute | solution.py:39
  39.1 5.5 %collective-permute-start.23 = (bf16[320,128]{1,0:T(8,128)(2,1)S(1)}, bf16[320,128]{1,0:T(8,128)(2,1)S(1)}, u32[]{:S(2)}, u32[]{:S(2)}) collective-permute-start(bf16[320,128]{1,0:T(8,128)(2,1)S(1)} %get-tuple-element.54), channel_id=1, source_target_pairs={{0,4},{4,0},{8,12},{12,8},{1,5},{5,1},{9,13},{13,9},{2,6},{6,2},{1... | collective-permute-start | bytes 245768 | tf_op jit(solution)/shard_map/ppermute | solution.py:39
  42.7 1.9 %collective-permute-start.24 = (bf16[320,128]{1,0:T(8,128)(2,1)S(1)}, bf16[320,128]{1,0:T(8,128)(2,1)S(1)}, u32[]{:S(2)}, u32[]{:S(2)}) collective-permute-start(bf16[320,128]{1,0:T(8,128)(2,1)S(1)} %get-tuple-element.52), channel_id=1, source_target_pairs={{0,4},{4,0},{8,12},{12,8},{1,5},{5,1},{9,13},{13,9},{2,6},{6,2},{1... | collective-permute-start | bytes 245768 | tf_op jit(solution)/shard_map/ppermute | solution.py:39

commit v9 on v8

--- a/solution.py
+++ b/solution.py
@@ -75,14 +75,14 @@
     first = jnp.where(band == 0, own, sibling)
     second = jnp.where(band == 0, sibling, own)
     low = lanes(first.shape) < HALF
-    return jnp.where(low, first, roll(second, HALF)), jnp.where(low, roll(first, HALF), second)
+    crossed = roll(jnp.where(low, second, first), HALF)
+    return jnp.where(low, first, crossed), jnp.where(low, crossed, second)
 
 
 def tile_of(frame0, frame1, band):
     low = lanes(frame0.shape) < HALF
-    upper = jnp.where(low, frame0, roll(frame1, HALF))
-    lower = jnp.where(low, roll(frame0, HALF), frame1)
-    return jnp.where(band == 0, upper, lower)
+    moved = roll(jnp.where(band == 0, frame1, frame0), HALF)
+    return jnp.where(band == 0, jnp.where(low, frame0, moved), jnp.where(low, moved, frame1))
 
 
 def time_pieces(own, before, after, m, n_x):

time: 46.7 us -> 46.6 us (level)
  transfers between devices with their start and end apart: 25 -> 25, of which waited for: 4 -> 5; matrix products, arithmetic and copies ran while one was open for 1% -> 1% of each run, Pallas kernels for 22% -> 21%
where the time goes in v9:
time: 46.6 us; the launch traced here: 46.4 us
  starting transfers between devices  24.4 us (52%)
  Pallas kernels  11.9 us (26%)
  waiting for transfers between devices  6.06 us (13%)
  local copies, waits for them, and re-layouts  3.06 us (7%)
  between operations  0.81 us (2%)
    ppermute x16, starting transfers between devices, send(): return lax.ppermute(data, axis, [(i, (i + by) % n) for i in range(n)])  23.5 us
    ppermute x16, waiting for transfers between devices, send(): return lax.ppermute(data, axis, [(i, (i + by) % n) for i in range(n)])  4.87 us
    pallas_call x1, Pallas kernels, spatial_grads(): pl.pallas_call(body, out_specs=[pl.BlockSpec(memory_space=pltpu.HBM)] * 2...  3.05 us
    unnamed x10, local copies, waits for them, and re-layouts  2.99 us
    pallas_call x1, Pallas kernels, spatial_forward(): pl.pallas_call(body, out_shape=jax.ShapeDtypeStruct((cb, TILE), BF), scra...  2.59 us
    pallas_call x1, Pallas kernels, temporal_grads(): pl.pallas_call(body, out_specs=pl.BlockSpec(memory_space=pltpu.HBM), out_...  1.95 us
    pallas_call x1, Pallas kernels, temporal_forward(): pl.pallas_call(body, out_shape=jax.ShapeDtypeStruct((cb, TILE), BF), scra...  1.78 us
    pallas_call x1, Pallas kernels, spatial_backward(): pl.pallas_call(body, out_shape=chunk_shapes(n_ch, cb), scratch_shapes=[pl...  1.64 us
  transfers between devices with their start and end apart: 25, of which 5 were waited for; matrix products, arithmetic and copies ran while one was open for 1% of the time, Pallas kernels for 21%

profile of v9, /device:TPU:0, one launch (start us, length us, event | category | flops | bytes accessed | tf_op | source)
XLA Modules:
  0.0 46.4 jit_solution(16706271372827976558)
XLA Ops:
  0.6 0.0 copy-start.3
  0.6 3.0 %collective-permute-start.3 = (bf16[320,128]{1,0:T(8,128)(2,1)}, bf16[320,128]{1,0:T(8,128)(2,1)S(1)}, u32[]{:S(2)}, u32[]{:S(2)}) collective-permute-start(bf16[320,128]{1,0:T(8,128)(2,1)} %refs_0_.1), channel_id=1, source_target_pairs={{0,8},{4,12},{8,0},{12,4},{1,9},{5,13},{9,1},{13,5},{2,10},{6,14},... | collective-permute-start | bytes 245768 | tf_op jit(solution)/shard_map/ppermute | solution.py:34
  3.6 3.6 %collective-permute-start.2 = (bf16[320,128]{1,0:T(8,128)(2,1)}, bf16[320,128]{1,0:T(8,128)(2,1)S(1)}, u32[]{:S(2)}, u32[]{:S(2)}) collective-permute-start(bf16[320,128]{1,0:T(8,128)(2,1)} %refs_0_.2), channel_id=1, source_target_pairs={{0,3},{1,0},{2,1},{3,2},{4,7},{5,4},{6,5},{7,6},{8,11},{9,8},{10,9... | collective-permute-start | bytes 245768 | tf_op jit(solution)/shard_map/ppermute | solution.py:34
  7.2 0.0 collective-permute-start.1
  7.2 1.0 %collective-permute-start = (bf16[320,128]{1,0:T(8,128)(2,1)}, bf16[320,128]{1,0:T(8,128)(2,1)S(1)}, u32[]{:S(2)}, u32[]{:S(2)}) collective-permute-start(bf16[320,128]{1,0:T(8,128)(2,1)} %refs_0_.2), channel_id=1, source_target_pairs={{0,1},{1,2},{2,3},{3,0},{4,5},{5,6},{6,7},{7,4},{8,9},{9,10},{10,1... | collective-permute-start | bytes 245768 | tf_op jit(solution)/shard_map/ppermute | solution.py:34
  8.3 0.0 collective-permute-start.4
  8.3 0.0 collective-permute-done.3.refs_1_
  8.3 0.0 copy-start.1
  8.3 1.8 %copy-done.1 = bf16[3,320,1280]{2,1,0:T(8,128)(2,1)S(1)} copy-done((bf16[3,320,1280]{2,1,0:T(8,128)(2,1)S(1)}, bf16[3,320,1280]{2,1,0:T(8,128)(2,1)}, u32[]{:S(2)}) %copy-start.1) | copy-done | bytes 2457624
  10.1 1.1 %copy-done.4 = bf16[320,128]{1,0:T(8,128)(2,1)S(1)} copy-done((bf16[320,128]{1,0:T(8,128)(2,1)S(1)}, bf16[320,128]{1,0:T(8,128)(2,1)}, u32[]{:S(2)}) %copy-start.4) | copy-done | bytes 81944
  11.3 0.9 %temporal_backward.1 = (f32[320,128]{1,0:T(8,128)S(1)}, bf16[320,128]{1,0:T(8,128)(2,1)S(1)}, bf16[320,128]{1,0:T(8,128)(2,1)S(1)}, bf16[320,128]{1,0:T(8,128)(2,1)S(1)}, bf16[2,320,128]{2,1,0:T(8,128)(2,1)S(1)}) custom-call(bf16[320,128]{1,0:T(8,128)(2,1)S(1)} %copy-done.4, bf16[320,128]{1,0:T(8,128)(2,1)S(1)} %collective-permute-done.3.refs_1_, ...), custom_call_target="tpu_custom_call" | custom-call | flops 2000000000 | bytes 3000000 | tf_op jit(solution)/shard_map/temporal_backward/pallas_call | solution.py:201
  12.1 2.5 %collective-permute-start.11 = (bf16[320,128]{1,0:T(8,128)(2,1)S(1)}, bf16[320,128]{1,0:T(8,128)(2,1)S(1)}, u32[]{:S(2)}, u32[]{:S(2)}) collective-permute-start(bf16[320,128]{1,0:T(8,128)(2,1)S(1)} %get-tuple-element.29), channel_id=1, source_target_pairs={{0,1},{1,2},{2,3},{3,0},{4,5},{5,6},{6,7},{7,4},{8,9},{9,10},{10,1... | collective-permute-start | bytes 245768 | tf_op jit(solution)/shard_map/ppermute | solution.py:34
  14.7 0.0 collective-permute-done.2.refs_3_
  14.7 0.0 collective-permute-done.1.refs_2_
  14.7 0.0 collective-permute-done.refs_1_
  14.7 0.3 collective-permute-start.5
  14.9 0.3 collective-permute-start.6
  15.2 0.2 collective-permute-start.7
  15.4 0.0 copy-done.3
  15.5 0.0 collective-permute-done.4.refs_4_
  15.5 1.9 %collective-permute-start.12 = (bf16[320,128]{1,0:T(8,128)(2,1)S(1)}, bf16[320,128]{1,0:T(8,128)(2,1)S(1)}, u32[]{:S(2)}, u32[]{:S(2)}) collective-permute-start(bf16[320,128]{1,0:T(8,128)(2,1)S(1)} %get-tuple-element.30), channel_id=1, source_target_pairs={{0,2},{1,3},{2,0},{3,1},{4,6},{5,7},{6,4},{7,5},{8,10},{9,11},{10,... | collective-permute-start | bytes 245768 | tf_op jit(solution)/shard_map/ppermute | solution.py:34
  17.4 0.0 collective-permute-done.5.refs_5_
  17.4 0.8 %collective-permute-start.13 = (bf16[320,128]{1,0:T(8,128)(2,1)S(1)}, bf16[320,128]{1,0:T(8,128)(2,1)S(1)}, u32[]{:S(2)}, u32[]{:S(2)}) collective-permute-start(bf16[320,128]{1,0:T(8,128)(2,1)S(1)} %get-tuple-element.31), channel_id=1, source_target_pairs={{0,3},{1,0},{2,1},{3,2},{4,7},{5,4},{6,5},{7,6},{8,11},{9,8},{10,9... | collective-permute-start | bytes 245768 | tf_op jit(solution)/shard_map/ppermute | solution.py:34
  18.3 0.0 collective-permute-done.6.refs_6_
  18.3 0.0 collective-permute-done.7.refs_7_
  18.3 0.0 copy-done
  18.3 2.6 %spatial_forward.1.refs_0_ = bf16[320,128]{1,0:T(8,128)(2,1)S(1)} custom-call(bf16[320,128]{1,0:T(8,128)(2,1)S(1)} %copy-done.3, bf16[320,128]{1,0:T(8,128)(2,1)S(1)} %collective-permute-done.refs_1_, bf16[320,128]{1,0:T(8,128)(2,1)S(1)} %collective-permute-done.1.refs_2_, bf16[320,128]{1,0:T(8,128)(2,1)S(1)} %collective-permute-done.2.refs_3_, ...), custom_call_target="tpu_custom_call" | custom-call | tf_op jit(solution)/shard_map/spatial_forward/pallas_call | solution.py:133
  20.9 1.8 %collective-permute-start.10 = (bf16[320,128]{1,0:T(8,128)(2,1)S(1)}, bf16[320,128]{1,0:T(8,128)(2,1)S(1)}, u32[]{:S(2)}, u32[]{:S(2)}) collective-permute-start(bf16[320,128]{1,0:T(8,128)(2,1)S(1)} %spatial_forward.1.refs_0_), channel_id=1, source_target_pairs={{0,3},{1,0},{2,1},{3,2},{4,7},{5,4},{6,5},{7,6},{8,11},{9,8},{10,9... | collective-permute-start | bytes 245768 | tf_op jit(solution)/shard_map/ppermute | solution.py:34
  22.7 1.0 %collective-permute-start.9 = (bf16[320,128]{1,0:T(8,128)(2,1)S(1)}, bf16[320,128]{1,0:T(8,128)(2,1)S(1)}, u32[]{:S(2)}, u32[]{:S(2)}) collective-permute-start(bf16[320,128]{1,0:T(8,128)(2,1)S(1)} %spatial_forward.1.refs_0_), channel_id=1, source_target_pairs={{0,2},{1,3},{2,0},{3,1},{4,6},{5,7},{6,4},{7,5},{8,10},{9,11},{10,... | collective-permute-start | bytes 245768 | tf_op jit(solution)/shard_map/ppermute | solution.py:34
  23.6 0.0 collective-permute-done.11
  23.6 0.6 %collective-permute-start.8 = (bf16[320,128]{1,0:T(8,128)(2,1)S(1)}, bf16[320,128]{1,0:T(8,128)(2,1)S(1)}, u32[]{:S(2)}, u32[]{:S(2)}) collective-permute-start(bf16[320,128]{1,0:T(8,128)(2,1)S(1)} %spatial_forward.1.refs_0_), channel_id=1, source_target_pairs={{0,1},{1,2},{2,3},{3,0},{4,5},{5,6},{6,7},{7,4},{8,9},{9,10},{10,1... | collective-permute-start | bytes 245768 | tf_op jit(solution)/shard_map/ppermute | solution.py:34
  24.2 0.0 collective-permute-done.12
  24.2 0.0 collective-permute-done.13
  24.2 0.1 add_convert_fusion.field_ref.refs_0_
  24.3 0.6 %collective-permute-start.16 = (bf16[320,128]{1,0:T(8,128)(2,1)S(1)}, bf16[320,128]{1,0:T(8,128)(2,1)S(1)}, u32[]{:S(2)}, u32[]{:S(2)}) collective-permute-start(bf16[320,128]{1,0:T(8,128)(2,1)S(1)} %add_convert_fusion.field_ref.refs_0_), channel_id=1, source_target_pairs={{0,8},{4,12},{8,0},{12,4},{1,9},{5,13},{9,1},{13,5},{2,10},{6,14},... | collective-permute-start | bytes 245768 | tf_op jit(solution)/shard_map/ppermute | solution.py:34
  24.9 0.0 collective-permute-start.14
  25.0 1.2 %collective-permute-done.14.sibling_ref.refs_2_ = bf16[320,128]{1,0:T(8,128)(2,1)S(1)} collective-permute-done((bf16[320,128]{1,0:T(8,128)(2,1)S(1)}, bf16[320,128]{1,0:T(8,128)(2,1)S(1)}, u32[]{:S(2)}, u32[]{:S(2)}) %collective-permute-start.14) | collective-permute-done | bytes 81952 | tf_op jit(solution)/shard_map/ppermute | solution.py:39
  26.2 1.5 %collective-permute-start.18 = (bf16[2,320,128]{2,1,0:T(8,128)(2,1)S(1)}, bf16[2,320,128]{2,1,0:T(8,128)(2,1)S(1)}, u32[]{:S(2)}, u32[]{:S(2)}) collective-permute-start(bf16[2,320,128]{2,1,0:T(8,128)(2,1)S(1)} %pad_maximum_fusion.3), channel_id=1, source_target_pairs={{0,8},{4,12},{8,0},{12,4},{1,9},{5,13},{9,1},{13,5},{2,10},{6,14},... | collective-permute-start | bytes 491528 | tf_op jit(solution)/shard_map/ppermute | solution.py:34
  27.7 1.6 %spatial_backward.1 = (f32[320,128]{1,0:T(8,128)S(1)}, bf16[320,128]{1,0:T(8,128)(2,1)S(1)}, bf16[320,128]{1,0:T(8,128)(2,1)S(1)}, bf16[320,128]{1,0:T(8,128)(2,1)S(1)}) custom-call(bf16[320,128]{1,0:T(8,128)(2,1)S(1)} %add_convert_fusion.field_ref.refs_0_, bf16[320,128]{1,0:T(8,128)(2,1)S(1)} %collective-permute-done.14.sibling_ref.refs_2_, ...), custom_call_target="tpu_custom_call" | custom-call | tf_op jit(solution)/shard_map/spatial_backward/pallas_call | solution.py:246
  29.3 0.0 collective-permute-done.10.refs_3_
  29.3 2.0 %collective-permute-start.19 = (bf16[320,128]{1,0:T(8,128)(2,1)S(1)}, bf16[320,128]{1,0:T(8,128)(2,1)S(1)}, u32[]{:S(2)}, u32[]{:S(2)}) collective-permute-start(bf16[320,128]{1,0:T(8,128)(2,1)S(1)} %get-tuple-element.38), channel_id=1, source_target_pairs={{0,1},{1,2},{2,3},{3,0},{4,5},{5,6},{6,7},{7,4},{8,9},{9,10},{10,1... | collective-permute-start | bytes 245768 | tf_op jit(solution)/shard_map/ppermute | solution.py:34
  31.3 0.1 collective-permute-done.9.refs_2_
  31.4 1.8 %collective-permute-start.20 = (bf16[320,128]{1,0:T(8,128)(2,1)S(1)}, bf16[320,128]{1,0:T(8,128)(2,1)S(1)}, u32[]{:S(2)}, u32[]{:S(2)}) collective-permute-start(bf16[320,128]{1,0:T(8,128)(2,1)S(1)} %get-tuple-element.39), channel_id=1, source_target_pairs={{0,2},{1,3},{2,0},{3,1},{4,6},{5,7},{6,4},{7,5},{8,10},{9,11},{10,... | collective-permute-start | bytes 245768 | tf_op jit(solution)/shard_map/ppermute | solution.py:34
  33.2 0.0 collective-permute-done.8.refs_1_
  33.2 0.6 %collective-permute-start.15 = (bf16[4,320,128]{2,1,0:T(8,128)(2,1)S(1)}, bf16[4,320,128]{2,1,0:T(8,128)(2,1)S(1)}, u32[]{:S(2)}, u32[]{:S(2)}) collective-permute-start(bf16[4,320,128]{2,1,0:T(8,128)(2,1)S(1)} %pad_maximum_fusion), channel_id=1, source_target_pairs={{0,8},{4,12},{8,0},{12,4},{1,9},{5,13},{9,1},{13,5},{2,10},{6,14},... | collective-permute-start | bytes 983048 | tf_op jit(solution)/shard_map/ppermute | solution.py:34
  33.8 0.0 collective-permute-done.16.refs_1_
  33.8 0.9 %collective-permute-start.21 = (bf16[320,128]{1,0:T(8,128)(2,1)S(1)}, bf16[320,128]{1,0:T(8,128)(2,1)S(1)}, u32[]{:S(2)}, u32[]{:S(2)}) collective-permute-start(bf16[320,128]{1,0:T(8,128)(2,1)S(1)} %get-tuple-element.40), channel_id=1, source_target_pairs={{0,3},{1,0},{2,1},{3,2},{4,7},{5,4},{6,5},{7,6},{8,11},{9,8},{10,9... | collective-permute-start | bytes 245768 | tf_op jit(solution)/shard_map/ppermute | solution.py:34
  34.7 0.0 collective-permute-done.18
  34.7 0.0 collective-permute-start.17
  34.7 1.9 %collective-permute-done.19.refs_9_ = bf16[320,128]{1,0:T(8,128)(2,1)S(1)} collective-permute-done((bf16[320,128]{1,0:T(8,128)(2,1)S(1)}, bf16[320,128]{1,0:T(8,128)(2,1)S(1)}, u32[]{:S(2)}, u32[]{:S(2)}) %collective-permute-start.19) | collective-permute-done | bytes 81952 | tf_op jit(solution)/shard_map/ppermute | solution.py:34
  36.6 0.0 collective-permute-start.22
  36.6 2.4 %collective-permute-done.20.refs_10_ = bf16[320,128]{1,0:T(8,128)(2,1)S(1)} collective-permute-done((bf16[320,128]{1,0:T(8,128)(2,1)S(1)}, bf16[320,128]{1,0:T(8,128)(2,1)S(1)}, u32[]{:S(2)}, u32[]{:S(2)}) %collective-permute-start.20) | collective-permute-done | bytes 81952 | tf_op jit(solution)/shard_map/ppermute | solution.py:34
  39.0 0.0 collective-permute-start.23
  39.0 0.5 %collective-permute-done.21.refs_11_ = bf16[320,128]{1,0:T(8,128)(2,1)S(1)} collective-permute-done((bf16[320,128]{1,0:T(8,128)(2,1)S(1)}, bf16[320,128]{1,0:T(8,128)(2,1)S(1)}, u32[]{:S(2)}, u32[]{:S(2)}) %collective-permute-start.21) | collective-permute-done | bytes 81952 | tf_op jit(solution)/shard_map/ppermute | solution.py:34
  39.5 0.0 collective-permute-done.17.refs_3_
  39.5 3.0 %spatial_grads.1 = (f32[9,320,320]{2,1,0:T(8,128)}, bf16[320,128]{1,0:T(8,128)(2,1)}) custom-call(bf16[320,128]{1,0:T(8,128)(2,1)S(1)} %add_convert_fusion.field_ref.refs_0_, bf16[320,128]{1,0:T(8,128)(2,1)S(1)} %collective-permute-done.16.refs_1_, bf16[320,128]{1,0:T(8,128)(2,1)S(1)} %collective-permute-done.14.sibling_ref.refs_2_, ...), custom_call_target="tpu_custom_call" | custom-call | tf_op jit(solution)/shard_map/spatial_grads/pallas_call | solution.py:297
  42.5 0.0 collective-permute-done.15.refs_4_.refs_5_
  42.6 0.1 collective-permute-start.24
  42.7 0.0 copy-done.2
  42.7 1.8 %temporal_forward.1 = bf16[320,128]{1,0:T(8,128)(2,1)} custom-call(bf16[320,128]{1,0:T(8,128)(2,1)S(1)} %spatial_forward.1.refs_0_, bf16[320,128]{1,0:T(8,128)(2,1)S(1)} %collective-permute-done.8.refs_1_, bf16[320,128]{1,0:T(8,128)(2,1)S(1)} %collective-permute-done.9.refs_2_, bf16[320,128]{1,0:T(8,128)(2,1)S(1)} %collective-permute-done.10.refs_3_, ...), custom_call_target="tpu_custom_call" | custom-call | tf_op jit(solution)/shard_map/temporal_forward/pallas_call | solution.py:161
  44.5 0.0 collective-permute-done.22.refs_1_
  44.5 0.0 collective-permute-done.23.refs_4_
  44.5 0.0 collective-permute-done.24.refs_5_
  44.5 2.0 %temporal_grads.1 = f32[3,320,320]{2,1,0:T(8,128)} custom-call(bf16[2,320,128]{2,1,0:T(8,128)(2,1)S(1)} %get-tuple-element.51.refs_0_, bf16[2,320,128]{2,1,0:T(8,128)(2,1)S(1)} %collective-permute-done.22.refs_1_, bf16[320,128]{1,0:T(8,128)(2,1)S(1)} %get-tuple-element.55.refs_2_, bf16[320,128]{1,0:T(8,128)(2,1)S(1)} %get-tuple-element.53.refs_3_, ...), custom_call_target="tpu_custom_call" | custom-call | tf_op jit(solution)/shard_map/temporal_grads/pallas_call | solution.py:342
  (12 shorter events, 0.2 us)
Async XLA Ops:
  0.6 14.8 %copy-start.3 = (bf16[320,128]{1,0:T(8,128)(2,1)S(1)}, bf16[320,128]{1,0:T(8,128)(2,1)}, u32[]{:S(2)}) copy-start(bf16[320,128]{1,0:T(8,128)(2,1)} %refs_0_.2) | copy-start | bytes 245764
  0.6 7.6 %collective-permute-start.3 = (bf16[320,128]{1,0:T(8,128)(2,1)}, bf16[320,128]{1,0:T(8,128)(2,1)S(1)}, u32[]{:S(2)}, u32[]{:S(2)}) collective-permute-start(bf16[320,128]{1,0:T(8,128)(2,1)} %refs_0_.1), channel_id=1, source_target_pairs={{0,8},{4,12},{8,0},{12,4},{1,9},{5,13},{9,1},{13,5},{2,10},{6,14},... | collective-permute-start | bytes 245768 | tf_op jit(solution)/shard_map/ppermute | solution.py:34
  3.6 11.0 %collective-permute-start.2 = (bf16[320,128]{1,0:T(8,128)(2,1)}, bf16[320,128]{1,0:T(8,128)(2,1)S(1)}, u32[]{:S(2)}, u32[]{:S(2)}) collective-permute-start(bf16[320,128]{1,0:T(8,128)(2,1)} %refs_0_.2), channel_id=1, source_target_pairs={{0,3},{1,0},{2,1},{3,2},{4,7},{5,4},{6,5},{7,6},{8,11},{9,8},{10,9... | collective-permute-start | bytes 245768 | tf_op jit(solution)/shard_map/ppermute | solution.py:34
  7.2 7.4 %collective-permute-start.1 = (bf16[320,128]{1,0:T(8,128)(2,1)}, bf16[320,128]{1,0:T(8,128)(2,1)S(1)}, u32[]{:S(2)}, u32[]{:S(2)}) collective-permute-start(bf16[320,128]{1,0:T(8,128)(2,1)} %refs_0_.2), channel_id=1, source_target_pairs={{0,2},{1,3},{2,0},{3,1},{4,6},{5,7},{6,4},{7,5},{8,10},{9,11},{10,... | collective-permute-start | bytes 245768 | tf_op jit(solution)/shard_map/ppermute | solution.py:34
  7.2 7.4 %collective-permute-start = (bf16[320,128]{1,0:T(8,128)(2,1)}, bf16[320,128]{1,0:T(8,128)(2,1)S(1)}, u32[]{:S(2)}, u32[]{:S(2)}) collective-permute-start(bf16[320,128]{1,0:T(8,128)(2,1)} %refs_0_.2), channel_id=1, source_target_pairs={{0,1},{1,2},{2,3},{3,0},{4,5},{5,6},{6,7},{7,4},{8,9},{9,10},{10,1... | collective-permute-start | bytes 245768 | tf_op jit(solution)/shard_map/ppermute | solution.py:34
  8.3 7.2 %collective-permute-start.4 = (bf16[320,128]{1,0:T(8,128)(2,1)}, bf16[320,128]{1,0:T(8,128)(2,1)S(1)}, u32[]{:S(2)}, u32[]{:S(2)}) collective-permute-start(bf16[320,128]{1,0:T(8,128)(2,1)} %refs_0_.2), channel_id=1, source_target_pairs={{0,4},{4,0},{8,12},{12,8},{1,5},{5,1},{9,13},{13,9},{2,6},{6,2},{1... | collective-permute-start | bytes 245768 | tf_op jit(solution)/shard_map/ppermute | solution.py:39
  8.3 10.0 %copy-start = (bf16[9,320,1280]{2,1,0:T(8,128)(2,1)S(1)}, bf16[9,320,1280]{2,1,0:T(8,128)(2,1)}, u32[]{:S(2)}) copy-start(bf16[9,320,1280]{2,1,0:T(8,128)(2,1)} %refs_8_.1) | copy-start | bytes 22118404
  8.3 1.8 %copy-start.1 = (bf16[3,320,1280]{2,1,0:T(8,128)(2,1)S(1)}, bf16[3,320,1280]{2,1,0:T(8,128)(2,1)}, u32[]{:S(2)}) copy-start(bf16[3,320,1280]{2,1,0:T(8,128)(2,1)} %refs_6_.1) | copy-start | bytes 7372804
  10.1 1.1 %copy-start.4 = (bf16[320,128]{1,0:T(8,128)(2,1)S(1)}, bf16[320,128]{1,0:T(8,128)(2,1)}, u32[]{:S(2)}) copy-start(bf16[320,128]{1,0:T(8,128)(2,1)} %refs_0_.1) | copy-start | bytes 245764
  12.1 11.5 %collective-permute-start.11 = (bf16[320,128]{1,0:T(8,128)(2,1)S(1)}, bf16[320,128]{1,0:T(8,128)(2,1)S(1)}, u32[]{:S(2)}, u32[]{:S(2)}) collective-permute-start(bf16[320,128]{1,0:T(8,128)(2,1)S(1)} %get-tuple-element.29), channel_id=1, source_target_pairs={{0,1},{1,2},{2,3},{3,0},{4,5},{5,6},{6,7},{7,4},{8,9},{9,10},{10,1... | collective-permute-start | bytes 245768 | tf_op jit(solution)/shard_map/ppermute | solution.py:34
  14.7 2.8 %collective-permute-start.5 = (bf16[320,128]{1,0:T(8,128)(2,1)S(1)}, bf16[320,128]{1,0:T(8,128)(2,1)S(1)}, u32[]{:S(2)}, u32[]{:S(2)}) collective-permute-start(bf16[320,128]{1,0:T(8,128)(2,1)S(1)} %collective-permute-done.refs_1_), channel_id=1, source_target_pairs={{0,4},{4,0},{8,12},{12,8},{1,5},{5,1},{9,13},{13,9},{2,6},{6,2},{1... | collective-permute-start | bytes 245768 | tf_op jit(solution)/shard_map/ppermute | solution.py:39
  14.9 3.3 %collective-permute-start.6 = (bf16[320,128]{1,0:T(8,128)(2,1)S(1)}, bf16[320,128]{1,0:T(8,128)(2,1)S(1)}, u32[]{:S(2)}, u32[]{:S(2)}) collective-permute-start(bf16[320,128]{1,0:T(8,128)(2,1)S(1)} %collective-permute-done.1.refs_2_), channel_id=1, source_target_pairs={{0,4},{4,0},{8,12},{12,8},{1,5},{5,1},{9,13},{13,9},{2,6},{6,2},{1... | collective-permute-start | bytes 245768 | tf_op jit(solution)/shard_map/ppermute | solution.py:39
  15.2 3.0 %collective-permute-start.7 = (bf16[320,128]{1,0:T(8,128)(2,1)S(1)}, bf16[320,128]{1,0:T(8,128)(2,1)S(1)}, u32[]{:S(2)}, u32[]{:S(2)}) collective-permute-start(bf16[320,128]{1,0:T(8,128)(2,1)S(1)} %collective-permute-done.2.refs_3_), channel_id=1, source_target_pairs={{0,4},{4,0},{8,12},{12,8},{1,5},{5,1},{9,13},{13,9},{2,6},{6,2},{1... | collective-permute-start | bytes 245768 | tf_op jit(solution)/shard_map/ppermute | solution.py:39
  15.5 8.7 %collective-permute-start.12 = (bf16[320,128]{1,0:T(8,128)(2,1)S(1)}, bf16[320,128]{1,0:T(8,128)(2,1)S(1)}, u32[]{:S(2)}, u32[]{:S(2)}) collective-permute-start(bf16[320,128]{1,0:T(8,128)(2,1)S(1)} %get-tuple-element.30), channel_id=1, source_target_pairs={{0,2},{1,3},{2,0},{3,1},{4,6},{5,7},{6,4},{7,5},{8,10},{9,11},{10,... | collective-permute-start | bytes 245768 | tf_op jit(solution)/shard_map/ppermute | solution.py:34
  17.4 6.8 %collective-permute-start.13 = (bf16[320,128]{1,0:T(8,128)(2,1)S(1)}, bf16[320,128]{1,0:T(8,128)(2,1)S(1)}, u32[]{:S(2)}, u32[]{:S(2)}) collective-permute-start(bf16[320,128]{1,0:T(8,128)(2,1)S(1)} %get-tuple-element.31), channel_id=1, source_target_pairs={{0,3},{1,0},{2,1},{3,2},{4,7},{5,4},{6,5},{7,6},{8,11},{9,8},{10,9... | collective-permute-start | bytes 245768 | tf_op jit(solution)/shard_map/ppermute | solution.py:34
  20.9 8.4 %collective-permute-start.10 = (bf16[320,128]{1,0:T(8,128)(2,1)S(1)}, bf16[320,128]{1,0:T(8,128)(2,1)S(1)}, u32[]{:S(2)}, u32[]{:S(2)}) collective-permute-start(bf16[320,128]{1,0:T(8,128)(2,1)S(1)} %spatial_forward.1.refs_0_), channel_id=1, source_target_pairs={{0,3},{1,0},{2,1},{3,2},{4,7},{5,4},{6,5},{7,6},{8,11},{9,8},{10,9... | collective-permute-start | bytes 245768 | tf_op jit(solution)/shard_map/ppermute | solution.py:34
  22.7 8.7 %collective-permute-start.9 = (bf16[320,128]{1,0:T(8,128)(2,1)S(1)}, bf16[320,128]{1,0:T(8,128)(2,1)S(1)}, u32[]{:S(2)}, u32[]{:S(2)}) collective-permute-start(bf16[320,128]{1,0:T(8,128)(2,1)S(1)} %spatial_forward.1.refs_0_), channel_id=1, source_target_pairs={{0,2},{1,3},{2,0},{3,1},{4,6},{5,7},{6,4},{7,5},{8,10},{9,11},{10,... | collective-permute-start | bytes 245768 | tf_op jit(solution)/shard_map/ppermute | solution.py:34
  23.6 9.5 %collective-permute-start.8 = (bf16[320,128]{1,0:T(8,128)(2,1)S(1)}, bf16[320,128]{1,0:T(8,128)(2,1)S(1)}, u32[]{:S(2)}, u32[]{:S(2)}) collective-permute-start(bf16[320,128]{1,0:T(8,128)(2,1)S(1)} %spatial_forward.1.refs_0_), channel_id=1, source_target_pairs={{0,1},{1,2},{2,3},{3,0},{4,5},{5,6},{6,7},{7,4},{8,9},{9,10},{10,1... | collective-permute-start | bytes 245768 | tf_op jit(solution)/shard_map/ppermute | solution.py:34
  24.3 9.6 %collective-permute-start.16 = (bf16[320,128]{1,0:T(8,128)(2,1)S(1)}, bf16[320,128]{1,0:T(8,128)(2,1)S(1)}, u32[]{:S(2)}, u32[]{:S(2)}) collective-permute-start(bf16[320,128]{1,0:T(8,128)(2,1)S(1)} %add_convert_fusion.field_ref.refs_0_), channel_id=1, source_target_pairs={{0,8},{4,12},{8,0},{12,4},{1,9},{5,13},{9,1},{13,5},{2,10},{6,14},... | collective-permute-start | bytes 245768 | tf_op jit(solution)/shard_map/ppermute | solution.py:34
  24.9 1.3 %collective-permute-start.14 = (bf16[320,128]{1,0:T(8,128)(2,1)S(1)}, bf16[320,128]{1,0:T(8,128)(2,1)S(1)}, u32[]{:S(2)}, u32[]{:S(2)}) collective-permute-start(bf16[320,128]{1,0:T(8,128)(2,1)S(1)} %add_convert_fusion.field_ref.refs_0_), channel_id=1, source_target_pairs={{0,4},{4,0},{8,12},{12,8},{1,5},{5,1},{9,13},{13,9},{2,6},{6,2},{1... | collective-permute-start | bytes 245768 | tf_op jit(solution)/shard_map/ppermute | solution.py:39
  26.2 8.5 %collective-permute-start.18 = (bf16[2,320,128]{2,1,0:T(8,128)(2,1)S(1)}, bf16[2,320,128]{2,1,0:T(8,128)(2,1)S(1)}, u32[]{:S(2)}, u32[]{:S(2)}) collective-permute-start(bf16[2,320,128]{2,1,0:T(8,128)(2,1)S(1)} %pad_maximum_fusion.3), channel_id=1, source_target_pairs={{0,8},{4,12},{8,0},{12,4},{1,9},{5,13},{9,1},{13,5},{2,10},{6,14},... | collective-permute-start | bytes 491528 | tf_op jit(solution)/shard_map/ppermute | solution.py:34
  27.6 15.0 %copy-start.2 = (bf16[3,320,1280]{2,1,0:T(8,128)(2,1)S(1)}, bf16[3,320,1280]{2,1,0:T(8,128)(2,1)}, u32[]{:S(2)}) copy-start(bf16[3,320,1280]{2,1,0:T(8,128)(2,1)} %refs_6_.1) | copy-start | bytes 7372804
  29.3 7.3 %collective-permute-start.19 = (bf16[320,128]{1,0:T(8,128)(2,1)S(1)}, bf16[320,128]{1,0:T(8,128)(2,1)S(1)}, u32[]{:S(2)}, u32[]{:S(2)}) collective-permute-start(bf16[320,128]{1,0:T(8,128)(2,1)S(1)} %get-tuple-element.38), channel_id=1, source_target_pairs={{0,1},{1,2},{2,3},{3,0},{4,5},{5,6},{6,7},{7,4},{8,9},{9,10},{10,1... | collective-permute-start | bytes 245768 | tf_op jit(solution)/shard_map/ppermute | solution.py:34
  31.4 7.6 %collective-permute-start.20 = (bf16[320,128]{1,0:T(8,128)(2,1)S(1)}, bf16[320,128]{1,0:T(8,128)(2,1)S(1)}, u32[]{:S(2)}, u32[]{:S(2)}) collective-permute-start(bf16[320,128]{1,0:T(8,128)(2,1)S(1)} %get-tuple-element.39), channel_id=1, source_target_pairs={{0,2},{1,3},{2,0},{3,1},{4,6},{5,7},{6,4},{7,5},{8,10},{9,11},{10,... | collective-permute-start | bytes 245768 | tf_op jit(solution)/shard_map/ppermute | solution.py:34
  33.2 9.3 %collective-permute-start.15 = (bf16[4,320,128]{2,1,0:T(8,128)(2,1)S(1)}, bf16[4,320,128]{2,1,0:T(8,128)(2,1)S(1)}, u32[]{:S(2)}, u32[]{:S(2)}) collective-permute-start(bf16[4,320,128]{2,1,0:T(8,128)(2,1)S(1)} %pad_maximum_fusion), channel_id=1, source_target_pairs={{0,8},{4,12},{8,0},{12,4},{1,9},{5,13},{9,1},{13,5},{2,10},{6,14},... | collective-permute-start | bytes 983048 | tf_op jit(solution)/shard_map/ppermute | solution.py:34
  33.8 5.6 %collective-permute-start.21 = (bf16[320,128]{1,0:T(8,128)(2,1)S(1)}, bf16[320,128]{1,0:T(8,128)(2,1)S(1)}, u32[]{:S(2)}, u32[]{:S(2)}) collective-permute-start(bf16[320,128]{1,0:T(8,128)(2,1)S(1)} %get-tuple-element.40), channel_id=1, source_target_pairs={{0,3},{1,0},{2,1},{3,2},{4,7},{5,4},{6,5},{7,6},{8,11},{9,8},{10,9... | collective-permute-start | bytes 245768 | tf_op jit(solution)/shard_map/ppermute | solution.py:34
  34.7 4.8 %collective-permute-start.17 = (bf16[320,128]{1,0:T(8,128)(2,1)S(1)}, bf16[320,128]{1,0:T(8,128)(2,1)S(1)}, u32[]{:S(2)}, u32[]{:S(2)}) collective-permute-start(bf16[320,128]{1,0:T(8,128)(2,1)S(1)} %collective-permute-done.16.refs_1_), channel_id=1, source_target_pairs={{0,4},{4,0},{8,12},{12,8},{1,5},{5,1},{9,13},{13,9},{2,6},{6,2},{1... | collective-permute-start | bytes 245768 | tf_op jit(solution)/shard_map/ppermute | solution.py:39
  36.6 7.9 %collective-permute-start.22 = (bf16[2,320,128]{2,1,0:T(8,128)(2,1)S(1)}, bf16[2,320,128]{2,1,0:T(8,128)(2,1)S(1)}, u32[]{:S(2)}, u32[]{:S(2)}) collective-permute-start(bf16[2,320,128]{2,1,0:T(8,128)(2,1)S(1)} %get-tuple-element.51.refs_0_), channel_id=1, source_target_pairs={{0,4},{4,0},{8,12},{12,8},{1,5},{5,1},{9,13},{13,9},{2,6},{6,2},{1... | collective-permute-start | bytes 491528 | tf_op jit(solution)/shard_map/ppermute | solution.py:39
  39.0 5.5 %collective-permute-start.23 = (bf16[320,128]{1,0:T(8,128)(2,1)S(1)}, bf16[320,128]{1,0:T(8,128)(2,1)S(1)}, u32[]{:S(2)}, u32[]{:S(2)}) collective-permute-start(bf16[320,128]{1,0:T(8,128)(2,1)S(1)} %get-tuple-element.54), channel_id=1, source_target_pairs={{0,4},{4,0},{8,12},{12,8},{1,5},{5,1},{9,13},{13,9},{2,6},{6,2},{1... | collective-permute-start | bytes 245768 | tf_op jit(solution)/shard_map/ppermute | solution.py:39
  42.6 1.9 %collective-permute-start.24 = (bf16[320,128]{1,0:T(8,128)(2,1)S(1)}, bf16[320,128]{1,0:T(8,128)(2,1)S(1)}, u32[]{:S(2)}, u32[]{:S(2)}) collective-permute-start(bf16[320,128]{1,0:T(8,128)(2,1)S(1)} %get-tuple-element.52), channel_id=1, source_target_pairs={{0,4},{4,0},{8,12},{12,8},{1,5},{5,1},{9,13},{13,9},{2,6},{6,2},{1... | collective-permute-start | bytes 245768 | tf_op jit(solution)/shard_map/ppermute | solution.py:39
